TPU v7x, 128 devices: a whole 4x4x4 slice. The times are simulated.
128 devices in a mesh: row: 8 (over x, core), col: 16 (over y, z).
Axes of the slice: x: 4, y: 4, z: 4, core: 2. Of those that a mesh axis runs over, the one named last changes fastest.
Arguments:
- factor: float32 [4, 8, 1024, 2048], P(None, 'row', None, 'col'), as said below
- cross_cov: float32 [4, 8, 1024, 1024], P(None, 'row', 'col'), may hold values from -6 to 6
Outputs:
- overwritten: float32 [4, 8, 1024, 1024], P(None, 'row', 'col')
Inputs may be any that keep to these rules, and one draw needn't show every extreme that they name: The diagonal entries of the factor lie between 1 and 3.
All inputs are finite; a program needn't handle non-finite values.
Results may differ from a plain program's by a relative error of at most 0.00014.
Values sent between devices are 32-bit elements; how exact they have to be, the bound alone decides.
No kernel may reach another device: no remote copies, remote signals or barrier semaphores. Data moves between devices by JAX's collectives and lax.ppermute only.
A program may use at most 128 MiB of HBM per device.

v0:
```python
import jax
import jax.numpy as jnp
from jax import lax
from jax.sharding import PartitionSpec as P


def broadcast(x, axis, root):
    mine = lax.axis_index(axis) == root
    return lax.psum(jnp.where(mine, x, jnp.zeros_like(x)), axis)


def spread(block, root):
    return broadcast(block, "row", root)


def reduce_turn(partial_value):
    return lax.psum_scatter(partial_value, "col", scatter_dimension=0, tiled=True)


def shards(factor, cross_cov):
    col_id = lax.axis_index("col")
    row_id = lax.axis_index("row")
    lead_rows = factor[0, 0]
    own_rhs = cross_cov[0, 0]
    block_row, block_rhs = (
        lax.all_gather(lead_rows, "col", axis=1, tiled=True),
        lax.all_gather(own_rhs, "col", axis=0, tiled=True),
    )
    block_size = block_row.shape[0]
    first_block = lax.linalg.triangular_solve(
        block_row[:, :block_size], block_rhs, left_side=True, lower=True
    )
    first_block = spread(first_block, 0)
    second_rhs = block_rhs - jnp.dot(
        block_row[:, :block_size], first_block, precision=lax.Precision.HIGHEST
    )
    second_block = lax.linalg.triangular_solve(
        block_row[:, block_size:], second_rhs, left_side=True, lower=True
    )
    second_block = spread(second_block, 1)
    solved = jnp.concatenate([first_block, second_block], 0)
    local_factor = factor[:, 0]
    col_width = local_factor.shape[2]
    my_rows = lax.dynamic_slice_in_dim(solved, col_id * col_width, col_width, 0)
    pieces = []
    for turn_id in range(local_factor.shape[0]):
        partial_value = jnp.dot(local_factor[turn_id], my_rows, precision=lax.Precision.HIGHEST)
        pieces.append(reduce_turn(partial_value))
    reduced = jnp.stack(pieces, 0)
    updated = cross_cov[:, 0] - reduced
    slice_rows = own_rhs.shape[0]
    first_piece = lax.dynamic_slice_in_dim(first_block, col_id * slice_rows, slice_rows, 0)
    second_piece = lax.dynamic_slice_in_dim(second_block, col_id * slice_rows, slice_rows, 0)
    head_rows = jnp.where(
        row_id == 0, first_piece, jnp.where(row_id == 1, second_piece, updated[0])
    )
    result = jnp.concatenate([head_rows[None], updated[1:]], 0)
    return result[:, None]


def solution(mesh):
    placed = (P(None, "row", None, "col"), P(None, "row", "col", None))
    return jax.shard_map(
        shards, mesh=mesh, in_specs=placed, out_specs=P(None, "row", "col", None), check_vma=False
    )
```

profile of v0, /device:TPU:5, one launch (start us, length us, event | category | flops | bytes accessed | tf_op | source)
XLA Modules:
  0.0 873.6 jit_solution(348379081481082438)
XLA Ops:
  10.5 53.0 %all-gather.7.cloned.1.call-done = f32[1,1,1024,1024]{3,1,0,2:T(1,128)} async-done(((f32[1,1,64,1024]{3,1,0,2:T(1,128)}), f32[1,1,1024,1024]{3,1,0,2:T(1,128)}) %all-gather.7.cloned.1.call-update) | async-done | bytes 4194320 | tf_op jit(solution)/shard_map/all_gather | solution.py:27
  63.5 11.0 %copy.10 = f32[1,1,1024,1024]{2,3,1,0:T(8,128)} copy(f32[1,1,1024,1024]{3,1,0,2:T(1,128)} %all-gather.7.cloned.1.call-done) | data formatting | bytes 8388608 | tf_op jit(solution)/shard_map/all_gather | solution.py:27
  74.5 68.4 %all-gather.5.cloned.1.call-done = f32[1,1,1024,2048]{3,2,1,0:T(8,128)} async-done(((f32[1,1,1024,128]{3,2,1,0:T(8,128)}), f32[1,1,1024,2048]{3,2,1,0:T(8,128)}) %all-gather.5.cloned.1.call-update) | async-done | bytes 8388624 | tf_op jit(solution)/shard_map/all_gather | solution.py:26
  142.9 8.0 slice_select_fusion
  150.9 22.5 %while.4 = (s32[]{:T(128)}, f32[1024,1024]{1,0:T(8,128)}, s32[8,2]{0,1:T(2,128)S(1)}, f32[8,128,128]{2,1,0:T(8,128)S(1)}, s32[]{:T(128)}) while((s32[]{:T(128)}, f32[1024,1024]{1,0:T(8,128)}, s32[8,2]{0,1:T(2,128)S(1)}, f32[8,128,128]{2,1,0:T(8,128)S(1)}, s32[]{:T(128)}) %tuple.80), condition=%wide.while_cond, body=%wide.while_body.sunk | while | flops 2 | bytes 131181 | solution.py:30
  173.4 78.8 %custom-call.4 = f32[8,128,128]{1,2,0:T(8,128)S(1)} custom-call(f32[8,128,128]{2,1,0:T(8,128)S(1)} %get-tuple-element.20), custom_call_target="InvertDiagBlocksLowerTriangular" | custom-call | tf_op jit(solution)/shard_map/triangular_solve/custom-call.1 | solution.py:30
  270.3 5.4 convolution_subtract_fusion.5
  276.4 6.0 convolution_subtract_fusion.3
  283.1 7.5 convolution_subtract_fusion.8
  293.8 22.5 %while.5 = (s32[]{:T(128)}, f32[1024,1024]{1,0:T(8,128)}, s32[8,2]{0,1:T(2,128)S(1)}, f32[8,128,128]{2,1,0:T(8,128)S(1)}, s32[]{:T(128)}) while((s32[]{:T(128)}, f32[1024,1024]{1,0:T(8,128)}, s32[8,2]{0,1:T(2,128)S(1)}, f32[8,128,128]{2,1,0:T(8,128)S(1)}, s32[]{:T(128)}) %tuple.102), condition=%wide.while_cond.clone, body=%wide.while_body.clone.sunk | while | flops 2 | bytes 131181 | solution.py:37
  316.3 78.6 %custom-call.5 = f32[8,128,128]{1,2,0:T(8,128)S(1)} custom-call(f32[8,128,128]{2,1,0:T(8,128)S(1)} %get-tuple-element.21), custom_call_target="InvertDiagBlocksLowerTriangular" | custom-call | tf_op jit(solution)/shard_map/triangular_solve/custom-call.1 | solution.py:37
  394.9 30.9 %bitcast_subtract_fusion = f32[1024,1024]{0,1:T(8,128)S(1)} fusion(f32[1024,1024]{1,0:T(8,128)} %all-reduce.3.cloned.1.call-done, f32[1024,2048]{1,0:T(8,128)} %bitcast.173, f32[1,1,1024,1024]{2,3,1,0:T(8,128)} %copy.10), kind=kOutput, calls=%fused_computation.7 | convolution fusion | flops 12885950464 | bytes 16777216 | tf_op jit(solution)/shard_map/dot_general | solution.py:34
  442.5 5.4 convolution_subtract_fusion.4
  448.5 6.2 convolution_subtract_fusion.2
  455.3 7.3 convolution_subtract_fusion.6
  465.9 70.1 %all-reduce.5.cloned.1.call-done = f32[1024,1024]{1,0:T(8,128)} async-done(((f32[1024,1024]{1,0:T(8,128)}), f32[1024,1024]{1,0:T(8,128)}) %all-reduce.5.cloned.1.call-update) | async-done | bytes 4194320 | tf_op jit(solution)/shard_map/psum | solution.py:9
  536.0 6.2 convolution_bitcast_fusion.3
  542.3 6.1 convolution_bitcast_fusion.2
  548.5 6.1 convolution_bitcast_fusion.1
  554.7 6.2 convolution_bitcast_fusion
  561.0 60.3 %reduce-scatter.5.cloned.1.call-done = f32[64,1024]{1,0:T(8,128)} async-done(((f32[1024,1024]{1,0:T(8,128)}), f32[64,1024]{1,0:T(8,128)}) %reduce-scatter.5.cloned.1.call-update) | async-done | bytes 262160 | tf_op jit(solution)/shard_map/reduce_scatter | solution.py:17
  621.3 80.6 %reduce-scatter.7.cloned.1.call-done = f32[64,1024]{1,0:T(8,128)} async-done(((f32[1024,1024]{1,0:T(8,128)}), f32[64,1024]{1,0:T(8,128)}) %reduce-scatter.7.cloned.1.call-update) | async-done | bytes 262160 | tf_op jit(solution)/shard_map/reduce_scatter | solution.py:17
  701.9 80.4 %reduce-scatter.9.cloned.1.call-done = f32[64,1024]{1,0:T(8,128)} async-done(((f32[1024,1024]{1,0:T(8,128)}), f32[64,1024]{1,0:T(8,128)}) %reduce-scatter.9.cloned.1.call-update) | async-done | bytes 262160 | tf_op jit(solution)/shard_map/reduce_scatter | solution.py:17
  782.3 80.7 %reduce-scatter.11.cloned.1.call-done = f32[64,1024]{1,0:T(8,128)} async-done(((f32[1024,1024]{1,0:T(8,128)}), f32[64,1024]{1,0:T(8,128)}) %reduce-scatter.11.cloned.1.call-update) | async-done | bytes 262160 | tf_op jit(solution)/shard_map/reduce_scatter | solution.py:17
  (108 shorter events, 96.1 us)
Async XLA Ops:
  6.5 57.0 %all-gather.7.cloned.1.call-start = ((), (), s32[]{:S(2)}) async-start(), calls=%async_computation.11 | async-start | bytes 4456448 | tf_op jit(solution)/shard_map/all_gather | solution.py:27
  8.5 134.4 %all-gather.5.cloned.1.call-start = ((), (), s32[]{:S(2)}) async-start(), calls=%async_computation.10 | async-start | bytes 8912896 | tf_op jit(solution)/shard_map/all_gather | solution.py:26
  10.5 384.5 %all-reduce.3.cloned.1.call-start = ((), (), s32[]{:S(2)}) async-start(), calls=%async_computation.4 | async-start | bytes 8388608 | tf_op jit(solution)/shard_map/psum | solution.py:9
  252.2 4.8 copy-start
  293.8 242.3 %all-reduce.5.cloned.1.call-start = ((), (), s32[]{:S(2)}) async-start(), calls=%async_computation.5 | async-start | bytes 8388608 | tf_op jit(solution)/shard_map/psum | solution.py:9
  465.8 70.2 %copy-start.1 = (f32[4,1,1024,128]{3,2,1,0:T(8,128)S(1)}, f32[4,1,1024,128]{3,2,1,0:T(8,128)}, u32[]{:S(2)}) copy-start(f32[4,1,1024,128]{3,2,1,0:T(8,128)} %param.4) | copy-start | bytes 6291460
  465.8 155.4 %reduce-scatter.5.cloned.1.call-start = ((), (), s32[]{:S(2)}) async-start(), calls=%async_computation.6 | async-start | bytes 4456448 | tf_op jit(solution)/shard_map/reduce_scatter | solution.py:17
  542.2 159.6 %reduce-scatter.7.cloned.1.call-start = ((), (), s32[]{:S(2)}) async-start(), calls=%async_computation.7 | async-start | bytes 4456448 | tf_op jit(solution)/shard_map/reduce_scatter | solution.py:17
  548.4 233.8 %reduce-scatter.9.cloned.1.call-start = ((), (), s32[]{:S(2)}) async-start(), calls=%async_computation.8 | async-start | bytes 4456448 | tf_op jit(solution)/shard_map/reduce_scatter | solution.py:17
  554.6 308.4 %reduce-scatter.11.cloned.1.call-start = ((), (), s32[]{:S(2)}) async-start(), calls=%async_computation.9 | async-start | bytes 4456448 | tf_op jit(solution)/shard_map/reduce_scatter | solution.py:17
  560.9 302.1 %copy-start.2 = (f32[4,1,64,1024]{3,2,1,0:T(8,128)S(1)}, f32[4,1,64,1024]{3,2,1,0:T(8,128)}, u32[]{:S(2)}) copy-start(f32[4,1,64,1024]{3,2,1,0:T(8,128)} %param.5) | copy-start | bytes 3145732
Sparse Core Ops, SparseCore 0:
  9.5 53.9 all-gather.6
  65.6 77.2 all-gather.4
  293.9 71.0 all-reduce.2
  466.0 70.0 all-reduce.4
  542.4 78.8 reduce-scatter.4
  624.8 77.0 reduce-scatter.6
  705.2 76.9 reduce-scatter.8
  786.0 77.0 reduce-scatter.10
where the time goes:
time: 880 us; the launch traced here: 874 us
  waiting for transfers between devices  494 us (56%)
  other arithmetic  174 us (20%)
  matrix products  132 us (15%)
  local copies, waits for them, and re-layouts  59.6 us (7%)
  between operations  14.1 us (2%)
    reduce_scatter x4, waiting for transfers between devices, reduce_turn(): lax.psum_scatter(partial_value, 'col', scatter_dimension=0, tiled=True)  302 us
    another operation x2, other arithmetic, shards(): lax.linalg.triangular_solve(block_row[:, block_size:], second_rhs, left_s...  86.6 us
    another operation x2, other arithmetic, shards(): lax.linalg.triangular_solve(block_row[:, :block_size], block_rhs, left_si...  78.8 us
    psum x2, waiting for transfers between devices, broadcast(): return lax.psum(jnp.where(mine, x, jnp.zeros_like(x)), axis)  70.1 us
    all_gather x1, waiting for transfers between devices, shards(): lax.all_gather(lead_rows, 'col', axis=1, tiled=True)  68.4 us
    all_gather x1, waiting for transfers between devices, shards(): lax.all_gather(own_rhs, 'col', axis=0, tiled=True)  53 us
    another operation x15, matrix products, shards(): lax.linalg.triangular_solve(block_row[:, :block_size], block_rhs, left_si...  38.9 us
    another operation x15, matrix products, shards(): lax.linalg.triangular_solve(block_row[:, block_size:], second_rhs, left_s...  37.4 us
  transfers between devices with their start and end apart: 8, of which 7 were waited for; matrix products, arithmetic and copies ran while one was open for 15% of the time, Pallas kernels for 0%

commit v1 on v0

v1 whole, which is shorter than its diff:
```python
import jax
import jax.numpy as jnp
import numpy as np
from jax import lax
from jax.experimental import pallas as pl
from jax.experimental.pallas import tpu as pltpu
from jax.sharding import Mesh, PartitionSpec as P

ROW = ("x", "core")
COL = ("yh", "yl", "z")
F32 = jnp.float32
BF16 = jnp.bfloat16
TILE = 128
PARAMS = pltpu.CompilerParams(vmem_limit_bytes=48 * 2**20)
VM = pl.BlockSpec(memory_space=pltpu.VMEM)
SM = pl.BlockSpec(memory_space=pltpu.SMEM)


def split(value):
    high = value.astype(BF16)
    return high, (value - high.astype(F32)).astype(BF16)


def mm(a, b):
    return jnp.dot(a, b, preferred_element_type=F32)


def pack_left(value):
    return jnp.concatenate(split(value), 1)


def pack_right(value):
    high, low = split(value)
    return jnp.concatenate(
        [jnp.concatenate([high, low], 1), jnp.concatenate([high, jnp.zeros_like(low)], 1)], 0
    )


def packed_product(left, right):
    out = mm(left, right)
    return out[:, :TILE] + out[:, TILE:]


def full_dot(a, b):
    return jnp.dot(a, b, precision=lax.Precision.HIGHEST, preferred_element_type=F32)


def invert_body(info, lead_ref, out_ref):
    out_ref[...] = lead_ref[...]

    @pl.when(info[0] == 1)
    def _():
        start = pl.multiple_of(info[1] * TILE, TILE)
        block = lead_ref[pl.ds(start, TILE), :]
        i = lax.broadcasted_iota(jnp.int32, (TILE, TILE), 0)
        j = lax.broadcasted_iota(jnp.int32, (TILE, TILE), 1)
        zero = jnp.zeros((TILE, TILE), F32)
        inverse = jnp.where(i == j, 1.0 / jnp.where(i == j, block, 1.0), zero)
        step = 1
        while step < TILE:
            below = ((i // (2 * step)) == (j // (2 * step))) & ((i // step) > (j // step))
            corner = jnp.where(below, block, zero)
            inverse = inverse - full_dot(inverse, full_dot(corner, inverse))
            step *= 2
        out_ref[pl.ds(start, TILE), :] = inverse


def invert_diagonal(info, lead):
    return pl.pallas_call(
        invert_body,
        out_shape=jax.ShapeDtypeStruct(lead.shape, F32),
        in_specs=[SM, VM],
        out_specs=VM,
        compiler_params=PARAMS,
        name="invert_diagonal",
    )(info, lead)


def solve_body(tri_ref, rhs_ref, out_ref):
    count = tri_ref.shape[0]
    out_ref[...] = rhs_ref[...]
    for k in range(count):
        here = pl.ds(k * TILE, TILE)
        solved = packed_product(pack_left(tri_ref[k, here, :]), pack_right(out_ref[here, :]))
        out_ref[here, :] = solved
        right = pack_right(solved)
        for i in range(k + 1, count):
            there = pl.ds(i * TILE, TILE)
            out_ref[there, :] = out_ref[there, :] - packed_product(pack_left(tri_ref[k, there, :]), right)


def solve(tri, rhs):
    return pl.pallas_call(
        solve_body,
        out_shape=jax.ShapeDtypeStruct(rhs.shape, F32),
        in_specs=[VM, VM],
        out_specs=VM,
        compiler_params=PARAMS,
        name="block_solve",
    )(tri, rhs)


def residual_body(tri_ref, rhs_ref, x_ref, out_ref):
    count = tri_ref.shape[0]
    for k in range(count):
        right = pack_right(x_ref[pl.ds(k * TILE, TILE), :])
        for i in range(count):
            there = pl.ds(i * TILE, TILE)
            base = rhs_ref[there, :] if k == 0 else out_ref[there, :]
            out_ref[there, :] = base - packed_product(pack_left(tri_ref[k, there, :]), right)


def residual(tri, rhs, x):
    return pl.pallas_call(
        residual_body,
        out_shape=jax.ShapeDtypeStruct(rhs.shape, F32),
        in_specs=[VM, VM, VM],
        out_specs=VM,
        compiler_params=PARAMS,
        name="block_residual",
    )(tri, rhs, x)


def update_body(half, info, base_ref, left_ref, own_ref, other_ref, out_ref):
    core = info[0]
    rows = base_ref.shape[0]
    lefts = []
    for side, swap in ((0, core), (1, 1 - core)):
        for q in range(2):
            first = 8 * half + 4 * swap + 2 * q
            lefts.append(split(jnp.concatenate([left_ref[first], left_ref[first + 1]], 1)))
    for pair in range(4):
        cols = pl.ds(pair * 2 * TILE, 2 * TILE)
        total = None
        for side, ref in ((0, own_ref), (1, other_ref)):
            for q in range(2):
                block = jnp.concatenate([ref[q * 8 + 2 * pair], ref[q * 8 + 2 * pair + 1]], 1)
                high, low = split(block)
                left_high, left_low = lefts[2 * side + q]
                term = mm(left_high, high) + (mm(left_high, low) + mm(left_low, high))
                total = term if total is None else total + term
        out_ref[:, cols] = base_ref[:, cols] - total

    slot = info[2]
    offset = pl.multiple_of(info[3], 64)

    if half == 1:

        @pl.when(info[1] == 0)
        def _():
            out_ref[pl.ds(0, 64), :] = base_ref[pl.ds(0, 64), :]

    for ref, want in ((own_ref, 0), (other_ref, 1)):

        @pl.when((info[1] == half) & (info[4] == want))
        def _():
            for n in range(8):
                out_ref[pl.ds(0, 64), pl.ds(n * TILE, TILE)] = ref[slot * 8 + n, pl.ds(offset, 64), :]


def update(half, info, base, left, own, other):
    def body(*refs):
        update_body(half, *refs)

    return pl.pallas_call(
        body,
        out_shape=jax.ShapeDtypeStruct(base.shape, F32),
        in_specs=[SM, VM, VM, VM, VM],
        out_specs=VM,
        compiler_params=PARAMS,
        name="update_first" if half == 0 else "update_second",
    )(info, base, left, own, other)


def deal(x, core, yh, xi, core_from, yh_from):
    half_there = x[512 * (1 - core_from) : 512 * (2 - core_from)]
    half_here = x[512 * core_from : 512 * (core_from + 1)]
    half = jnp.where(
        core == core_from, half_here, lax.ppermute(half_there, "core", [(core_from, 1 - core_from)])
    )
    there = half[256 * (1 - yh_from) : 256 * (2 - yh_from)]
    here = half[256 * yh_from : 256 * (yh_from + 1)]
    quarter = jnp.where(yh == yh_from, here, lax.ppermute(there, "yh", [(yh_from, 1 - yh_from)]))
    sent = [lax.ppermute(quarter, "x", [(0, k)]) for k in (2, 1, 3)]
    return jnp.where(xi == 0, quarter, sent[0] + sent[1] + sent[2])


def gather_solution(quarter):
    own = lax.all_gather(quarter, COL, axis=0, tiled=False)
    other = lax.ppermute(own, "core", [(0, 1), (1, 0)])
    return own, other


def shards(factor, cross_cov):
    xi, core = lax.axis_index("x"), lax.axis_index("core")
    yh, yl, z = lax.axis_index("yh"), lax.axis_index("yl"), lax.axis_index("z")
    row_id = 2 * xi + core
    col_id = 8 * yh + 4 * yl + z
    slice_id = 4 * yl + z
    local = factor[:, 0]
    rhs = cross_cov[:, 0]

    own_rhs = rhs[0].reshape(64, 8, TILE).transpose(1, 0, 2)
    columns = lax.all_to_all(jnp.concatenate([own_rhs, own_rhs], 0), COL, 0, 0, tiled=True)
    columns = columns.reshape(1024, TILE)

    diagonal = ((row_id == 0) & (yh == 0)) | ((row_id == 1) & (yh == 1))
    info = jnp.stack([diagonal.astype(jnp.int32), slice_id.astype(jnp.int32)])
    lead = invert_diagonal(info, local[0])
    tri = lax.all_gather(lead, ("yl", "z"), axis=0, tiled=False)

    first = solve(tri, columns)
    sent = lax.ppermute(first, "core", [(0, 1)])
    second_rhs = lax.ppermute(residual(tri, columns, sent), "yh", [(0, 1)])
    second = solve(tri, second_rhs)

    by_rows = local.reshape(4, 16, 64, TILE).transpose(1, 0, 2, 3).reshape(16, 256, TILE)
    by_rows, _ = lax.optimization_barrier((by_rows, tri[0, :8]))
    left = lax.all_to_all(by_rows, COL, 0, 0, tiled=True)

    quarter_of_mine = col_id // 4
    info2 = jnp.stack(
        [
            core,
            row_id,
            quarter_of_mine % 2,
            (col_id % 4) * 64,
            (quarter_of_mine // 2 != core).astype(jnp.int32),
        ]
    ).astype(jnp.int32)
    base = rhs.reshape(256, 1024)
    own0, other0 = gather_solution(deal(first, core, yh, xi, 0, 0))
    partly = update(0, info2, base, left, own0, other0)
    own1, other1 = gather_solution(deal(second, core, yh, xi, 1, 1))
    out = update(1, info2, partly, left, own1, other1)
    return out.reshape(4, 1, 64, 1024)


def solution(mesh):
    fine = Mesh(mesh.devices.reshape(4, 2, 2, 2, 4), ROW + COL)
    return jax.shard_map(
        shards,
        mesh=fine,
        in_specs=(P(None, ROW, None, COL), P(None, ROW, COL, None)),
        out_specs=P(None, ROW, COL, None),
        check_vma=False,
    )
```

time: 880 us -> 249 us (0.28)
  waiting for transfers between devices: 494 us -> 158 us
  other arithmetic: 174 us -> 1.57 us
  matrix products: 132 us -> 0 us
  local copies, waits for them, and re-layouts: 59.6 us -> 9.04 us
  starting transfers between devices: 0.29 us -> 29.6 us
  blocking collectives: 0 us -> 18.6 us
  Pallas kernels: 0 us -> 16.6 us
    reduce_scatter x4 -> x0, waiting for transfers between devices: 302 us -> none  [reduce_turn(): lax.psum_scatter(partial_value, 'col', scatter_dimension=0, tiled=True)]
    another operation x4 -> x1, other arithmetic: 165 us -> 0.08 us  [shards(): info = jnp.stack([diagonal.astype(jnp.int32), slice_id.astype(jnp.int32)])]
    another operation x30 -> x0, matrix products: 76.4 us -> none  [the longest x15 38.9 us: shards(): lax.linalg.triangular_solve(block_row[:, :block_size], block_rhs, left_si...]
    psum x2 -> x0, waiting for transfers between devices: 70.1 us -> none  [broadcast(): return lax.psum(jnp.where(mine, x, jnp.zeros_like(x)), axis)]
    dot_general x5 -> x0, matrix products: 55.5 us -> none  [the longest x1 30.9 us: shards(): jnp.dot(block_row[:, :block_size], first_block, precision=lax.Precision.H...]
    ppermute x0 -> x14, waiting for transfers between devices: none -> 47.3 us  [the longest x6 14.9 us: deal(): sent = [lax.ppermute(quarter, 'x', [(0, k)]) for k in (2, 1, 3)]]
    another operation x50 -> x3, local copies, waits for them, and re-layouts: 44.7 us -> 3.37 us  [the longest x1 3.23 us: shards(): local.reshape(4, 16, 64, TILE).transpose(1, 0, 2, 3).reshape(16, 256, TILE)]
    all_gather x2 -> x3, waiting for transfers between devices: 121 us -> 81.5 us  [the longest x2 41.7 us: gather_solution(): own = lax.all_gather(quarter, COL, axis=0, tiled=False)]
  transfers between devices with their start and end apart: 8 -> 18, of which waited for: 7 -> 11; matrix products, arithmetic and copies ran while one was open for 15% -> 2% of each run, Pallas kernels for 0% -> 3%
where the time goes in v1:
time: 249 us; the launch traced here: 247 us
  waiting for transfers between devices  158 us (63%)
  starting transfers between devices  29.6 us (12%)
  blocking collectives  18.6 us (7%)
  Pallas kernels  16.6 us (7%)
  between operations  13.5 us (5%)
  local copies, waits for them, and re-layouts  9.04 us (4%)
    all_gather x2, waiting for transfers between devices, gather_solution(): own = lax.all_gather(quarter, COL, axis=0, tiled=False)  41.7 us
    all_gather x1, waiting for transfers between devices, shards(): tri = lax.all_gather(lead, ('yl', 'z'), axis=0, tiled=False)  39.8 us
    all_to_all x1, waiting for transfers between devices, shards(): left = lax.all_to_all(by_rows, COL, 0, 0, tiled=True)  29 us
    all_to_all x1, blocking collectives, shards(): lax.all_to_all(jnp.concatenate([own_rhs, own_rhs], 0), COL, 0, 0, tiled=T...  18.6 us
    ppermute x6, waiting for transfers between devices, deal(): sent = [lax.ppermute(quarter, 'x', [(0, k)]) for k in (2, 1, 3)]  14.9 us
    ppermute x2, waiting for transfers between devices, deal(): lax.ppermute(there, 'yh', [(yh_from, 1 - yh_from)])  13.1 us
    ppermute x1, waiting for transfers between devices, shards(): second_rhs = lax.ppermute(residual(tri, columns, sent), 'yh', [(0, 1)])  12.5 us
    pallas_call x2, Pallas kernels, update(): pl.pallas_call(body, out_shape=jax.ShapeDtypeStruct(base.shape, F32), in_...  8.62 us
  transfers between devices with their start and end apart: 18, of which 11 were waited for; matrix products, arithmetic and copies ran while one was open for 2% of the time, Pallas kernels for 3%

profile of v1, /device:TPU:5, one launch (start us, length us, event | category | flops | bytes accessed | tf_op | source)
XLA Modules:
  0.0 246.7 jit_solution(12197225285951563521)
XLA Ops:
  9.4 18.6 %all_to_all.10 = f32[16,64,128]{2,1,0:T(8,128)S(1)} all-to-all(f32[16,64,128]{2,1,0:T(8,128)S(1)} %pad_maximum_fusion), channel_id=1, replica_groups=mesh['x'=4,'core'=2,'yh'=2,'yl'=2,'z'=4] {'yh','yl','z'}, dimensions={0} | all-to-all | bytes 1048576 | tf_op jit(solution)/shard_map/all_to_all | solution.py:204
  28.0 39.8 %all-gather.7.cloned.1.call-done = f32[8192,128]{1,0:T(8,128)} async-done(((f32[1024,128]{1,0:T(8,128)}), f32[8192,128]{1,0:T(8,128)}) %all-gather.7.cloned.1.call-update) | async-done | bytes 4194320 | tf_op jit(solution)/shard_map/all_gather | solution.py:210
  67.9 2.2 copy-done
  70.1 2.7 %block_solve.2 = f32[1024,128]{1,0:T(8,128)S(1)} custom-call(f32[8,1024,128]{2,1,0:T(8,128)S(1)} %bitcast.29, f32[1024,128]{1,0:T(8,128)S(1)} %bitcast.32), custom_call_target="tpu_custom_call" | custom-call | tf_op jit(solution)/shard_map/block_solve/pallas_call | solution.py:93
  74.1 2.1 collective-permute-done
  76.3 3.9 %collective-permute-start.1 = (f32[256,128]{1,0:T(8,128)S(1)}, f32[256,128]{1,0:T(8,128)S(1)}, u32[]{:S(2)}, u32[]{:S(2)}) collective-permute-start(f32[256,128]{1,0:T(8,128)S(1)} %slice.46), channel_id=1, source_target_pairs={{0,8},{1,9},{2,10},{3,11},{4,12},{5,13},{6,14},{7,15},{16,24},{17,... | collective-permute-start | bytes 393224 | tf_op jit(solution)/shard_map/ppermute | solution.py:183
  80.2 2.7 %collective-permute-done.1 = f32[256,128]{1,0:T(8,128)S(1)} collective-permute-done((f32[256,128]{1,0:T(8,128)S(1)}, f32[256,128]{1,0:T(8,128)S(1)}, u32[]{:S(2)}, u32[]{:S(2)}) %collective-permute-start.1) | collective-permute-done | bytes 131104 | tf_op jit(solution)/shard_map/ppermute | solution.py:183
  85.6 8.3 %collective-permute-done.2 = f32[256,128]{1,0:T(8,128)S(1)} collective-permute-done((f32[256,128]{1,0:T(8,128)S(1)}, f32[256,128]{1,0:T(8,128)S(1)}, u32[]{:S(2)}, u32[]{:S(2)}) %collective-permute-start.2) | collective-permute-done | bytes 131104 | tf_op jit(solution)/shard_map/ppermute | solution.py:184
  96.0 3.5 %collective-permute-done.6.x_ref = f32[1024,128]{1,0:T(8,128)S(1)} collective-permute-done((f32[1024,128]{1,0:T(8,128)S(1)}, f32[1024,128]{1,0:T(8,128)S(1)}, u32[]{:S(2)}, u32[]{:S(2)}) %collective-permute-start.6) | collective-permute-done | bytes 524320 | tf_op jit(solution)/shard_map/ppermute | solution.py:213
  99.6 2.2 copy-done.1
  103.0 5.6 %collective-permute-start.7 = (f32[1024,128]{1,0:T(8,128)S(1)}, f32[1024,128]{1,0:T(8,128)S(1)}, u32[]{:S(2)}, u32[]{:S(2)}) collective-permute-start(f32[1024,128]{1,0:T(8,128)S(1)} %block_residual.1), channel_id=1, source_target_pairs={{0,8},{1,9},{2,10},{3,11},{4,12},{5,13},{6,14},{7,15},{16,24},{17,... | collective-permute-start | bytes 1572872 | tf_op jit(solution)/shard_map/ppermute | solution.py:214
  108.7 12.5 %collective-permute-done.7.rhs_ref = f32[1024,128]{1,0:T(8,128)S(1)} collective-permute-done((f32[1024,128]{1,0:T(8,128)S(1)}, f32[1024,128]{1,0:T(8,128)S(1)}, u32[]{:S(2)}, u32[]{:S(2)}) %collective-permute-start.7) | collective-permute-done | bytes 524320 | tf_op jit(solution)/shard_map/ppermute | solution.py:214
  121.2 2.7 %block_solve.3 = f32[1024,128]{1,0:T(8,128)S(1)} custom-call(f32[8,1024,128]{2,1,0:T(8,128)S(1)} %bitcast.31, f32[1024,128]{1,0:T(8,128)S(1)} %collective-permute-done.7.rhs_ref), custom_call_target="tpu_custom_call" | custom-call | tf_op jit(solution)/shard_map/block_solve/pallas_call | solution.py:93
  123.9 2.9 %collective-permute-start.8 = (f32[512,128]{1,0:T(8,128)S(1)}, f32[512,128]{1,0:T(8,128)S(1)}, u32[]{:S(2)}, u32[]{:S(2)}) collective-permute-start(f32[512,128]{1,0:T(8,128)S(1)} %slice.48), channel_id=1, source_target_pairs={{16,0},{17,1},{18,2},{19,3},{20,4},{21,5},{22,6},{23,7},{24,8},{25... | collective-permute-start | bytes 786440 | tf_op jit(solution)/shard_map/ppermute | solution.py:179
  129.3 10.4 %collective-permute-done.9 = f32[256,128]{1,0:T(8,128)S(1)} collective-permute-done((f32[256,128]{1,0:T(8,128)S(1)}, f32[256,128]{1,0:T(8,128)S(1)}, u32[]{:S(2)}, u32[]{:S(2)}) %collective-permute-start.9) | collective-permute-done | bytes 131104 | tf_op jit(solution)/shard_map/ppermute | solution.py:183
  142.4 6.5 %collective-permute-done.10 = f32[256,128]{1,0:T(8,128)S(1)} collective-permute-done((f32[256,128]{1,0:T(8,128)S(1)}, f32[256,128]{1,0:T(8,128)S(1)}, u32[]{:S(2)}, u32[]{:S(2)}) %collective-permute-start.10) | collective-permute-done | bytes 131104 | tf_op jit(solution)/shard_map/ppermute | solution.py:184
  149.6 1.5 collective-permute-start.5
  151.2 41.7 %all-gather.11.cloned.1.call-done = f32[4096,128]{1,0:T(8,128)} async-done(((f32[256,128]{1,0:T(8,128)}), f32[4096,128]{1,0:T(8,128)}) %all-gather.11.cloned.1.call-update) | async-done | bytes 2097168 | tf_op jit(solution)/shard_map/all_gather | solution.py:189
  192.8 1.7 collective-permute-start.13
  194.5 3.2 %copy.3 = f32[4,16,64,128]{3,2,0,1:T(8,128)} copy(f32[4,16,64,128]{3,2,1,0:T(8,128)} %bitcast.38) | data formatting | bytes 4194304 | tf_op jit(solution)/shard_map/reshape;squeeze | solution.py:217
  197.8 4.7 %all-to-all-start = ((f32[16,256,128]{2,1,0:T(8,128)}), f32[16,256,128]{2,1,0:T(8,128)S(1)}, u32[]{:S(2)}, u32[]{:S(2)}) async-start(f32[16,256,128]{2,1,0:T(8,128)} %bitcast.37), calls=%async_computation | async-start | bytes 4194304 | tf_op jit(solution)/shard_map/all_to_all | solution.py:219
  202.6 29.0 %all-to-all-done.refs_2_ = f32[16,256,128]{2,1,0:T(8,128)S(1)} async-done(((f32[16,256,128]{2,1,0:T(8,128)}), f32[16,256,128]{2,1,0:T(8,128)S(1)}, u32[]{:S(2)}, u32[]{:S(2)}) %all-to-all-start) | async-done | bytes 2097184 | tf_op jit(solution)/shard_map/all_to_all | solution.py:219
  231.6 4.2 %update_first.1.refs_1_ = f32[256,1024]{1,0:T(8,128)S(1)} custom-call(s32[5]{0:T(128)S(1)} %stack.39.refs_0_, f32[256,1024]{1,0:T(8,128)S(1)} %bitcast.36, f32[16,256,128]{2,1,0:T(8,128)S(1)} %all-to-all-done.refs_2_, f32[16,256,128]{2,1,0:T(8,128)} %bitcast.40, f32[16,256,128]{2,1,0:T(8,128)} %collective-permute-done.5.refs_4_), custom_call_target="tpu_custom_call" | custom-call | tf_op jit(solution)/shard_map/update_first/pallas_call | solution.py:165
  235.8 4.4 %update_second.1 = f32[256,1024]{1,0:T(8,128)} custom-call(s32[5]{0:T(128)S(1)} %stack.39.refs_0_, f32[256,1024]{1,0:T(8,128)S(1)} %update_first.1.refs_1_, f32[16,256,128]{2,1,0:T(8,128)S(1)} %all-to-all-done.refs_2_, f32[16,256,128]{2,1,0:T(8,128)S(1)} %bitcast.35, f32[16,256,128]{2,1,0:T(8,128)} %collective-permute-done.13.refs_4_), custom_call_target="tpu_custom_call" | custom-call | tf_op jit(solution)/shard_map/update_second/pallas_call | solution.py:165
  (48 shorter events, 16.1 us)
Async XLA Ops:
  6.5 2.7 %copy-start.3 = (f32[4,1,64,1024]{3,2,1,0:T(8,128)S(1)}, f32[4,1,64,1024]{3,2,1,0:T(8,128)}, u32[]{:S(2)}) copy-start(f32[4,1,64,1024]{3,2,1,0:T(8,128)} %param.3) | copy-start | bytes 3145732
  6.5 61.3 %all-gather.7.cloned.1.call-start = ((), (), s32[]{:S(2)}) async-start(), calls=%async_computation.2 | async-start | bytes 4718592 | tf_op jit(solution)/shard_map/all_gather | solution.py:210
  9.2 140.4 %all-gather.9.cloned.1.call-start = ((), (), s32[]{:S(2)}) async-start(), calls=%async_computation.3 | async-start | bytes 2228224 | tf_op jit(solution)/shard_map/all_gather | solution.py:189
  67.9 2.2 copy-start
  72.8 3.4 %collective-permute-start = (f32[512,128]{1,0:T(8,128)S(1)}, f32[512,128]{1,0:T(8,128)S(1)}, u32[]{:S(2)}, u32[]{:S(2)}) collective-permute-start(f32[512,128]{1,0:T(8,128)S(1)} %slice.44), channel_id=1, source_target_pairs={{0,16},{1,17},{2,18},{3,19},{4,20},{5,21},{6,22},{7,23},{8,24},{9,... | collective-permute-start | bytes 786440 | tf_op jit(solution)/shard_map/ppermute | solution.py:179
  76.3 6.7 %collective-permute-start.1 = (f32[256,128]{1,0:T(8,128)S(1)}, f32[256,128]{1,0:T(8,128)S(1)}, u32[]{:S(2)}, u32[]{:S(2)}) collective-permute-start(f32[256,128]{1,0:T(8,128)S(1)} %slice.46), channel_id=1, source_target_pairs={{0,8},{1,9},{2,10},{3,11},{4,12},{5,13},{6,14},{7,15},{16,24},{17,... | collective-permute-start | bytes 393224 | tf_op jit(solution)/shard_map/ppermute | solution.py:183
  83.0 2.7 %collective-permute-start.4 = (f32[256,128]{1,0:T(8,128)S(1)}, f32[256,128]{1,0:T(8,128)S(1)}, u32[]{:S(2)}, u32[]{:S(2)}) collective-permute-start(f32[256,128]{1,0:T(8,128)S(1)} %slice_select_fusion.3), channel_id=1, source_target_pairs={{0,96},{1,97},{2,98},{3,99},{4,100},{5,101},{6,102},{7,103},{8,104... | collective-permute-start | bytes 393224 | tf_op jit(solution)/shard_map/ppermute | solution.py:184
  83.6 2.0 collective-permute-start.3
  84.3 9.6 %collective-permute-start.2 = (f32[256,128]{1,0:T(8,128)S(1)}, f32[256,128]{1,0:T(8,128)S(1)}, u32[]{:S(2)}, u32[]{:S(2)}) collective-permute-start(f32[256,128]{1,0:T(8,128)S(1)} %slice_select_fusion.3), channel_id=1, source_target_pairs={{0,64},{1,65},{2,66},{3,67},{4,68},{5,69},{6,70},{7,71},{8,72},{9,... | collective-permute-start | bytes 393224 | tf_op jit(solution)/shard_map/ppermute | solution.py:184
  94.7 98.1 %all-gather.11.cloned.1.call-start = ((), (), s32[]{:S(2)}) async-start(), calls=%async_computation.4 | async-start | bytes 2228224 | tf_op jit(solution)/shard_map/all_gather | solution.py:189
  94.7 4.8 %collective-permute-start.6 = (f32[1024,128]{1,0:T(8,128)S(1)}, f32[1024,128]{1,0:T(8,128)S(1)}, u32[]{:S(2)}, u32[]{:S(2)}) collective-permute-start(f32[1024,128]{1,0:T(8,128)S(1)} %block_solve.2), channel_id=1, source_target_pairs={{0,16},{1,17},{2,18},{3,19},{4,20},{5,21},{6,22},{7,23},{8,24},{9,... | collective-permute-start | bytes 1572872 | tf_op jit(solution)/shard_map/ppermute | solution.py:213
  99.6 2.2 copy-start.1
  103.0 18.2 %collective-permute-start.7 = (f32[1024,128]{1,0:T(8,128)S(1)}, f32[1024,128]{1,0:T(8,128)S(1)}, u32[]{:S(2)}, u32[]{:S(2)}) collective-permute-start(f32[1024,128]{1,0:T(8,128)S(1)} %block_residual.1), channel_id=1, source_target_pairs={{0,8},{1,9},{2,10},{3,11},{4,12},{5,13},{6,14},{7,15},{16,24},{17,... | collective-permute-start | bytes 1572872 | tf_op jit(solution)/shard_map/ppermute | solution.py:214
  123.9 4.0 %collective-permute-start.8 = (f32[512,128]{1,0:T(8,128)S(1)}, f32[512,128]{1,0:T(8,128)S(1)}, u32[]{:S(2)}, u32[]{:S(2)}) collective-permute-start(f32[512,128]{1,0:T(8,128)S(1)} %slice.48), channel_id=1, source_target_pairs={{16,0},{17,1},{18,2},{19,3},{20,4},{21,5},{22,6},{23,7},{24,8},{25... | collective-permute-start | bytes 786440 | tf_op jit(solution)/shard_map/ppermute | solution.py:179
  128.0 11.7 %collective-permute-start.9 = (f32[256,128]{1,0:T(8,128)S(1)}, f32[256,128]{1,0:T(8,128)S(1)}, u32[]{:S(2)}, u32[]{:S(2)}) collective-permute-start(f32[256,128]{1,0:T(8,128)S(1)} %slice.50), channel_id=1, source_target_pairs={{8,0},{9,1},{10,2},{11,3},{12,4},{13,5},{14,6},{15,7},{24,16},{25,... | collective-permute-start | bytes 393224 | tf_op jit(solution)/shard_map/ppermute | solution.py:183
  139.7 2.7 %collective-permute-start.12 = (f32[256,128]{1,0:T(8,128)S(1)}, f32[256,128]{1,0:T(8,128)S(1)}, u32[]{:S(2)}, u32[]{:S(2)}) collective-permute-start(f32[256,128]{1,0:T(8,128)S(1)} %slice_select_fusion.2), channel_id=1, source_target_pairs={{0,96},{1,97},{2,98},{3,99},{4,100},{5,101},{6,102},{7,103},{8,104... | collective-permute-start | bytes 393224 | tf_op jit(solution)/shard_map/ppermute | solution.py:184
  140.4 2.0 collective-permute-start.11
  141.0 7.9 %collective-permute-start.10 = (f32[256,128]{1,0:T(8,128)S(1)}, f32[256,128]{1,0:T(8,128)S(1)}, u32[]{:S(2)}, u32[]{:S(2)}) collective-permute-start(f32[256,128]{1,0:T(8,128)S(1)} %slice_select_fusion.2), channel_id=1, source_target_pairs={{0,64},{1,65},{2,66},{3,67},{4,68},{5,69},{6,70},{7,71},{8,72},{9,... | collective-permute-start | bytes 393224 | tf_op jit(solution)/shard_map/ppermute | solution.py:184
  149.6 81.9 %collective-permute-start.5 = (f32[16,256,128]{2,1,0:T(8,128)}, f32[16,256,128]{2,1,0:T(8,128)}, u32[]{:S(2)}, u32[]{:S(2)}) collective-permute-start(f32[16,256,128]{2,1,0:T(8,128)} %bitcast.39), channel_id=1, source_target_pairs={{0,16},{16,0},{1,17},{17,1},{2,18},{18,2},{3,19},{19,3},{4,20},{20... | collective-permute-start | bytes 6291464 | tf_op jit(solution)/shard_map/ppermute | solution.py:190
  192.8 43.0 %collective-permute-start.13 = (f32[16,256,128]{2,1,0:T(8,128)}, f32[16,256,128]{2,1,0:T(8,128)}, u32[]{:S(2)}, u32[]{:S(2)}) collective-permute-start(f32[16,256,128]{2,1,0:T(8,128)} %bitcast.34), channel_id=1, source_target_pairs={{0,16},{16,0},{1,17},{17,1},{2,18},{18,2},{3,19},{19,3},{4,20},{20... | collective-permute-start | bytes 6291464 | tf_op jit(solution)/shard_map/ppermute | solution.py:190
  197.8 33.8 %all-to-all-start = ((f32[16,256,128]{2,1,0:T(8,128)}), f32[16,256,128]{2,1,0:T(8,128)S(1)}, u32[]{:S(2)}, u32[]{:S(2)}) async-start(f32[16,256,128]{2,1,0:T(8,128)} %bitcast.37), calls=%async_computation | async-start | bytes 4194304 | tf_op jit(solution)/shard_map/all_to_all | solution.py:219
  231.6 4.2 %copy-start.2 = (f32[4096,128]{1,0:T(8,128)S(1)}, f32[4096,128]{1,0:T(8,128)}, u32[]{:S(2)}) copy-start(f32[4096,128]{1,0:T(8,128)} %all-gather.11.cloned.1.call-done) | copy-start | bytes 6291460
Sparse Core Ops, SparseCore 0:
  9.3 58.5 all-gather.6
  94.8 50.8 all-gather.8
  149.7 43.0 all-gather.10

commit v2 on v1

--- a/solution.py
+++ b/solution.py
@@ -121,74 +121,122 @@
     )(tri, rhs, x)
 
 
-def update_body(half, info, base_ref, left_ref, own_ref, other_ref, out_ref):
-    core = info[0]
-    rows = base_ref.shape[0]
-    lefts = []
-    for side, swap in ((0, core), (1, 1 - core)):
-        for q in range(2):
-            first = 8 * half + 4 * swap + 2 * q
-            lefts.append(split(jnp.concatenate([left_ref[first], left_ref[first + 1]], 1)))
-    for pair in range(4):
-        cols = pl.ds(pair * 2 * TILE, 2 * TILE)
-        total = None
-        for side, ref in ((0, own_ref), (1, other_ref)):
-            for q in range(2):
-                block = jnp.concatenate([ref[q * 8 + 2 * pair], ref[q * 8 + 2 * pair + 1]], 1)
-                high, low = split(block)
-                left_high, left_low = lefts[2 * side + q]
-                term = mm(left_high, high) + (mm(left_high, low) + mm(left_low, high))
-                total = term if total is None else total + term
-        out_ref[:, cols] = base_ref[:, cols] - total
-
-    slot = info[2]
-    offset = pl.multiple_of(info[3], 64)
-
-    if half == 1:
-
-        @pl.when(info[1] == 0)
-        def _():
-            out_ref[pl.ds(0, 64), :] = base_ref[pl.ds(0, 64), :]
-
-    for ref, want in ((own_ref, 0), (other_ref, 1)):
-
-        @pl.when((info[1] == half) & (info[4] == want))
-        def _():
-            for n in range(8):
-                out_ref[pl.ds(0, 64), pl.ds(n * TILE, TILE)] = ref[slot * 8 + n, pl.ds(offset, 64), :]
-
-
-def update(half, info, base, left, own, other):
-    def body(*refs):
-        update_body(half, *refs)
+def prepare_body(info, left_ref, base_ref, high_ref, low_ref, out_ref):
+    for h in range(2):
+        for q in range(4):
+            c = 8 * h + 2 * q
+            high, low = split(jnp.concatenate([left_ref[c], left_ref[c + 1]], 1))
+            high_ref[4 * h + q] = high
+            low_ref[4 * h + q] = low
+    out_ref[...] = base_ref[...]
+
+    @pl.when(info[0] < 2)
+    def _():
+        for n in range(8):
+            high_ref[n, pl.ds(0, 64), :] = jnp.zeros((64, 256), BF16)
+            low_ref[n, pl.ds(0, 64), :] = jnp.zeros((64, 256), BF16)
+        out_ref[pl.ds(0, 64), :] = jnp.zeros((64, 1024), F32)
+
+
+def prepare(info, left, base):
+    return pl.pallas_call(
+        prepare_body,
+        out_shape=[
+            jax.ShapeDtypeStruct((8, 256, 256), BF16),
+            jax.ShapeDtypeStruct((8, 256, 256), BF16),
+            jax.ShapeDtypeStruct(base.shape, F32),
+        ],
+        in_specs=[SM, VM, VM],
+        out_specs=[VM, VM, VM],
+        compiler_params=PARAMS,
+        name="prepare_update",
+    )(info, left, base)
+
+
+def accumulate(info, base, high, low, pieces, places, name):
+    def body(info, base_ref, high_ref, low_ref, *refs):
+        out_ref = refs[-1]
+        row, core, y, z, col = (info[k] for k in range(5))
+        out_ref[...] = base_ref[...]
+        for ref, (side, far, slot) in zip(refs, places):
+            holder = core if side == 0 else 1 - core
+            for n in range(ref.shape[0]):
+                near = slot + n
+                py = lax.rem(y + jnp.where(holder == 0, far, near), 4)
+                pz = lax.rem(z + jnp.where(holder == 0, near, far), 4)
+                upper = py // 2
+                bit = jnp.where(upper == 0, py, 3 - py)
+                cols = pl.ds(pl.multiple_of((4 * bit + pz) * TILE, TILE), TILE)
+                q = 2 * holder + upper
+                total = None
+                for h in range(2):
+                    x_high, x_low = split(ref[n, h])
+                    left_high = high_ref[4 * h + q]
+                    wide = mm(left_high, jnp.concatenate([x_high, x_low], 1))
+                    term = wide[:, :TILE] + (wide[:, TILE:] + mm(low_ref[4 * h + q], x_high))
+                    total = term if total is None else total + term
+                out_ref[:, cols] = out_ref[:, cols] - total
+
+                @pl.when((row < 2) & (col // 4 == q))
+                def _():
+                    there = pl.ds(pl.multiple_of(lax.rem(col, 4) * 64, 64), 64)
+                    out_ref[pl.ds(0, 64), cols] = out_ref[pl.ds(0, 64), cols] + ref[n, row, there, :]
 
     return pl.pallas_call(
         body,
         out_shape=jax.ShapeDtypeStruct(base.shape, F32),
-        in_specs=[SM, VM, VM, VM, VM],
+        in_specs=[SM] + [VM] * (3 + len(pieces)),
         out_specs=VM,
-        compiler_params=PARAMS,
-        name="update_first" if half == 0 else "update_second",
-    )(info, base, left, own, other)
+        input_output_aliases={1: 0},
+        compiler_params=PARAMS,
+        name=name,
+    )(info, base, high, low, *pieces)
+
+
+AXES = ROW + COL
+
+
+def move(value, where):
+    pairs = []
+    for x in range(4):
+        for core in range(2):
+            for y in range(4):
+                for z in range(4):
+                    to = where(x, core, y, z)
+                    if to is not None:
+                        a, b, c, d = to
+                        pairs.append((((x * 2 + core) * 4 + y) * 4 + z, ((a * 2 + b) * 4 + c % 4) * 4 + d % 4))
+    return lax.ppermute(value, AXES, pairs)
 
 
 def deal(x, core, yh, xi, core_from, yh_from):
-    half_there = x[512 * (1 - core_from) : 512 * (2 - core_from)]
-    half_here = x[512 * core_from : 512 * (core_from + 1)]
-    half = jnp.where(
-        core == core_from, half_here, lax.ppermute(half_there, "core", [(core_from, 1 - core_from)])
-    )
-    there = half[256 * (1 - yh_from) : 256 * (2 - yh_from)]
-    here = half[256 * yh_from : 256 * (yh_from + 1)]
-    quarter = jnp.where(yh == yh_from, here, lax.ppermute(there, "yh", [(yh_from, 1 - yh_from)]))
-    sent = [lax.ppermute(quarter, "x", [(0, k)]) for k in (2, 1, 3)]
-    return jnp.where(xi == 0, quarter, sent[0] + sent[1] + sent[2])
-
-
-def gather_solution(quarter):
-    own = lax.all_gather(quarter, COL, axis=0, tiled=False)
-    other = lax.ppermute(own, "core", [(0, 1), (1, 0)])
-    return own, other
+    top = core_from == 0
+    half_here, half_there = (x[:512], x[512:]) if top else (x[512:], x[:512])
+    got = move(half_there, lambda a, b, c, d: (0, 1 - b, c, d) if a == 0 and b == core_from else None)
+    half = jnp.where(core == core_from, half_here, got)
+    here, there = (half[:256], half[256:]) if yh_from == 0 else (half[256:], half[:256])
+    got = move(there, lambda a, b, c, d: (0, b, 3 - c, d) if a == 0 and c // 2 == yh_from else None)
+    quarter = jnp.where(yh == yh_from, here, got)
+    one = move(quarter, lambda a, b, c, d: (1 if b == 0 else 3, b, c, d) if a == 0 else None)
+    two = move(quarter, lambda a, b, c, d: (3 if b == 0 else 1, b, c, d) if a == 0 else None)
+    far = move(one, lambda a, b, c, d: (2, b, c, d) if a == (1 if b == 0 else 3) else None)
+    return jnp.where(xi == 0, quarter, one + two + far)
+
+
+def ring(value, first):
+    def along(step):
+        def where(a, b, c, d):
+            on_z = (b == 0) == first
+            return (a, b, c, d + step) if on_z else (a, b, c + step, d)
+
+        return where
+
+    before = move(value, along(1))
+    after = move(value, along(-1))
+    cut = value.shape[0] // 2
+    far_low = move(before[:cut], along(1))
+    far_high = move(after[cut:], along(-1))
+    return after, far_low, far_high, before
 
 
 def shards(factor, cross_cov):
@@ -209,30 +257,41 @@
     lead = invert_diagonal(info, local[0])
     tri = lax.all_gather(lead, ("yl", "z"), axis=0, tiled=False)
 
+    by_rows = local.reshape(4, 16, 64, TILE).transpose(1, 0, 2, 3).reshape(16, 256, TILE)
+    by_rows, tri = lax.optimization_barrier((by_rows, tri))
+    left = lax.all_to_all(by_rows, COL, 0, 0, tiled=True)
+
     first = solve(tri, columns)
-    sent = lax.ppermute(first, "core", [(0, 1)])
-    second_rhs = lax.ppermute(residual(tri, columns, sent), "yh", [(0, 1)])
+    sent = move(first, lambda a, b, c, d: (0, 1, c, d) if a == 0 and b == 0 and c < 2 else None)
+    second_rhs = move(
+        residual(tri, columns, sent),
+        lambda a, b, c, d: (0, 1, 3 - c, d) if a == 0 and b == 1 and c < 2 else None,
+    )
     second = solve(tri, second_rhs)
-
-    by_rows = local.reshape(4, 16, 64, TILE).transpose(1, 0, 2, 3).reshape(16, 256, TILE)
-    by_rows, _ = lax.optimization_barrier((by_rows, tri[0, :8]))
-    left = lax.all_to_all(by_rows, COL, 0, 0, tiled=True)
-
-    quarter_of_mine = col_id // 4
-    info2 = jnp.stack(
-        [
-            core,
-            row_id,
-            quarter_of_mine % 2,
-            (col_id % 4) * 64,
-            (quarter_of_mine // 2 != core).astype(jnp.int32),
-        ]
-    ).astype(jnp.int32)
-    base = rhs.reshape(256, 1024)
-    own0, other0 = gather_solution(deal(first, core, yh, xi, 0, 0))
-    partly = update(0, info2, base, left, own0, other0)
-    own1, other1 = gather_solution(deal(second, core, yh, xi, 1, 1))
-    out = update(1, info2, partly, left, own1, other1)
+    dealt0 = deal(first, core, yh, xi, 0, 0)
+    second, left = lax.optimization_barrier((second, left))
+    dealt1 = deal(second, core, yh, xi, 1, 1)
+
+    info2 = jnp.stack([row_id, core, 2 * yh + yl, z, col_id]).astype(jnp.int32)
+    high, low, out = prepare(info2[:1], left, rhs.reshape(256, 1024))
+
+    def swap(value):
+        return move(value, lambda a, b, c, d: (a, 1 - b, c, d))
+
+    mine = jnp.stack([dealt0, dealt1])
+    after, far_low, far_high, before = ring(mine, True)
+    near = jnp.stack([mine, after, jnp.concatenate([far_low, far_high], 0), before])
+    near_other = swap(near)
+    after, far_low, far_high, before = ring(near, False)
+    out = accumulate(info2, out, high, low, [near, near_other], [(0, 0, 0), (1, 0, 0)], "update_near")
+    out = accumulate(
+        info2, out, high, low, [after, before, swap(after), swap(before)],
+        [(0, 1, 0), (0, 3, 0), (1, 1, 0), (1, 3, 0)], "update_next",
+    )
+    out = accumulate(
+        info2, out, high, low, [far_low, far_high, swap(far_low), swap(far_high)],
+        [(0, 2, 0), (0, 2, 2), (1, 2, 0), (1, 2, 2)], "update_far",
+    )
     return out.reshape(4, 1, 64, 1024)
 
 

time: 249 us -> 204 us (0.82)
  waiting for transfers between devices: 158 us -> 111 us
  blocking collectives: 18.6 us -> 0 us
  Pallas kernels: 16.6 us -> 27.8 us
  starting transfers between devices: 29.6 us -> 37.2 us
    all_gather x2 -> x0, waiting for transfers between devices: 41.7 us -> none  [gather_solution(): own = lax.all_gather(quarter, COL, axis=0, tiled=False)]
    all_to_all x1 -> x0, blocking collectives: 18.6 us -> none  [shards(): lax.all_to_all(jnp.concatenate([own_rhs, own_rhs], 0), COL, 0, 0, tiled=T...]
    all_to_all x1, waiting for transfers between devices: 29 us -> 15.1 us  [shards(): left = lax.all_to_all(by_rows, COL, 0, 0, tiled=True)]
    pallas_call x2 -> x4, Pallas kernels: 8.62 us -> 19.7 us  [the longest x3 18.4 us: accumulate(): pl.pallas_call(body, out_shape=jax.ShapeDtypeStruct(base.shape, F32), in_...]
    all_gather x1, waiting for transfers between devices: 39.8 us -> 48.8 us  [shards(): tri = lax.all_gather(lead, ('yl', 'z'), axis=0, tiled=False)]
    all_to_all x0 -> x1, starting transfers between devices: none -> 7.77 us  [shards(): lax.all_to_all(jnp.concatenate([own_rhs, own_rhs], 0), COL, 0, 0, tiled=T...]
    slice x4 -> x8, local copies, waits for them, and re-layouts: 0.06 us -> 2.93 us  [the longest x2 1.09 us: ring(): far_low = move(before[:cut], along(1))]
    ppermute x14 -> x25, starting transfers between devices: 24.8 us -> 25.4 us  [move(): return lax.ppermute(value, AXES, pairs)]
  transfers between devices with their start and end apart: 18 -> 28, of which waited for: 11 -> 9; matrix products, arithmetic and copies ran while one was open for 2% -> 4% of each run, Pallas kernels for 3% -> 10%
where the time goes in v2:
time: 204 us; the launch traced here: 202 us
  waiting for transfers between devices  111 us (54%)
  starting transfers between devices  37.2 us (18%)
  Pallas kernels  27.8 us (14%)
  between operations  13.8 us (7%)
  local copies, waits for them, and re-layouts  10.4 us (5%)
  other arithmetic  2.18 us (1%)
    all_gather x1, waiting for transfers between devices, shards(): tri = lax.all_gather(lead, ('yl', 'z'), axis=0, tiled=False)  48.8 us
    ppermute x25, waiting for transfers between devices, move(): return lax.ppermute(value, AXES, pairs)  47.2 us
    ppermute x25, starting transfers between devices, move(): return lax.ppermute(value, AXES, pairs)  25.4 us
    pallas_call x3, Pallas kernels, accumulate(): pl.pallas_call(body, out_shape=jax.ShapeDtypeStruct(base.shape, F32), in_...  18.4 us
    all_to_all x1, waiting for transfers between devices, shards(): left = lax.all_to_all(by_rows, COL, 0, 0, tiled=True)  15.1 us
    all_to_all x1, starting transfers between devices, shards(): lax.all_to_all(jnp.concatenate([own_rhs, own_rhs], 0), COL, 0, 0, tiled=T...  7.77 us
    pallas_call x2, Pallas kernels, solve(): pl.pallas_call(solve_body, out_shape=jax.ShapeDtypeStruct(rhs.shape, F32)...  5.39 us
    unnamed x8, local copies, waits for them, and re-layouts  4.57 us
  transfers between devices with their start and end apart: 28, of which 9 were waited for; matrix products, arithmetic and copies ran while one was open for 4% of the time, Pallas kernels for 10%

profile of v2, /device:TPU:5, one launch (start us, length us, event | category | flops | bytes accessed | tf_op | source)
XLA Modules:
  0.0 202.4 jit_solution(16239024223959643058)
XLA Ops:
  7.7 1.4 invert_diagonal.1
  11.2 7.8 %all-to-all-start = ((f32[16,64,128]{2,1,0:T(8,128)}), f32[16,64,128]{2,1,0:T(8,128)S(1)}, u32[]{:S(2)}, u32[]{:S(2)}) async-start(f32[16,64,128]{2,1,0:T(8,128)} %pad_maximum_fusion.1), calls=%async_computation | async-start | bytes 1048576 | tf_op jit(solution)/shard_map/all_to_all | solution.py:252
  19.0 1.6 copy.6
  20.6 48.8 %all-gather.3.cloned.1.call-done = f32[8192,128]{1,0:T(8,128)} async-done(((f32[1024,128]{1,0:T(8,128)}), f32[8192,128]{1,0:T(8,128)}) %all-gather.3.cloned.1.call-update) | async-done | bytes 4194320 | tf_op jit(solution)/shard_map/all_gather | solution.py:258
  69.4 4.0 %all-to-all-start.1 = ((f32[16,256,128]{2,1,0:T(8,128)}), f32[16,256,128]{2,1,0:T(8,128)S(1)}, u32[]{:S(2)}, u32[]{:S(2)}) async-start(f32[16,256,128]{2,1,0:T(8,128)} %bitcast.43), calls=%async_computation.1 | async-start | bytes 4194304 | tf_op jit(solution)/shard_map/all_to_all | solution.py:262
  73.5 2.2 %copy-done = f32[8192,128]{1,0:T(8,128)S(1)} copy-done((f32[8192,128]{1,0:T(8,128)S(1)}, f32[8192,128]{1,0:T(8,128)}, u32[]{:S(2)}) %copy-start) | copy-done | bytes 4194328
  75.7 2.7 %block_solve.2 = f32[1024,128]{1,0:T(8,128)S(1)} custom-call(f32[8,1024,128]{2,1,0:T(8,128)S(1)} %bitcast.37, f32[1024,128]{1,0:T(8,128)S(1)} %bitcast.40), custom_call_target="tpu_custom_call" | custom-call | tf_op jit(solution)/shard_map/block_solve/pallas_call | solution.py:93
  82.4 2.7 %block_solve.3 = f32[1024,128]{1,0:T(8,128)S(1)} custom-call(f32[8,1024,128]{2,1,0:T(8,128)S(1)} %bitcast.39, f32[1024,128]{1,0:T(8,128)S(1)} %collective-permute-done.1.rhs_ref), custom_call_target="tpu_custom_call" | custom-call | tf_op jit(solution)/shard_map/block_solve/pallas_call | solution.py:93
  85.1 15.1 %all-to-all-done.1.left_ref = f32[16,256,128]{2,1,0:T(8,128)S(1)} async-done(((f32[16,256,128]{2,1,0:T(8,128)}), f32[16,256,128]{2,1,0:T(8,128)S(1)}, u32[]{:S(2)}, u32[]{:S(2)}) %all-to-all-start.1) | async-done | bytes 2097184 | tf_op jit(solution)/shard_map/all_to_all | solution.py:262
  110.1 15.1 %collective-permute-done.6 = f32[256,128]{1,0:T(8,128)S(1)} collective-permute-done((f32[256,128]{1,0:T(8,128)S(1)}, f32[256,128]{1,0:T(8,128)S(1)}, u32[]{:S(2)}, u32[]{:S(2)}) %collective-permute-start.6) | collective-permute-done | bytes 131104 | tf_op jit(solution)/shard_map/ppermute | solution.py:209
  125.2 6.3 %collective-permute-done.11 = f32[256,128]{1,0:T(8,128)S(1)} collective-permute-done((f32[256,128]{1,0:T(8,128)S(1)}, f32[256,128]{1,0:T(8,128)S(1)}, u32[]{:S(2)}, u32[]{:S(2)}) %collective-permute-start.11) | collective-permute-done | bytes 131104 | tf_op jit(solution)/shard_map/ppermute | solution.py:209
  131.6 1.6 collective-permute-start.12
  133.2 4.0 %collective-permute-done.12 = f32[2,256,128]{2,1,0:T(8,128)S(1)} collective-permute-done((f32[2,256,128]{2,1,0:T(8,128)S(1)}, f32[2,256,128]{2,1,0:T(8,128)S(1)}, u32[]{:S(2)}, u32[]{:S(2)}) %collective-permute-start.12) | collective-permute-done | bytes 262176 | tf_op jit(solution)/shard_map/ppermute | solution.py:209
  137.2 2.5 %collective-permute-start.15 = (f32[1,256,128]{2,1,0:T(8,128)S(1)}, f32[1,256,128]{2,1,0:T(8,128)S(1)}, u32[]{:S(2)}, u32[]{:S(2)}) collective-permute-start(f32[1,256,128]{2,1,0:T(8,128)S(1)} %slice.65), channel_id=1, source_target_pairs={{0,3},{1,0},{2,1},{3,2},{4,7},{5,4},{6,5},{7,6},{8,11},{9,8},{10,9... | collective-permute-start | bytes 393224 | tf_op jit(solution)/shard_map/ppermute | solution.py:209
  139.8 1.8 collective-permute-done.15
  141.7 3.2 %collective-permute-done.14 = f32[1,256,128]{2,1,0:T(8,128)S(1)} collective-permute-done((f32[1,256,128]{2,1,0:T(8,128)S(1)}, f32[1,256,128]{2,1,0:T(8,128)S(1)}, u32[]{:S(2)}, u32[]{:S(2)}) %collective-permute-start.14) | collective-permute-done | bytes 131104 | tf_op jit(solution)/shard_map/ppermute | solution.py:209
  144.9 1.5 collective-permute-start.18
  148.6 11.6 %collective-permute-done.18.refs_1_ = f32[4,2,256,128]{3,2,1,0:T(8,128)} collective-permute-done((f32[4,2,256,128]{3,2,1,0:T(8,128)S(1)}, f32[4,2,256,128]{3,2,1,0:T(8,128)}, u32[]{:S(2)}, u32[]{:S(2)}) %collective-permute-start.18) | collective-permute-done | bytes 1048608 | tf_op jit(solution)/shard_map/ppermute | solution.py:209
  163.9 2.0 collective-permute-start.22
  165.9 5.1 %collective-permute-done.21.refs_0_ = f32[2,2,256,128]{3,2,1,0:T(8,128)} collective-permute-done((f32[2,2,256,128]{3,2,1,0:T(8,128)S(1)}, f32[2,2,256,128]{3,2,1,0:T(8,128)}, u32[]{:S(2)}, u32[]{:S(2)}) %collective-permute-start.21) | collective-permute-done | bytes 524320 | tf_op jit(solution)/shard_map/ppermute | solution.py:209
  171.1 2.1 %collective-permute-start.23 = (f32[2,2,256,128]{3,2,1,0:T(8,128)}, f32[2,2,256,128]{3,2,1,0:T(8,128)}, u32[]{:S(2)}, u32[]{:S(2)}) collective-permute-start(f32[2,2,256,128]{3,2,1,0:T(8,128)} %collective-permute-done.21.refs_0_), channel_id=1, source_target_pairs={{0,16},{1,17},{2,18},{3,19},{4,20},{5,21},{6,22},{7,23},{8,24},{9,... | collective-permute-start | bytes 1572872 | tf_op jit(solution)/shard_map/ppermute | solution.py:209
  177.1 4.9 %update_near.1.base_ref = f32[256,1024]{1,0:T(8,128)} custom-call(s32[5]{0:T(128)S(1)} %stack.59.info, f32[256,1024]{1,0:T(8,128)} %get-tuple-element.15.base_ref, bf16[8,256,256]{2,1,0:T(8,128)(2,1)S(1)} %get-tuple-element.16.high_ref, bf16[8,256,256]{2,1,0:T(8,128)(2,1)S(1)} %get-tuple-element.17.low_ref, ...), custom_call_target="tpu_custom_call", output_to_operand_aliasing={{}: (1, {})} | custom-call | tf_op jit(solution)/shard_map/update_near/pallas_call | solution.py:185
  182.0 8.3 %update_next.1.base_ref = f32[256,1024]{1,0:T(8,128)} custom-call(s32[5]{0:T(128)S(1)} %stack.59.info, f32[256,1024]{1,0:T(8,128)} %update_near.1.base_ref, bf16[8,256,256]{2,1,0:T(8,128)(2,1)S(1)} %get-tuple-element.16.high_ref, bf16[8,256,256]{2,1,0:T(8,128)(2,1)S(1)} %get-tuple-element.17.low_ref, ...), custom_call_target="tpu_custom_call", output_to_operand_aliasing={{}: (1, {})} | custom-call | tf_op jit(solution)/shard_map/update_next/pallas_call | solution.py:185
  190.3 5.2 %update_far.1 = f32[256,1024]{1,0:T(8,128)} custom-call(s32[5]{0:T(128)S(1)} %stack.59.info, f32[256,1024]{1,0:T(8,128)} %update_next.1.base_ref, bf16[8,256,256]{2,1,0:T(8,128)(2,1)S(1)} %get-tuple-element.16.high_ref, bf16[8,256,256]{2,1,0:T(8,128)(2,1)S(1)} %get-tuple-element.17.low_ref, ...), custom_call_target="tpu_custom_call", output_to_operand_aliasing={{}: (1, {})} | custom-call | tf_op jit(solution)/shard_map/update_far/pallas_call | solution.py:185
  (72 shorter events, 27.2 us)
Async XLA Ops:
  6.5 62.9 %all-gather.3.cloned.1.call-start = ((), (), s32[]{:S(2)}) async-start(), calls=%async_computation.2 | async-start | bytes 4718592 | tf_op jit(solution)/shard_map/all_gather | solution.py:258
  11.2 58.2 %all-to-all-start = ((f32[16,64,128]{2,1,0:T(8,128)}), f32[16,64,128]{2,1,0:T(8,128)S(1)}, u32[]{:S(2)}, u32[]{:S(2)}) async-start(f32[16,64,128]{2,1,0:T(8,128)} %pad_maximum_fusion.1), calls=%async_computation | async-start | bytes 1048576 | tf_op jit(solution)/shard_map/all_to_all | solution.py:252
  69.4 30.8 %all-to-all-start.1 = ((f32[16,256,128]{2,1,0:T(8,128)}), f32[16,256,128]{2,1,0:T(8,128)S(1)}, u32[]{:S(2)}, u32[]{:S(2)}) async-start(f32[16,256,128]{2,1,0:T(8,128)} %bitcast.43), calls=%async_computation.1 | async-start | bytes 4194304 | tf_op jit(solution)/shard_map/all_to_all | solution.py:262
  80.3 2.1 %collective-permute-start.1 = (f32[1024,128]{1,0:T(8,128)S(1)}, f32[1024,128]{1,0:T(8,128)S(1)}, u32[]{:S(2)}, u32[]{:S(2)}) collective-permute-start(f32[1024,128]{1,0:T(8,128)S(1)} %block_residual.1), channel_id=1, source_target_pairs={{16,28},{17,29},{18,30},{19,31},{20,24},{21,25},{22,26},{23,27}} | collective-permute-start | bytes 1572872 | tf_op jit(solution)/shard_map/ppermute | solution.py:209
  81.1 21.2 %collective-permute-start.2 = (f32[512,128]{1,0:T(8,128)S(1)}, f32[512,128]{1,0:T(8,128)}, u32[]{:S(2)}, u32[]{:S(2)}) collective-permute-start(f32[512,128]{1,0:T(8,128)S(1)} %slice.59), channel_id=1, source_target_pairs={{0,16},{1,17},{2,18},{3,19},{4,20},{5,21},{6,22},{7,23},{8,24},{9,... | collective-permute-start | bytes 786440 | tf_op jit(solution)/shard_map/ppermute | solution.py:209
  100.9 3.0 %collective-permute-start.7 = (f32[512,128]{1,0:T(8,128)}, f32[512,128]{1,0:T(8,128)}, u32[]{:S(2)}, u32[]{:S(2)}) collective-permute-start(f32[512,128]{1,0:T(8,128)} %slice.51), channel_id=1, source_target_pairs={{16,0},{17,1},{18,2},{19,3},{20,4},{21,5},{22,6},{23,7},{24,8},{25... | collective-permute-start | bytes 786440 | tf_op jit(solution)/shard_map/ppermute | solution.py:209
  105.5 3.3 %collective-permute-start.9 = (f32[256,128]{1,0:T(8,128)S(1)}, f32[256,128]{1,0:T(8,128)S(1)}, u32[]{:S(2)}, u32[]{:S(2)}) collective-permute-start(f32[256,128]{1,0:T(8,128)S(1)} %slice_select_fusion.2), channel_id=1, source_target_pairs={{0,32},{1,33},{2,34},{3,35},{4,36},{5,37},{6,38},{7,39},{8,40},{9,... | collective-permute-start | bytes 393224 | tf_op jit(solution)/shard_map/ppermute | solution.py:209
  106.1 4.0 %collective-permute-start.5 = (f32[256,128]{1,0:T(8,128)S(1)}, f32[256,128]{1,0:T(8,128)S(1)}, u32[]{:S(2)}, u32[]{:S(2)}) collective-permute-start(f32[256,128]{1,0:T(8,128)S(1)} %slice_select_fusion.3), channel_id=1, source_target_pairs={{0,96},{1,97},{2,98},{3,99},{4,100},{5,101},{6,102},{7,103},{8,104... | collective-permute-start | bytes 393224 | tf_op jit(solution)/shard_map/ppermute | solution.py:209
  106.8 18.4 %collective-permute-start.6 = (f32[256,128]{1,0:T(8,128)S(1)}, f32[256,128]{1,0:T(8,128)S(1)}, u32[]{:S(2)}, u32[]{:S(2)}) collective-permute-start(f32[256,128]{1,0:T(8,128)S(1)} %collective-permute-done.4), channel_id=1, source_target_pairs={{32,64},{33,65},{34,66},{35,67},{36,68},{37,69},{38,70},{39,71},{4... | collective-permute-start | bytes 393224 | tf_op jit(solution)/shard_map/ppermute | solution.py:209
  108.1 17.1 %collective-permute-start.10 = (f32[256,128]{1,0:T(8,128)S(1)}, f32[256,128]{1,0:T(8,128)S(1)}, u32[]{:S(2)}, u32[]{:S(2)}) collective-permute-start(f32[256,128]{1,0:T(8,128)S(1)} %slice_select_fusion.2), channel_id=1, source_target_pairs={{0,96},{1,97},{2,98},{3,99},{4,100},{5,101},{6,102},{7,103},{8,104... | collective-permute-start | bytes 393224 | tf_op jit(solution)/shard_map/ppermute | solution.py:209
  108.8 22.7 %collective-permute-start.11 = (f32[256,128]{1,0:T(8,128)S(1)}, f32[256,128]{1,0:T(8,128)S(1)}, u32[]{:S(2)}, u32[]{:S(2)}) collective-permute-start(f32[256,128]{1,0:T(8,128)S(1)} %collective-permute-done.9), channel_id=1, source_target_pairs={{32,64},{33,65},{34,66},{35,67},{36,68},{37,69},{38,70},{39,71},{4... | collective-permute-start | bytes 393224 | tf_op jit(solution)/shard_map/ppermute | solution.py:209
  131.6 5.6 %collective-permute-start.12 = (f32[2,256,128]{2,1,0:T(8,128)S(1)}, f32[2,256,128]{2,1,0:T(8,128)S(1)}, u32[]{:S(2)}, u32[]{:S(2)}) collective-permute-start(f32[2,256,128]{2,1,0:T(8,128)S(1)} %get-tuple-element.20), channel_id=1, source_target_pairs={{0,3},{1,0},{2,1},{3,2},{4,7},{5,4},{6,5},{7,6},{8,11},{9,8},{10,9... | collective-permute-start | bytes 786440 | tf_op jit(solution)/shard_map/ppermute | solution.py:209
  133.2 6.5 %collective-permute-start.13 = (f32[2,256,128]{2,1,0:T(8,128)S(1)}, f32[2,256,128]{2,1,0:T(8,128)S(1)}, u32[]{:S(2)}, u32[]{:S(2)}) collective-permute-start(f32[2,256,128]{2,1,0:T(8,128)S(1)} %get-tuple-element.20), channel_id=1, source_target_pairs={{0,1},{1,2},{2,3},{3,0},{4,5},{5,6},{6,7},{7,4},{8,9},{9,10},{10,1... | collective-permute-start | bytes 786440 | tf_op jit(solution)/shard_map/ppermute | solution.py:209
  137.2 4.4 %collective-permute-start.15 = (f32[1,256,128]{2,1,0:T(8,128)S(1)}, f32[1,256,128]{2,1,0:T(8,128)S(1)}, u32[]{:S(2)}, u32[]{:S(2)}) collective-permute-start(f32[1,256,128]{2,1,0:T(8,128)S(1)} %slice.65), channel_id=1, source_target_pairs={{0,3},{1,0},{2,1},{3,2},{4,7},{5,4},{6,5},{7,6},{8,11},{9,8},{10,9... | collective-permute-start | bytes 393224 | tf_op jit(solution)/shard_map/ppermute | solution.py:209
  139.7 5.1 %collective-permute-start.14 = (f32[1,256,128]{2,1,0:T(8,128)S(1)}, f32[1,256,128]{2,1,0:T(8,128)S(1)}, u32[]{:S(2)}, u32[]{:S(2)}) collective-permute-start(f32[1,256,128]{2,1,0:T(8,128)S(1)} %slice.64), channel_id=1, source_target_pairs={{0,1},{1,2},{2,3},{3,0},{4,5},{5,6},{6,7},{7,4},{8,9},{9,10},{10,1... | collective-permute-start | bytes 393224 | tf_op jit(solution)/shard_map/ppermute | solution.py:209
  144.9 15.3 %collective-permute-start.18 = (f32[4,2,256,128]{3,2,1,0:T(8,128)S(1)}, f32[4,2,256,128]{3,2,1,0:T(8,128)}, u32[]{:S(2)}, u32[]{:S(2)}) collective-permute-start(f32[4,2,256,128]{3,2,1,0:T(8,128)S(1)} %pad_maximum_fusion.refs_0_), channel_id=1, source_target_pairs={{0,4},{1,5},{2,6},{3,7},{4,8},{5,9},{6,10},{7,11},{8,12},{9,13},{1... | collective-permute-start | bytes 3145736 | tf_op jit(solution)/shard_map/ppermute | solution.py:209
  146.5 15.0 %collective-permute-start.17 = (f32[4,2,256,128]{3,2,1,0:T(8,128)S(1)}, f32[4,2,256,128]{3,2,1,0:T(8,128)}, u32[]{:S(2)}, u32[]{:S(2)}) collective-permute-start(f32[4,2,256,128]{3,2,1,0:T(8,128)S(1)} %pad_maximum_fusion.refs_0_), channel_id=1, source_target_pairs={{0,12},{1,13},{2,14},{3,15},{4,0},{5,1},{6,2},{7,3},{8,4},{9,5},{1... | collective-permute-start | bytes 3145736 | tf_op jit(solution)/shard_map/ppermute | solution.py:209
  147.7 29.4 %collective-permute-start.16 = (f32[4,2,256,128]{3,2,1,0:T(8,128)S(1)}, f32[4,2,256,128]{3,2,1,0:T(8,128)}, u32[]{:S(2)}, u32[]{:S(2)}) collective-permute-start(f32[4,2,256,128]{3,2,1,0:T(8,128)S(1)} %pad_maximum_fusion.refs_0_), channel_id=1, source_target_pairs={{0,16},{1,17},{2,18},{3,19},{4,20},{5,21},{6,22},{7,23},{8,24},{9,... | collective-permute-start | bytes 3145736 | tf_op jit(solution)/shard_map/ppermute | solution.py:209
  161.3 9.7 %collective-permute-start.21 = (f32[2,2,256,128]{3,2,1,0:T(8,128)S(1)}, f32[2,2,256,128]{3,2,1,0:T(8,128)}, u32[]{:S(2)}, u32[]{:S(2)}) collective-permute-start(f32[2,2,256,128]{3,2,1,0:T(8,128)S(1)} %slice.66), channel_id=1, source_target_pairs={{0,4},{1,5},{2,6},{3,7},{4,8},{5,9},{6,10},{7,11},{8,12},{9,13},{1... | collective-permute-start | bytes 1572872 | tf_op jit(solution)/shard_map/ppermute | solution.py:209
  161.4 20.6 %collective-permute-start.19 = (f32[4,2,256,128]{3,2,1,0:T(8,128)}, f32[4,2,256,128]{3,2,1,0:T(8,128)}, u32[]{:S(2)}, u32[]{:S(2)}) collective-permute-start(f32[4,2,256,128]{3,2,1,0:T(8,128)} %collective-permute-done.17.refs_0_), channel_id=1, source_target_pairs={{0,16},{1,17},{2,18},{3,19},{4,20},{5,21},{6,22},{7,23},{8,24},{9,... | collective-permute-start | bytes 3145736 | tf_op jit(solution)/shard_map/ppermute | solution.py:209
  162.8 19.3 %collective-permute-start.20 = (f32[4,2,256,128]{3,2,1,0:T(8,128)}, f32[4,2,256,128]{3,2,1,0:T(8,128)}, u32[]{:S(2)}, u32[]{:S(2)}) collective-permute-start(f32[4,2,256,128]{3,2,1,0:T(8,128)} %collective-permute-done.18.refs_1_), channel_id=1, source_target_pairs={{0,16},{1,17},{2,18},{3,19},{4,20},{5,21},{6,22},{7,23},{8,24},{9,... | collective-permute-start | bytes 3145736 | tf_op jit(solution)/shard_map/ppermute | solution.py:209
  163.9 9.2 %collective-permute-start.22 = (f32[2,2,256,128]{3,2,1,0:T(8,128)S(1)}, f32[2,2,256,128]{3,2,1,0:T(8,128)}, u32[]{:S(2)}, u32[]{:S(2)}) collective-permute-start(f32[2,2,256,128]{3,2,1,0:T(8,128)S(1)} %slice.67), channel_id=1, source_target_pairs={{0,12},{1,13},{2,14},{3,15},{4,0},{5,1},{6,2},{7,3},{8,4},{9,5},{1... | collective-permute-start | bytes 1572872 | tf_op jit(solution)/shard_map/ppermute | solution.py:209
  171.1 19.2 %collective-permute-start.23 = (f32[2,2,256,128]{3,2,1,0:T(8,128)}, f32[2,2,256,128]{3,2,1,0:T(8,128)}, u32[]{:S(2)}, u32[]{:S(2)}) collective-permute-start(f32[2,2,256,128]{3,2,1,0:T(8,128)} %collective-permute-done.21.refs_0_), channel_id=1, source_target_pairs={{0,16},{1,17},{2,18},{3,19},{4,20},{5,21},{6,22},{7,23},{8,24},{9,... | collective-permute-start | bytes 1572872 | tf_op jit(solution)/shard_map/ppermute | solution.py:209
  173.2 17.1 %collective-permute-start.24 = (f32[2,2,256,128]{3,2,1,0:T(8,128)}, f32[2,2,256,128]{3,2,1,0:T(8,128)}, u32[]{:S(2)}, u32[]{:S(2)}) collective-permute-start(f32[2,2,256,128]{3,2,1,0:T(8,128)} %collective-permute-done.22.refs_1_), channel_id=1, source_target_pairs={{0,16},{1,17},{2,18},{3,19},{4,20},{5,21},{6,22},{7,23},{8,24},{9,... | collective-permute-start | bytes 1572872 | tf_op jit(solution)/shard_map/ppermute | solution.py:209
  (7 other events, 18.9 us)
Sparse Core Ops, SparseCore 0:
  9.2 60.1 all-gather.2

commit v3 on v2

--- a/solution.py
+++ b/solution.py
@@ -39,10 +39,6 @@
 def packed_product(left, right):
     out = mm(left, right)
     return out[:, :TILE] + out[:, TILE:]
-
-
-def full_dot(a, b):
-    return jnp.dot(a, b, precision=lax.Precision.HIGHEST, preferred_element_type=F32)
 
 
 def invert_body(info, lead_ref, out_ref):
@@ -60,7 +56,8 @@
         while step < TILE:
             below = ((i // (2 * step)) == (j // (2 * step))) & ((i // step) > (j // step))
             corner = jnp.where(below, block, zero)
-            inverse = inverse - full_dot(inverse, full_dot(corner, inverse))
+            product = packed_product(pack_left(corner), pack_right(inverse))
+            inverse = inverse - packed_product(pack_left(inverse), pack_right(product))
             step *= 2
         out_ref[pl.ds(start, TILE), :] = inverse
 
@@ -74,6 +71,25 @@
         compiler_params=PARAMS,
         name="invert_diagonal",
     )(info, lead)
+
+
+def pack_slices(info, pieces, places, name):
+    def body(info, *refs):
+        out_ref = refs[-1]
+        for ref, parts in zip(refs, places):
+            for group, steps, start, to, rows in parts:
+                half = {"own": info[0], "pair": 1 - info[0]}.get(group, group)
+                k = 4 * half + lax.rem(info[1] + steps, 4)
+                out_ref[k, pl.ds(to, rows), :] = pack_left(ref[pl.ds(start, rows), :])
+
+    return pl.pallas_call(
+        body,
+        out_shape=jax.ShapeDtypeStruct((8, 1024, 256), BF16),
+        in_specs=[SM] + [VM] * len(pieces),
+        out_specs=VM,
+        compiler_params=PARAMS,
+        name=name,
+    )(info, *pieces)
 
 
 def solve_body(tri_ref, rhs_ref, out_ref):
@@ -81,12 +97,12 @@
     out_ref[...] = rhs_ref[...]
     for k in range(count):
         here = pl.ds(k * TILE, TILE)
-        solved = packed_product(pack_left(tri_ref[k, here, :]), pack_right(out_ref[here, :]))
+        solved = packed_product(tri_ref[k, here, :], pack_right(out_ref[here, :]))
         out_ref[here, :] = solved
         right = pack_right(solved)
         for i in range(k + 1, count):
             there = pl.ds(i * TILE, TILE)
-            out_ref[there, :] = out_ref[there, :] - packed_product(pack_left(tri_ref[k, there, :]), right)
+            out_ref[there, :] = out_ref[there, :] - packed_product(tri_ref[k, there, :], right)
 
 
 def solve(tri, rhs):
@@ -107,7 +123,7 @@
         for i in range(count):
             there = pl.ds(i * TILE, TILE)
             base = rhs_ref[there, :] if k == 0 else out_ref[there, :]
-            out_ref[there, :] = base - packed_product(pack_left(tri_ref[k, there, :]), right)
+            out_ref[there, :] = base - packed_product(tri_ref[k, there, :], right)
 
 
 def residual(tri, rhs, x):
@@ -239,6 +255,43 @@
     return after, far_low, far_high, before
 
 
+def gather_first(lead, yl):
+    swapped = move(lead, lambda a, b, c, d: (0, 0, 1 - c, d) if a == 0 and b == 0 and c < 2 else None)
+    full = jnp.where(yl == 0, lead, swapped)
+    lower = jnp.where(yl == 0, swapped[512:], lead[512:])
+    pair = jnp.concatenate([full, lower], 0)
+
+    def along(step):
+        return lambda a, b, c, d: (0, 0, c, d + step) if a == 0 and b == 0 and c < 2 else None
+
+    before, after = move(pair, along(1)), move(pair, along(-1))
+    far_low, far_high = move(before[:768], along(1)), move(after[768:], along(-1))
+    pieces, places = [], []
+    for piece, steps in ((pair, 0), (after, 1), (before, 3)):
+        pieces.append(piece)
+        places.append([(0, steps, 0, 0, 1024), (1, steps, 1024, 512, 512)])
+    pieces += [far_low, far_high]
+    places += [[(0, 2, 0, 0, 768)], [(0, 2, 0, 768, 256), (1, 2, 256, 512, 512)]]
+    return pieces, places
+
+
+def gather_second(lead):
+    def along(step):
+        return lambda a, b, c, d: (0, 1, c, d + step) if a == 0 and b == 1 else None
+
+    def pair(value):
+        return move(value, lambda a, b, c, d: (0, 1, c + 1 - 2 * (c % 2), d) if a == 0 and b == 1 else None)
+
+    before, after = move(lead, along(1)), move(lead, along(-1))
+    far_low, far_high = move(before[:512], along(1)), move(after[512:], along(-1))
+    pieces, places = [], []
+    for piece, steps, row in ((lead, 0, 0), (after, 1, 0), (before, 3, 0), (far_low, 2, 0), (far_high, 2, 512)):
+        for group, value in (("own", piece), ("pair", pair(piece))):
+            pieces.append(value)
+            places.append([(group, steps, 0, row, value.shape[0])])
+    return pieces, places
+
+
 def shards(factor, cross_cov):
     xi, core = lax.axis_index("x"), lax.axis_index("core")
     yh, yl, z = lax.axis_index("yh"), lax.axis_index("yl"), lax.axis_index("z")
@@ -248,50 +301,62 @@
     local = factor[:, 0]
     rhs = cross_cov[:, 0]
 
-    own_rhs = rhs[0].reshape(64, 8, TILE).transpose(1, 0, 2)
-    columns = lax.all_to_all(jnp.concatenate([own_rhs, own_rhs], 0), COL, 0, 0, tiled=True)
-    columns = columns.reshape(1024, TILE)
-
     diagonal = ((row_id == 0) & (yh == 0)) | ((row_id == 1) & (yh == 1))
     info = jnp.stack([diagonal.astype(jnp.int32), slice_id.astype(jnp.int32)])
     lead = invert_diagonal(info, local[0])
-    tri = lax.all_gather(lead, ("yl", "z"), axis=0, tiled=False)
-
-    by_rows = local.reshape(4, 16, 64, TILE).transpose(1, 0, 2, 3).reshape(16, 256, TILE)
-    by_rows, tri = lax.optimization_barrier((by_rows, tri))
-    left = lax.all_to_all(by_rows, COL, 0, 0, tiled=True)
-
-    first = solve(tri, columns)
+
+    own_rhs = rhs[0].reshape(64, 2, 4, TILE).transpose(1, 2, 0, 3)
+    own_rhs = jnp.where(yh == 0, own_rhs, own_rhs[::-1]).reshape(8, 64, TILE)
+    half = lax.all_to_all(own_rhs, ("yl", "z"), 0, 0, tiled=True).reshape(512, TILE)
+    other_half = move(half, lambda a, b, c, d: (0, b, 3 - c, d) if a == 0 and c >= 2 else None)
+    columns = jnp.concatenate([half, other_half], 0)
+
+    place = jnp.stack([yl, z]).astype(jnp.int32)
+    tri_first = pack_slices(place, *gather_first(lead, yl), "pack_first")
+    tri_second = pack_slices(place, *gather_second(lead), "pack_second")
+
+    first = solve(tri_first, columns)
     sent = move(first, lambda a, b, c, d: (0, 1, c, d) if a == 0 and b == 0 and c < 2 else None)
     second_rhs = move(
-        residual(tri, columns, sent),
+        residual(tri_second, columns, sent),
         lambda a, b, c, d: (0, 1, 3 - c, d) if a == 0 and b == 1 and c < 2 else None,
     )
-    second = solve(tri, second_rhs)
+    by_rows = local.reshape(4, 16, 64, TILE).transpose(1, 0, 2, 3).reshape(16, 256, TILE)
+    by_rows, second_rhs = lax.optimization_barrier((by_rows, second_rhs))
+    left = lax.all_to_all(by_rows, COL, 0, 0, tiled=True)
+    second = solve(tri_second, second_rhs)
     dealt0 = deal(first, core, yh, xi, 0, 0)
-    second, left = lax.optimization_barrier((second, left))
     dealt1 = deal(second, core, yh, xi, 1, 1)
 
     info2 = jnp.stack([row_id, core, 2 * yh + yl, z, col_id]).astype(jnp.int32)
-    high, low, out = prepare(info2[:1], left, rhs.reshape(256, 1024))
 
     def swap(value):
         return move(value, lambda a, b, c, d: (a, 1 - b, c, d))
+
+    def add(out, pieces, places, name):
+        return accumulate(info2, out, high, low, pieces, places, name)
 
     mine = jnp.stack([dealt0, dealt1])
     after, far_low, far_high, before = ring(mine, True)
     near = jnp.stack([mine, after, jnp.concatenate([far_low, far_high], 0), before])
-    near_other = swap(near)
-    after, far_low, far_high, before = ring(near, False)
-    out = accumulate(info2, out, high, low, [near, near_other], [(0, 0, 0), (1, 0, 0)], "update_near")
-    out = accumulate(
-        info2, out, high, low, [after, before, swap(after), swap(before)],
-        [(0, 1, 0), (0, 3, 0), (1, 1, 0), (1, 3, 0)], "update_next",
+
+    def along(step):
+        return lambda a, b, c, d: (a, b, c + step, d) if b == 0 else (a, b, c, d + step)
+
+    before, after, near_other = move(near, along(1)), move(near, along(-1)), swap(near)
+    high, low, out = prepare(info2[:1], left, rhs.reshape(256, 1024))
+    out = add(out, [near], [(0, 0, 0)], "update_near")
+    before, after, out = lax.optimization_barrier((before, after, out))
+    far_low, far_high = move(before[:2], along(1)), move(after[2:], along(-1))
+    before_other, after_other = swap(before), swap(after)
+    out = add(out, [near_other, after, before], [(1, 0, 0), (0, 1, 0), (0, 3, 0)], "update_next")
+    far_low, far_high, out = lax.optimization_barrier((far_low, far_high, out))
+    far_low_other, far_high_other = swap(far_low), swap(far_high)
+    out = add(
+        out, [after_other, before_other, far_low, far_high],
+        [(1, 1, 0), (1, 3, 0), (0, 2, 0), (0, 2, 2)], "update_far",
     )
-    out = accumulate(
-        info2, out, high, low, [far_low, far_high, swap(far_low), swap(far_high)],
-        [(0, 2, 0), (0, 2, 2), (1, 2, 0), (1, 2, 2)], "update_far",
-    )
+    out = add(out, [far_low_other, far_high_other], [(1, 2, 0), (1, 2, 2)], "update_last")
     return out.reshape(4, 1, 64, 1024)
 
 

time: 204 us -> 185 us (0.907)
  waiting for transfers between devices: 111 us -> 81.9 us
  between operations: 13.8 us -> 0.72 us
  blocking collectives: 0 us -> 11.9 us
  starting transfers between devices: 37.2 us -> 43.9 us
  Pallas kernels: 27.8 us -> 33.8 us
    all_gather x1 -> x0, waiting for transfers between devices: 48.8 us -> none  [shards(): tri = lax.all_gather(lead, ('yl', 'z'), axis=0, tiled=False)]
    ppermute x25 -> x40, waiting for transfers between devices: 47.2 us -> 81.9 us  [move(): return lax.ppermute(value, AXES, pairs)]
    all_to_all x1, waiting for transfers between devices: 15.1 us -> 0.01 us  [shards(): left = lax.all_to_all(by_rows, COL, 0, 0, tiled=True)]
    all_to_all x0 -> x1, blocking collectives: none -> 11.9 us  [shards(): lax.all_to_all(own_rhs, ('yl', 'z'), 0, 0, tiled=True).reshape(512, TILE)]
    ppermute x25 -> x40, starting transfers between devices: 25.4 us -> 34.9 us  [move(): return lax.ppermute(value, AXES, pairs)]
    all_to_all x1 -> x0, starting transfers between devices: 7.77 us -> none  [shards(): lax.all_to_all(jnp.concatenate([own_rhs, own_rhs], 0), COL, 0, 0, tiled=T...]
    pallas_call x0 -> x2, Pallas kernels: none -> 5.9 us  [pack_slices(): pl.pallas_call(body, out_shape=jax.ShapeDtypeStruct((8, 1024, 256), BF16)...]
    all_to_all x1, starting transfers between devices: 4.05 us -> 9 us  [shards(): left = lax.all_to_all(by_rows, COL, 0, 0, tiled=True)]
  transfers between devices with their start and end apart: 28 -> 41, of which waited for: 9 -> 4; matrix products, arithmetic and copies ran while one was open for 4% -> 3% of each run, Pallas kernels for 10% -> 16%
where the time goes in v3:
time: 185 us; the launch traced here: 184 us
  waiting for transfers between devices  81.9 us (44%)
  starting transfers between devices  43.9 us (24%)
  Pallas kernels  33.8 us (18%)
  blocking collectives  11.9 us (6%)
  local copies, waits for them, and re-layouts  10.9 us (6%)
    ppermute x40, waiting for transfers between devices, move(): return lax.ppermute(value, AXES, pairs)  81.9 us
    ppermute x40, starting transfers between devices, move(): return lax.ppermute(value, AXES, pairs)  34.9 us
    pallas_call x4, Pallas kernels, accumulate(): pl.pallas_call(body, out_shape=jax.ShapeDtypeStruct(base.shape, F32), in_...  19.4 us
    all_to_all x1, blocking collectives, shards(): lax.all_to_all(own_rhs, ('yl', 'z'), 0, 0, tiled=True).reshape(512, TILE)  11.9 us
    all_to_all x1, starting transfers between devices, shards(): left = lax.all_to_all(by_rows, COL, 0, 0, tiled=True)  9 us
    pallas_call x2, Pallas kernels, pack_slices(): pl.pallas_call(body, out_shape=jax.ShapeDtypeStruct((8, 1024, 256), BF16)...  5.9 us
    unnamed x8, local copies, waits for them, and re-layouts  5.61 us
    pallas_call x2, Pallas kernels, solve(): pl.pallas_call(solve_body, out_shape=jax.ShapeDtypeStruct(rhs.shape, F32)...  5.36 us
  transfers between devices with their start and end apart: 41, of which 4 were waited for; matrix products, arithmetic and copies ran while one was open for 3% of the time, Pallas kernels for 16%

profile of v3, /device:TPU:5, one launch (start us, length us, event | category | flops | bytes accessed | tf_op | source)
XLA Modules:
  0.0 183.9 jit_solution(10441648575706883793)
XLA Ops:
  4.3 11.9 %all_to_all.10 = f32[8,64,128]{2,1,0:T(8,128)S(1)} all-to-all(f32[8,64,128]{2,1,0:T(8,128)S(1)} %bitcast.37), channel_id=1, replica_groups=mesh['x'=4,'core'=2,'yh'=2,'yl'=2,'z'=4] {'yl','z'}, dimensions={0} | all-to-all | bytes 524288 | tf_op jit(solution)/shard_map/all_to_all | solution.py:310
  23.5 2.9 %pack_first.1.tri_ref = bf16[8,1024,256]{2,1,0:T(8,128)(2,1)} custom-call(s32[2]{0:T(128)S(1)} %pad_add_fusion.info, f32[1536,128]{1,0:T(8,128)S(1)} %pad_maximum_fusion.1.refs_0_, f32[1536,128]{1,0:T(8,128)S(1)} %collective-permute-done.1.refs_1_, f32[1536,128]{1,0:T(8,128)S(1)} %collective-permute-done.2.refs_2_, ...), custom_call_target="tpu_custom_call" | custom-call | tf_op jit(solution)/shard_map/pack_first/pallas_call | solution.py:85
  26.4 2.2 %copy-done.1 = bf16[8,1024,256]{2,1,0:T(8,128)(2,1)S(1)} copy-done((bf16[8,1024,256]{2,1,0:T(8,128)(2,1)S(1)}, bf16[8,1024,256]{2,1,0:T(8,128)(2,1)}, u32[]{:S(2)}) %copy-start.1) | copy-done | bytes 4194328
  28.6 2.7 %block_solve.2 = f32[1024,128]{1,0:T(8,128)S(1)} custom-call(bf16[8,1024,256]{2,1,0:T(8,128)(2,1)S(1)} %copy-done.1, f32[1024,128]{1,0:T(8,128)S(1)} %pad_maximum_fusion.2.rhs_ref), custom_call_target="tpu_custom_call" | custom-call | tf_op jit(solution)/shard_map/block_solve/pallas_call | solution.py:109
  33.4 3.0 %pack_second.1.tri_ref = bf16[8,1024,256]{2,1,0:T(8,128)(2,1)} custom-call(s32[2]{0:T(128)S(1)} %pad_add_fusion.info, f32[1024,128]{1,0:T(8,128)S(1)} %invert_diagonal.1.refs_0_, f32[1024,128]{1,0:T(8,128)S(1)} %collective-permute-done.11.refs_1_, f32[1024,128]{1,0:T(8,128)S(1)} %collective-permute-done.12.refs_2_, ...), custom_call_target="tpu_custom_call" | custom-call | tf_op jit(solution)/shard_map/pack_second/pallas_call | solution.py:85
  36.5 2.2 %copy-done = bf16[8,1024,256]{2,1,0:T(8,128)(2,1)S(1)} copy-done((bf16[8,1024,256]{2,1,0:T(8,128)(2,1)S(1)}, bf16[8,1024,256]{2,1,0:T(8,128)(2,1)}, u32[]{:S(2)}) %copy-start) | copy-done | bytes 4194328
  41.4 1.6 copy.8
  42.9 2.7 %block_solve.3 = f32[1024,128]{1,0:T(8,128)S(1)} custom-call(bf16[8,1024,256]{2,1,0:T(8,128)(2,1)S(1)} %copy-done, f32[1024,128]{1,0:T(8,128)S(1)} %collective-permute-done.21.rhs_ref), custom_call_target="tpu_custom_call" | custom-call | tf_op jit(solution)/shard_map/block_solve/pallas_call | solution.py:109
  53.3 49.7 %collective-permute-done.10 = f32[256,128]{1,0:T(8,128)S(1)} collective-permute-done((f32[256,128]{1,0:T(8,128)S(1)}, f32[256,128]{1,0:T(8,128)S(1)}, u32[]{:S(2)}, u32[]{:S(2)}) %collective-permute-start.10) | collective-permute-done | bytes 131104 | tf_op jit(solution)/shard_map/ppermute | solution.py:225
  103.0 9.0 %all-to-all-start.1 = ((f32[16,256,128]{2,1,0:T(8,128)}), f32[16,256,128]{2,1,0:T(8,128)S(1)}, u32[]{:S(2)}, u32[]{:S(2)}) async-start(f32[16,256,128]{2,1,0:T(8,128)} %bitcast.34), calls=%async_computation.1 | async-start | bytes 4194304 | tf_op jit(solution)/shard_map/all_to_all | solution.py:326
  112.2 1.4 collective-permute-start.28
  114.9 24.2 %collective-permute-done.28 = f32[2,256,128]{2,1,0:T(8,128)S(1)} collective-permute-done((f32[2,256,128]{2,1,0:T(8,128)S(1)}, f32[2,256,128]{2,1,0:T(8,128)S(1)}, u32[]{:S(2)}, u32[]{:S(2)}) %collective-permute-start.28) | collective-permute-done | bytes 262176 | tf_op jit(solution)/shard_map/ppermute | solution.py:225
  139.2 2.7 %collective-permute-start.30 = (f32[1,256,128]{2,1,0:T(8,128)S(1)}, f32[1,256,128]{2,1,0:T(8,128)S(1)}, u32[]{:S(2)}, u32[]{:S(2)}) collective-permute-start(f32[1,256,128]{2,1,0:T(8,128)S(1)} %slice.97), channel_id=1, source_target_pairs={{0,3},{1,0},{2,1},{3,2},{4,7},{5,4},{6,5},{7,6},{8,11},{9,8},{10,9... | collective-permute-start | bytes 393224 | tf_op jit(solution)/shard_map/ppermute | solution.py:225
  141.9 2.3 %collective-permute-done.29 = f32[1,256,128]{2,1,0:T(8,128)S(1)} collective-permute-done((f32[1,256,128]{2,1,0:T(8,128)S(1)}, f32[1,256,128]{2,1,0:T(8,128)S(1)}, u32[]{:S(2)}, u32[]{:S(2)}) %collective-permute-start.29) | collective-permute-done | bytes 131104 | tf_op jit(solution)/shard_map/ppermute | solution.py:225
  144.3 1.4 collective-permute-start.31
  145.7 1.5 collective-permute-start.32
  149.4 1.4 prepare_update.1
  150.7 3.4 %update_near.1.base_ref = f32[256,1024]{1,0:T(8,128)} custom-call(s32[5]{0:T(128)S(1)} %stack.66.info, f32[256,1024]{1,0:T(8,128)} %get-tuple-element.18.base_ref, bf16[8,256,256]{2,1,0:T(8,128)(2,1)S(1)} %get-tuple-element.19.high_ref, bf16[8,256,256]{2,1,0:T(8,128)(2,1)S(1)} %get-tuple-element.20.low_ref, ...), custom_call_target="tpu_custom_call", output_to_operand_aliasing={{}: (1, {})} | custom-call | tf_op jit(solution)/shard_map/update_near/pallas_call | solution.py:201
  154.2 5.6 %collective-permute-done.31.refs_2_ = f32[4,2,256,128]{3,2,1,0:T(8,128)} collective-permute-done((f32[4,2,256,128]{3,2,1,0:T(8,128)S(1)}, f32[4,2,256,128]{3,2,1,0:T(8,128)}, u32[]{:S(2)}, u32[]{:S(2)}) %collective-permute-start.31) | collective-permute-done | bytes 1048608 | tf_op jit(solution)/shard_map/ppermute | solution.py:225
  162.1 2.7 %collective-permute-start.34 = (f32[2,2,256,128]{3,2,1,0:T(8,128)S(1)}, f32[2,2,256,128]{3,2,1,0:T(8,128)S(1)}, u32[]{:S(2)}, u32[]{:S(2)}) collective-permute-start(f32[2,2,256,128]{3,2,1,0:T(8,128)S(1)} %slice.81), channel_id=1, source_target_pairs={{0,12},{1,13},{2,14},{3,15},{4,0},{5,1},{6,2},{7,3},{8,4},{9,5},{1... | collective-permute-start | bytes 1572872 | tf_op jit(solution)/shard_map/ppermute | solution.py:225
  164.8 2.4 %collective-permute-start.36 = (f32[4,2,256,128]{3,2,1,0:T(8,128)}, f32[4,2,256,128]{3,2,1,0:T(8,128)S(1)}, u32[]{:S(2)}, u32[]{:S(2)}) collective-permute-start(f32[4,2,256,128]{3,2,1,0:T(8,128)} %collective-permute-done.32.refs_1_), channel_id=1, source_target_pairs={{0,16},{1,17},{2,18},{3,19},{4,20},{5,21},{6,22},{7,23},{8,24},{9,... | collective-permute-start | bytes 3145736 | tf_op jit(solution)/shard_map/ppermute | solution.py:225
  167.2 6.7 %update_next.1.base_ref = f32[256,1024]{1,0:T(8,128)} custom-call(s32[5]{0:T(128)S(1)} %stack.66.info, f32[256,1024]{1,0:T(8,128)} %update_near.1.base_ref, bf16[8,256,256]{2,1,0:T(8,128)(2,1)S(1)} %get-tuple-element.19.high_ref, bf16[8,256,256]{2,1,0:T(8,128)(2,1)S(1)} %get-tuple-element.20.low_ref, ...), custom_call_target="tpu_custom_call", output_to_operand_aliasing={{}: (1, {})} | custom-call | tf_op jit(solution)/shard_map/update_next/pallas_call | solution.py:201
  174.6 5.8 %update_far.1.base_ref = f32[256,1024]{1,0:T(8,128)} custom-call(s32[5]{0:T(128)S(1)} %stack.66.info, f32[256,1024]{1,0:T(8,128)} %update_next.1.base_ref, bf16[8,256,256]{2,1,0:T(8,128)(2,1)S(1)} %get-tuple-element.19.high_ref, bf16[8,256,256]{2,1,0:T(8,128)(2,1)S(1)} %get-tuple-element.20.low_ref, ...), custom_call_target="tpu_custom_call", output_to_operand_aliasing={{}: (1, {})} | custom-call | tf_op jit(solution)/shard_map/update_far/pallas_call | solution.py:201
  180.4 3.4 %update_last.1 = f32[256,1024]{1,0:T(8,128)} custom-call(s32[5]{0:T(128)S(1)} %stack.66.info, f32[256,1024]{1,0:T(8,128)} %update_far.1.base_ref, bf16[8,256,256]{2,1,0:T(8,128)(2,1)S(1)} %get-tuple-element.19.high_ref, bf16[8,256,256]{2,1,0:T(8,128)(2,1)S(1)} %get-tuple-element.20.low_ref, ...), custom_call_target="tpu_custom_call", output_to_operand_aliasing={{}: (1, {})} | custom-call | tf_op jit(solution)/shard_map/update_last/pallas_call | solution.py:201
  (113 shorter events, 30.3 us)
Async XLA Ops:
  2.6 15.7 %collective-permute-start.2 = (f32[1536,128]{1,0:T(8,128)S(1)}, f32[1536,128]{1,0:T(8,128)S(1)}, u32[]{:S(2)}, u32[]{:S(2)}) collective-permute-start(f32[1536,128]{1,0:T(8,128)S(1)} %pad_maximum_fusion.1.refs_0_), channel_id=1, source_target_pairs={{0,1},{1,2},{2,3},{3,0},{4,5},{5,6},{6,7},{7,4}} | collective-permute-start | bytes 2359304 | tf_op jit(solution)/shard_map/ppermute | solution.py:225
  3.4 15.8 %collective-permute-start.1 = (f32[1536,128]{1,0:T(8,128)S(1)}, f32[1536,128]{1,0:T(8,128)S(1)}, u32[]{:S(2)}, u32[]{:S(2)}) collective-permute-start(f32[1536,128]{1,0:T(8,128)S(1)} %pad_maximum_fusion.1.refs_0_), channel_id=1, source_target_pairs={{0,3},{1,0},{2,1},{3,2},{4,7},{5,4},{6,5},{7,6}} | collective-permute-start | bytes 2359304 | tf_op jit(solution)/shard_map/ppermute | solution.py:225
  18.4 12.9 %collective-permute-start.11 = (f32[1024,128]{1,0:T(8,128)S(1)}, f32[1024,128]{1,0:T(8,128)S(1)}, u32[]{:S(2)}, u32[]{:S(2)}) collective-permute-start(f32[1024,128]{1,0:T(8,128)S(1)} %invert_diagonal.1.refs_0_), channel_id=1, source_target_pairs={{16,20},{17,21},{18,22},{19,23},{20,16},{21,17},{22,18},{23,19},{2... | collective-permute-start | bytes 1572872 | tf_op jit(solution)/shard_map/ppermute | solution.py:225
  20.7 11.3 %collective-permute-start.16 = (f32[512,128]{1,0:T(8,128)S(1)}, f32[512,128]{1,0:T(8,128)S(1)}, u32[]{:S(2)}, u32[]{:S(2)}) collective-permute-start(f32[512,128]{1,0:T(8,128)S(1)} %slice.90), channel_id=1, source_target_pairs={{16,17},{17,18},{18,19},{19,16},{20,21},{21,22},{22,23},{23,20},{2... | collective-permute-start | bytes 786440 | tf_op jit(solution)/shard_map/ppermute | solution.py:225
  21.4 11.3 %collective-permute-start.18 = (f32[512,128]{1,0:T(8,128)S(1)}, f32[512,128]{1,0:T(8,128)S(1)}, u32[]{:S(2)}, u32[]{:S(2)}) collective-permute-start(f32[512,128]{1,0:T(8,128)S(1)} %slice.91), channel_id=1, source_target_pairs={{16,19},{17,16},{18,17},{19,18},{20,23},{21,20},{22,21},{23,22},{2... | collective-permute-start | bytes 786440 | tf_op jit(solution)/shard_map/ppermute | solution.py:225
  22.1 11.3 %collective-permute-start.13 = (f32[1024,128]{1,0:T(8,128)S(1)}, f32[1024,128]{1,0:T(8,128)S(1)}, u32[]{:S(2)}, u32[]{:S(2)}) collective-permute-start(f32[1024,128]{1,0:T(8,128)S(1)} %collective-permute-done.12.refs_2_), channel_id=1, source_target_pairs={{16,20},{17,21},{18,22},{19,23},{20,16},{21,17},{22,18},{23,19},{2... | collective-permute-start | bytes 1572872 | tf_op jit(solution)/shard_map/ppermute | solution.py:225
  22.8 10.6 %collective-permute-start.15 = (f32[1024,128]{1,0:T(8,128)S(1)}, f32[1024,128]{1,0:T(8,128)S(1)}, u32[]{:S(2)}, u32[]{:S(2)}) collective-permute-start(f32[1024,128]{1,0:T(8,128)S(1)} %collective-permute-done.14.refs_4_), channel_id=1, source_target_pairs={{16,20},{17,21},{18,22},{19,23},{20,16},{21,17},{22,18},{23,19},{2... | collective-permute-start | bytes 1572872 | tf_op jit(solution)/shard_map/ppermute | solution.py:225
  31.3 5.2 %collective-permute-start.20 = (f32[1024,128]{1,0:T(8,128)S(1)}, f32[1024,128]{1,0:T(8,128)S(1)}, u32[]{:S(2)}, u32[]{:S(2)}) collective-permute-start(f32[1024,128]{1,0:T(8,128)S(1)} %block_solve.2), channel_id=1, source_target_pairs={{0,16},{1,17},{2,18},{3,19},{4,20},{5,21},{6,22},{7,23}} | collective-permute-start | bytes 1572872 | tf_op jit(solution)/shard_map/ppermute | solution.py:225
  40.7 5.7 %collective-permute-start.6 = (f32[512,128]{1,0:T(8,128)S(1)}, f32[512,128]{1,0:T(8,128)S(1)}, u32[]{:S(2)}, u32[]{:S(2)}) collective-permute-start(f32[512,128]{1,0:T(8,128)S(1)} %slice.87), channel_id=1, source_target_pairs={{0,16},{1,17},{2,18},{3,19},{4,20},{5,21},{6,22},{7,23},{8,24},{9,... | collective-permute-start | bytes 786440 | tf_op jit(solution)/shard_map/ppermute | solution.py:225
  50.0 53.1 %collective-permute-start.10 = (f32[256,128]{1,0:T(8,128)S(1)}, f32[256,128]{1,0:T(8,128)S(1)}, u32[]{:S(2)}, u32[]{:S(2)}) collective-permute-start(f32[256,128]{1,0:T(8,128)S(1)} %collective-permute-done.8), channel_id=1, source_target_pairs={{32,64},{33,65},{34,66},{35,67},{36,68},{37,69},{38,70},{39,71},{4... | collective-permute-start | bytes 393224 | tf_op jit(solution)/shard_map/ppermute | solution.py:225
  51.3 60.8 %collective-permute-start.25 = (f32[256,128]{1,0:T(8,128)S(1)}, f32[256,128]{1,0:T(8,128)S(1)}, u32[]{:S(2)}, u32[]{:S(2)}) collective-permute-start(f32[256,128]{1,0:T(8,128)S(1)} %slice_select_fusion.3), channel_id=1, source_target_pairs={{0,96},{1,97},{2,98},{3,99},{4,100},{5,101},{6,102},{7,103},{8,104... | collective-permute-start | bytes 393224 | tf_op jit(solution)/shard_map/ppermute | solution.py:225
  51.9 60.1 %collective-permute-start.26 = (f32[256,128]{1,0:T(8,128)S(1)}, f32[256,128]{1,0:T(8,128)S(1)}, u32[]{:S(2)}, u32[]{:S(2)}) collective-permute-start(f32[256,128]{1,0:T(8,128)S(1)} %collective-permute-done.24), channel_id=1, source_target_pairs={{32,64},{33,65},{34,66},{35,67},{36,68},{37,69},{38,70},{39,71},{4... | collective-permute-start | bytes 393224 | tf_op jit(solution)/shard_map/ppermute | solution.py:225
  103.0 45.1 %all-to-all-start.1 = ((f32[16,256,128]{2,1,0:T(8,128)}), f32[16,256,128]{2,1,0:T(8,128)S(1)}, u32[]{:S(2)}, u32[]{:S(2)}) async-start(f32[16,256,128]{2,1,0:T(8,128)} %bitcast.34), calls=%async_computation.1 | async-start | bytes 4194304 | tf_op jit(solution)/shard_map/all_to_all | solution.py:326
  112.2 26.9 %collective-permute-start.28 = (f32[2,256,128]{2,1,0:T(8,128)S(1)}, f32[2,256,128]{2,1,0:T(8,128)S(1)}, u32[]{:S(2)}, u32[]{:S(2)}) collective-permute-start(f32[2,256,128]{2,1,0:T(8,128)S(1)} %get-tuple-element.28), channel_id=1, source_target_pairs={{0,1},{1,2},{2,3},{3,0},{4,5},{5,6},{6,7},{7,4},{8,9},{9,10},{10,1... | collective-permute-start | bytes 786440 | tf_op jit(solution)/shard_map/ppermute | solution.py:225
  113.6 25.6 %collective-permute-start.27 = (f32[2,256,128]{2,1,0:T(8,128)S(1)}, f32[2,256,128]{2,1,0:T(8,128)S(1)}, u32[]{:S(2)}, u32[]{:S(2)}) collective-permute-start(f32[2,256,128]{2,1,0:T(8,128)S(1)} %get-tuple-element.28), channel_id=1, source_target_pairs={{0,3},{1,0},{2,1},{3,2},{4,7},{5,4},{6,5},{7,6},{8,11},{9,8},{10,9... | collective-permute-start | bytes 786440 | tf_op jit(solution)/shard_map/ppermute | solution.py:225
  144.3 15.5 %collective-permute-start.31 = (f32[4,2,256,128]{3,2,1,0:T(8,128)S(1)}, f32[4,2,256,128]{3,2,1,0:T(8,128)}, u32[]{:S(2)}, u32[]{:S(2)}) collective-permute-start(f32[4,2,256,128]{3,2,1,0:T(8,128)S(1)} %pad_maximum_fusion.refs_0_), channel_id=1, source_target_pairs={{0,4},{1,5},{2,6},{3,7},{4,8},{5,9},{6,10},{7,11},{8,12},{9,13},{1... | collective-permute-start | bytes 3145736 | tf_op jit(solution)/shard_map/ppermute | solution.py:225
  145.7 14.1 %collective-permute-start.32 = (f32[4,2,256,128]{3,2,1,0:T(8,128)S(1)}, f32[4,2,256,128]{3,2,1,0:T(8,128)}, u32[]{:S(2)}, u32[]{:S(2)}) collective-permute-start(f32[4,2,256,128]{3,2,1,0:T(8,128)S(1)} %pad_maximum_fusion.refs_0_), channel_id=1, source_target_pairs={{0,12},{1,13},{2,14},{3,15},{4,0},{5,1},{6,2},{7,3},{8,4},{9,5},{1... | collective-permute-start | bytes 3145736 | tf_op jit(solution)/shard_map/ppermute | solution.py:225
  147.2 20.0 %collective-permute-start.35 = (f32[4,2,256,128]{3,2,1,0:T(8,128)S(1)}, f32[4,2,256,128]{3,2,1,0:T(8,128)}, u32[]{:S(2)}, u32[]{:S(2)}) collective-permute-start(f32[4,2,256,128]{3,2,1,0:T(8,128)S(1)} %pad_maximum_fusion.refs_0_), channel_id=1, source_target_pairs={{0,16},{1,17},{2,18},{3,19},{4,20},{5,21},{6,22},{7,23},{8,24},{9,... | collective-permute-start | bytes 3145736 | tf_op jit(solution)/shard_map/ppermute | solution.py:225
  160.9 13.1 %collective-permute-start.33 = (f32[2,2,256,128]{3,2,1,0:T(8,128)S(1)}, f32[2,2,256,128]{3,2,1,0:T(8,128)S(1)}, u32[]{:S(2)}, u32[]{:S(2)}) collective-permute-start(f32[2,2,256,128]{3,2,1,0:T(8,128)S(1)} %slice.80), channel_id=1, source_target_pairs={{0,4},{1,5},{2,6},{3,7},{4,8},{5,9},{6,10},{7,11},{8,12},{9,13},{1... | collective-permute-start | bytes 1572872 | tf_op jit(solution)/shard_map/ppermute | solution.py:225
  162.1 11.9 %collective-permute-start.34 = (f32[2,2,256,128]{3,2,1,0:T(8,128)S(1)}, f32[2,2,256,128]{3,2,1,0:T(8,128)S(1)}, u32[]{:S(2)}, u32[]{:S(2)}) collective-permute-start(f32[2,2,256,128]{3,2,1,0:T(8,128)S(1)} %slice.81), channel_id=1, source_target_pairs={{0,12},{1,13},{2,14},{3,15},{4,0},{5,1},{6,2},{7,3},{8,4},{9,5},{1... | collective-permute-start | bytes 1572872 | tf_op jit(solution)/shard_map/ppermute | solution.py:225
  164.8 9.9 %collective-permute-start.36 = (f32[4,2,256,128]{3,2,1,0:T(8,128)}, f32[4,2,256,128]{3,2,1,0:T(8,128)S(1)}, u32[]{:S(2)}, u32[]{:S(2)}) collective-permute-start(f32[4,2,256,128]{3,2,1,0:T(8,128)} %collective-permute-done.32.refs_1_), channel_id=1, source_target_pairs={{0,16},{1,17},{2,18},{3,19},{4,20},{5,21},{6,22},{7,23},{8,24},{9,... | collective-permute-start | bytes 3145736 | tf_op jit(solution)/shard_map/ppermute | solution.py:225
  167.2 7.4 %collective-permute-start.37 = (f32[4,2,256,128]{3,2,1,0:T(8,128)}, f32[4,2,256,128]{3,2,1,0:T(8,128)S(1)}, u32[]{:S(2)}, u32[]{:S(2)}) collective-permute-start(f32[4,2,256,128]{3,2,1,0:T(8,128)} %collective-permute-done.31.refs_2_), channel_id=1, source_target_pairs={{0,16},{1,17},{2,18},{3,19},{4,20},{5,21},{6,22},{7,23},{8,24},{9,... | collective-permute-start | bytes 3145736 | tf_op jit(solution)/shard_map/ppermute | solution.py:225
  174.0 6.5 %collective-permute-start.38 = (f32[2,2,256,128]{3,2,1,0:T(8,128)S(1)}, f32[2,2,256,128]{3,2,1,0:T(8,128)S(1)}, u32[]{:S(2)}, u32[]{:S(2)}) collective-permute-start(f32[2,2,256,128]{3,2,1,0:T(8,128)S(1)} %collective-permute-done.33.refs_2_), channel_id=1, source_target_pairs={{0,16},{1,17},{2,18},{3,19},{4,20},{5,21},{6,22},{7,23},{8,24},{9,... | collective-permute-start | bytes 1572872 | tf_op jit(solution)/shard_map/ppermute | solution.py:225
  174.6 5.8 %collective-permute-start.39 = (f32[2,2,256,128]{3,2,1,0:T(8,128)S(1)}, f32[2,2,256,128]{3,2,1,0:T(8,128)S(1)}, u32[]{:S(2)}, u32[]{:S(2)}) collective-permute-start(f32[2,2,256,128]{3,2,1,0:T(8,128)S(1)} %collective-permute-done.34.refs_3_), channel_id=1, source_target_pairs={{0,16},{1,17},{2,18},{3,19},{4,20},{5,21},{6,22},{7,23},{8,24},{9,... | collective-permute-start | bytes 1572872 | tf_op jit(solution)/shard_map/ppermute | solution.py:225
  (22 other events, 56.5 us)

commit v4 on v3

--- a/solution.py
+++ b/solution.py
@@ -11,7 +11,7 @@
 F32 = jnp.float32
 BF16 = jnp.bfloat16
 TILE = 128
-PARAMS = pltpu.CompilerParams(vmem_limit_bytes=48 * 2**20)
+PARAMS = pltpu.CompilerParams(vmem_limit_bytes=20 * 2**20)
 VM = pl.BlockSpec(memory_space=pltpu.VMEM)
 SM = pl.BlockSpec(memory_space=pltpu.SMEM)
 
@@ -73,23 +73,23 @@
     )(info, lead)
 
 
-def pack_slices(info, pieces, places, name):
+def pack_and_solve(info, pieces, places, rhs):
     def body(info, *refs):
-        out_ref = refs[-1]
-        for ref, parts in zip(refs, places):
-            for group, steps, start, to, rows in parts:
-                half = {"own": info[0], "pair": 1 - info[0]}.get(group, group)
-                k = 4 * half + lax.rem(info[1] + steps, 4)
-                out_ref[k, pl.ds(to, rows), :] = pack_left(ref[pl.ds(start, rows), :])
+        rhs_ref, tri_ref, out_ref = refs[-3:]
+        for ref, (other, steps, row) in zip(refs, places):
+            half = 1 - info[0] if other else info[0]
+            k = 4 * half + lax.rem(info[1] + steps, 4)
+            tri_ref[k, pl.ds(row, ref.shape[0]), :] = pack_left(ref[...])
+        solve_body(tri_ref, rhs_ref, out_ref)
 
     return pl.pallas_call(
         body,
-        out_shape=jax.ShapeDtypeStruct((8, 1024, 256), BF16),
-        in_specs=[SM] + [VM] * len(pieces),
-        out_specs=VM,
-        compiler_params=PARAMS,
-        name=name,
-    )(info, *pieces)
+        out_shape=[jax.ShapeDtypeStruct((8, 1024, 256), BF16), jax.ShapeDtypeStruct(rhs.shape, F32)],
+        in_specs=[SM] + [VM] * (len(pieces) + 1),
+        out_specs=[VM, VM],
+        compiler_params=PARAMS,
+        name="pack_and_solve",
+    )(info, *pieces, rhs)
 
 
 def solve_body(tri_ref, rhs_ref, out_ref):
@@ -255,40 +255,29 @@
     return after, far_low, far_high, before
 
 
-def gather_first(lead, yl):
-    swapped = move(lead, lambda a, b, c, d: (0, 0, 1 - c, d) if a == 0 and b == 0 and c < 2 else None)
-    full = jnp.where(yl == 0, lead, swapped)
-    lower = jnp.where(yl == 0, swapped[512:], lead[512:])
-    pair = jnp.concatenate([full, lower], 0)
+def holds(a, b, c):
+    return (a, b, c // 2) in ((0, 0, 0), (0, 1, 1), (1, 0, 0))
+
+
+def gather_slices(lead, xi):
+    def flip(c):
+        return c + 1 - 2 * (c % 2)
+
+    def across(a, b, c, d):
+        return (1 if b == 1 and c < 2 else 0, 0 if c < 2 else 1, flip(c), d) if a == 0 and (b == 1 or c < 2) else None
 
     def along(step):
-        return lambda a, b, c, d: (0, 0, c, d + step) if a == 0 and b == 0 and c < 2 else None
-
-    before, after = move(pair, along(1)), move(pair, along(-1))
-    far_low, far_high = move(before[:768], along(1)), move(after[768:], along(-1))
+        return lambda a, b, c, d: (a, b, c, d + step) if holds(a, b, c) else None
+
+    hop = move(lead, lambda a, b, c, d: (1, 0, c, d) if (a, b) == (0, 1) and c < 2 else None)
+    pair = move(lead, across)
+    own = jnp.where(xi == 1, hop, lead)
     pieces, places = [], []
-    for piece, steps in ((pair, 0), (after, 1), (before, 3)):
-        pieces.append(piece)
-        places.append([(0, steps, 0, 0, 1024), (1, steps, 1024, 512, 512)])
-    pieces += [far_low, far_high]
-    places += [[(0, 2, 0, 0, 768)], [(0, 2, 0, 768, 256), (1, 2, 256, 512, 512)]]
-    return pieces, places
-
-
-def gather_second(lead):
-    def along(step):
-        return lambda a, b, c, d: (0, 1, c, d + step) if a == 0 and b == 1 else None
-
-    def pair(value):
-        return move(value, lambda a, b, c, d: (0, 1, c + 1 - 2 * (c % 2), d) if a == 0 and b == 1 else None)
-
-    before, after = move(lead, along(1)), move(lead, along(-1))
-    far_low, far_high = move(before[:512], along(1)), move(after[512:], along(-1))
-    pieces, places = [], []
-    for piece, steps, row in ((lead, 0, 0), (after, 1, 0), (before, 3, 0), (far_low, 2, 0), (far_high, 2, 512)):
-        for group, value in (("own", piece), ("pair", pair(piece))):
-            pieces.append(value)
-            places.append([(group, steps, 0, row, value.shape[0])])
+    for other, value in ((False, own), (True, pair)):
+        before, after = move(value, along(1)), move(value, along(-1))
+        far_low, far_high = move(before[:512], along(1)), move(after[512:], along(-1))
+        pieces += [value, after, before, far_low, far_high]
+        places += [(other, 0, 0), (other, 1, 0), (other, 3, 0), (other, 2, 0), (other, 2, 512)]
     return pieces, places
 
 
@@ -304,29 +293,30 @@
     diagonal = ((row_id == 0) & (yh == 0)) | ((row_id == 1) & (yh == 1))
     info = jnp.stack([diagonal.astype(jnp.int32), slice_id.astype(jnp.int32)])
     lead = invert_diagonal(info, local[0])
+    pieces, places = gather_slices(lead, xi)
 
     own_rhs = rhs[0].reshape(64, 2, 4, TILE).transpose(1, 2, 0, 3)
     own_rhs = jnp.where(yh == 0, own_rhs, own_rhs[::-1]).reshape(8, 64, TILE)
     half = lax.all_to_all(own_rhs, ("yl", "z"), 0, 0, tiled=True).reshape(512, TILE)
-    other_half = move(half, lambda a, b, c, d: (0, b, 3 - c, d) if a == 0 and c >= 2 else None)
-    columns = jnp.concatenate([half, other_half], 0)
+    half, pieces[6] = lax.optimization_barrier((half, pieces[6]))
+    low_half = move(half, lambda a, b, c, d: (1, 0, c, d) if (a, b) == (0, 1) and c < 2 else None)
+    high_half = move(half, lambda a, b, c, d: (b, 0, 3 - c, d) if a == 0 and c >= 2 else None)
+    columns = jnp.concatenate([jnp.where(xi == 1, low_half, half), high_half], 0)
 
     place = jnp.stack([yl, z]).astype(jnp.int32)
-    tri_first = pack_slices(place, *gather_first(lead, yl), "pack_first")
-    tri_second = pack_slices(place, *gather_second(lead), "pack_second")
-
-    first = solve(tri_first, columns)
-    sent = move(first, lambda a, b, c, d: (0, 1, c, d) if a == 0 and b == 0 and c < 2 else None)
-    second_rhs = move(
-        residual(tri_second, columns, sent),
-        lambda a, b, c, d: (0, 1, 3 - c, d) if a == 0 and b == 1 and c < 2 else None,
-    )
+    tri, first = pack_and_solve(place, pieces, places, columns)
+    sent = move(first, lambda a, b, c, d: (1, 0, c, d) if a == 0 and b == 0 and c < 2 else None)
+    rest = residual(tri, columns, sent)
+    second_rhs = move(rest, lambda a, b, c, d: (0, 1, 3 - c, d) if (a, b) == (1, 0) and c < 2 else None)
+
     by_rows = local.reshape(4, 16, 64, TILE).transpose(1, 0, 2, 3).reshape(16, 256, TILE)
-    by_rows, second_rhs = lax.optimization_barrier((by_rows, second_rhs))
+    by_rows, rest = lax.optimization_barrier((by_rows, sent))
     left = lax.all_to_all(by_rows, COL, 0, 0, tiled=True)
-    second = solve(tri_second, second_rhs)
     dealt0 = deal(first, core, yh, xi, 0, 0)
+    second_rhs, dealt0 = lax.optimization_barrier((second_rhs, dealt0))
+    second = solve(tri, second_rhs)
     dealt1 = deal(second, core, yh, xi, 1, 1)
+    dealt1, left = lax.optimization_barrier((dealt1, left))
 
     info2 = jnp.stack([row_id, core, 2 * yh + yl, z, col_id]).astype(jnp.int32)
 

time: 185 us -> 188 us (1.016)
  starting transfers between devices: 43.9 us -> 48.4 us
  Pallas kernels: 33.8 us -> 29.5 us
  local copies, waits for them, and re-layouts: 10.9 us -> 13.1 us
    ppermute x40 -> x37, starting transfers between devices: 34.9 us -> 43.8 us  [move(): return lax.ppermute(value, AXES, pairs)]
    all_to_all x1, starting transfers between devices: 9 us -> 4.63 us  [shards(): left = lax.all_to_all(by_rows, COL, 0, 0, tiled=True)]
    pallas_call x2 -> x1, Pallas kernels: 5.36 us -> 2.68 us  [solve(): pl.pallas_call(solve_body, out_shape=jax.ShapeDtypeStruct(rhs.shape, F32)...]
    pallas_call x2 -> x1, Pallas kernels: 5.9 us -> 4.22 us  [pack_and_solve(): pl.pallas_call(body, out_shape=[jax.ShapeDtypeStruct((8, 1024, 256), BF16...]
    unnamed x8 -> x10, local copies, waits for them, and re-layouts: 5.61 us -> 6.02 us
    ppermute x40 -> x37, waiting for transfers between devices: 81.9 us -> 82.1 us  [move(): return lax.ppermute(value, AXES, pairs)]
  transfers between devices with their start and end apart: 41 -> 38, of which waited for: 4 -> 5; matrix products, arithmetic and copies ran while one was open for 3% -> 4% of each run, Pallas kernels for 16% -> 11%
where the time goes in v4:
time: 188 us; the launch traced here: 187 us
  waiting for transfers between devices  82.1 us (44%)
  starting transfers between devices  48.4 us (26%)
  Pallas kernels  29.5 us (16%)
  local copies, waits for them, and re-layouts  13.1 us (7%)
  blocking collectives  11.9 us (6%)
    ppermute x37, waiting for transfers between devices, move(): return lax.ppermute(value, AXES, pairs)  82.1 us
    ppermute x37, starting transfers between devices, move(): return lax.ppermute(value, AXES, pairs)  43.8 us
    pallas_call x4, Pallas kernels, accumulate(): pl.pallas_call(body, out_shape=jax.ShapeDtypeStruct(base.shape, F32), in_...  19.4 us
    all_to_all x1, blocking collectives, shards(): lax.all_to_all(own_rhs, ('yl', 'z'), 0, 0, tiled=True).reshape(512, TILE)  11.9 us
    unnamed x10, local copies, waits for them, and re-layouts  6.02 us
    all_to_all x1, starting transfers between devices, shards(): left = lax.all_to_all(by_rows, COL, 0, 0, tiled=True)  4.63 us
    pallas_call x1, Pallas kernels, pack_and_solve(): pl.pallas_call(body, out_shape=[jax.ShapeDtypeStruct((8, 1024, 256), BF16...  4.22 us
  transfers between devices with their start and end apart: 38, of which 5 were waited for; matrix products, arithmetic and copies ran while one was open for 4% of the time, Pallas kernels for 11%

profile of v4, /device:TPU:5, one launch (start us, length us, event | category | flops | bytes accessed | tf_op | source)
XLA Modules:
  0.0 187.2 jit_solution(15873879152763387585)
XLA Ops:
  6.4 11.9 %all_to_all.10 = f32[8,64,128]{2,1,0:T(8,128)S(1)} all-to-all(f32[8,64,128]{2,1,0:T(8,128)S(1)} %bitcast.35), channel_id=1, replica_groups=mesh['x'=4,'core'=2,'yh'=2,'yl'=2,'z'=4] {'yl','z'}, dimensions={0} | all-to-all | bytes 524288 | tf_op jit(solution)/shard_map/all_to_all | solution.py:300
  22.8 4.2 %pack_and_solve.1 = (bf16[8,1024,256]{2,1,0:T(8,128)(2,1)S(1)}, f32[1024,128]{1,0:T(8,128)S(1)}) custom-call(s32[2]{0:T(128)S(1)} %pad_add_fusion.info, f32[1024,128]{1,0:T(8,128)S(1)} %broadcast_select_fusion.refs_0_, f32[1024,128]{1,0:T(8,128)S(1)} %collective-permute-done.1.refs_1_, f32[1024,128]{1,0:T(8,128)S(1)} %collective-permute-done.2.refs_2_, ...), custom_call_target="tpu_custom_call" | custom-call | tf_op jit(solution)/shard_map/pack_and_solve/pallas_call | solution.py:85
  27.0 2.0 %copy-done = bf16[8,1024,256]{2,1,0:T(8,128)(2,1)} copy-done((bf16[8,1024,256]{2,1,0:T(8,128)(2,1)}, bf16[8,1024,256]{2,1,0:T(8,128)(2,1)S(1)}, u32[]{:S(2)}) %copy-start) | copy-done | bytes 4194328
  30.4 1.3 collective-permute-start.15
  31.8 3.4 %copy.8 = f32[4,16,64,128]{3,2,0,1:T(8,128)} copy(f32[4,16,64,128]{3,2,1,0:T(8,128)} %bitcast.33) | data formatting | bytes 4194304 | tf_op jit(solution)/shard_map/reshape;squeeze | solution.py:312
  37.1 4.6 %all-to-all-start.1 = ((f32[16,256,128]{2,1,0:T(8,128)}), f32[16,256,128]{2,1,0:T(8,128)S(1)}, u32[]{:S(2)}, u32[]{:S(2)}) async-start(f32[16,256,128]{2,1,0:T(8,128)} %bitcast.32), calls=%async_computation.1 | async-start | bytes 4194304 | tf_op jit(solution)/shard_map/all_to_all | solution.py:314
  45.1 53.7 %collective-permute-done.18 = f32[256,128]{1,0:T(8,128)} collective-permute-done((f32[256,128]{1,0:T(8,128)S(1)}, f32[256,128]{1,0:T(8,128)}, u32[]{:S(2)}, u32[]{:S(2)}) %collective-permute-start.18) | collective-permute-done | bytes 131104 | tf_op jit(solution)/shard_map/ppermute | solution.py:225
  99.8 2.2 %copy-done.2 = bf16[8,1024,256]{2,1,0:T(8,128)(2,1)S(1)} copy-done((bf16[8,1024,256]{2,1,0:T(8,128)(2,1)S(1)}, bf16[8,1024,256]{2,1,0:T(8,128)(2,1)}, u32[]{:S(2)}) %copy-start.2) | copy-done | bytes 4194328
  102.0 2.7 %block_solve.1 = f32[1024,128]{1,0:T(8,128)S(1)} custom-call(bf16[8,1024,256]{2,1,0:T(8,128)(2,1)S(1)} %copy-done.2, f32[1024,128]{1,0:T(8,128)S(1)} %collective-permute-done.13.rhs_ref), custom_call_target="tpu_custom_call" | custom-call | tf_op jit(solution)/shard_map/block_solve/pallas_call | solution.py:109
  107.5 1.3 collective-permute-start.23
  108.8 20.0 %collective-permute-done.23 = f32[256,128]{1,0:T(8,128)S(1)} collective-permute-done((f32[256,128]{1,0:T(8,128)S(1)}, f32[256,128]{1,0:T(8,128)S(1)}, u32[]{:S(2)}, u32[]{:S(2)}) %collective-permute-start.23) | collective-permute-done | bytes 131104 | tf_op jit(solution)/shard_map/ppermute | solution.py:225
  129.0 1.5 collective-permute-start.25
  130.5 3.8 %collective-permute-done.24 = f32[2,256,128]{2,1,0:T(8,128)S(1)} collective-permute-done((f32[2,256,128]{2,1,0:T(8,128)S(1)}, f32[2,256,128]{2,1,0:T(8,128)S(1)}, u32[]{:S(2)}, u32[]{:S(2)}) %collective-permute-start.24) | collective-permute-done | bytes 262176 | tf_op jit(solution)/shard_map/ppermute | solution.py:225
  136.1 2.4 %collective-permute-done.27 = f32[1,256,128]{2,1,0:T(8,128)S(1)} collective-permute-done((f32[1,256,128]{2,1,0:T(8,128)S(1)}, f32[1,256,128]{2,1,0:T(8,128)S(1)}, u32[]{:S(2)}, u32[]{:S(2)}) %collective-permute-start.27) | collective-permute-done | bytes 131104 | tf_op jit(solution)/shard_map/ppermute | solution.py:225
  138.4 2.2 %collective-permute-done.26 = f32[1,256,128]{2,1,0:T(8,128)S(1)} collective-permute-done((f32[1,256,128]{2,1,0:T(8,128)S(1)}, f32[1,256,128]{2,1,0:T(8,128)S(1)}, u32[]{:S(2)}, u32[]{:S(2)}) %collective-permute-start.26) | collective-permute-done | bytes 131104 | tf_op jit(solution)/shard_map/ppermute | solution.py:225
  140.7 1.5 collective-permute-start.28
  143.5 8.5 %collective-permute-start.32 = (f32[4,2,256,128]{3,2,1,0:T(8,128)S(1)}, f32[4,2,256,128]{3,2,1,0:T(8,128)}, u32[]{:S(2)}, u32[]{:S(2)}) collective-permute-start(f32[4,2,256,128]{3,2,1,0:T(8,128)S(1)} %pad_maximum_fusion.refs_0_), channel_id=1, source_target_pairs={{0,16},{1,17},{2,18},{3,19},{4,20},{5,21},{6,22},{7,23},{8,24},{9,... | collective-permute-start | bytes 3145736 | tf_op jit(solution)/shard_map/ppermute | solution.py:225
  153.3 1.4 prepare_update.1
  154.6 3.4 %update_near.1.base_ref = f32[256,1024]{1,0:T(8,128)} custom-call(s32[5]{0:T(128)S(1)} %stack.66.info, f32[256,1024]{1,0:T(8,128)} %get-tuple-element.32.base_ref, bf16[8,256,256]{2,1,0:T(8,128)(2,1)S(1)} %get-tuple-element.33.high_ref, bf16[8,256,256]{2,1,0:T(8,128)(2,1)S(1)} %get-tuple-element.34.low_ref, ...), custom_call_target="tpu_custom_call", output_to_operand_aliasing={{}: (1, {})} | custom-call | tf_op jit(solution)/shard_map/update_near/pallas_call | solution.py:201
  160.3 2.7 %collective-permute-start.31 = (f32[2,2,256,128]{3,2,1,0:T(8,128)S(1)}, f32[2,2,256,128]{3,2,1,0:T(8,128)S(1)}, u32[]{:S(2)}, u32[]{:S(2)}) collective-permute-start(f32[2,2,256,128]{3,2,1,0:T(8,128)S(1)} %slice.73), channel_id=1, source_target_pairs={{0,12},{1,13},{2,14},{3,15},{4,0},{5,1},{6,2},{7,3},{8,4},{9,5},{1... | collective-permute-start | bytes 1572872 | tf_op jit(solution)/shard_map/ppermute | solution.py:225
  163.0 7.5 %collective-permute-start.33 = (f32[4,2,256,128]{3,2,1,0:T(8,128)}, f32[4,2,256,128]{3,2,1,0:T(8,128)S(1)}, u32[]{:S(2)}, u32[]{:S(2)}) collective-permute-start(f32[4,2,256,128]{3,2,1,0:T(8,128)} %collective-permute-done.29.refs_1_), channel_id=1, source_target_pairs={{0,16},{1,17},{2,18},{3,19},{4,20},{5,21},{6,22},{7,23},{8,24},{9,... | collective-permute-start | bytes 3145736 | tf_op jit(solution)/shard_map/ppermute | solution.py:225
  170.5 6.7 %update_next.1.base_ref = f32[256,1024]{1,0:T(8,128)} custom-call(s32[5]{0:T(128)S(1)} %stack.66.info, f32[256,1024]{1,0:T(8,128)} %update_near.1.base_ref, bf16[8,256,256]{2,1,0:T(8,128)(2,1)S(1)} %get-tuple-element.33.high_ref, bf16[8,256,256]{2,1,0:T(8,128)(2,1)S(1)} %get-tuple-element.34.low_ref, ...), custom_call_target="tpu_custom_call", output_to_operand_aliasing={{}: (1, {})} | custom-call | tf_op jit(solution)/shard_map/update_next/pallas_call | solution.py:201
  178.0 5.8 %update_far.1.base_ref = f32[256,1024]{1,0:T(8,128)} custom-call(s32[5]{0:T(128)S(1)} %stack.66.info, f32[256,1024]{1,0:T(8,128)} %update_next.1.base_ref, bf16[8,256,256]{2,1,0:T(8,128)(2,1)S(1)} %get-tuple-element.33.high_ref, bf16[8,256,256]{2,1,0:T(8,128)(2,1)S(1)} %get-tuple-element.34.low_ref, ...), custom_call_target="tpu_custom_call", output_to_operand_aliasing={{}: (1, {})} | custom-call | tf_op jit(solution)/shard_map/update_far/pallas_call | solution.py:201
  183.8 3.4 %update_last.1 = f32[256,1024]{1,0:T(8,128)} custom-call(s32[5]{0:T(128)S(1)} %stack.66.info, f32[256,1024]{1,0:T(8,128)} %update_far.1.base_ref, bf16[8,256,256]{2,1,0:T(8,128)(2,1)S(1)} %get-tuple-element.33.high_ref, bf16[8,256,256]{2,1,0:T(8,128)(2,1)S(1)} %get-tuple-element.34.low_ref, ...), custom_call_target="tpu_custom_call", output_to_operand_aliasing={{}: (1, {})} | custom-call | tf_op jit(solution)/shard_map/update_last/pallas_call | solution.py:201
  (106 shorter events, 28.6 us)
Async XLA Ops:
  3.4 15.0 %collective-permute-start.6 = (f32[1024,128]{1,0:T(8,128)S(1)}, f32[1024,128]{1,0:T(8,128)S(1)}, u32[]{:S(2)}, u32[]{:S(2)}) collective-permute-start(f32[1024,128]{1,0:T(8,128)S(1)} %collective-permute-done.5.refs_5_), channel_id=1, source_target_pairs={{0,3},{1,0},{2,1},{3,2},{4,7},{5,4},{6,5},{7,6},{24,27},{25,24},{2... | collective-permute-start | bytes 1572872 | tf_op jit(solution)/shard_map/ppermute | solution.py:225
  4.1 16.3 %collective-permute-start.1 = (f32[1024,128]{1,0:T(8,128)S(1)}, f32[1024,128]{1,0:T(8,128)S(1)}, u32[]{:S(2)}, u32[]{:S(2)}) collective-permute-start(f32[1024,128]{1,0:T(8,128)S(1)} %broadcast_select_fusion.refs_0_), channel_id=1, source_target_pairs={{0,3},{1,0},{2,1},{3,2},{4,7},{5,4},{6,5},{7,6},{24,27},{25,24},{2... | collective-permute-start | bytes 1572872 | tf_op jit(solution)/shard_map/ppermute | solution.py:225
  4.8 14.9 %collective-permute-start.2 = (f32[1024,128]{1,0:T(8,128)S(1)}, f32[1024,128]{1,0:T(8,128)S(1)}, u32[]{:S(2)}, u32[]{:S(2)}) collective-permute-start(f32[1024,128]{1,0:T(8,128)S(1)} %broadcast_select_fusion.refs_0_), channel_id=1, source_target_pairs={{0,1},{1,2},{2,3},{3,0},{4,5},{5,6},{6,7},{7,4},{24,25},{25,26},{2... | collective-permute-start | bytes 1572872 | tf_op jit(solution)/shard_map/ppermute | solution.py:225
  5.5 15.6 %collective-permute-start.7 = (f32[1024,128]{1,0:T(8,128)S(1)}, f32[1024,128]{1,0:T(8,128)S(1)}, u32[]{:S(2)}, u32[]{:S(2)}) collective-permute-start(f32[1024,128]{1,0:T(8,128)S(1)} %collective-permute-done.5.refs_5_), channel_id=1, source_target_pairs={{0,1},{1,2},{2,3},{3,0},{4,5},{5,6},{6,7},{7,4},{24,25},{25,26},{2... | collective-permute-start | bytes 1572872 | tf_op jit(solution)/shard_map/ppermute | solution.py:225
  19.0 3.7 %collective-permute-start.11 = (f32[512,128]{1,0:T(8,128)S(1)}, f32[512,128]{1,0:T(8,128)S(1)}, u32[]{:S(2)}, u32[]{:S(2)}) collective-permute-start(f32[512,128]{1,0:T(8,128)S(1)} %bitcast.37), channel_id=1, source_target_pairs={{8,4},{9,5},{10,6},{11,7},{12,0},{13,1},{14,2},{15,3},{24,36},{25,... | collective-permute-start | bytes 786440 | tf_op jit(solution)/shard_map/ppermute | solution.py:225
  29.7 5.5 %collective-permute-start.12 = (f32[1024,128]{1,0:T(8,128)S(1)}, f32[1024,128]{1,0:T(8,128)S(1)}, u32[]{:S(2)}, u32[]{:S(2)}) collective-permute-start(f32[1024,128]{1,0:T(8,128)S(1)} %get-tuple-element.26), channel_id=1, source_target_pairs={{0,32},{1,33},{2,34},{3,35},{4,36},{5,37},{6,38},{7,39}} | collective-permute-start | bytes 1572872 | tf_op jit(solution)/shard_map/ppermute | solution.py:225
  30.4 11.3 %collective-permute-start.15 = (f32[256,128]{1,0:T(8,128)S(1)}, f32[256,128]{1,0:T(8,128)}, u32[]{:S(2)}, u32[]{:S(2)}) collective-permute-start(f32[256,128]{1,0:T(8,128)S(1)} %slice.79), channel_id=1, source_target_pairs={{0,12},{1,13},{2,14},{3,15},{4,8},{5,9},{6,10},{7,11},{16,28},{17,... | collective-permute-start | bytes 393224 | tf_op jit(solution)/shard_map/ppermute | solution.py:225
  36.4 63.4 %collective-permute-start.13 = (f32[1024,128]{1,0:T(8,128)S(1)}, f32[1024,128]{1,0:T(8,128)S(1)}, u32[]{:S(2)}, u32[]{:S(2)}) collective-permute-start(f32[1024,128]{1,0:T(8,128)S(1)} %block_residual.1), channel_id=1, source_target_pairs={{32,28},{33,29},{34,30},{35,31},{36,24},{37,25},{38,26},{39,27}} | collective-permute-start | bytes 1572872 | tf_op jit(solution)/shard_map/ppermute | solution.py:225
  37.1 91.8 %all-to-all-start.1 = ((f32[16,256,128]{2,1,0:T(8,128)}), f32[16,256,128]{2,1,0:T(8,128)S(1)}, u32[]{:S(2)}, u32[]{:S(2)}) async-start(f32[16,256,128]{2,1,0:T(8,128)} %bitcast.32), calls=%async_computation.1 | async-start | bytes 4194304 | tf_op jit(solution)/shard_map/all_to_all | solution.py:314
  43.2 55.6 %collective-permute-start.18 = (f32[256,128]{1,0:T(8,128)S(1)}, f32[256,128]{1,0:T(8,128)}, u32[]{:S(2)}, u32[]{:S(2)}) collective-permute-start(f32[256,128]{1,0:T(8,128)S(1)} %collective-permute-done.16), channel_id=1, source_target_pairs={{32,64},{33,65},{34,66},{35,67},{36,68},{37,69},{38,70},{39,71},{4... | collective-permute-start | bytes 393224 | tf_op jit(solution)/shard_map/ppermute | solution.py:225
  107.5 21.3 %collective-permute-start.23 = (f32[256,128]{1,0:T(8,128)S(1)}, f32[256,128]{1,0:T(8,128)S(1)}, u32[]{:S(2)}, u32[]{:S(2)}) collective-permute-start(f32[256,128]{1,0:T(8,128)S(1)} %collective-permute-done.21), channel_id=1, source_target_pairs={{32,64},{33,65},{34,66},{35,67},{36,68},{37,69},{38,70},{39,71},{4... | collective-permute-start | bytes 393224 | tf_op jit(solution)/shard_map/ppermute | solution.py:225
  128.9 5.3 %collective-permute-start.24 = (f32[2,256,128]{2,1,0:T(8,128)S(1)}, f32[2,256,128]{2,1,0:T(8,128)S(1)}, u32[]{:S(2)}, u32[]{:S(2)}) collective-permute-start(f32[2,256,128]{2,1,0:T(8,128)S(1)} %get-tuple-element.42), channel_id=1, source_target_pairs={{0,3},{1,0},{2,1},{3,2},{4,7},{5,4},{6,5},{7,6},{8,11},{9,8},{10,9... | collective-permute-start | bytes 786440 | tf_op jit(solution)/shard_map/ppermute | solution.py:225
  129.0 6.5 %collective-permute-start.25 = (f32[2,256,128]{2,1,0:T(8,128)S(1)}, f32[2,256,128]{2,1,0:T(8,128)S(1)}, u32[]{:S(2)}, u32[]{:S(2)}) collective-permute-start(f32[2,256,128]{2,1,0:T(8,128)S(1)} %get-tuple-element.42), channel_id=1, source_target_pairs={{0,1},{1,2},{2,3},{3,0},{4,5},{5,6},{6,7},{7,4},{8,9},{9,10},{10,1... | collective-permute-start | bytes 786440 | tf_op jit(solution)/shard_map/ppermute | solution.py:225
  134.2 4.2 %collective-permute-start.27 = (f32[1,256,128]{2,1,0:T(8,128)S(1)}, f32[1,256,128]{2,1,0:T(8,128)S(1)}, u32[]{:S(2)}, u32[]{:S(2)}) collective-permute-start(f32[1,256,128]{2,1,0:T(8,128)S(1)} %slice.85), channel_id=1, source_target_pairs={{0,3},{1,0},{2,1},{3,2},{4,7},{5,4},{6,5},{7,6},{8,11},{9,8},{10,9... | collective-permute-start | bytes 393224 | tf_op jit(solution)/shard_map/ppermute | solution.py:225
  135.5 5.1 %collective-permute-start.26 = (f32[1,256,128]{2,1,0:T(8,128)S(1)}, f32[1,256,128]{2,1,0:T(8,128)S(1)}, u32[]{:S(2)}, u32[]{:S(2)}) collective-permute-start(f32[1,256,128]{2,1,0:T(8,128)S(1)} %slice.84), channel_id=1, source_target_pairs={{0,1},{1,2},{2,3},{3,0},{4,5},{5,6},{6,7},{7,4},{8,9},{9,10},{10,1... | collective-permute-start | bytes 393224 | tf_op jit(solution)/shard_map/ppermute | solution.py:225
  140.7 17.3 %collective-permute-start.28 = (f32[4,2,256,128]{3,2,1,0:T(8,128)S(1)}, f32[4,2,256,128]{3,2,1,0:T(8,128)}, u32[]{:S(2)}, u32[]{:S(2)}) collective-permute-start(f32[4,2,256,128]{3,2,1,0:T(8,128)S(1)} %pad_maximum_fusion.refs_0_), channel_id=1, source_target_pairs={{0,4},{1,5},{2,6},{3,7},{4,8},{5,9},{6,10},{7,11},{8,12},{9,13},{1... | collective-permute-start | bytes 3145736 | tf_op jit(solution)/shard_map/ppermute | solution.py:225
  142.3 15.8 %collective-permute-start.29 = (f32[4,2,256,128]{3,2,1,0:T(8,128)S(1)}, f32[4,2,256,128]{3,2,1,0:T(8,128)}, u32[]{:S(2)}, u32[]{:S(2)}) collective-permute-start(f32[4,2,256,128]{3,2,1,0:T(8,128)S(1)} %pad_maximum_fusion.refs_0_), channel_id=1, source_target_pairs={{0,12},{1,13},{2,14},{3,15},{4,0},{5,1},{6,2},{7,3},{8,4},{9,5},{1... | collective-permute-start | bytes 3145736 | tf_op jit(solution)/shard_map/ppermute | solution.py:225
  143.5 27.1 %collective-permute-start.32 = (f32[4,2,256,128]{3,2,1,0:T(8,128)S(1)}, f32[4,2,256,128]{3,2,1,0:T(8,128)}, u32[]{:S(2)}, u32[]{:S(2)}) collective-permute-start(f32[4,2,256,128]{3,2,1,0:T(8,128)S(1)} %pad_maximum_fusion.refs_0_), channel_id=1, source_target_pairs={{0,16},{1,17},{2,18},{3,19},{4,20},{5,21},{6,22},{7,23},{8,24},{9,... | collective-permute-start | bytes 3145736 | tf_op jit(solution)/shard_map/ppermute | solution.py:225
  159.1 18.1 %collective-permute-start.30 = (f32[2,2,256,128]{3,2,1,0:T(8,128)S(1)}, f32[2,2,256,128]{3,2,1,0:T(8,128)S(1)}, u32[]{:S(2)}, u32[]{:S(2)}) collective-permute-start(f32[2,2,256,128]{3,2,1,0:T(8,128)S(1)} %slice.72), channel_id=1, source_target_pairs={{0,4},{1,5},{2,6},{3,7},{4,8},{5,9},{6,10},{7,11},{8,12},{9,13},{1... | collective-permute-start | bytes 1572872 | tf_op jit(solution)/shard_map/ppermute | solution.py:225
  160.3 17.0 %collective-permute-start.31 = (f32[2,2,256,128]{3,2,1,0:T(8,128)S(1)}, f32[2,2,256,128]{3,2,1,0:T(8,128)S(1)}, u32[]{:S(2)}, u32[]{:S(2)}) collective-permute-start(f32[2,2,256,128]{3,2,1,0:T(8,128)S(1)} %slice.73), channel_id=1, source_target_pairs={{0,12},{1,13},{2,14},{3,15},{4,0},{5,1},{6,2},{7,3},{8,4},{9,5},{1... | collective-permute-start | bytes 1572872 | tf_op jit(solution)/shard_map/ppermute | solution.py:225
  163.0 14.9 %collective-permute-start.33 = (f32[4,2,256,128]{3,2,1,0:T(8,128)}, f32[4,2,256,128]{3,2,1,0:T(8,128)S(1)}, u32[]{:S(2)}, u32[]{:S(2)}) collective-permute-start(f32[4,2,256,128]{3,2,1,0:T(8,128)} %collective-permute-done.29.refs_1_), channel_id=1, source_target_pairs={{0,16},{1,17},{2,18},{3,19},{4,20},{5,21},{6,22},{7,23},{8,24},{9,... | collective-permute-start | bytes 3145736 | tf_op jit(solution)/shard_map/ppermute | solution.py:225
  170.5 7.4 %collective-permute-start.34 = (f32[4,2,256,128]{3,2,1,0:T(8,128)}, f32[4,2,256,128]{3,2,1,0:T(8,128)S(1)}, u32[]{:S(2)}, u32[]{:S(2)}) collective-permute-start(f32[4,2,256,128]{3,2,1,0:T(8,128)} %collective-permute-done.28.refs_2_), channel_id=1, source_target_pairs={{0,16},{1,17},{2,18},{3,19},{4,20},{5,21},{6,22},{7,23},{8,24},{9,... | collective-permute-start | bytes 3145736 | tf_op jit(solution)/shard_map/ppermute | solution.py:225
  177.3 6.5 %collective-permute-start.35 = (f32[2,2,256,128]{3,2,1,0:T(8,128)S(1)}, f32[2,2,256,128]{3,2,1,0:T(8,128)S(1)}, u32[]{:S(2)}, u32[]{:S(2)}) collective-permute-start(f32[2,2,256,128]{3,2,1,0:T(8,128)S(1)} %collective-permute-done.30.refs_2_), channel_id=1, source_target_pairs={{0,16},{1,17},{2,18},{3,19},{4,20},{5,21},{6,22},{7,23},{8,24},{9,... | collective-permute-start | bytes 1572872 | tf_op jit(solution)/shard_map/ppermute | solution.py:225
  177.9 5.9 %collective-permute-start.36 = (f32[2,2,256,128]{3,2,1,0:T(8,128)S(1)}, f32[2,2,256,128]{3,2,1,0:T(8,128)S(1)}, u32[]{:S(2)}, u32[]{:S(2)}) collective-permute-start(f32[2,2,256,128]{3,2,1,0:T(8,128)S(1)} %collective-permute-done.31.refs_3_), channel_id=1, source_target_pairs={{0,16},{1,17},{2,18},{3,19},{4,20},{5,21},{6,22},{7,23},{8,24},{9,... | collective-permute-start | bytes 1572872 | tf_op jit(solution)/shard_map/ppermute | solution.py:225
  (20 other events, 36.3 us)

commit v5 on v4

--- a/solution.py
+++ b/solution.py
@@ -137,76 +137,77 @@
     )(tri, rhs, x)
 
 
-def prepare_body(info, left_ref, base_ref, high_ref, low_ref, out_ref):
-    for h in range(2):
-        for q in range(4):
-            c = 8 * h + 2 * q
-            high, low = split(jnp.concatenate([left_ref[c], left_ref[c + 1]], 1))
-            high_ref[4 * h + q] = high
-            low_ref[4 * h + q] = low
-    out_ref[...] = base_ref[...]
-
-    @pl.when(info[0] < 2)
+def prepare_body(info, mine_ref, other_ref, high_ref, low_ref):
+    for side, ref in enumerate((mine_ref, other_ref)):
+        rows = pl.ds(256 * side, 256)
+        for n in range(4):
+            high, low = split(jnp.concatenate([ref[2 * n], ref[2 * n + 1]], 1))
+            high_ref[n, rows, :] = high
+            low_ref[n, rows, :] = low
+
+    @pl.when(info[0] == 0)
     def _():
-        for n in range(8):
-            high_ref[n, pl.ds(0, 64), :] = jnp.zeros((64, 256), BF16)
-            low_ref[n, pl.ds(0, 64), :] = jnp.zeros((64, 256), BF16)
-        out_ref[pl.ds(0, 64), :] = jnp.zeros((64, 1024), F32)
-
-
-def prepare(info, left, base):
+        for n in range(4):
+            for side in range(2):
+                high_ref[n, pl.ds(256 * side, 64), :] = jnp.zeros((64, 256), BF16)
+                low_ref[n, pl.ds(256 * side, 64), :] = jnp.zeros((64, 256), BF16)
+
+
+def prepare(info, mine, other):
     return pl.pallas_call(
         prepare_body,
-        out_shape=[
-            jax.ShapeDtypeStruct((8, 256, 256), BF16),
-            jax.ShapeDtypeStruct((8, 256, 256), BF16),
-            jax.ShapeDtypeStruct(base.shape, F32),
-        ],
+        out_shape=[jax.ShapeDtypeStruct((4, 512, 256), BF16)] * 2,
         in_specs=[SM, VM, VM],
-        out_specs=[VM, VM, VM],
+        out_specs=[VM, VM],
         compiler_params=PARAMS,
         name="prepare_update",
-    )(info, left, base)
-
-
-def accumulate(info, base, high, low, pieces, places, name):
-    def body(info, base_ref, high_ref, low_ref, *refs):
+    )(info, mine, other)
+
+
+def accumulate(info, sums, high, low, pieces, places, name):
+    first = sums is None
+
+    def body(info, high_ref, low_ref, *refs):
         out_ref = refs[-1]
-        row, core, y, z, col = (info[k] for k in range(5))
-        out_ref[...] = base_ref[...]
-        for ref, (side, far, slot) in zip(refs, places):
-            holder = core if side == 0 else 1 - core
+        x, core, y, z, col = (info[k] for k in range(5))
+        if first:
+            out_ref[...] = jnp.zeros(out_ref.shape, F32)
+        else:
+            out_ref[...] = refs[0][...]
+        for ref, (far, slot) in zip(refs[0 if first else 1 :], places):
             for n in range(ref.shape[0]):
                 near = slot + n
-                py = lax.rem(y + jnp.where(holder == 0, far, near), 4)
-                pz = lax.rem(z + jnp.where(holder == 0, near, far), 4)
+                py = lax.rem(y + jnp.where(core == 0, far, near), 4)
+                pz = lax.rem(z + jnp.where(core == 0, near, far), 4)
                 upper = py // 2
                 bit = jnp.where(upper == 0, py, 3 - py)
                 cols = pl.ds(pl.multiple_of((4 * bit + pz) * TILE, TILE), TILE)
-                q = 2 * holder + upper
                 total = None
                 for h in range(2):
                     x_high, x_low = split(ref[n, h])
-                    left_high = high_ref[4 * h + q]
-                    wide = mm(left_high, jnp.concatenate([x_high, x_low], 1))
-                    term = wide[:, :TILE] + (wide[:, TILE:] + mm(low_ref[4 * h + q], x_high))
+                    wide = mm(high_ref[2 * h + upper], jnp.concatenate([x_high, x_low], 1))
+                    term = wide[:, :TILE] + (wide[:, TILE:] + mm(low_ref[2 * h + upper], x_high))
                     total = term if total is None else total + term
-                out_ref[:, cols] = out_ref[:, cols] - total
-
-                @pl.when((row < 2) & (col // 4 == q))
+                out_ref[:, cols] = out_ref[:, cols] + total
+
+                @pl.when((x == 0) & (col // 4 == 2 * core + upper))
                 def _():
                     there = pl.ds(pl.multiple_of(lax.rem(col, 4) * 64, 64), 64)
-                    out_ref[pl.ds(0, 64), cols] = out_ref[pl.ds(0, 64), cols] + ref[n, row, there, :]
-
+                    for side in range(2):
+                        here = pl.ds(256 * side, 64)
+                        block = core if side == 0 else 1 - core
+                        out_ref[here, cols] = out_ref[here, cols] - ref[n, block, there, :]
+
+    start = [] if first else [sums]
     return pl.pallas_call(
         body,
-        out_shape=jax.ShapeDtypeStruct(base.shape, F32),
-        in_specs=[SM] + [VM] * (3 + len(pieces)),
+        out_shape=jax.ShapeDtypeStruct((512, 1024), F32),
+        in_specs=[SM] + [VM] * (2 + len(start) + len(pieces)),
         out_specs=VM,
-        input_output_aliases={1: 0},
+        input_output_aliases={} if first else {3: 0},
         compiler_params=PARAMS,
         name=name,
-    )(info, base, high, low, *pieces)
+    )(info, high, low, *start, *pieces)
 
 
 AXES = ROW + COL
@@ -295,22 +296,19 @@
     lead = invert_diagonal(info, local[0])
     pieces, places = gather_slices(lead, xi)
 
-    own_rhs = rhs[0].reshape(64, 2, 4, TILE).transpose(1, 2, 0, 3)
-    own_rhs = jnp.where(yh == 0, own_rhs, own_rhs[::-1]).reshape(8, 64, TILE)
-    half = lax.all_to_all(own_rhs, ("yl", "z"), 0, 0, tiled=True).reshape(512, TILE)
-    half, pieces[6] = lax.optimization_barrier((half, pieces[6]))
-    low_half = move(half, lambda a, b, c, d: (1, 0, c, d) if (a, b) == (0, 1) and c < 2 else None)
-    high_half = move(half, lambda a, b, c, d: (b, 0, 3 - c, d) if a == 0 and c >= 2 else None)
-    columns = jnp.concatenate([jnp.where(xi == 1, low_half, half), high_half], 0)
+    own_rhs = rhs[0].reshape(64, 8, TILE).transpose(1, 0, 2)
+    columns = lax.all_to_all(jnp.concatenate([own_rhs, own_rhs], 0), COL, 0, 0, tiled=True).reshape(1024, TILE)
 
     place = jnp.stack([yl, z]).astype(jnp.int32)
     tri, first = pack_and_solve(place, pieces, places, columns)
+    columns, first = lax.optimization_barrier((columns, first))
     sent = move(first, lambda a, b, c, d: (1, 0, c, d) if a == 0 and b == 0 and c < 2 else None)
+    columns = move(columns, lambda a, b, c, d: (1, 0, c, d) if (a, b) == (0, 1) and c < 2 else None)
     rest = residual(tri, columns, sent)
     second_rhs = move(rest, lambda a, b, c, d: (0, 1, 3 - c, d) if (a, b) == (1, 0) and c < 2 else None)
 
     by_rows = local.reshape(4, 16, 64, TILE).transpose(1, 0, 2, 3).reshape(16, 256, TILE)
-    by_rows, rest = lax.optimization_barrier((by_rows, sent))
+    by_rows, sent = lax.optimization_barrier((by_rows, sent))
     left = lax.all_to_all(by_rows, COL, 0, 0, tiled=True)
     dealt0 = deal(first, core, yh, xi, 0, 0)
     second_rhs, dealt0 = lax.optimization_barrier((second_rhs, dealt0))
@@ -318,13 +316,13 @@
     dealt1 = deal(second, core, yh, xi, 1, 1)
     dealt1, left = lax.optimization_barrier((dealt1, left))
 
-    info2 = jnp.stack([row_id, core, 2 * yh + yl, z, col_id]).astype(jnp.int32)
-
     def swap(value):
         return move(value, lambda a, b, c, d: (a, 1 - b, c, d))
 
-    def add(out, pieces, places, name):
-        return accumulate(info2, out, high, low, pieces, places, name)
+    left = left.reshape(2, 2, 4, 256, TILE)
+    kept = jnp.where(core == 0, left[:, 0], left[:, 1]).reshape(8, 256, TILE)
+    given = jnp.where(core == 0, left[:, 1], left[:, 0]).reshape(8, 256, TILE)
+    info2 = jnp.stack([xi, core, 2 * yh + yl, z, col_id]).astype(jnp.int32)
 
     mine = jnp.stack([dealt0, dealt1])
     after, far_low, far_high, before = ring(mine, True)
@@ -333,20 +331,18 @@
     def along(step):
         return lambda a, b, c, d: (a, b, c + step, d) if b == 0 else (a, b, c, d + step)
 
-    before, after, near_other = move(near, along(1)), move(near, along(-1)), swap(near)
-    high, low, out = prepare(info2[:1], left, rhs.reshape(256, 1024))
-    out = add(out, [near], [(0, 0, 0)], "update_near")
-    before, after, out = lax.optimization_barrier((before, after, out))
+    before, after = move(near, along(1)), move(near, along(-1))
+    high, low = prepare(info2[:1], kept, swap(given))
+    sums = accumulate(info2, None, high, low, [near], [(0, 0)], "update_near")
+    before, after, sums = lax.optimization_barrier((before, after, sums))
     far_low, far_high = move(before[:2], along(1)), move(after[2:], along(-1))
-    before_other, after_other = swap(before), swap(after)
-    out = add(out, [near_other, after, before], [(1, 0, 0), (0, 1, 0), (0, 3, 0)], "update_next")
-    far_low, far_high, out = lax.optimization_barrier((far_low, far_high, out))
-    far_low_other, far_high_other = swap(far_low), swap(far_high)
-    out = add(
-        out, [after_other, before_other, far_low, far_high],
-        [(1, 1, 0), (1, 3, 0), (0, 2, 0), (0, 2, 2)], "update_far",
-    )
-    out = add(out, [far_low_other, far_high_other], [(1, 2, 0), (1, 2, 2)], "update_last")
+    sums = accumulate(info2, sums, high, low, [after, before], [(1, 0), (3, 0)], "update_next")
+    far_low, far_high, sums = lax.optimization_barrier((far_low, far_high, sums))
+    sums = accumulate(info2, sums, high, low, [far_low, far_high], [(2, 0), (2, 2)], "update_far")
+
+    replaced = (xi == 0) & (lax.broadcasted_iota(jnp.int32, (256, 1024), 0) < 64)
+    base = jnp.where(replaced, 0.0, rhs.reshape(256, 1024))
+    out = base - (sums[:256] + swap(sums[256:]))
     return out.reshape(4, 1, 64, 1024)
 
 

time: 188 us -> 189 us (level)
  blocking collectives: 11.9 us -> 0 us
  Pallas kernels: 29.5 us -> 22 us
  starting transfers between devices: 48.4 us -> 55.4 us
  waiting for transfers between devices: 82.1 us -> 88.9 us
  other arithmetic: 1.59 us -> 5.63 us
    all_to_all x1 -> x0, blocking collectives: 11.9 us -> none  [shards(): lax.all_to_all(own_rhs, ('yl', 'z'), 0, 0, tiled=True).reshape(512, TILE)]
    pallas_call x5 -> x4, Pallas kernels: 20.7 us -> 11.7 us  [the longest x3 10.2 us: accumulate(): pl.pallas_call(body, out_shape=jax.ShapeDtypeStruct((512, 1024), F32), in...]
    all_to_all x0 -> x1, starting transfers between devices: none -> 7.77 us  [shards(): lax.all_to_all(jnp.concatenate([own_rhs, own_rhs], 0), COL, 0, 0, tiled=T...]
    ppermute x37 -> x33, waiting for transfers between devices: 82.1 us -> 86.4 us  [move(): return lax.ppermute(value, AXES, pairs)]
    another operation x3 -> x2, local copies, waits for them, and re-layouts: 3.56 us -> 0.14 us  [the longest x1 0.08 us: shards(): info2 = jnp.stack([xi, core, 2 * yh + yl, z, col_id]).astype(jnp.int32)]
    transpose x0 -> x1, local copies, waits for them, and re-layouts: none -> 3.37 us  [shards(): local.reshape(4, 16, 64, TILE).transpose(1, 0, 2, 3).reshape(16, 256, TILE)]
    all_to_all x0 -> x1, waiting for transfers between devices: none -> 2.51 us  [shards(): lax.all_to_all(jnp.concatenate([own_rhs, own_rhs], 0), COL, 0, 0, tiled=T...]
    ppermute x37 -> x33, starting transfers between devices: 43.8 us -> 43.5 us  [move(): return lax.ppermute(value, AXES, pairs)]
  transfers between devices with their start and end apart: 38 -> 35, of which waited for: 5 -> 8; matrix products, arithmetic and copies ran while one was open for 4% -> 7% of each run, Pallas kernels for 11% -> 7%
where the time goes in v5:
time: 189 us; the launch traced here: 187 us
  waiting for transfers between devices  88.9 us (47%)
  starting transfers between devices  55.4 us (29%)
  Pallas kernels  22 us (12%)
  local copies, waits for them, and re-layouts  14.9 us (8%)
  other arithmetic  5.63 us (3%)
    ppermute x33, waiting for transfers between devices, move(): return lax.ppermute(value, AXES, pairs)  86.4 us
    ppermute x33, starting transfers between devices, move(): return lax.ppermute(value, AXES, pairs)  43.5 us
    pallas_call x3, Pallas kernels, accumulate(): pl.pallas_call(body, out_shape=jax.ShapeDtypeStruct((512, 1024), F32), in...  10.2 us
    all_to_all x1, starting transfers between devices, shards(): lax.all_to_all(jnp.concatenate([own_rhs, own_rhs], 0), COL, 0, 0, tiled=T...  7.77 us
    pallas_call x1, Pallas kernels, pack_and_solve(): pl.pallas_call(body, out_shape=[jax.ShapeDtypeStruct((8, 1024, 256), BF16...  5.74 us
    unnamed x10, local copies, waits for them, and re-layouts  5.18 us
    all_to_all x1, starting transfers between devices, shards(): left = lax.all_to_all(by_rows, COL, 0, 0, tiled=True)  4.16 us
  transfers between devices with their start and end apart: 35, of which 8 were waited for; matrix products, arithmetic and copies ran while one was open for 7% of the time, Pallas kernels for 7%

profile of v5, /device:TPU:5, one launch (start us, length us, event | category | flops | bytes accessed | tf_op | source)
XLA Modules:
  0.0 187.4 jit_solution(13256575267161919996)
XLA Ops:
  2.4 1.5 collective-permute-start.5
  8.7 7.8 %all-to-all-start = ((f32[16,64,128]{2,1,0:T(8,128)}), f32[16,64,128]{2,1,0:T(8,128)S(1)}, u32[]{:S(2)}, u32[]{:S(2)}) async-start(f32[16,64,128]{2,1,0:T(8,128)} %pad_maximum_fusion.1), calls=%async_computation | async-start | bytes 1048576 | tf_op jit(solution)/shard_map/all_to_all | solution.py:300
  18.7 1.4 collective-permute-start.4
  24.3 2.5 %all-to-all-done = f32[16,64,128]{2,1,0:T(8,128)S(1)} async-done(((f32[16,64,128]{2,1,0:T(8,128)}), f32[16,64,128]{2,1,0:T(8,128)S(1)}, u32[]{:S(2)}, u32[]{:S(2)}) %all-to-all-start) | async-done | bytes 524320 | tf_op jit(solution)/shard_map/all_to_all | solution.py:300
  26.8 5.7 %pack_and_solve.1 = (bf16[8,1024,256]{2,1,0:T(8,128)(2,1)S(1)}, f32[1024,128]{1,0:T(8,128)}) custom-call(s32[2]{0:T(128)S(1)} %pad_add_fusion.info, f32[1024,128]{1,0:T(8,128)S(1)} %broadcast_select_fusion.refs_0_, f32[1024,128]{1,0:T(8,128)S(1)} %collective-permute-done.1.refs_1_, f32[1024,128]{1,0:T(8,128)S(1)} %collective-permute-done.2.refs_2_, ...), custom_call_target="tpu_custom_call" | custom-call | tf_op jit(solution)/shard_map/pack_and_solve/pallas_call | solution.py:85
  32.6 2.0 %copy-done = bf16[8,1024,256]{2,1,0:T(8,128)(2,1)} copy-done((bf16[8,1024,256]{2,1,0:T(8,128)(2,1)}, bf16[8,1024,256]{2,1,0:T(8,128)(2,1)S(1)}, u32[]{:S(2)}) %copy-start) | copy-done | bytes 4194328
  39.9 3.4 %copy.10 = f32[16,4,64,128]{3,2,1,0:T(8,128)} copy(f32[16,4,64,128]{3,2,0,1:T(8,128)} %bitcast.46) | data formatting | bytes 4194304 | tf_op jit(solution)/shard_map/transpose | solution.py:310
  45.3 4.2 %all-to-all-start.1 = ((f32[16,256,128]{2,1,0:T(8,128)}), f32[16,256,128]{2,1,0:T(8,128)S(1)}, u32[]{:S(2)}, u32[]{:S(2)}) async-start(f32[16,256,128]{2,1,0:T(8,128)} %bitcast.45), calls=%async_computation.1 | async-start | bytes 4194304 | tf_op jit(solution)/shard_map/all_to_all | solution.py:312
  52.8 51.2 %collective-permute-done.17 = f32[256,128]{1,0:T(8,128)} collective-permute-done((f32[256,128]{1,0:T(8,128)S(1)}, f32[256,128]{1,0:T(8,128)}, u32[]{:S(2)}, u32[]{:S(2)}) %collective-permute-start.17) | collective-permute-done | bytes 131104 | tf_op jit(solution)/shard_map/ppermute | solution.py:226
  105.1 2.2 %copy-done.2 = bf16[8,1024,256]{2,1,0:T(8,128)(2,1)S(1)} copy-done((bf16[8,1024,256]{2,1,0:T(8,128)(2,1)S(1)}, bf16[8,1024,256]{2,1,0:T(8,128)(2,1)}, u32[]{:S(2)}) %copy-start.2) | copy-done | bytes 4194328
  107.3 2.7 %block_solve.1 = f32[1024,128]{1,0:T(8,128)S(1)} custom-call(bf16[8,1024,256]{2,1,0:T(8,128)(2,1)S(1)} %copy-done.2, f32[1024,128]{1,0:T(8,128)S(1)} %collective-permute-done.12.rhs_ref), custom_call_target="tpu_custom_call" | custom-call | tf_op jit(solution)/shard_map/block_solve/pallas_call | solution.py:109
  114.1 19.5 %collective-permute-done.22 = f32[256,128]{1,0:T(8,128)S(1)} collective-permute-done((f32[256,128]{1,0:T(8,128)S(1)}, f32[256,128]{1,0:T(8,128)S(1)}, u32[]{:S(2)}, u32[]{:S(2)}) %collective-permute-start.22) | collective-permute-done | bytes 131104 | tf_op jit(solution)/shard_map/ppermute | solution.py:226
  133.8 1.5 collective-permute-start.25
  135.2 3.8 %collective-permute-done.24 = f32[2,256,128]{2,1,0:T(8,128)S(1)} collective-permute-done((f32[2,256,128]{2,1,0:T(8,128)S(1)}, f32[2,256,128]{2,1,0:T(8,128)S(1)}, u32[]{:S(2)}, u32[]{:S(2)}) %collective-permute-start.24) | collective-permute-done | bytes 262176 | tf_op jit(solution)/shard_map/ppermute | solution.py:226
  142.0 6.4 %collective-permute-start.23 = (f32[8,256,128]{2,1,0:T(8,128)}, f32[8,256,128]{2,1,0:T(8,128)}, u32[]{:S(2)}, u32[]{:S(2)}) collective-permute-start(f32[8,256,128]{2,1,0:T(8,128)} %bitcast.17), channel_id=1, source_target_pairs={{0,16},{1,17},{2,18},{3,19},{4,20},{5,21},{6,22},{7,23},{8,24},{9,... | collective-permute-start | bytes 3145736 | tf_op jit(solution)/shard_map/ppermute | solution.py:226
  148.6 3.2 %collective-permute-start.29 = (f32[4,2,256,128]{3,2,1,0:T(8,128)S(1)}, f32[4,2,256,128]{3,2,1,0:T(8,128)}, u32[]{:S(2)}, u32[]{:S(2)}) collective-permute-start(f32[4,2,256,128]{3,2,1,0:T(8,128)S(1)} %pad_maximum_fusion.refs_0_), channel_id=1, source_target_pairs={{0,12},{1,13},{2,14},{3,15},{4,0},{5,1},{6,2},{7,3},{8,4},{9,5},{1... | collective-permute-start | bytes 3145736 | tf_op jit(solution)/shard_map/ppermute | solution.py:226
  151.9 1.6 prepare_update.1
  153.4 2.5 %update_near.1.refs_0_ = f32[512,1024]{1,0:T(8,128)S(1)} custom-call(s32[5]{0:T(128)S(1)} %stack.66.info, bf16[4,512,256]{2,1,0:T(8,128)(2,1)S(1)} %get-tuple-element.29.high_ref, bf16[4,512,256]{2,1,0:T(8,128)(2,1)S(1)} %get-tuple-element.30.low_ref, f32[4,2,256,128]{3,2,1,0:T(8,128)S(1)} %pad_maximum_fusion.refs_0_), custom_call_target="tpu_custom_call" | custom-call | tf_op jit(solution)/shard_map/update_near/pallas_call | solution.py:202
  155.9 8.3 %collective-permute-done.28.refs_2_ = f32[4,2,256,128]{3,2,1,0:T(8,128)S(1)} collective-permute-done((f32[4,2,256,128]{3,2,1,0:T(8,128)S(1)}, f32[4,2,256,128]{3,2,1,0:T(8,128)S(1)}, u32[]{:S(2)}, u32[]{:S(2)}) %collective-permute-start.28) | collective-permute-done | bytes 1048608 | tf_op jit(solution)/shard_map/ppermute | solution.py:226
  166.1 2.1 %collective-permute-start.31 = (f32[2,2,256,128]{3,2,1,0:T(8,128)S(1)}, f32[2,2,256,128]{3,2,1,0:T(8,128)S(1)}, u32[]{:S(2)}, u32[]{:S(2)}) collective-permute-start(f32[2,2,256,128]{3,2,1,0:T(8,128)S(1)} %slice.89), channel_id=1, source_target_pairs={{0,12},{1,13},{2,14},{3,15},{4,0},{5,1},{6,2},{7,3},{8,4},{9,5},{1... | collective-permute-start | bytes 1572872 | tf_op jit(solution)/shard_map/ppermute | solution.py:226
  168.2 5.1 %update_next.1.refs_0_ = f32[512,1024]{1,0:T(8,128)S(1)} custom-call(s32[5]{0:T(128)S(1)} %stack.66.info, bf16[4,512,256]{2,1,0:T(8,128)(2,1)S(1)} %get-tuple-element.29.high_ref, bf16[4,512,256]{2,1,0:T(8,128)(2,1)S(1)} %get-tuple-element.30.low_ref, f32[512,1024]{1,0:T(8,128)S(1)} %update_near.1.refs_0_, ...), custom_call_target="tpu_custom_call", output_to_operand_aliasing={{}: (3, {})} | custom-call | tf_op jit(solution)/shard_map/update_next/pallas_call | solution.py:202
  174.5 2.6 %update_far.1 = f32[512,1024]{1,0:T(8,128)S(1)} custom-call(s32[5]{0:T(128)S(1)} %stack.66.info, bf16[4,512,256]{2,1,0:T(8,128)(2,1)S(1)} %get-tuple-element.29.high_ref, bf16[4,512,256]{2,1,0:T(8,128)(2,1)S(1)} %get-tuple-element.30.low_ref, f32[512,1024]{1,0:T(8,128)S(1)} %update_next.1.refs_0_, ...), custom_call_target="tpu_custom_call", output_to_operand_aliasing={{}: (3, {})} | custom-call | tf_op jit(solution)/shard_map/update_far/pallas_call | solution.py:202
  177.3 6.6 %collective-permute-start.32 = (f32[256,1024]{1,0:T(8,128)S(1)}, f32[256,1024]{1,0:T(8,128)S(1)}, u32[]{:S(2)}, u32[]{:S(2)}) collective-permute-start(f32[256,1024]{1,0:T(8,128)S(1)} %slice.107), channel_id=1, source_target_pairs={{0,16},{1,17},{2,18},{3,19},{4,20},{5,21},{6,22},{7,23},{8,24},{9,... | collective-permute-start | bytes 3145736 | tf_op jit(solution)/shard_map/ppermute | solution.py:226
  183.9 2.3 %collective-permute-done.32 = f32[256,1024]{1,0:T(8,128)S(1)} collective-permute-done((f32[256,1024]{1,0:T(8,128)S(1)}, f32[256,1024]{1,0:T(8,128)S(1)}, u32[]{:S(2)}, u32[]{:S(2)}) %collective-permute-start.32) | collective-permute-done | bytes 1048608 | tf_op jit(solution)/shard_map/ppermute | solution.py:226
  (97 shorter events, 37.1 us)
Async XLA Ops:
  4.0 14.0 %collective-permute-start.1 = (f32[1024,128]{1,0:T(8,128)S(1)}, f32[1024,128]{1,0:T(8,128)S(1)}, u32[]{:S(2)}, u32[]{:S(2)}) collective-permute-start(f32[1024,128]{1,0:T(8,128)S(1)} %broadcast_select_fusion.refs_0_), channel_id=1, source_target_pairs={{0,3},{1,0},{2,1},{3,2},{4,7},{5,4},{6,5},{7,6},{24,27},{25,24},{2... | collective-permute-start | bytes 1572872 | tf_op jit(solution)/shard_map/ppermute | solution.py:226
  4.7 11.8 %collective-permute-start.2 = (f32[1024,128]{1,0:T(8,128)S(1)}, f32[1024,128]{1,0:T(8,128)S(1)}, u32[]{:S(2)}, u32[]{:S(2)}) collective-permute-start(f32[1024,128]{1,0:T(8,128)S(1)} %broadcast_select_fusion.refs_0_), channel_id=1, source_target_pairs={{0,1},{1,2},{2,3},{3,0},{4,5},{5,6},{6,7},{7,4},{24,25},{25,26},{2... | collective-permute-start | bytes 1572872 | tf_op jit(solution)/shard_map/ppermute | solution.py:226
  5.4 16.7 %collective-permute-start.6 = (f32[1024,128]{1,0:T(8,128)}, f32[1024,128]{1,0:T(8,128)S(1)}, u32[]{:S(2)}, u32[]{:S(2)}) collective-permute-start(f32[1024,128]{1,0:T(8,128)} %collective-permute-done.5.refs_5_), channel_id=1, source_target_pairs={{0,3},{1,0},{2,1},{3,2},{4,7},{5,4},{6,5},{7,6},{24,27},{25,24},{2... | collective-permute-start | bytes 1572872 | tf_op jit(solution)/shard_map/ppermute | solution.py:226
  6.1 14.0 %collective-permute-start.7 = (f32[1024,128]{1,0:T(8,128)}, f32[1024,128]{1,0:T(8,128)S(1)}, u32[]{:S(2)}, u32[]{:S(2)}) collective-permute-start(f32[1024,128]{1,0:T(8,128)} %collective-permute-done.5.refs_5_), channel_id=1, source_target_pairs={{0,1},{1,2},{2,3},{3,0},{4,5},{5,6},{6,7},{7,4},{24,25},{25,26},{2... | collective-permute-start | bytes 1572872 | tf_op jit(solution)/shard_map/ppermute | solution.py:226
  8.7 18.1 %all-to-all-start = ((f32[16,64,128]{2,1,0:T(8,128)}), f32[16,64,128]{2,1,0:T(8,128)S(1)}, u32[]{:S(2)}, u32[]{:S(2)}) async-start(f32[16,64,128]{2,1,0:T(8,128)} %pad_maximum_fusion.1), calls=%async_computation | async-start | bytes 1048576 | tf_op jit(solution)/shard_map/all_to_all | solution.py:300
  17.3 9.5 %collective-permute-start.3 = (f32[512,128]{1,0:T(8,128)}, f32[512,128]{1,0:T(8,128)S(1)}, u32[]{:S(2)}, u32[]{:S(2)}) collective-permute-start(f32[512,128]{1,0:T(8,128)} %slice.92), channel_id=1, source_target_pairs={{0,1},{1,2},{2,3},{3,0},{4,5},{5,6},{6,7},{7,4},{24,25},{25,26},{2... | collective-permute-start | bytes 786440 | tf_op jit(solution)/shard_map/ppermute | solution.py:226
  18.7 8.2 %collective-permute-start.4 = (f32[512,128]{1,0:T(8,128)}, f32[512,128]{1,0:T(8,128)}, u32[]{:S(2)}, u32[]{:S(2)}) collective-permute-start(f32[512,128]{1,0:T(8,128)} %slice.93), channel_id=1, source_target_pairs={{0,3},{1,0},{2,1},{3,2},{4,7},{5,4},{6,5},{7,6},{24,27},{25,24},{2... | collective-permute-start | bytes 786440 | tf_op jit(solution)/shard_map/ppermute | solution.py:226
  20.8 6.1 %collective-permute-start.8 = (f32[512,128]{1,0:T(8,128)}, f32[512,128]{1,0:T(8,128)}, u32[]{:S(2)}, u32[]{:S(2)}) collective-permute-start(f32[512,128]{1,0:T(8,128)} %slice.94), channel_id=1, source_target_pairs={{0,1},{1,2},{2,3},{3,0},{4,5},{5,6},{6,7},{7,4},{24,25},{25,26},{2... | collective-permute-start | bytes 786440 | tf_op jit(solution)/shard_map/ppermute | solution.py:226
  36.2 7.1 %collective-permute-start.10 = (f32[1024,128]{1,0:T(8,128)S(1)}, f32[1024,128]{1,0:T(8,128)S(1)}, u32[]{:S(2)}, u32[]{:S(2)}) collective-permute-start(f32[1024,128]{1,0:T(8,128)S(1)} %bitcast.43), channel_id=1, source_target_pairs={{16,32},{17,33},{18,34},{19,35},{20,36},{21,37},{22,38},{23,39}} | collective-permute-start | bytes 1572872 | tf_op jit(solution)/shard_map/ppermute | solution.py:226
  36.9 6.4 %collective-permute-start.11 = (f32[1024,128]{1,0:T(8,128)}, f32[1024,128]{1,0:T(8,128)S(1)}, u32[]{:S(2)}, u32[]{:S(2)}) collective-permute-start(f32[1024,128]{1,0:T(8,128)} %get-tuple-element.25), channel_id=1, source_target_pairs={{0,32},{1,33},{2,34},{3,35},{4,36},{5,37},{6,38},{7,39}} | collective-permute-start | bytes 1572872 | tf_op jit(solution)/shard_map/ppermute | solution.py:226
  38.6 10.8 %collective-permute-start.14 = (f32[256,128]{1,0:T(8,128)S(1)}, f32[256,128]{1,0:T(8,128)}, u32[]{:S(2)}, u32[]{:S(2)}) collective-permute-start(f32[256,128]{1,0:T(8,128)S(1)} %slice.97), channel_id=1, source_target_pairs={{0,12},{1,13},{2,14},{3,15},{4,8},{5,9},{6,10},{7,11},{16,28},{17,... | collective-permute-start | bytes 393224 | tf_op jit(solution)/shard_map/ppermute | solution.py:226
  44.6 60.5 %collective-permute-start.12 = (f32[1024,128]{1,0:T(8,128)S(1)}, f32[1024,128]{1,0:T(8,128)S(1)}, u32[]{:S(2)}, u32[]{:S(2)}) collective-permute-start(f32[1024,128]{1,0:T(8,128)S(1)} %block_residual.1), channel_id=1, source_target_pairs={{32,28},{33,29},{34,30},{35,31},{36,24},{37,25},{38,26},{39,27}} | collective-permute-start | bytes 1572872 | tf_op jit(solution)/shard_map/ppermute | solution.py:226
  45.3 88.4 %all-to-all-start.1 = ((f32[16,256,128]{2,1,0:T(8,128)}), f32[16,256,128]{2,1,0:T(8,128)S(1)}, u32[]{:S(2)}, u32[]{:S(2)}) async-start(f32[16,256,128]{2,1,0:T(8,128)} %bitcast.45), calls=%async_computation.1 | async-start | bytes 4194304 | tf_op jit(solution)/shard_map/all_to_all | solution.py:312
  51.5 52.5 %collective-permute-start.17 = (f32[256,128]{1,0:T(8,128)S(1)}, f32[256,128]{1,0:T(8,128)}, u32[]{:S(2)}, u32[]{:S(2)}) collective-permute-start(f32[256,128]{1,0:T(8,128)S(1)} %collective-permute-done.15), channel_id=1, source_target_pairs={{32,64},{33,65},{34,66},{35,67},{36,68},{37,69},{38,70},{39,71},{4... | collective-permute-start | bytes 393224 | tf_op jit(solution)/shard_map/ppermute | solution.py:226
  112.8 20.8 %collective-permute-start.22 = (f32[256,128]{1,0:T(8,128)S(1)}, f32[256,128]{1,0:T(8,128)S(1)}, u32[]{:S(2)}, u32[]{:S(2)}) collective-permute-start(f32[256,128]{1,0:T(8,128)S(1)} %collective-permute-done.20), channel_id=1, source_target_pairs={{32,64},{33,65},{34,66},{35,67},{36,68},{37,69},{38,70},{39,71},{4... | collective-permute-start | bytes 393224 | tf_op jit(solution)/shard_map/ppermute | solution.py:226
  133.8 6.5 %collective-permute-start.25 = (f32[2,256,128]{2,1,0:T(8,128)S(1)}, f32[2,256,128]{2,1,0:T(8,128)S(1)}, u32[]{:S(2)}, u32[]{:S(2)}) collective-permute-start(f32[2,256,128]{2,1,0:T(8,128)S(1)} %get-tuple-element.42), channel_id=1, source_target_pairs={{0,1},{1,2},{2,3},{3,0},{4,5},{5,6},{6,7},{7,4},{8,9},{9,10},{10,1... | collective-permute-start | bytes 786440 | tf_op jit(solution)/shard_map/ppermute | solution.py:226
  139.0 9.4 %collective-permute-start.27 = (f32[1,256,128]{2,1,0:T(8,128)S(1)}, f32[1,256,128]{2,1,0:T(8,128)S(1)}, u32[]{:S(2)}, u32[]{:S(2)}) collective-permute-start(f32[1,256,128]{2,1,0:T(8,128)S(1)} %slice.105), channel_id=1, source_target_pairs={{0,3},{1,0},{2,1},{3,2},{4,7},{5,4},{6,5},{7,6},{8,11},{9,8},{10,9... | collective-permute-start | bytes 393224 | tf_op jit(solution)/shard_map/ppermute | solution.py:226
  140.3 8.1 %collective-permute-start.26 = (f32[1,256,128]{2,1,0:T(8,128)S(1)}, f32[1,256,128]{2,1,0:T(8,128)S(1)}, u32[]{:S(2)}, u32[]{:S(2)}) collective-permute-start(f32[1,256,128]{2,1,0:T(8,128)S(1)} %slice.104), channel_id=1, source_target_pairs={{0,1},{1,2},{2,3},{3,0},{4,5},{5,6},{6,7},{7,4},{8,9},{9,10},{10,1... | collective-permute-start | bytes 393224 | tf_op jit(solution)/shard_map/ppermute | solution.py:226
  142.0 9.8 %collective-permute-start.23 = (f32[8,256,128]{2,1,0:T(8,128)}, f32[8,256,128]{2,1,0:T(8,128)}, u32[]{:S(2)}, u32[]{:S(2)}) collective-permute-start(f32[8,256,128]{2,1,0:T(8,128)} %bitcast.17), channel_id=1, source_target_pairs={{0,16},{1,17},{2,18},{3,19},{4,20},{5,21},{6,22},{7,23},{8,24},{9,... | collective-permute-start | bytes 3145736 | tf_op jit(solution)/shard_map/ppermute | solution.py:226
  148.5 15.7 %collective-permute-start.28 = (f32[4,2,256,128]{3,2,1,0:T(8,128)S(1)}, f32[4,2,256,128]{3,2,1,0:T(8,128)S(1)}, u32[]{:S(2)}, u32[]{:S(2)}) collective-permute-start(f32[4,2,256,128]{3,2,1,0:T(8,128)S(1)} %pad_maximum_fusion.refs_0_), channel_id=1, source_target_pairs={{0,4},{1,5},{2,6},{3,7},{4,8},{5,9},{6,10},{7,11},{8,12},{9,13},{1... | collective-permute-start | bytes 3145736 | tf_op jit(solution)/shard_map/ppermute | solution.py:226
  148.6 15.6 %collective-permute-start.29 = (f32[4,2,256,128]{3,2,1,0:T(8,128)S(1)}, f32[4,2,256,128]{3,2,1,0:T(8,128)}, u32[]{:S(2)}, u32[]{:S(2)}) collective-permute-start(f32[4,2,256,128]{3,2,1,0:T(8,128)S(1)} %pad_maximum_fusion.refs_0_), channel_id=1, source_target_pairs={{0,12},{1,13},{2,14},{3,15},{4,0},{5,1},{6,2},{7,3},{8,4},{9,5},{1... | collective-permute-start | bytes 3145736 | tf_op jit(solution)/shard_map/ppermute | solution.py:226
  164.3 9.3 %collective-permute-start.30 = (f32[2,2,256,128]{3,2,1,0:T(8,128)S(1)}, f32[2,2,256,128]{3,2,1,0:T(8,128)S(1)}, u32[]{:S(2)}, u32[]{:S(2)}) collective-permute-start(f32[2,2,256,128]{3,2,1,0:T(8,128)S(1)} %slice.88), channel_id=1, source_target_pairs={{0,4},{1,5},{2,6},{3,7},{4,8},{5,9},{6,10},{7,11},{8,12},{9,13},{1... | collective-permute-start | bytes 1572872 | tf_op jit(solution)/shard_map/ppermute | solution.py:226
  166.1 8.4 %collective-permute-start.31 = (f32[2,2,256,128]{3,2,1,0:T(8,128)S(1)}, f32[2,2,256,128]{3,2,1,0:T(8,128)S(1)}, u32[]{:S(2)}, u32[]{:S(2)}) collective-permute-start(f32[2,2,256,128]{3,2,1,0:T(8,128)S(1)} %slice.89), channel_id=1, source_target_pairs={{0,12},{1,13},{2,14},{3,15},{4,0},{5,1},{6,2},{7,3},{8,4},{9,5},{1... | collective-permute-start | bytes 1572872 | tf_op jit(solution)/shard_map/ppermute | solution.py:226
  177.3 8.9 %collective-permute-start.32 = (f32[256,1024]{1,0:T(8,128)S(1)}, f32[256,1024]{1,0:T(8,128)S(1)}, u32[]{:S(2)}, u32[]{:S(2)}) collective-permute-start(f32[256,1024]{1,0:T(8,128)S(1)} %slice.107), channel_id=1, source_target_pairs={{0,16},{1,17},{2,18},{3,19},{4,20},{5,21},{6,22},{7,23},{8,24},{9,... | collective-permute-start | bytes 3145736 | tf_op jit(solution)/shard_map/ppermute | solution.py:226
  (15 other events, 42.4 us)

commit v6 on v5

--- a/solution.py
+++ b/solution.py
@@ -73,36 +73,17 @@
     )(info, lead)
 
 
-def pack_and_solve(info, pieces, places, rhs):
-    def body(info, *refs):
-        rhs_ref, tri_ref, out_ref = refs[-3:]
-        for ref, (other, steps, row) in zip(refs, places):
-            half = 1 - info[0] if other else info[0]
-            k = 4 * half + lax.rem(info[1] + steps, 4)
-            tri_ref[k, pl.ds(row, ref.shape[0]), :] = pack_left(ref[...])
-        solve_body(tri_ref, rhs_ref, out_ref)
-
-    return pl.pallas_call(
-        body,
-        out_shape=[jax.ShapeDtypeStruct((8, 1024, 256), BF16), jax.ShapeDtypeStruct(rhs.shape, F32)],
-        in_specs=[SM] + [VM] * (len(pieces) + 1),
-        out_specs=[VM, VM],
-        compiler_params=PARAMS,
-        name="pack_and_solve",
-    )(info, *pieces, rhs)
-
-
 def solve_body(tri_ref, rhs_ref, out_ref):
     count = tri_ref.shape[0]
     out_ref[...] = rhs_ref[...]
     for k in range(count):
         here = pl.ds(k * TILE, TILE)
-        solved = packed_product(tri_ref[k, here, :], pack_right(out_ref[here, :]))
+        solved = packed_product(pack_left(tri_ref[k, here, :]), pack_right(out_ref[here, :]))
         out_ref[here, :] = solved
         right = pack_right(solved)
         for i in range(k + 1, count):
             there = pl.ds(i * TILE, TILE)
-            out_ref[there, :] = out_ref[there, :] - packed_product(tri_ref[k, there, :], right)
+            out_ref[there, :] = out_ref[there, :] - packed_product(pack_left(tri_ref[k, there, :]), right)
 
 
 def solve(tri, rhs):
@@ -123,7 +104,7 @@
         for i in range(count):
             there = pl.ds(i * TILE, TILE)
             base = rhs_ref[there, :] if k == 0 else out_ref[there, :]
-            out_ref[there, :] = base - packed_product(tri_ref[k, there, :], right)
+            out_ref[there, :] = base - packed_product(pack_left(tri_ref[k, there, :]), right)
 
 
 def residual(tri, rhs, x):
@@ -256,32 +237,6 @@
     return after, far_low, far_high, before
 
 
-def holds(a, b, c):
-    return (a, b, c // 2) in ((0, 0, 0), (0, 1, 1), (1, 0, 0))
-
-
-def gather_slices(lead, xi):
-    def flip(c):
-        return c + 1 - 2 * (c % 2)
-
-    def across(a, b, c, d):
-        return (1 if b == 1 and c < 2 else 0, 0 if c < 2 else 1, flip(c), d) if a == 0 and (b == 1 or c < 2) else None
-
-    def along(step):
-        return lambda a, b, c, d: (a, b, c, d + step) if holds(a, b, c) else None
-
-    hop = move(lead, lambda a, b, c, d: (1, 0, c, d) if (a, b) == (0, 1) and c < 2 else None)
-    pair = move(lead, across)
-    own = jnp.where(xi == 1, hop, lead)
-    pieces, places = [], []
-    for other, value in ((False, own), (True, pair)):
-        before, after = move(value, along(1)), move(value, along(-1))
-        far_low, far_high = move(before[:512], along(1)), move(after[512:], along(-1))
-        pieces += [value, after, before, far_low, far_high]
-        places += [(other, 0, 0), (other, 1, 0), (other, 3, 0), (other, 2, 0), (other, 2, 512)]
-    return pieces, places
-
-
 def shards(factor, cross_cov):
     xi, core = lax.axis_index("x"), lax.axis_index("core")
     yh, yl, z = lax.axis_index("yh"), lax.axis_index("yl"), lax.axis_index("z")
@@ -294,27 +249,23 @@
     diagonal = ((row_id == 0) & (yh == 0)) | ((row_id == 1) & (yh == 1))
     info = jnp.stack([diagonal.astype(jnp.int32), slice_id.astype(jnp.int32)])
     lead = invert_diagonal(info, local[0])
-    pieces, places = gather_slices(lead, xi)
+    tri = lax.all_gather(lead, ("yl", "z"), axis=0, tiled=False)
 
     own_rhs = rhs[0].reshape(64, 8, TILE).transpose(1, 0, 2)
     columns = lax.all_to_all(jnp.concatenate([own_rhs, own_rhs], 0), COL, 0, 0, tiled=True).reshape(1024, TILE)
-
-    place = jnp.stack([yl, z]).astype(jnp.int32)
-    tri, first = pack_and_solve(place, pieces, places, columns)
-    columns, first = lax.optimization_barrier((columns, first))
-    sent = move(first, lambda a, b, c, d: (1, 0, c, d) if a == 0 and b == 0 and c < 2 else None)
-    columns = move(columns, lambda a, b, c, d: (1, 0, c, d) if (a, b) == (0, 1) and c < 2 else None)
+    by_rows = local.reshape(4, 16, 64, TILE).transpose(1, 0, 2, 3).reshape(16, 256, TILE)
+    by_rows, columns = lax.optimization_barrier((by_rows, columns))
+    left = lax.all_to_all(by_rows, COL, 0, 0, tiled=True)
+
+    first = solve(tri, columns)
+    sent = move(first, lambda a, b, c, d: (0, 1, c, d) if a == 0 and b == 0 and c < 2 else None)
     rest = residual(tri, columns, sent)
-    second_rhs = move(rest, lambda a, b, c, d: (0, 1, 3 - c, d) if (a, b) == (1, 0) and c < 2 else None)
-
-    by_rows = local.reshape(4, 16, 64, TILE).transpose(1, 0, 2, 3).reshape(16, 256, TILE)
-    by_rows, sent = lax.optimization_barrier((by_rows, sent))
-    left = lax.all_to_all(by_rows, COL, 0, 0, tiled=True)
+    second_rhs = move(rest, lambda a, b, c, d: (0, 1, 3 - c, d) if (a, b) == (0, 1) and c < 2 else None)
+    first, left, rest = lax.optimization_barrier((first, left, rest))
     dealt0 = deal(first, core, yh, xi, 0, 0)
     second_rhs, dealt0 = lax.optimization_barrier((second_rhs, dealt0))
     second = solve(tri, second_rhs)
     dealt1 = deal(second, core, yh, xi, 1, 1)
-    dealt1, left = lax.optimization_barrier((dealt1, left))
 
     def swap(value):
         return move(value, lambda a, b, c, d: (a, 1 - b, c, d))

time: 189 us -> 207 us (1.095)
  waiting for transfers between devices: 88.9 us -> 120 us
  starting transfers between devices: 55.4 us -> 38.6 us
  between operations: 0.5 us -> 13.8 us
  local copies, waits for them, and re-layouts: 14.9 us -> 9.57 us
  Pallas kernels: 22 us -> 19.9 us
    all_gather x0 -> x1, waiting for transfers between devices: none -> 59.5 us  [shards(): tri = lax.all_gather(lead, ('yl', 'z'), axis=0, tiled=False)]
    ppermute x33 -> x22, waiting for transfers between devices: 86.4 us -> 48.8 us  [move(): return lax.ppermute(value, AXES, pairs)]
    ppermute x33 -> x22, starting transfers between devices: 43.5 us -> 25.2 us  [move(): return lax.ppermute(value, AXES, pairs)]
    all_to_all x1, waiting for transfers between devices: 2.51 us -> 11.3 us  [shards(): lax.all_to_all(jnp.concatenate([own_rhs, own_rhs], 0), COL, 0, 0, tiled=T...]
    pallas_call x1 -> x0, Pallas kernels: 5.74 us -> none  [pack_and_solve(): pl.pallas_call(body, out_shape=[jax.ShapeDtypeStruct((8, 1024, 256), BF16...]
    slice x4 -> x0, local copies, waits for them, and re-layouts: 2.9 us -> none  [the longest x2 1.47 us: gather_slices(): before[:512]]
    pallas_call x1 -> x2, Pallas kernels: 2.69 us -> 5.39 us  [solve(): pl.pallas_call(solve_body, out_shape=jax.ShapeDtypeStruct(rhs.shape, F32)...]
  transfers between devices with their start and end apart: 35 -> 25, of which waited for: 8 -> 10; matrix products, arithmetic and copies ran while one was open for 7% -> 3% of each run, Pallas kernels for 7% -> 6%
where the time goes in v6:
time: 207 us
  waiting for transfers between devices  120 us (58%)
  starting transfers between devices  38.6 us (19%)
  Pallas kernels  19.9 us (10%)
  between operations  13.8 us (7%)
  local copies, waits for them, and re-layouts  9.57 us (5%)
  other arithmetic  5.13 us (2%)
    all_gather x1, waiting for transfers between devices, shards(): tri = lax.all_gather(lead, ('yl', 'z'), axis=0, tiled=False)  59.5 us
    ppermute x22, waiting for transfers between devices, move(): return lax.ppermute(value, AXES, pairs)  48.8 us
    ppermute x22, starting transfers between devices, move(): return lax.ppermute(value, AXES, pairs)  25.2 us
    all_to_all x1, waiting for transfers between devices, shards(): lax.all_to_all(jnp.concatenate([own_rhs, own_rhs], 0), COL, 0, 0, tiled=T...  11.3 us
    pallas_call x3, Pallas kernels, accumulate(): pl.pallas_call(body, out_shape=jax.ShapeDtypeStruct((512, 1024), F32), in...  10.3 us
    all_to_all x1, starting transfers between devices, shards(): lax.all_to_all(jnp.concatenate([own_rhs, own_rhs], 0), COL, 0, 0, tiled=T...  7.77 us
    all_to_all x1, starting transfers between devices, shards(): left = lax.all_to_all(by_rows, COL, 0, 0, tiled=True)  5.6 us
    unnamed x10, local copies, waits for them, and re-layouts  5.54 us
  transfers between devices with their start and end apart: 25, of which 10 were waited for; matrix products, arithmetic and copies ran while one was open for 3% of the time, Pallas kernels for 6%

profile of v6, /device:TPU:5, one launch (start us, length us, event | category | flops | bytes accessed | tf_op | source)
XLA Modules:
  0.0 206.7 jit_solution(17222223792499258977)
XLA Ops:
  11.2 7.8 %all-to-all-start = ((f32[16,64,128]{2,1,0:T(8,128)}), f32[16,64,128]{2,1,0:T(8,128)S(1)}, u32[]{:S(2)}, u32[]{:S(2)}) async-start(f32[16,64,128]{2,1,0:T(8,128)} %pad_maximum_fusion.1), calls=%async_computation | async-start | bytes 1048576 | tf_op jit(solution)/shard_map/all_to_all | solution.py:255
  19.0 1.5 copy.9
  20.5 11.3 %all-to-all-done = f32[16,64,128]{2,1,0:T(8,128)S(1)} async-done(((f32[16,64,128]{2,1,0:T(8,128)}), f32[16,64,128]{2,1,0:T(8,128)S(1)}, u32[]{:S(2)}, u32[]{:S(2)}) %all-to-all-start) | async-done | bytes 524320 | tf_op jit(solution)/shard_map/all_to_all | solution.py:255
  31.9 5.6 %all-to-all-start.1 = ((f32[16,256,128]{2,1,0:T(8,128)}), f32[16,256,128]{2,1,0:T(8,128)}, u32[]{:S(2)}, u32[]{:S(2)}) async-start(f32[16,256,128]{2,1,0:T(8,128)} %bitcast.12), calls=%async_computation.1 | async-start | bytes 4194304 | tf_op jit(solution)/shard_map/all_to_all | solution.py:258
  37.5 59.5 %all-gather.3.cloned.1.call-done = f32[8192,128]{1,0:T(8,128)} async-done(((f32[1024,128]{1,0:T(8,128)}), f32[8192,128]{1,0:T(8,128)}) %all-gather.3.cloned.1.call-update) | async-done | bytes 4194320 | tf_op jit(solution)/shard_map/all_gather | solution.py:252
  96.9 2.2 %copy-done = f32[8192,128]{1,0:T(8,128)S(1)} copy-done((f32[8192,128]{1,0:T(8,128)S(1)}, f32[8192,128]{1,0:T(8,128)}, u32[]{:S(2)}) %copy-start) | copy-done | bytes 4194328
  99.1 2.7 %block_solve.2 = f32[1024,128]{1,0:T(8,128)S(1)} custom-call(f32[8,1024,128]{2,1,0:T(8,128)S(1)} %bitcast.42, f32[1024,128]{1,0:T(8,128)S(1)} %bitcast.45), custom_call_target="tpu_custom_call" | custom-call | tf_op jit(solution)/shard_map/block_solve/pallas_call | solution.py:90
  108.7 14.9 %collective-permute-done.7 = f32[256,128]{1,0:T(8,128)S(1)} collective-permute-done((f32[256,128]{1,0:T(8,128)S(1)}, f32[256,128]{1,0:T(8,128)S(1)}, u32[]{:S(2)}, u32[]{:S(2)}) %collective-permute-start.7) | collective-permute-done | bytes 131104 | tf_op jit(solution)/shard_map/ppermute | solution.py:207
  123.6 2.2 %copy-done.1 = f32[8192,128]{1,0:T(8,128)S(1)} copy-done((f32[8192,128]{1,0:T(8,128)S(1)}, f32[8192,128]{1,0:T(8,128)}, u32[]{:S(2)}) %copy-start.1) | copy-done | bytes 4194328
  125.8 2.7 %block_solve.3 = f32[1024,128]{1,0:T(8,128)S(1)} custom-call(f32[8,1024,128]{2,1,0:T(8,128)S(1)} %bitcast.44, f32[1024,128]{1,0:T(8,128)S(1)} %collective-permute-done.2.rhs_ref), custom_call_target="tpu_custom_call" | custom-call | tf_op jit(solution)/shard_map/block_solve/pallas_call | solution.py:90
  132.7 13.8 %collective-permute-done.12 = f32[256,128]{1,0:T(8,128)S(1)} collective-permute-done((f32[256,128]{1,0:T(8,128)S(1)}, f32[256,128]{1,0:T(8,128)S(1)}, u32[]{:S(2)}, u32[]{:S(2)}) %collective-permute-start.12) | collective-permute-done | bytes 131104 | tf_op jit(solution)/shard_map/ppermute | solution.py:207
  148.2 3.8 %collective-permute-done.13 = f32[2,256,128]{2,1,0:T(8,128)S(1)} collective-permute-done((f32[2,256,128]{2,1,0:T(8,128)S(1)}, f32[2,256,128]{2,1,0:T(8,128)S(1)}, u32[]{:S(2)}, u32[]{:S(2)}) %collective-permute-start.13) | collective-permute-done | bytes 262176 | tf_op jit(solution)/shard_map/ppermute | solution.py:207
  153.8 2.7 %slice_select_fusion = (f32[2,1,4,256,128]{4,3,2,1,0:T(8,128)}, f32[2,1,4,256,128]{4,3,2,1,0:T(8,128)S(1)}) fusion(f32[2,2,4,256,128]{4,3,2,1,0:T(8,128)} %bitcast.15, pred[]{:T(512)S(6)} %eq.28), kind=kLoop, calls=%fused_computation.4 | loop fusion | flops 524288 | bytes 4194305 | tf_op jit(solution)/shard_map/jit(_where)/select_n | solution.py:275
  156.5 5.6 %collective-permute-start.1 = (f32[8,256,128]{2,1,0:T(8,128)}, f32[8,256,128]{2,1,0:T(8,128)}, u32[]{:S(2)}, u32[]{:S(2)}) collective-permute-start(f32[8,256,128]{2,1,0:T(8,128)} %bitcast.17), channel_id=1, source_target_pairs={{0,16},{1,17},{2,18},{3,19},{4,20},{5,21},{6,22},{7,23},{8,24},{9,... | collective-permute-start | bytes 3145736 | tf_op jit(solution)/shard_map/ppermute | solution.py:207
  162.2 3.0 %collective-permute-start.18 = (f32[4,2,256,128]{3,2,1,0:T(8,128)S(1)}, f32[4,2,256,128]{3,2,1,0:T(8,128)S(1)}, u32[]{:S(2)}, u32[]{:S(2)}) collective-permute-start(f32[4,2,256,128]{3,2,1,0:T(8,128)S(1)} %pad_maximum_fusion.refs_0_), channel_id=1, source_target_pairs={{0,12},{1,13},{2,14},{3,15},{4,0},{5,1},{6,2},{7,3},{8,4},{9,5},{1... | collective-permute-start | bytes 3145736 | tf_op jit(solution)/shard_map/ppermute | solution.py:207
  165.3 1.6 prepare_update.1
  166.8 2.6 %update_near.1.refs_0_ = f32[512,1024]{1,0:T(8,128)S(1)} custom-call(s32[5]{0:T(128)S(1)} %stack.59.info, bf16[4,512,256]{2,1,0:T(8,128)(2,1)S(1)} %get-tuple-element.22.high_ref, bf16[4,512,256]{2,1,0:T(8,128)(2,1)S(1)} %get-tuple-element.23.low_ref, f32[4,2,256,128]{3,2,1,0:T(8,128)S(1)} %pad_maximum_fusion.refs_0_), custom_call_target="tpu_custom_call" | custom-call | tf_op jit(solution)/shard_map/update_near/pallas_call | solution.py:183
  169.5 7.4 %collective-permute-done.18.refs_1_ = f32[4,2,256,128]{3,2,1,0:T(8,128)S(1)} collective-permute-done((f32[4,2,256,128]{3,2,1,0:T(8,128)S(1)}, f32[4,2,256,128]{3,2,1,0:T(8,128)S(1)}, u32[]{:S(2)}, u32[]{:S(2)}) %collective-permute-start.18) | collective-permute-done | bytes 1048608 | tf_op jit(solution)/shard_map/ppermute | solution.py:207
  176.9 3.5 %collective-permute-done.17.refs_2_ = f32[4,2,256,128]{3,2,1,0:T(8,128)} collective-permute-done((f32[4,2,256,128]{3,2,1,0:T(8,128)S(1)}, f32[4,2,256,128]{3,2,1,0:T(8,128)}, u32[]{:S(2)}, u32[]{:S(2)}) %collective-permute-start.17) | collective-permute-done | bytes 1048608 | tf_op jit(solution)/shard_map/ppermute | solution.py:207
  183.1 5.1 %update_next.1.refs_0_ = f32[512,1024]{1,0:T(8,128)S(1)} custom-call(s32[5]{0:T(128)S(1)} %stack.59.info, bf16[4,512,256]{2,1,0:T(8,128)(2,1)S(1)} %get-tuple-element.22.high_ref, bf16[4,512,256]{2,1,0:T(8,128)(2,1)S(1)} %get-tuple-element.23.low_ref, f32[512,1024]{1,0:T(8,128)S(1)} %update_near.1.refs_0_, ...), custom_call_target="tpu_custom_call", output_to_operand_aliasing={{}: (3, {})} | custom-call | tf_op jit(solution)/shard_map/update_next/pallas_call | solution.py:183
  188.2 1.8 collective-permute-done.20.refs_2_
  191.2 2.6 %update_far.1 = f32[512,1024]{1,0:T(8,128)S(1)} custom-call(s32[5]{0:T(128)S(1)} %stack.59.info, bf16[4,512,256]{2,1,0:T(8,128)(2,1)S(1)} %get-tuple-element.22.high_ref, bf16[4,512,256]{2,1,0:T(8,128)(2,1)S(1)} %get-tuple-element.23.low_ref, f32[512,1024]{1,0:T(8,128)S(1)} %update_next.1.refs_0_, ...), custom_call_target="tpu_custom_call", output_to_operand_aliasing={{}: (3, {})} | custom-call | tf_op jit(solution)/shard_map/update_far/pallas_call | solution.py:183
  194.0 2.4 %collective-permute-start.21 = (f32[256,1024]{1,0:T(8,128)S(1)}, f32[256,1024]{1,0:T(8,128)S(1)}, u32[]{:S(2)}, u32[]{:S(2)}) collective-permute-start(f32[256,1024]{1,0:T(8,128)S(1)} %slice.87), channel_id=1, source_target_pairs={{0,16},{1,17},{2,18},{3,19},{4,20},{5,21},{6,22},{7,23},{8,24},{9,... | collective-permute-start | bytes 3145736 | tf_op jit(solution)/shard_map/ppermute | solution.py:207
  196.4 2.3 %collective-permute-done.21 = f32[256,1024]{1,0:T(8,128)S(1)} collective-permute-done((f32[256,1024]{1,0:T(8,128)S(1)}, f32[256,1024]{1,0:T(8,128)S(1)}, u32[]{:S(2)}, u32[]{:S(2)}) %collective-permute-start.21) | collective-permute-done | bytes 1048608 | tf_op jit(solution)/shard_map/ppermute | solution.py:207
  (72 shorter events, 24.3 us)
Async XLA Ops:
  6.5 90.4 %all-gather.3.cloned.1.call-start = ((), (), s32[]{:S(2)}) async-start(), calls=%async_computation.2 | async-start | bytes 4718592 | tf_op jit(solution)/shard_map/all_gather | solution.py:252
  11.2 20.7 %all-to-all-start = ((f32[16,64,128]{2,1,0:T(8,128)}), f32[16,64,128]{2,1,0:T(8,128)S(1)}, u32[]{:S(2)}, u32[]{:S(2)}) async-start(f32[16,64,128]{2,1,0:T(8,128)} %pad_maximum_fusion.1), calls=%async_computation | async-start | bytes 1048576 | tf_op jit(solution)/shard_map/all_to_all | solution.py:255
  31.9 71.9 %all-to-all-start.1 = ((f32[16,256,128]{2,1,0:T(8,128)}), f32[16,256,128]{2,1,0:T(8,128)}, u32[]{:S(2)}, u32[]{:S(2)}) async-start(f32[16,256,128]{2,1,0:T(8,128)} %bitcast.12), calls=%async_computation.1 | async-start | bytes 4194304 | tf_op jit(solution)/shard_map/all_to_all | solution.py:258
  101.8 0.7 collective-permute-start
  103.8 0.7 collective-permute-start.3
  104.6 1.4 collective-permute-start.4
  105.3 18.3 %collective-permute-start.2 = (f32[1024,128]{1,0:T(8,128)S(1)}, f32[1024,128]{1,0:T(8,128)S(1)}, u32[]{:S(2)}, u32[]{:S(2)}) collective-permute-start(f32[1024,128]{1,0:T(8,128)S(1)} %block_residual.1), channel_id=1, source_target_pairs={{16,28},{17,29},{18,30},{19,31},{20,24},{21,25},{22,26},{23,27}} | collective-permute-start | bytes 1572872 | tf_op jit(solution)/shard_map/ppermute | solution.py:207
  106.0 1.4 collective-permute-start.5
  106.7 2.0 collective-permute-start.6
  107.4 16.2 %collective-permute-start.7 = (f32[256,128]{1,0:T(8,128)S(1)}, f32[256,128]{1,0:T(8,128)S(1)}, u32[]{:S(2)}, u32[]{:S(2)}) collective-permute-start(f32[256,128]{1,0:T(8,128)S(1)} %collective-permute-done.5), channel_id=1, source_target_pairs={{32,64},{33,65},{34,66},{35,67},{36,68},{37,69},{38,70},{39,71},{4... | collective-permute-start | bytes 393224 | tf_op jit(solution)/shard_map/ppermute | solution.py:207
  128.5 0.7 collective-permute-start.8
  130.0 1.4 collective-permute-start.10
  130.7 2.0 collective-permute-start.11
  131.4 15.2 %collective-permute-start.12 = (f32[256,128]{1,0:T(8,128)S(1)}, f32[256,128]{1,0:T(8,128)S(1)}, u32[]{:S(2)}, u32[]{:S(2)}) collective-permute-start(f32[256,128]{1,0:T(8,128)S(1)} %collective-permute-done.10), channel_id=1, source_target_pairs={{32,64},{33,65},{34,66},{35,67},{36,68},{37,69},{38,70},{39,71},{4... | collective-permute-start | bytes 393224 | tf_op jit(solution)/shard_map/ppermute | solution.py:207
  146.6 5.3 %collective-permute-start.13 = (f32[2,256,128]{2,1,0:T(8,128)S(1)}, f32[2,256,128]{2,1,0:T(8,128)S(1)}, u32[]{:S(2)}, u32[]{:S(2)}) collective-permute-start(f32[2,256,128]{2,1,0:T(8,128)S(1)} %get-tuple-element.36), channel_id=1, source_target_pairs={{0,3},{1,0},{2,1},{3,2},{4,7},{5,4},{6,5},{7,6},{8,11},{9,8},{10,9... | collective-permute-start | bytes 786440 | tf_op jit(solution)/shard_map/ppermute | solution.py:207
  146.7 6.5 %collective-permute-start.14 = (f32[2,256,128]{2,1,0:T(8,128)S(1)}, f32[2,256,128]{2,1,0:T(8,128)S(1)}, u32[]{:S(2)}, u32[]{:S(2)}) collective-permute-start(f32[2,256,128]{2,1,0:T(8,128)S(1)} %get-tuple-element.36), channel_id=1, source_target_pairs={{0,1},{1,2},{2,3},{3,0},{4,5},{5,6},{6,7},{7,4},{8,9},{9,10},{10,1... | collective-permute-start | bytes 786440 | tf_op jit(solution)/shard_map/ppermute | solution.py:207
  151.9 10.1 %collective-permute-start.16 = (f32[1,256,128]{2,1,0:T(8,128)S(1)}, f32[1,256,128]{2,1,0:T(8,128)S(1)}, u32[]{:S(2)}, u32[]{:S(2)}) collective-permute-start(f32[1,256,128]{2,1,0:T(8,128)S(1)} %slice.85), channel_id=1, source_target_pairs={{0,3},{1,0},{2,1},{3,2},{4,7},{5,4},{6,5},{7,6},{8,11},{9,8},{10,9... | collective-permute-start | bytes 393224 | tf_op jit(solution)/shard_map/ppermute | solution.py:207
  153.2 8.8 %collective-permute-start.15 = (f32[1,256,128]{2,1,0:T(8,128)S(1)}, f32[1,256,128]{2,1,0:T(8,128)S(1)}, u32[]{:S(2)}, u32[]{:S(2)}) collective-permute-start(f32[1,256,128]{2,1,0:T(8,128)S(1)} %slice.84), channel_id=1, source_target_pairs={{0,1},{1,2},{2,3},{3,0},{4,5},{5,6},{6,7},{7,4},{8,9},{9,10},{10,1... | collective-permute-start | bytes 393224 | tf_op jit(solution)/shard_map/ppermute | solution.py:207
  156.5 8.8 %collective-permute-start.1 = (f32[8,256,128]{2,1,0:T(8,128)}, f32[8,256,128]{2,1,0:T(8,128)}, u32[]{:S(2)}, u32[]{:S(2)}) collective-permute-start(f32[8,256,128]{2,1,0:T(8,128)} %bitcast.17), channel_id=1, source_target_pairs={{0,16},{1,17},{2,18},{3,19},{4,20},{5,21},{6,22},{7,23},{8,24},{9,... | collective-permute-start | bytes 3145736 | tf_op jit(solution)/shard_map/ppermute | solution.py:207
  162.2 14.7 %collective-permute-start.18 = (f32[4,2,256,128]{3,2,1,0:T(8,128)S(1)}, f32[4,2,256,128]{3,2,1,0:T(8,128)S(1)}, u32[]{:S(2)}, u32[]{:S(2)}) collective-permute-start(f32[4,2,256,128]{3,2,1,0:T(8,128)S(1)} %pad_maximum_fusion.refs_0_), channel_id=1, source_target_pairs={{0,12},{1,13},{2,14},{3,15},{4,0},{5,1},{6,2},{7,3},{8,4},{9,5},{1... | collective-permute-start | bytes 3145736 | tf_op jit(solution)/shard_map/ppermute | solution.py:207
  165.2 15.3 %collective-permute-start.17 = (f32[4,2,256,128]{3,2,1,0:T(8,128)S(1)}, f32[4,2,256,128]{3,2,1,0:T(8,128)}, u32[]{:S(2)}, u32[]{:S(2)}) collective-permute-start(f32[4,2,256,128]{3,2,1,0:T(8,128)S(1)} %pad_maximum_fusion.refs_0_), channel_id=1, source_target_pairs={{0,4},{1,5},{2,6},{3,7},{4,8},{5,9},{6,10},{7,11},{8,12},{9,13},{1... | collective-permute-start | bytes 3145736 | tf_op jit(solution)/shard_map/ppermute | solution.py:207
  181.6 8.4 %collective-permute-start.20 = (f32[2,2,256,128]{3,2,1,0:T(8,128)S(1)}, f32[2,2,256,128]{3,2,1,0:T(8,128)S(1)}, u32[]{:S(2)}, u32[]{:S(2)}) collective-permute-start(f32[2,2,256,128]{3,2,1,0:T(8,128)S(1)} %slice.73), channel_id=1, source_target_pairs={{0,12},{1,13},{2,14},{3,15},{4,0},{5,1},{6,2},{7,3},{8,4},{9,5},{1... | collective-permute-start | bytes 1572872 | tf_op jit(solution)/shard_map/ppermute | solution.py:207
  181.6 9.6 %collective-permute-start.19 = (f32[2,2,256,128]{3,2,1,0:T(8,128)S(1)}, f32[2,2,256,128]{3,2,1,0:T(8,128)S(1)}, u32[]{:S(2)}, u32[]{:S(2)}) collective-permute-start(f32[2,2,256,128]{3,2,1,0:T(8,128)S(1)} %slice.72), channel_id=1, source_target_pairs={{0,4},{1,5},{2,6},{3,7},{4,8},{5,9},{6,10},{7,11},{8,12},{9,13},{1... | collective-permute-start | bytes 1572872 | tf_op jit(solution)/shard_map/ppermute | solution.py:207
  194.0 4.7 %collective-permute-start.21 = (f32[256,1024]{1,0:T(8,128)S(1)}, f32[256,1024]{1,0:T(8,128)S(1)}, u32[]{:S(2)}, u32[]{:S(2)}) collective-permute-start(f32[256,1024]{1,0:T(8,128)S(1)} %slice.87), channel_id=1, source_target_pairs={{0,16},{1,17},{2,18},{3,19},{4,20},{5,21},{6,22},{7,23},{8,24},{9,... | collective-permute-start | bytes 3145736 | tf_op jit(solution)/shard_map/ppermute | solution.py:207
  (5 other events, 19.8 us)
Sparse Core Ops, SparseCore 0:
  9.2 87.6 all-gather.2

commit v7 on v6

--- a/solution.py
+++ b/solution.py
@@ -73,49 +73,71 @@
     )(info, lead)
 
 
-def solve_body(tri_ref, rhs_ref, out_ref):
-    count = tri_ref.shape[0]
-    out_ref[...] = rhs_ref[...]
-    for k in range(count):
-        here = pl.ds(k * TILE, TILE)
-        solved = packed_product(pack_left(tri_ref[k, here, :]), pack_right(out_ref[here, :]))
-        out_ref[here, :] = solved
-        right = pack_right(solved)
-        for i in range(k + 1, count):
-            there = pl.ds(i * TILE, TILE)
-            out_ref[there, :] = out_ref[there, :] - packed_product(pack_left(tri_ref[k, there, :]), right)
-
-
-def solve(tri, rhs):
-    return pl.pallas_call(
-        solve_body,
+def solve(info, pieces, places, rhs):
+    def body(info, *refs):
+        rhs_ref, out_ref, tri_ref = refs[-3:]
+        for ref, parts in zip(refs, places):
+            for half, steps, start, to, rows in parts:
+                k = 4 * half + lax.rem(info[1] + steps, 4)
+                tri_ref[k, pl.ds(to, rows), :] = pack_left(ref[pl.ds(start, rows), :])
+        out_ref[...] = rhs_ref[...]
+        for k in range(8):
+            here = pl.ds(k * TILE, TILE)
+            solved = packed_product(tri_ref[k, here, :], pack_right(out_ref[here, :]))
+            out_ref[here, :] = solved
+            right = pack_right(solved)
+            for i in range(k + 1, 8):
+                there = pl.ds(i * TILE, TILE)
+                out_ref[there, :] = out_ref[there, :] - packed_product(tri_ref[k, there, :], right)
+
+    return pl.pallas_call(
+        body,
         out_shape=jax.ShapeDtypeStruct(rhs.shape, F32),
-        in_specs=[VM, VM],
-        out_specs=VM,
+        in_specs=[SM] + [VM] * (len(pieces) + 1),
+        out_specs=VM,
+        scratch_shapes=[pltpu.VMEM((8, 1024, 256), BF16)],
         compiler_params=PARAMS,
         name="block_solve",
-    )(tri, rhs)
-
-
-def residual_body(tri_ref, rhs_ref, x_ref, out_ref):
-    count = tri_ref.shape[0]
-    for k in range(count):
-        right = pack_right(x_ref[pl.ds(k * TILE, TILE), :])
-        for i in range(count):
-            there = pl.ds(i * TILE, TILE)
-            base = rhs_ref[there, :] if k == 0 else out_ref[there, :]
-            out_ref[there, :] = base - packed_product(pack_left(tri_ref[k, there, :]), right)
-
-
-def residual(tri, rhs, x):
-    return pl.pallas_call(
-        residual_body,
+    )(info, *pieces, rhs)
+
+
+def residual(info, pieces, places, rhs, x):
+    def body(info, *refs):
+        rhs_ref, x_ref, out_ref = refs[-3:]
+        out_ref[...] = rhs_ref[...]
+        for ref, (other, steps, row) in zip(refs, places):
+            half = 1 - info[0] if other else info[0]
+            k = 4 * half + lax.rem(info[1] + steps, 4)
+            right = pack_right(x_ref[pl.ds(pl.multiple_of(k * TILE, TILE), TILE), :])
+            for start in range(0, ref.shape[0], TILE):
+                there = pl.ds(row + start, TILE)
+                out_ref[there, :] = out_ref[there, :] - packed_product(pack_left(ref[pl.ds(start, TILE), :]), right)
+
+    return pl.pallas_call(
+        body,
         out_shape=jax.ShapeDtypeStruct(rhs.shape, F32),
-        in_specs=[VM, VM, VM],
+        in_specs=[SM] + [VM] * (len(pieces) + 2),
         out_specs=VM,
         compiler_params=PARAMS,
         name="block_residual",
-    )(tri, rhs, x)
+    )(info, *pieces, rhs, x)
+
+
+def arrange_body(factor_ref, out_ref):
+    for c in range(16):
+        for a in range(4):
+            out_ref[c, pl.ds(64 * a, 64), :] = factor_ref[a, pl.ds(64 * c, 64), :]
+
+
+def arrange(factor):
+    return pl.pallas_call(
+        arrange_body,
+        out_shape=jax.ShapeDtypeStruct((16, 256, TILE), F32),
+        in_specs=[VM],
+        out_specs=VM,
+        compiler_params=PARAMS,
+        name="arrange_rows",
+    )(factor)
 
 
 def prepare_body(info, mine_ref, other_ref, high_ref, low_ref):
@@ -207,18 +229,20 @@
     return lax.ppermute(value, AXES, pairs)
 
 
-def deal(x, core, yh, xi, core_from, yh_from):
-    top = core_from == 0
-    half_here, half_there = (x[:512], x[512:]) if top else (x[512:], x[:512])
-    got = move(half_there, lambda a, b, c, d: (0, 1 - b, c, d) if a == 0 and b == core_from else None)
-    half = jnp.where(core == core_from, half_here, got)
-    here, there = (half[:256], half[256:]) if yh_from == 0 else (half[256:], half[:256])
-    got = move(there, lambda a, b, c, d: (0, b, 3 - c, d) if a == 0 and c // 2 == yh_from else None)
-    quarter = jnp.where(yh == yh_from, here, got)
-    one = move(quarter, lambda a, b, c, d: (1 if b == 0 else 3, b, c, d) if a == 0 else None)
-    two = move(quarter, lambda a, b, c, d: (3 if b == 0 else 1, b, c, d) if a == 0 else None)
+def deal(first, second, core, yh, xi):
+    lower = yh == 0
+    here = jnp.where(lower, first[:512], second[512:])
+    there = jnp.where(lower, first[512:], second[:512])
+    got = move(there, lambda a, b, c, d: (0, 1 - b, c, d) if a == 0 and b == c // 2 else None)
+    half = jnp.where(core == yh, here, got)
+    here = jnp.where(lower, half[:256], half[256:])
+    there = jnp.where(lower, half[256:], half[:256])
+    got = move(there, lambda a, b, c, d: (0, b, 3 - c, d) if a == 0 else None)
+    both = jnp.stack([jnp.where(lower, here, got), jnp.where(lower, got, here)])
+    one = move(both, lambda a, b, c, d: (1 if b == 0 else 3, b, c, d) if a == 0 else None)
+    two = move(both, lambda a, b, c, d: (3 if b == 0 else 1, b, c, d) if a == 0 else None)
     far = move(one, lambda a, b, c, d: (2, b, c, d) if a == (1 if b == 0 else 3) else None)
-    return jnp.where(xi == 0, quarter, one + two + far)
+    return jnp.where(xi == 0, both, one + two + far)
 
 
 def ring(value, first):
@@ -237,35 +261,79 @@
     return after, far_low, far_high, before
 
 
+def gather_triangles(lead, yl):
+    def holds(a, b, c):
+        return a == 0 and b == c // 2
+
+    swapped = move(lead, lambda a, b, c, d: (a, b, c + 1 - 2 * (c % 2), d) if holds(a, b, c) else None)
+    full = jnp.where(yl == 0, lead, swapped)
+    lower = jnp.where(yl == 0, swapped[512:], lead[512:])
+    pair = jnp.concatenate([full, lower], 0)
+
+    def along(step):
+        return lambda a, b, c, d: (a, b, c, d + step) if holds(a, b, c) else None
+
+    before, after = move(pair, along(1)), move(pair, along(-1))
+    far_low, far_high = move(before[:768], along(1)), move(after[768:], along(-1))
+    pieces, places = [], []
+    for piece, steps in ((pair, 0), (after, 1), (before, 3)):
+        pieces.append(piece)
+        places.append([(0, steps, 0, 0, 1024), (1, steps, 1024, 512, 512)])
+    pieces += [far_low, far_high]
+    places += [[(0, 2, 0, 0, 768)], [(0, 2, 0, 768, 256), (1, 2, 256, 512, 512)]]
+    return pieces, places
+
+
+def gather_square(lead):
+    def holds(a, b, c):
+        return a == 0 and b == 0 and c >= 2
+
+    def along(step):
+        return lambda a, b, c, d: (a, b, c, d + step) if holds(a, b, c) else None
+
+    def pair(value):
+        return move(value, lambda a, b, c, d: (a, b, 5 - c, d) if holds(a, b, c) else None)
+
+    own = move(lead, lambda a, b, c, d: (0, 0, 3 - c, d) if (a, b) == (0, 1) and c < 2 else None)
+    before, after = move(own, along(1)), move(own, along(-1))
+    far_low, far_high = move(before[:512], along(1)), move(after[512:], along(-1))
+    pieces, places = [], []
+    for piece, steps, row in ((own, 0, 0), (after, 1, 0), (before, 3, 0), (far_low, 2, 0), (far_high, 2, 512)):
+        pieces += [piece, pair(piece)]
+        places += [(False, steps, row), (True, steps, row)]
+    return pieces, places
+
+
 def shards(factor, cross_cov):
     xi, core = lax.axis_index("x"), lax.axis_index("core")
     yh, yl, z = lax.axis_index("yh"), lax.axis_index("yl"), lax.axis_index("z")
     row_id = 2 * xi + core
     col_id = 8 * yh + 4 * yl + z
-    slice_id = 4 * yl + z
     local = factor[:, 0]
     rhs = cross_cov[:, 0]
 
     diagonal = ((row_id == 0) & (yh == 0)) | ((row_id == 1) & (yh == 1))
-    info = jnp.stack([diagonal.astype(jnp.int32), slice_id.astype(jnp.int32)])
+    info = jnp.stack([diagonal.astype(jnp.int32), (4 * yl + z).astype(jnp.int32)])
     lead = invert_diagonal(info, local[0])
-    tri = lax.all_gather(lead, ("yl", "z"), axis=0, tiled=False)
-
-    own_rhs = rhs[0].reshape(64, 8, TILE).transpose(1, 0, 2)
-    columns = lax.all_to_all(jnp.concatenate([own_rhs, own_rhs], 0), COL, 0, 0, tiled=True).reshape(1024, TILE)
-    by_rows = local.reshape(4, 16, 64, TILE).transpose(1, 0, 2, 3).reshape(16, 256, TILE)
-    by_rows, columns = lax.optimization_barrier((by_rows, columns))
+
+    own_rhs = rhs[0].reshape(64, 2, 4, TILE).transpose(1, 2, 0, 3)
+    own_rhs = jnp.stack([own_rhs, own_rhs[::-1]]).reshape(16, 64, TILE)
+    columns = lax.all_to_all(own_rhs, COL, 0, 0, tiled=True).reshape(1024, TILE)
+
+    place = jnp.stack([1 - yl, z]).astype(jnp.int32)
+    triangle = gather_triangles(lead, yl)
+    square = gather_square(lead)
+    first = solve(place, *triangle, columns)
+    sent = move(first, lambda a, b, c, d: (0, 0, 3 - c, d) if (a, b) == (0, 0) and c < 2 else None)
+    columns = move(columns, lambda a, b, c, d: (0, 0, c, d) if (a, b) == (0, 1) and c >= 2 else None)
+    rest = residual(place, *square, columns, sent)
+    second_rhs = move(rest, lambda a, b, c, d: (0, 1, c, d) if (a, b) == (0, 0) and c >= 2 else None)
+
+    by_rows, sent = lax.optimization_barrier((arrange(local), sent))
     left = lax.all_to_all(by_rows, COL, 0, 0, tiled=True)
-
-    first = solve(tri, columns)
-    sent = move(first, lambda a, b, c, d: (0, 1, c, d) if a == 0 and b == 0 and c < 2 else None)
-    rest = residual(tri, columns, sent)
-    second_rhs = move(rest, lambda a, b, c, d: (0, 1, 3 - c, d) if (a, b) == (0, 1) and c < 2 else None)
-    first, left, rest = lax.optimization_barrier((first, left, rest))
-    dealt0 = deal(first, core, yh, xi, 0, 0)
-    second_rhs, dealt0 = lax.optimization_barrier((second_rhs, dealt0))
-    second = solve(tri, second_rhs)
-    dealt1 = deal(second, core, yh, xi, 1, 1)
+    second = solve(place, *triangle, second_rhs)
+    mine = deal(first, second, core, yh, xi)
+    mine, left = lax.optimization_barrier((mine, left))
 
     def swap(value):
         return move(value, lambda a, b, c, d: (a, 1 - b, c, d))
@@ -275,7 +343,6 @@
     given = jnp.where(core == 0, left[:, 1], left[:, 0]).reshape(8, 256, TILE)
     info2 = jnp.stack([xi, core, 2 * yh + yl, z, col_id]).astype(jnp.int32)
 
-    mine = jnp.stack([dealt0, dealt1])
     after, far_low, far_high, before = ring(mine, True)
     near = jnp.stack([mine, after, jnp.concatenate([far_low, far_high], 0), before])
 

time: 207 us -> 198 us (0.957)
  waiting for transfers between devices: 120 us -> 101 us
  starting transfers between devices: 38.6 us -> 54.8 us
  between operations: 13.8 us -> 0.57 us
  Pallas kernels: 19.9 us -> 24.4 us
    all_gather x1 -> x0, waiting for transfers between devices: 59.5 us -> none  [shards(): tri = lax.all_gather(lead, ('yl', 'z'), axis=0, tiled=False)]
    ppermute x22 -> x33, waiting for transfers between devices: 48.8 us -> 93.7 us  [move(): return lax.ppermute(value, AXES, pairs)]
    ppermute x22 -> x33, starting transfers between devices: 25.2 us -> 43.4 us  [move(): return lax.ppermute(value, AXES, pairs)]
    pallas_call x3 -> x4, Pallas kernels: 6.66 us -> 12.1 us  [the longest x2 7.68 us: solve(): pl.pallas_call(body, out_shape=jax.ShapeDtypeStruct(rhs.shape, F32), in_s...]
    all_to_all x1, waiting for transfers between devices: 11.3 us -> 7.33 us  [shards(): columns = lax.all_to_all(own_rhs, COL, 0, 0, tiled=True).reshape(1024, TILE)]
    unnamed x10 -> x16, local copies, waits for them, and re-layouts: 5.54 us -> 1.76 us
    slice x4 -> x6, local copies, waits for them, and re-layouts: 0.06 us -> 3.56 us  [the longest x1 0.97 us: gather_square(): after[512:]]
  transfers between devices with their start and end apart: 25 -> 35, of which waited for: 10 -> 7; matrix products, arithmetic and copies ran while one was open for 3% -> 6% of each run, Pallas kernels for 6% -> 7%
where the time goes in v7:
time: 198 us; the launch traced here: 196 us
  waiting for transfers between devices  101 us (51%)
  starting transfers between devices  54.8 us (28%)
  Pallas kernels  24.4 us (12%)
  local copies, waits for them, and re-layouts  8.77 us (4%)
  other arithmetic  6.56 us (3%)
    ppermute x33, waiting for transfers between devices, move(): return lax.ppermute(value, AXES, pairs)  93.7 us
    ppermute x33, starting transfers between devices, move(): return lax.ppermute(value, AXES, pairs)  43.4 us
    pallas_call x3, Pallas kernels, accumulate(): pl.pallas_call(body, out_shape=jax.ShapeDtypeStruct((512, 1024), F32), in...  10.2 us
    all_to_all x1, starting transfers between devices, shards(): columns = lax.all_to_all(own_rhs, COL, 0, 0, tiled=True).reshape(1024, TILE)  7.77 us
    pallas_call x2, Pallas kernels, solve(): pl.pallas_call(body, out_shape=jax.ShapeDtypeStruct(rhs.shape, F32), in_s...  7.68 us
    all_to_all x1, waiting for transfers between devices, shards(): columns = lax.all_to_all(own_rhs, COL, 0, 0, tiled=True).reshape(1024, TILE)  7.33 us
  transfers between devices with their start and end apart: 35, of which 7 were waited for; matrix products, arithmetic and copies ran while one was open for 6% of the time, Pallas kernels for 7%

profile of v7, /device:TPU:5, one launch (start us, length us, event | category | flops | bytes accessed | tf_op | source)
XLA Modules:
  0.0 196.2 jit_solution(18406107942408632208)
XLA Ops:
  6.8 7.8 %all-to-all-start = ((f32[16,64,128]{2,1,0:T(8,128)}), f32[16,64,128]{2,1,0:T(8,128)S(1)}, u32[]{:S(2)}, u32[]{:S(2)}) async-start(f32[16,64,128]{2,1,0:T(8,128)} %bitcast.58), calls=%async_computation | async-start | bytes 1048576 | tf_op jit(solution)/shard_map/all_to_all | solution.py:321
  14.6 1.5 collective-permute-start.9
  16.1 1.5 collective-permute-start.7
  17.5 7.3 %all-to-all-done = f32[16,64,128]{2,1,0:T(8,128)S(1)} async-done(((f32[16,64,128]{2,1,0:T(8,128)}), f32[16,64,128]{2,1,0:T(8,128)S(1)}, u32[]{:S(2)}, u32[]{:S(2)}) %all-to-all-start) | async-done | bytes 524320 | tf_op jit(solution)/shard_map/all_to_all | solution.py:321
  26.3 1.5 collective-permute-start.6
  37.3 3.8 %block_solve.2 = f32[1024,128]{1,0:T(8,128)S(1)} custom-call(s32[2]{0:T(128)S(1)} %pad_add_fusion.info, f32[1536,128]{1,0:T(8,128)S(1)} %pad_maximum_fusion.1.refs_0_, f32[1536,128]{1,0:T(8,128)S(1)} %collective-permute-done.1.refs_1_, f32[1536,128]{1,0:T(8,128)S(1)} %collective-permute-done.2.refs_2_, f32[768,128]{1,0:T(8,128)S(1)} %copy-done.2, ...), custom_call_target="tpu_custom_call" | custom-call | tf_op jit(solution)/shard_map/block_solve/pallas_call | solution.py:93
  44.2 3.0 %block_residual.1 = f32[1024,128]{1,0:T(8,128)S(1)} custom-call(s32[2]{0:T(128)S(1)} %pad_add_fusion.info, f32[1024,128]{1,0:T(8,128)} %collective-permute-done.5.refs_0_, f32[1024,128]{1,0:T(8,128)} %collective-permute-done.6.refs_1_, f32[1024,128]{1,0:T(8,128)} %collective-permute-done.7.refs_2_, f32[1024,128]{1,0:T(8,128)S(1)} %collective-permute-done.8.refs_3_, ...), custom_call_target="tpu_custom_call" | custom-call | tf_op jit(solution)/shard_map/block_residual/pallas_call | solution.py:116
  48.0 3.8 %block_solve.3 = f32[1024,128]{1,0:T(8,128)S(1)} custom-call(s32[2]{0:T(128)S(1)} %pad_add_fusion.info, f32[1536,128]{1,0:T(8,128)S(1)} %pad_maximum_fusion.1.refs_0_, f32[1536,128]{1,0:T(8,128)S(1)} %collective-permute-done.1.refs_1_, f32[1536,128]{1,0:T(8,128)S(1)} %collective-permute-done.2.refs_2_, f32[768,128]{1,0:T(8,128)S(1)} %copy-done.3, ...), custom_call_target="tpu_custom_call" | custom-call | tf_op jit(solution)/shard_map/block_solve/pallas_call | solution.py:93
  54.8 3.7 %all-to-all-start.1 = ((f32[16,256,128]{2,1,0:T(8,128)}), f32[16,256,128]{2,1,0:T(8,128)S(1)}, u32[]{:S(2)}, u32[]{:S(2)}) async-start(f32[16,256,128]{2,1,0:T(8,128)} %arrange_rows.1), calls=%async_computation.1 | async-start | bytes 4194304 | tf_op jit(solution)/shard_map/all_to_all | solution.py:333
  63.0 78.0 %collective-permute-done.22 = f32[2,256,128]{2,1,0:T(8,128)S(1)} collective-permute-done((f32[2,256,128]{2,1,0:T(8,128)S(1)}, f32[2,256,128]{2,1,0:T(8,128)S(1)}, u32[]{:S(2)}, u32[]{:S(2)}) %collective-permute-start.22) | collective-permute-done | bytes 262176 | tf_op jit(solution)/shard_map/ppermute | solution.py:229
  141.1 3.5 %collective-permute-start.24 = (f32[2,256,128]{2,1,0:T(8,128)S(1)}, f32[2,256,128]{2,1,0:T(8,128)S(1)}, u32[]{:S(2)}, u32[]{:S(2)}) collective-permute-start(f32[2,256,128]{2,1,0:T(8,128)S(1)} %add_select_fusion), channel_id=1, source_target_pairs={{0,3},{1,0},{2,1},{3,2},{4,7},{5,4},{6,5},{7,6},{8,11},{9,8},{10,9... | collective-permute-start | bytes 786440 | tf_op jit(solution)/shard_map/ppermute | solution.py:229
  144.6 2.1 %collective-permute-start.25 = (f32[2,256,128]{2,1,0:T(8,128)S(1)}, f32[2,256,128]{2,1,0:T(8,128)S(1)}, u32[]{:S(2)}, u32[]{:S(2)}) collective-permute-start(f32[2,256,128]{2,1,0:T(8,128)S(1)} %add_select_fusion), channel_id=1, source_target_pairs={{0,1},{1,2},{2,3},{3,0},{4,5},{5,6},{6,7},{7,4},{8,9},{9,10},{10,1... | collective-permute-start | bytes 786440 | tf_op jit(solution)/shard_map/ppermute | solution.py:229
  146.7 3.7 %collective-permute-done.24 = f32[2,256,128]{2,1,0:T(8,128)S(1)} collective-permute-done((f32[2,256,128]{2,1,0:T(8,128)S(1)}, f32[2,256,128]{2,1,0:T(8,128)S(1)}, u32[]{:S(2)}, u32[]{:S(2)}) %collective-permute-start.24) | collective-permute-done | bytes 262176 | tf_op jit(solution)/shard_map/ppermute | solution.py:229
  152.3 2.7 %fusion.1 = (f32[2,1,4,256,128]{4,3,2,0,1:T(8,128)}, f32[2,1,4,256,128]{4,3,2,0,1:T(8,128)S(1)}) fusion(f32[2,2,4,256,128]{4,3,2,1,0:T(8,128)} %bitcast.55, pred[]{:T(512)S(6)} %eq.29), kind=kLoop, calls=%fused_computation.6 | loop fusion | flops 524288 | bytes 4194305 | tf_op jit(solution)/shard_map/jit(_where)/select_n | solution.py:343
  155.0 2.4 %collective-permute-start.23 = (f32[8,256,128]{2,1,0:T(8,128)}, f32[8,256,128]{2,1,0:T(8,128)}, u32[]{:S(2)}, u32[]{:S(2)}) collective-permute-start(f32[8,256,128]{2,1,0:T(8,128)} %bitcast.20), channel_id=1, source_target_pairs={{0,16},{1,17},{2,18},{3,19},{4,20},{5,21},{6,22},{7,23},{8,24},{9,... | collective-permute-start | bytes 3145736 | tf_op jit(solution)/shard_map/ppermute | solution.py:229
  158.9 3.0 %collective-permute-start.29 = (f32[4,2,256,128]{3,2,1,0:T(8,128)S(1)}, f32[4,2,256,128]{3,2,1,0:T(8,128)}, u32[]{:S(2)}, u32[]{:S(2)}) collective-permute-start(f32[4,2,256,128]{3,2,1,0:T(8,128)S(1)} %pad_maximum_fusion.refs_0_), channel_id=1, source_target_pairs={{0,12},{1,13},{2,14},{3,15},{4,0},{5,1},{6,2},{7,3},{8,4},{9,5},{1... | collective-permute-start | bytes 3145736 | tf_op jit(solution)/shard_map/ppermute | solution.py:229
  161.9 1.6 prepare_update.1
  163.5 2.5 %update_near.1.refs_0_ = f32[512,1024]{1,0:T(8,128)S(1)} custom-call(s32[5]{0:T(128)S(1)} %stack.75.info, bf16[4,512,256]{2,1,0:T(8,128)(2,1)S(1)} %get-tuple-element.18.high_ref, bf16[4,512,256]{2,1,0:T(8,128)(2,1)S(1)} %get-tuple-element.19.low_ref, f32[4,2,256,128]{3,2,1,0:T(8,128)S(1)} %pad_maximum_fusion.refs_0_), custom_call_target="tpu_custom_call" | custom-call | tf_op jit(solution)/shard_map/update_near/pallas_call | solution.py:205
  166.0 8.3 %collective-permute-done.28.refs_2_ = f32[4,2,256,128]{3,2,1,0:T(8,128)S(1)} collective-permute-done((f32[4,2,256,128]{3,2,1,0:T(8,128)S(1)}, f32[4,2,256,128]{3,2,1,0:T(8,128)S(1)}, u32[]{:S(2)}, u32[]{:S(2)}) %collective-permute-start.28) | collective-permute-done | bytes 1048608 | tf_op jit(solution)/shard_map/ppermute | solution.py:229
  176.4 1.9 collective-permute-start.31
  178.3 5.1 %update_next.1.refs_0_ = f32[512,1024]{1,0:T(8,128)S(1)} custom-call(s32[5]{0:T(128)S(1)} %stack.75.info, bf16[4,512,256]{2,1,0:T(8,128)(2,1)S(1)} %get-tuple-element.18.high_ref, bf16[4,512,256]{2,1,0:T(8,128)(2,1)S(1)} %get-tuple-element.19.low_ref, f32[512,1024]{1,0:T(8,128)S(1)} %update_near.1.refs_0_, ...), custom_call_target="tpu_custom_call", output_to_operand_aliasing={{}: (3, {})} | custom-call | tf_op jit(solution)/shard_map/update_next/pallas_call | solution.py:205
  184.8 2.6 %update_far.1 = f32[512,1024]{1,0:T(8,128)S(1)} custom-call(s32[5]{0:T(128)S(1)} %stack.75.info, bf16[4,512,256]{2,1,0:T(8,128)(2,1)S(1)} %get-tuple-element.18.high_ref, bf16[4,512,256]{2,1,0:T(8,128)(2,1)S(1)} %get-tuple-element.19.low_ref, f32[512,1024]{1,0:T(8,128)S(1)} %update_next.1.refs_0_, ...), custom_call_target="tpu_custom_call", output_to_operand_aliasing={{}: (3, {})} | custom-call | tf_op jit(solution)/shard_map/update_far/pallas_call | solution.py:205
  187.5 5.2 %collective-permute-start.32 = (f32[256,1024]{1,0:T(8,128)S(1)}, f32[256,1024]{1,0:T(8,128)S(1)}, u32[]{:S(2)}, u32[]{:S(2)}) collective-permute-start(f32[256,1024]{1,0:T(8,128)S(1)} %slice.111), channel_id=1, source_target_pairs={{0,16},{1,17},{2,18},{3,19},{4,20},{5,21},{6,22},{7,23},{8,24},{9,... | collective-permute-start | bytes 3145736 | tf_op jit(solution)/shard_map/ppermute | solution.py:229
  192.8 2.3 %collective-permute-done.32 = f32[256,1024]{1,0:T(8,128)S(1)} collective-permute-done((f32[256,1024]{1,0:T(8,128)S(1)}, f32[256,1024]{1,0:T(8,128)S(1)}, u32[]{:S(2)}, u32[]{:S(2)}) %collective-permute-start.32) | collective-permute-done | bytes 1048608 | tf_op jit(solution)/shard_map/ppermute | solution.py:229
  (104 shorter events, 37.0 us)
Async XLA Ops:
  2.4 12.1 %collective-permute-start.5 = (f32[1024,128]{1,0:T(8,128)S(1)}, f32[1024,128]{1,0:T(8,128)}, u32[]{:S(2)}, u32[]{:S(2)}) collective-permute-start(f32[1024,128]{1,0:T(8,128)S(1)} %invert_diagonal.1), channel_id=1, source_target_pairs={{16,12},{17,13},{18,14},{19,15},{20,8},{21,9},{22,10},{23,11}} | collective-permute-start | bytes 1572872 | tf_op jit(solution)/shard_map/ppermute | solution.py:229
  4.1 22.3 %collective-permute-start.2 = (f32[1536,128]{1,0:T(8,128)S(1)}, f32[1536,128]{1,0:T(8,128)S(1)}, u32[]{:S(2)}, u32[]{:S(2)}) collective-permute-start(f32[1536,128]{1,0:T(8,128)S(1)} %pad_maximum_fusion.1.refs_0_), channel_id=1, source_target_pairs={{0,1},{1,2},{2,3},{3,0},{4,5},{5,6},{6,7},{7,4},{24,25},{25,26},{2... | collective-permute-start | bytes 2359304 | tf_op jit(solution)/shard_map/ppermute | solution.py:229
  5.0 23.6 %collective-permute-start.1 = (f32[1536,128]{1,0:T(8,128)S(1)}, f32[1536,128]{1,0:T(8,128)S(1)}, u32[]{:S(2)}, u32[]{:S(2)}) collective-permute-start(f32[1536,128]{1,0:T(8,128)S(1)} %pad_maximum_fusion.1.refs_0_), channel_id=1, source_target_pairs={{0,3},{1,0},{2,1},{3,2},{4,7},{5,4},{6,5},{7,6},{24,27},{25,24},{2... | collective-permute-start | bytes 2359304 | tf_op jit(solution)/shard_map/ppermute | solution.py:229
  6.8 18.1 %all-to-all-start = ((f32[16,64,128]{2,1,0:T(8,128)}), f32[16,64,128]{2,1,0:T(8,128)S(1)}, u32[]{:S(2)}, u32[]{:S(2)}) async-start(f32[16,64,128]{2,1,0:T(8,128)} %bitcast.58), calls=%async_computation | async-start | bytes 1048576 | tf_op jit(solution)/shard_map/all_to_all | solution.py:321
  14.6 15.5 %collective-permute-start.9 = (f32[1024,128]{1,0:T(8,128)}, f32[1024,128]{1,0:T(8,128)}, u32[]{:S(2)}, u32[]{:S(2)}) collective-permute-start(f32[1024,128]{1,0:T(8,128)} %collective-permute-done.5.refs_0_), channel_id=1, source_target_pairs={{8,9},{9,10},{10,11},{11,8},{12,13},{13,14},{14,15},{15,12}} | collective-permute-start | bytes 1572872 | tf_op jit(solution)/shard_map/ppermute | solution.py:229
  16.1 16.5 %collective-permute-start.7 = (f32[1024,128]{1,0:T(8,128)}, f32[1024,128]{1,0:T(8,128)}, u32[]{:S(2)}, u32[]{:S(2)}) collective-permute-start(f32[1024,128]{1,0:T(8,128)} %collective-permute-done.5.refs_0_), channel_id=1, source_target_pairs={{8,11},{9,8},{10,9},{11,10},{12,15},{13,12},{14,13},{15,14}} | collective-permute-start | bytes 1572872 | tf_op jit(solution)/shard_map/ppermute | solution.py:229
  24.9 16.3 %collective-permute-start.15 = (f32[1024,128]{1,0:T(8,128)S(1)}, f32[1024,128]{1,0:T(8,128)}, u32[]{:S(2)}, u32[]{:S(2)}) collective-permute-start(f32[1024,128]{1,0:T(8,128)S(1)} %bitcast.53), channel_id=1, source_target_pairs={{24,8},{25,9},{26,10},{27,11},{28,12},{29,13},{30,14},{31,15}} | collective-permute-start | bytes 1572872 | tf_op jit(solution)/shard_map/ppermute | solution.py:229
  26.3 15.7 %collective-permute-start.6 = (f32[1024,128]{1,0:T(8,128)}, f32[1024,128]{1,0:T(8,128)}, u32[]{:S(2)}, u32[]{:S(2)}) collective-permute-start(f32[1024,128]{1,0:T(8,128)} %collective-permute-done.5.refs_0_), channel_id=1, source_target_pairs={{8,12},{9,13},{10,14},{11,15},{12,8},{13,9},{14,10},{15,11}} | collective-permute-start | bytes 1572872 | tf_op jit(solution)/shard_map/ppermute | solution.py:229
  32.5 10.2 %collective-permute-start.11 = (f32[512,128]{1,0:T(8,128)S(1)}, f32[512,128]{1,0:T(8,128)S(1)}, u32[]{:S(2)}, u32[]{:S(2)}) collective-permute-start(f32[512,128]{1,0:T(8,128)S(1)} %slice.99), channel_id=1, source_target_pairs={{8,9},{9,10},{10,11},{11,8},{12,13},{13,14},{14,15},{15,12}} | collective-permute-start | bytes 786440 | tf_op jit(solution)/shard_map/ppermute | solution.py:229
  34.9 9.2 %collective-permute-start.8 = (f32[1024,128]{1,0:T(8,128)}, f32[1024,128]{1,0:T(8,128)S(1)}, u32[]{:S(2)}, u32[]{:S(2)}) collective-permute-start(f32[1024,128]{1,0:T(8,128)} %collective-permute-done.7.refs_2_), channel_id=1, source_target_pairs={{8,12},{9,13},{10,14},{11,15},{12,8},{13,9},{14,10},{15,11}} | collective-permute-start | bytes 1572872 | tf_op jit(solution)/shard_map/ppermute | solution.py:229
  35.6 8.5 %collective-permute-start.10 = (f32[1024,128]{1,0:T(8,128)}, f32[1024,128]{1,0:T(8,128)S(1)}, u32[]{:S(2)}, u32[]{:S(2)}) collective-permute-start(f32[1024,128]{1,0:T(8,128)} %collective-permute-done.9.refs_4_), channel_id=1, source_target_pairs={{8,12},{9,13},{10,14},{11,15},{12,8},{13,9},{14,10},{15,11}} | collective-permute-start | bytes 1572872 | tf_op jit(solution)/shard_map/ppermute | solution.py:229
  51.9 6.6 %collective-permute-start.18 = (f32[512,128]{1,0:T(8,128)S(1)}, f32[512,128]{1,0:T(8,128)}, u32[]{:S(2)}, u32[]{:S(2)}) collective-permute-start(f32[512,128]{1,0:T(8,128)S(1)} %slice_select_fusion), channel_id=1, source_target_pairs={{0,16},{1,17},{2,18},{3,19},{4,20},{5,21},{6,22},{7,23},{24,8},{25... | collective-permute-start | bytes 786440 | tf_op jit(solution)/shard_map/ppermute | solution.py:229
  54.8 86.3 %all-to-all-start.1 = ((f32[16,256,128]{2,1,0:T(8,128)}), f32[16,256,128]{2,1,0:T(8,128)S(1)}, u32[]{:S(2)}, u32[]{:S(2)}) async-start(f32[16,256,128]{2,1,0:T(8,128)} %arrange_rows.1), calls=%async_computation.1 | async-start | bytes 4194304 | tf_op jit(solution)/shard_map/all_to_all | solution.py:333
  61.7 79.3 %collective-permute-start.22 = (f32[2,256,128]{2,1,0:T(8,128)S(1)}, f32[2,256,128]{2,1,0:T(8,128)S(1)}, u32[]{:S(2)}, u32[]{:S(2)}) collective-permute-start(f32[2,256,128]{2,1,0:T(8,128)S(1)} %collective-permute-done.20), channel_id=1, source_target_pairs={{32,64},{33,65},{34,66},{35,67},{36,68},{37,69},{38,70},{39,71},{4... | collective-permute-start | bytes 786440 | tf_op jit(solution)/shard_map/ppermute | solution.py:229
  141.1 9.3 %collective-permute-start.24 = (f32[2,256,128]{2,1,0:T(8,128)S(1)}, f32[2,256,128]{2,1,0:T(8,128)S(1)}, u32[]{:S(2)}, u32[]{:S(2)}) collective-permute-start(f32[2,256,128]{2,1,0:T(8,128)S(1)} %add_select_fusion), channel_id=1, source_target_pairs={{0,3},{1,0},{2,1},{3,2},{4,7},{5,4},{6,5},{7,6},{8,11},{9,8},{10,9... | collective-permute-start | bytes 786440 | tf_op jit(solution)/shard_map/ppermute | solution.py:229
  144.6 6.5 %collective-permute-start.25 = (f32[2,256,128]{2,1,0:T(8,128)S(1)}, f32[2,256,128]{2,1,0:T(8,128)S(1)}, u32[]{:S(2)}, u32[]{:S(2)}) collective-permute-start(f32[2,256,128]{2,1,0:T(8,128)S(1)} %add_select_fusion), channel_id=1, source_target_pairs={{0,1},{1,2},{2,3},{3,0},{4,5},{5,6},{6,7},{7,4},{8,9},{9,10},{10,1... | collective-permute-start | bytes 786440 | tf_op jit(solution)/shard_map/ppermute | solution.py:229
  150.4 7.1 %collective-permute-start.27 = (f32[1,256,128]{2,1,0:T(8,128)S(1)}, f32[1,256,128]{2,1,0:T(8,128)S(1)}, u32[]{:S(2)}, u32[]{:S(2)}) collective-permute-start(f32[1,256,128]{2,1,0:T(8,128)S(1)} %slice.109), channel_id=1, source_target_pairs={{0,3},{1,0},{2,1},{3,2},{4,7},{5,4},{6,5},{7,6},{8,11},{9,8},{10,9... | collective-permute-start | bytes 393224 | tf_op jit(solution)/shard_map/ppermute | solution.py:229
  151.1 6.4 %collective-permute-start.26 = (f32[1,256,128]{2,1,0:T(8,128)S(1)}, f32[1,256,128]{2,1,0:T(8,128)S(1)}, u32[]{:S(2)}, u32[]{:S(2)}) collective-permute-start(f32[1,256,128]{2,1,0:T(8,128)S(1)} %slice.108), channel_id=1, source_target_pairs={{0,1},{1,2},{2,3},{3,0},{4,5},{5,6},{6,7},{7,4},{8,9},{9,10},{10,1... | collective-permute-start | bytes 393224 | tf_op jit(solution)/shard_map/ppermute | solution.py:229
  155.0 6.9 %collective-permute-start.23 = (f32[8,256,128]{2,1,0:T(8,128)}, f32[8,256,128]{2,1,0:T(8,128)}, u32[]{:S(2)}, u32[]{:S(2)}) collective-permute-start(f32[8,256,128]{2,1,0:T(8,128)} %bitcast.20), channel_id=1, source_target_pairs={{0,16},{1,17},{2,18},{3,19},{4,20},{5,21},{6,22},{7,23},{8,24},{9,... | collective-permute-start | bytes 3145736 | tf_op jit(solution)/shard_map/ppermute | solution.py:229
  158.6 15.7 %collective-permute-start.28 = (f32[4,2,256,128]{3,2,1,0:T(8,128)S(1)}, f32[4,2,256,128]{3,2,1,0:T(8,128)S(1)}, u32[]{:S(2)}, u32[]{:S(2)}) collective-permute-start(f32[4,2,256,128]{3,2,1,0:T(8,128)S(1)} %pad_maximum_fusion.refs_0_), channel_id=1, source_target_pairs={{0,4},{1,5},{2,6},{3,7},{4,8},{5,9},{6,10},{7,11},{8,12},{9,13},{1... | collective-permute-start | bytes 3145736 | tf_op jit(solution)/shard_map/ppermute | solution.py:229
  158.9 15.4 %collective-permute-start.29 = (f32[4,2,256,128]{3,2,1,0:T(8,128)S(1)}, f32[4,2,256,128]{3,2,1,0:T(8,128)}, u32[]{:S(2)}, u32[]{:S(2)}) collective-permute-start(f32[4,2,256,128]{3,2,1,0:T(8,128)S(1)} %pad_maximum_fusion.refs_0_), channel_id=1, source_target_pairs={{0,12},{1,13},{2,14},{3,15},{4,0},{5,1},{6,2},{7,3},{8,4},{9,5},{1... | collective-permute-start | bytes 3145736 | tf_op jit(solution)/shard_map/ppermute | solution.py:229
  174.3 9.7 %collective-permute-start.30 = (f32[2,2,256,128]{3,2,1,0:T(8,128)S(1)}, f32[2,2,256,128]{3,2,1,0:T(8,128)S(1)}, u32[]{:S(2)}, u32[]{:S(2)}) collective-permute-start(f32[2,2,256,128]{3,2,1,0:T(8,128)S(1)} %slice.90), channel_id=1, source_target_pairs={{0,4},{1,5},{2,6},{3,7},{4,8},{5,9},{6,10},{7,11},{8,12},{9,13},{1... | collective-permute-start | bytes 1572872 | tf_op jit(solution)/shard_map/ppermute | solution.py:229
  176.4 8.4 %collective-permute-start.31 = (f32[2,2,256,128]{3,2,1,0:T(8,128)S(1)}, f32[2,2,256,128]{3,2,1,0:T(8,128)S(1)}, u32[]{:S(2)}, u32[]{:S(2)}) collective-permute-start(f32[2,2,256,128]{3,2,1,0:T(8,128)S(1)} %slice.91), channel_id=1, source_target_pairs={{0,12},{1,13},{2,14},{3,15},{4,0},{5,1},{6,2},{7,3},{8,4},{9,5},{1... | collective-permute-start | bytes 1572872 | tf_op jit(solution)/shard_map/ppermute | solution.py:229
  187.5 7.5 %collective-permute-start.32 = (f32[256,1024]{1,0:T(8,128)S(1)}, f32[256,1024]{1,0:T(8,128)S(1)}, u32[]{:S(2)}, u32[]{:S(2)}) collective-permute-start(f32[256,1024]{1,0:T(8,128)S(1)} %slice.111), channel_id=1, source_target_pairs={{0,16},{1,17},{2,18},{3,19},{4,20},{5,21},{6,22},{7,23},{8,24},{9,... | collective-permute-start | bytes 3145736 | tf_op jit(solution)/shard_map/ppermute | solution.py:229
  (20 other events, 68.0 us)

commit v8 on v7

--- a/solution.py
+++ b/solution.py
@@ -41,7 +41,8 @@
     return out[:, :TILE] + out[:, TILE:]
 
 
-def invert_body(info, lead_ref, out_ref):
+def invert_body(info, factor_ref, out_ref):
+    lead_ref = factor_ref.at[0]
     out_ref[...] = lead_ref[...]
 
     @pl.when(info[0] == 1)
@@ -62,15 +63,16 @@
         out_ref[pl.ds(start, TILE), :] = inverse
 
 
-def invert_diagonal(info, lead):
+def invert_diagonal(info, factor):
     return pl.pallas_call(
         invert_body,
-        out_shape=jax.ShapeDtypeStruct(lead.shape, F32),
-        in_specs=[SM, VM],
-        out_specs=VM,
+        grid=(1,),
+        out_shape=jax.ShapeDtypeStruct(factor.shape[1:], F32),
+        in_specs=[SM, pl.BlockSpec((1, 1024, TILE), lambda i: (0, 0, 0))],
+        out_specs=pl.BlockSpec((1024, TILE), lambda i: (0, 0)),
         compiler_params=PARAMS,
         name="invert_diagonal",
-    )(info, lead)
+    )(info, factor)
 
 
 def solve(info, pieces, places, rhs):
@@ -123,26 +125,47 @@
     )(info, *pieces, rhs, x)
 
 
-def arrange_body(factor_ref, out_ref):
+def arrange_body(factor_ref, first_ref, second_ref):
     for c in range(16):
-        for a in range(4):
-            out_ref[c, pl.ds(64 * a, 64), :] = factor_ref[a, pl.ds(64 * c, 64), :]
+        for a in range(2):
+            rows = pl.ds(64 * a, 64)
+            first_ref[c, rows, :] = factor_ref[a, pl.ds(64 * c, 64), :]
+            second_ref[c, rows, :] = factor_ref[2 + a, pl.ds(64 * c, 64), :]
 
 
 def arrange(factor):
     return pl.pallas_call(
         arrange_body,
-        out_shape=jax.ShapeDtypeStruct((16, 256, TILE), F32),
+        out_shape=[jax.ShapeDtypeStruct((16, 128, TILE), F32)] * 2,
         in_specs=[VM],
-        out_specs=VM,
+        out_specs=[VM, VM],
         compiler_params=PARAMS,
         name="arrange_rows",
     )(factor)
 
 
-def prepare_body(info, mine_ref, other_ref, high_ref, low_ref):
-    for side, ref in enumerate((mine_ref, other_ref)):
-        rows = pl.ds(256 * side, 256)
+def arrange_rhs_body(rhs_ref, out_ref):
+    for n in range(8):
+        out_ref[n, :, :] = rhs_ref[0, :, pl.ds(n * TILE, TILE)]
+        out_ref[8 + n, :, :] = rhs_ref[0, :, pl.ds((n + 4) % 8 * TILE, TILE)]
+
+
+def arrange_rhs(rhs):
+    return pl.pallas_call(
+        arrange_rhs_body,
+        grid=(1,),
+        out_shape=jax.ShapeDtypeStruct((16, 64, TILE), F32),
+        in_specs=[pl.BlockSpec((1, 64, 1024), lambda i: (0, 0, 0))],
+        out_specs=pl.BlockSpec((16, 64, TILE), lambda i: (0, 0, 0)),
+        compiler_params=PARAMS,
+        name="arrange_rhs",
+    )(rhs)
+
+
+def prepare_body(info, *refs):
+    high_ref, low_ref = refs[-2:]
+    for place, ref in enumerate(refs[:4]):
+        rows = pl.ds(128 * place, 128)
         for n in range(4):
             high, low = split(jnp.concatenate([ref[2 * n], ref[2 * n + 1]], 1))
             high_ref[n, rows, :] = high
@@ -156,15 +179,15 @@
                 low_ref[n, pl.ds(256 * side, 64), :] = jnp.zeros((64, 256), BF16)
 
 
-def prepare(info, mine, other):
+def prepare(info, *parts):
     return pl.pallas_call(
         prepare_body,
         out_shape=[jax.ShapeDtypeStruct((4, 512, 256), BF16)] * 2,
-        in_specs=[SM, VM, VM],
+        in_specs=[SM, VM, VM, VM, VM],
         out_specs=[VM, VM],
         compiler_params=PARAMS,
         name="prepare_update",
-    )(info, mine, other)
+    )(info, *parts)
 
 
 def accumulate(info, sums, high, low, pieces, places, name):
@@ -229,7 +252,7 @@
     return lax.ppermute(value, AXES, pairs)
 
 
-def deal(first, second, core, yh, xi):
+def deal(first, second, core, yh, xi, by_rows):
     lower = yh == 0
     here = jnp.where(lower, first[:512], second[512:])
     there = jnp.where(lower, first[512:], second[:512])
@@ -238,11 +261,13 @@
     here = jnp.where(lower, half[:256], half[256:])
     there = jnp.where(lower, half[256:], half[:256])
     got = move(there, lambda a, b, c, d: (0, b, 3 - c, d) if a == 0 else None)
+    got, by_rows = lax.optimization_barrier((got, by_rows))
+    left = lax.all_to_all(by_rows, COL, 0, 0, tiled=True)
     both = jnp.stack([jnp.where(lower, here, got), jnp.where(lower, got, here)])
     one = move(both, lambda a, b, c, d: (1 if b == 0 else 3, b, c, d) if a == 0 else None)
     two = move(both, lambda a, b, c, d: (3 if b == 0 else 1, b, c, d) if a == 0 else None)
     far = move(one, lambda a, b, c, d: (2, b, c, d) if a == (1 if b == 0 else 3) else None)
-    return jnp.where(xi == 0, both, one + two + far)
+    return lax.optimization_barrier((jnp.where(xi == 0, both, one + two + far), left))
 
 
 def ring(value, first):
@@ -314,33 +339,32 @@
 
     diagonal = ((row_id == 0) & (yh == 0)) | ((row_id == 1) & (yh == 1))
     info = jnp.stack([diagonal.astype(jnp.int32), (4 * yl + z).astype(jnp.int32)])
-    lead = invert_diagonal(info, local[0])
-
-    own_rhs = rhs[0].reshape(64, 2, 4, TILE).transpose(1, 2, 0, 3)
-    own_rhs = jnp.stack([own_rhs, own_rhs[::-1]]).reshape(16, 64, TILE)
-    columns = lax.all_to_all(own_rhs, COL, 0, 0, tiled=True).reshape(1024, TILE)
+    columns = lax.all_to_all(arrange_rhs(rhs), COL, 0, 0, tiled=True).reshape(1024, TILE)
+    lead, columns = lax.optimization_barrier((invert_diagonal(info, local), columns))
 
     place = jnp.stack([1 - yl, z]).astype(jnp.int32)
     triangle = gather_triangles(lead, yl)
     square = gather_square(lead)
+    early, late = arrange(local)
     first = solve(place, *triangle, columns)
     sent = move(first, lambda a, b, c, d: (0, 0, 3 - c, d) if (a, b) == (0, 0) and c < 2 else None)
+    early, first = lax.optimization_barrier((early, first))
+    left_early = lax.all_to_all(early, COL, 0, 0, tiled=True)
     columns = move(columns, lambda a, b, c, d: (0, 0, c, d) if (a, b) == (0, 1) and c >= 2 else None)
     rest = residual(place, *square, columns, sent)
     second_rhs = move(rest, lambda a, b, c, d: (0, 1, c, d) if (a, b) == (0, 0) and c >= 2 else None)
-
-    by_rows, sent = lax.optimization_barrier((arrange(local), sent))
-    left = lax.all_to_all(by_rows, COL, 0, 0, tiled=True)
+    second_rhs, left_early = lax.optimization_barrier((second_rhs, left_early))
     second = solve(place, *triangle, second_rhs)
-    mine = deal(first, second, core, yh, xi)
-    mine, left = lax.optimization_barrier((mine, left))
+    mine, left_late = deal(first, second, core, yh, xi, late)
 
     def swap(value):
         return move(value, lambda a, b, c, d: (a, 1 - b, c, d))
 
-    left = left.reshape(2, 2, 4, 256, TILE)
-    kept = jnp.where(core == 0, left[:, 0], left[:, 1]).reshape(8, 256, TILE)
-    given = jnp.where(core == 0, left[:, 1], left[:, 0]).reshape(8, 256, TILE)
+    kept, given = [], []
+    for left in (left_early, left_late):
+        left = left.reshape(2, 2, 4, 128, TILE)
+        kept.append(jnp.where(core == 0, left[:, 0], left[:, 1]).reshape(8, 128, TILE))
+        given.append(swap(jnp.where(core == 0, left[:, 1], left[:, 0]).reshape(8, 128, TILE)))
     info2 = jnp.stack([xi, core, 2 * yh + yl, z, col_id]).astype(jnp.int32)
 
     after, far_low, far_high, before = ring(mine, True)
@@ -350,7 +374,7 @@
         return lambda a, b, c, d: (a, b, c + step, d) if b == 0 else (a, b, c, d + step)
 
     before, after = move(near, along(1)), move(near, along(-1))
-    high, low = prepare(info2[:1], kept, swap(given))
+    high, low = prepare(info2[:1], *kept, *given)
     sums = accumulate(info2, None, high, low, [near], [(0, 0)], "update_near")
     before, after, sums = lax.optimization_barrier((before, after, sums))
     far_low, far_high = move(before[:2], along(1)), move(after[2:], along(-1))

time: 198 us -> 207 us (1.045)
  starting transfers between devices: 54.8 us -> 66.6 us
  waiting for transfers between devices: 101 us -> 91.2 us
  local copies, waits for them, and re-layouts: 8.77 us -> 12.8 us
    ppermute x33 -> x34, waiting for transfers between devices: 93.7 us -> 73.4 us  [move(): return lax.ppermute(value, AXES, pairs)]
    all_to_all x2 -> x3, waiting for transfers between devices: 7.33 us -> 17.8 us  [the longest x1 9.61 us: shards(): lax.all_to_all(arrange_rhs(rhs), COL, 0, 0, tiled=True).reshape(1024, TILE)]
    ppermute x33 -> x34, starting transfers between devices: 43.4 us -> 49.9 us  [move(): return lax.ppermute(value, AXES, pairs)]
    unnamed x16 -> x32, local copies, waits for them, and re-layouts: 1.76 us -> 7.61 us
    all_to_all x2 -> x3, starting transfers between devices: 11.5 us -> 16.7 us  [the longest x1 7.77 us: shards(): lax.all_to_all(arrange_rhs(rhs), COL, 0, 0, tiled=True).reshape(1024, TILE)]
  transfers between devices with their start and end apart: 35 -> 37, of which waited for: 7 -> 10; matrix products, arithmetic and copies ran while one was open for 6% -> 5% of each run, Pallas kernels for 7% -> 9%
where the time goes in v8:
time: 207 us; the launch traced here: 206 us
  waiting for transfers between devices  91.2 us (44%)
  starting transfers between devices  66.6 us (32%)
  Pallas kernels  26.4 us (13%)
  local copies, waits for them, and re-layouts  12.8 us (6%)
  other arithmetic  7.98 us (4%)
    ppermute x34, waiting for transfers between devices, move(): return lax.ppermute(value, AXES, pairs)  73.4 us
    ppermute x34, starting transfers between devices, move(): return lax.ppermute(value, AXES, pairs)  49.9 us
    all_to_all x1, waiting for transfers between devices, shards(): lax.all_to_all(arrange_rhs(rhs), COL, 0, 0, tiled=True).reshape(1024, TILE)  9.61 us
    pallas_call x3, Pallas kernels, accumulate(): pl.pallas_call(body, out_shape=jax.ShapeDtypeStruct((512, 1024), F32), in...  9.48 us
    pallas_call x2, Pallas kernels, solve(): pl.pallas_call(body, out_shape=jax.ShapeDtypeStruct(rhs.shape, F32), in_s...  8.71 us
    all_to_all x1, waiting for transfers between devices, shards(): left_early = lax.all_to_all(early, COL, 0, 0, tiled=True)  8.2 us
    all_to_all x1, starting transfers between devices, shards(): lax.all_to_all(arrange_rhs(rhs), COL, 0, 0, tiled=True).reshape(1024, TILE)  7.77 us
    unnamed x32, local copies, waits for them, and re-layouts  7.61 us
  transfers between devices with their start and end apart: 37, of which 10 were waited for; matrix products, arithmetic and copies ran while one was open for 5% of the time, Pallas kernels for 9%

profile of v8, /device:TPU:5, one launch (start us, length us, event | category | flops | bytes accessed | tf_op | source)
XLA Modules:
  0.0 205.6 jit_solution(4327158638613555309)
XLA Ops:
  2.2 7.8 %all-to-all-start = ((f32[16,64,128]{2,1,0:T(8,128)}), f32[16,64,128]{2,1,0:T(8,128)S(1)}, u32[]{:S(2)}, u32[]{:S(2)}) async-start(f32[16,64,128]{2,1,0:T(8,128)} %arrange_rhs.1), calls=%async_computation | async-start | bytes 1048576 | tf_op jit(solution)/shard_map/all_to_all | solution.py:342
  10.7 9.6 %all-to-all-done = f32[16,64,128]{2,1,0:T(8,128)S(1)} async-done(((f32[16,64,128]{2,1,0:T(8,128)}), f32[16,64,128]{2,1,0:T(8,128)S(1)}, u32[]{:S(2)}, u32[]{:S(2)}) %all-to-all-start) | async-done | bytes 524320 | tf_op jit(solution)/shard_map/all_to_all | solution.py:342
  47.1 4.8 %block_solve.2 = f32[1024,128]{1,0:T(8,128)} custom-call(s32[2]{0:T(128)S(1)} %pad_add_fusion.info, f32[1536,128]{1,0:T(8,128)S(1)} %pad_maximum_fusion.1.refs_0_, f32[1536,128]{1,0:T(8,128)S(1)} %copy-done.5, f32[1536,128]{1,0:T(8,128)S(1)} %copy-done.2, f32[768,128]{1,0:T(8,128)} %collective-permute-done.14.refs_3_, ...), custom_call_target="tpu_custom_call" | custom-call | tf_op jit(solution)/shard_map/block_solve/pallas_call | solution.py:95
  56.2 4.4 %all-to-all-start.1 = ((f32[16,128,128]{2,1,0:T(8,128)}), f32[16,128,128]{2,1,0:T(8,128)}, u32[]{:S(2)}, u32[]{:S(2)}) async-start(f32[16,128,128]{2,1,0:T(8,128)} %copy-done.13), calls=%async_computation.1 | async-start | bytes 2097152 | tf_op jit(solution)/shard_map/all_to_all | solution.py:352
  62.1 4.3 %block_residual.1 = f32[1024,128]{1,0:T(8,128)} custom-call(s32[2]{0:T(128)S(1)} %pad_add_fusion.info, f32[1024,128]{1,0:T(8,128)} %collective-permute-done.refs_0_, f32[1024,128]{1,0:T(8,128)} %collective-permute-done.1.refs_1_, f32[1024,128]{1,0:T(8,128)} %collective-permute-done.2.refs_2_, f32[1024,128]{1,0:T(8,128)} %collective-permute-done.3.refs_3_, ...), custom_call_target="tpu_custom_call" | custom-call | tf_op jit(solution)/shard_map/block_residual/pallas_call | solution.py:118
  67.1 8.2 %all-to-all-done.1 = f32[16,128,128]{2,1,0:T(8,128)} async-done(((f32[16,128,128]{2,1,0:T(8,128)}), f32[16,128,128]{2,1,0:T(8,128)}, u32[]{:S(2)}, u32[]{:S(2)}) %all-to-all-start.1) | async-done | bytes 1048608 | tf_op jit(solution)/shard_map/all_to_all | solution.py:352
  75.4 3.9 %block_solve.3 = f32[1024,128]{1,0:T(8,128)S(1)} custom-call(s32[2]{0:T(128)S(1)} %pad_add_fusion.info, f32[1536,128]{1,0:T(8,128)S(1)} %pad_maximum_fusion.1.refs_0_, f32[1536,128]{1,0:T(8,128)S(1)} %copy-done.6, f32[1536,128]{1,0:T(8,128)S(1)} %copy-done.3, f32[768,128]{1,0:T(8,128)} %collective-permute-done.14.refs_3_, ...), custom_call_target="tpu_custom_call" | custom-call | tf_op jit(solution)/shard_map/block_solve/pallas_call | solution.py:95
  82.7 4.5 %all-to-all-start.2 = ((f32[16,128,128]{2,1,0:T(8,128)}), f32[16,128,128]{2,1,0:T(8,128)S(1)}, u32[]{:S(2)}, u32[]{:S(2)}) async-start(f32[16,128,128]{2,1,0:T(8,128)} %get-tuple-element.34), calls=%async_computation.2 | async-start | bytes 2097152 | tf_op jit(solution)/shard_map/all_to_all | solution.py:265
  90.0 57.9 %collective-permute-done.22 = f32[2,256,128]{2,1,0:T(8,128)S(1)} collective-permute-done((f32[2,256,128]{2,1,0:T(8,128)S(1)}, f32[2,256,128]{2,1,0:T(8,128)S(1)}, u32[]{:S(2)}, u32[]{:S(2)}) %collective-permute-start.22) | collective-permute-done | bytes 262176 | tf_op jit(solution)/shard_map/ppermute | solution.py:252
  148.0 2.6 %collective-permute-start.25 = (f32[2,256,128]{2,1,0:T(8,128)S(1)}, f32[2,256,128]{2,1,0:T(8,128)S(1)}, u32[]{:S(2)}, u32[]{:S(2)}) collective-permute-start(f32[2,256,128]{2,1,0:T(8,128)S(1)} %add_select_fusion), channel_id=1, source_target_pairs={{0,3},{1,0},{2,1},{3,2},{4,7},{5,4},{6,5},{7,6},{8,11},{9,8},{10,9... | collective-permute-start | bytes 786440 | tf_op jit(solution)/shard_map/ppermute | solution.py:252
  150.6 3.3 %collective-permute-done.25 = f32[2,256,128]{2,1,0:T(8,128)S(1)} collective-permute-done((f32[2,256,128]{2,1,0:T(8,128)S(1)}, f32[2,256,128]{2,1,0:T(8,128)S(1)}, u32[]{:S(2)}, u32[]{:S(2)}) %collective-permute-start.25) | collective-permute-done | bytes 262176 | tf_op jit(solution)/shard_map/ppermute | solution.py:252
  154.0 3.2 %collective-permute-start.28 = (f32[1,256,128]{2,1,0:T(8,128)S(1)}, f32[1,256,128]{2,1,0:T(8,128)S(1)}, u32[]{:S(2)}, u32[]{:S(2)}) collective-permute-start(f32[1,256,128]{2,1,0:T(8,128)S(1)} %slice.108), channel_id=1, source_target_pairs={{0,3},{1,0},{2,1},{3,2},{4,7},{5,4},{6,5},{7,6},{8,11},{9,8},{10,9... | collective-permute-start | bytes 393224 | tf_op jit(solution)/shard_map/ppermute | solution.py:252
  157.3 1.8 collective-permute-done.28
  159.1 3.5 %collective-permute-done.27 = f32[1,256,128]{2,1,0:T(8,128)S(1)} collective-permute-done((f32[1,256,128]{2,1,0:T(8,128)S(1)}, f32[1,256,128]{2,1,0:T(8,128)S(1)}, u32[]{:S(2)}, u32[]{:S(2)}) %collective-permute-start.27) | collective-permute-done | bytes 131104 | tf_op jit(solution)/shard_map/ppermute | solution.py:252
  163.6 1.8 collective-permute-start.30
  165.4 2.3 %fusion.1 = (f32[2,1,4,128,128]{4,3,2,0,1:T(8,128)}, f32[2,1,4,128,128]{4,3,2,0,1:T(8,128)}) fusion(f32[2,2,4,128,128]{4,3,2,1,0:T(8,128)} %bitcast.12, pred[]{:T(512)S(6)} %eq.31), kind=kLoop, calls=%fused_computation.9 | loop fusion | flops 262144 | bytes 2097153 | tf_op jit(solution)/shard_map/jit(_where)/select_n | solution.py:367
  167.7 9.4 %collective-permute-start.23 = (f32[8,128,128]{2,1,0:T(8,128)}, f32[8,128,128]{2,1,0:T(8,128)}, u32[]{:S(2)}, u32[]{:S(2)}) collective-permute-start(f32[8,128,128]{2,1,0:T(8,128)} %bitcast.18), channel_id=1, source_target_pairs={{0,16},{1,17},{2,18},{3,19},{4,20},{5,21},{6,22},{7,23},{8,24},{9,... | collective-permute-start | bytes 1572872 | tf_op jit(solution)/shard_map/ppermute | solution.py:252
  184.0 2.5 %update_near.1.refs_0_ = f32[512,1024]{1,0:T(8,128)S(1)} custom-call(s32[5]{0:T(128)S(1)} %stack.66.info, bf16[4,512,256]{2,1,0:T(8,128)(2,1)S(1)} %get-tuple-element.36.high_ref, bf16[4,512,256]{2,1,0:T(8,128)(2,1)S(1)} %get-tuple-element.37.low_ref, f32[4,2,256,128]{3,2,1,0:T(8,128)S(1)} %pad_maximum_fusion.refs_0_), custom_call_target="tpu_custom_call" | custom-call | tf_op jit(solution)/shard_map/update_near/pallas_call | solution.py:228
  186.7 2.7 %collective-permute-start.32 = (f32[2,2,256,128]{3,2,1,0:T(8,128)S(1)}, f32[2,2,256,128]{3,2,1,0:T(8,128)S(1)}, u32[]{:S(2)}, u32[]{:S(2)}) collective-permute-start(f32[2,2,256,128]{3,2,1,0:T(8,128)S(1)} %slice.91), channel_id=1, source_target_pairs={{0,12},{1,13},{2,14},{3,15},{4,0},{5,1},{6,2},{7,3},{8,4},{9,5},{1... | collective-permute-start | bytes 1572872 | tf_op jit(solution)/shard_map/ppermute | solution.py:252
  189.4 4.4 %update_next.1.refs_0_ = f32[512,1024]{1,0:T(8,128)S(1)} custom-call(s32[5]{0:T(128)S(1)} %stack.66.info, bf16[4,512,256]{2,1,0:T(8,128)(2,1)S(1)} %get-tuple-element.36.high_ref, bf16[4,512,256]{2,1,0:T(8,128)(2,1)S(1)} %get-tuple-element.37.low_ref, f32[512,1024]{1,0:T(8,128)S(1)} %update_near.1.refs_0_, ...), custom_call_target="tpu_custom_call", output_to_operand_aliasing={{}: (3, {})} | custom-call | tf_op jit(solution)/shard_map/update_next/pallas_call | solution.py:228
  193.8 2.3 %collective-permute-done.31.refs_1_ = f32[2,2,256,128]{3,2,1,0:T(8,128)S(1)} collective-permute-done((f32[2,2,256,128]{3,2,1,0:T(8,128)S(1)}, f32[2,2,256,128]{3,2,1,0:T(8,128)S(1)}, u32[]{:S(2)}, u32[]{:S(2)}) %collective-permute-start.31) | collective-permute-done | bytes 524320 | tf_op jit(solution)/shard_map/ppermute | solution.py:252
  196.1 2.6 %update_far.1 = f32[512,1024]{1,0:T(8,128)S(1)} custom-call(s32[5]{0:T(128)S(1)} %stack.66.info, bf16[4,512,256]{2,1,0:T(8,128)(2,1)S(1)} %get-tuple-element.36.high_ref, bf16[4,512,256]{2,1,0:T(8,128)(2,1)S(1)} %get-tuple-element.37.low_ref, f32[512,1024]{1,0:T(8,128)S(1)} %update_next.1.refs_0_, ...), custom_call_target="tpu_custom_call", output_to_operand_aliasing={{}: (3, {})} | custom-call | tf_op jit(solution)/shard_map/update_far/pallas_call | solution.py:228
  198.9 3.3 %collective-permute-start.33 = (f32[256,1024]{1,0:T(8,128)S(1)}, f32[256,1024]{1,0:T(8,128)S(1)}, u32[]{:S(2)}, u32[]{:S(2)}) collective-permute-start(f32[256,1024]{1,0:T(8,128)S(1)} %slice.110), channel_id=1, source_target_pairs={{0,16},{1,17},{2,18},{3,19},{4,20},{5,21},{6,22},{7,23},{8,24},{9,... | collective-permute-start | bytes 3145736 | tf_op jit(solution)/shard_map/ppermute | solution.py:252
  202.1 2.3 %collective-permute-done.33 = f32[256,1024]{1,0:T(8,128)S(1)} collective-permute-done((f32[256,1024]{1,0:T(8,128)S(1)}, f32[256,1024]{1,0:T(8,128)S(1)}, u32[]{:S(2)}, u32[]{:S(2)}) %collective-permute-start.33) | collective-permute-done | bytes 1048608 | tf_op jit(solution)/shard_map/ppermute | solution.py:252
  (119 shorter events, 51.7 us)
Async XLA Ops:
  2.2 18.1 %all-to-all-start = ((f32[16,64,128]{2,1,0:T(8,128)}), f32[16,64,128]{2,1,0:T(8,128)S(1)}, u32[]{:S(2)}, u32[]{:S(2)}) async-start(f32[16,64,128]{2,1,0:T(8,128)} %arrange_rhs.1), calls=%async_computation | async-start | bytes 1048576 | tf_op jit(solution)/shard_map/all_to_all | solution.py:342
  24.4 6.0 %collective-permute-start.13 = (f32[1536,128]{1,0:T(8,128)S(1)}, f32[1536,128]{1,0:T(8,128)S(1)}, u32[]{:S(2)}, u32[]{:S(2)}) collective-permute-start(f32[1536,128]{1,0:T(8,128)S(1)} %pad_maximum_fusion.1.refs_0_), channel_id=1, source_target_pairs={{0,1},{1,2},{2,3},{3,0},{4,5},{5,6},{6,7},{7,4},{24,25},{25,26},{2... | collective-permute-start | bytes 2359304 | tf_op jit(solution)/shard_map/ppermute | solution.py:252
  25.1 7.6 %collective-permute-start.12 = (f32[1536,128]{1,0:T(8,128)S(1)}, f32[1536,128]{1,0:T(8,128)S(1)}, u32[]{:S(2)}, u32[]{:S(2)}) collective-permute-start(f32[1536,128]{1,0:T(8,128)S(1)} %pad_maximum_fusion.1.refs_0_), channel_id=1, source_target_pairs={{0,3},{1,0},{2,1},{3,2},{4,7},{5,4},{6,5},{7,6},{24,27},{25,24},{2... | collective-permute-start | bytes 2359304 | tf_op jit(solution)/shard_map/ppermute | solution.py:252
  25.8 9.9 %collective-permute-start.4 = (f32[1024,128]{1,0:T(8,128)}, f32[1024,128]{1,0:T(8,128)}, u32[]{:S(2)}, u32[]{:S(2)}) collective-permute-start(f32[1024,128]{1,0:T(8,128)} %collective-permute-done.refs_0_), channel_id=1, source_target_pairs={{8,9},{9,10},{10,11},{11,8},{12,13},{13,14},{14,15},{15,12}} | collective-permute-start | bytes 1572872 | tf_op jit(solution)/shard_map/ppermute | solution.py:252
  27.4 11.5 %collective-permute-start.2 = (f32[1024,128]{1,0:T(8,128)}, f32[1024,128]{1,0:T(8,128)}, u32[]{:S(2)}, u32[]{:S(2)}) collective-permute-start(f32[1024,128]{1,0:T(8,128)} %collective-permute-done.refs_0_), channel_id=1, source_target_pairs={{8,11},{9,8},{10,9},{11,10},{12,15},{13,12},{14,13},{15,14}} | collective-permute-start | bytes 1572872 | tf_op jit(solution)/shard_map/ppermute | solution.py:252
  28.9 23.0 %collective-permute-start.10 = (f32[1024,128]{1,0:T(8,128)}, f32[1024,128]{1,0:T(8,128)}, u32[]{:S(2)}, u32[]{:S(2)}) collective-permute-start(f32[1024,128]{1,0:T(8,128)} %bitcast.62), channel_id=1, source_target_pairs={{24,8},{25,9},{26,10},{27,11},{28,12},{29,13},{30,14},{31,15}} | collective-permute-start | bytes 1572872 | tf_op jit(solution)/shard_map/ppermute | solution.py:252
  30.4 22.2 %collective-permute-start.1 = (f32[1024,128]{1,0:T(8,128)}, f32[1024,128]{1,0:T(8,128)}, u32[]{:S(2)}, u32[]{:S(2)}) collective-permute-start(f32[1024,128]{1,0:T(8,128)} %collective-permute-done.refs_0_), channel_id=1, source_target_pairs={{8,12},{9,13},{10,14},{11,15},{12,8},{13,9},{14,10},{15,11}} | collective-permute-start | bytes 1572872 | tf_op jit(solution)/shard_map/ppermute | solution.py:252
  32.6 9.3 %collective-permute-start.14 = (f32[768,128]{1,0:T(8,128)}, f32[768,128]{1,0:T(8,128)}, u32[]{:S(2)}, u32[]{:S(2)}) collective-permute-start(f32[768,128]{1,0:T(8,128)} %slice.97), channel_id=1, source_target_pairs={{0,1},{1,2},{2,3},{3,0},{4,5},{5,6},{6,7},{7,4},{24,25},{25,26},{2... | collective-permute-start | bytes 1179656 | tf_op jit(solution)/shard_map/ppermute | solution.py:252
  35.7 7.6 %collective-permute-start.15 = (f32[768,128]{1,0:T(8,128)}, f32[768,128]{1,0:T(8,128)}, u32[]{:S(2)}, u32[]{:S(2)}) collective-permute-start(f32[768,128]{1,0:T(8,128)} %slice.98), channel_id=1, source_target_pairs={{0,3},{1,0},{2,1},{3,2},{4,7},{5,4},{6,5},{7,6},{24,27},{25,24},{2... | collective-permute-start | bytes 1179656 | tf_op jit(solution)/shard_map/ppermute | solution.py:252
  38.9 21.6 %collective-permute-start.6 = (f32[512,128]{1,0:T(8,128)}, f32[512,128]{1,0:T(8,128)}, u32[]{:S(2)}, u32[]{:S(2)}) collective-permute-start(f32[512,128]{1,0:T(8,128)} %slice.94), channel_id=1, source_target_pairs={{8,9},{9,10},{10,11},{11,8},{12,13},{13,14},{14,15},{15,12}} | collective-permute-start | bytes 786440 | tf_op jit(solution)/shard_map/ppermute | solution.py:252
  42.0 19.4 %collective-permute-start.8 = (f32[512,128]{1,0:T(8,128)}, f32[512,128]{1,0:T(8,128)}, u32[]{:S(2)}, u32[]{:S(2)}) collective-permute-start(f32[512,128]{1,0:T(8,128)} %slice.95), channel_id=1, source_target_pairs={{8,11},{9,8},{10,9},{11,10},{12,15},{13,12},{14,13},{15,14}} | collective-permute-start | bytes 786440 | tf_op jit(solution)/shard_map/ppermute | solution.py:252
  43.4 18.8 %collective-permute-start.3 = (f32[1024,128]{1,0:T(8,128)}, f32[1024,128]{1,0:T(8,128)}, u32[]{:S(2)}, u32[]{:S(2)}) collective-permute-start(f32[1024,128]{1,0:T(8,128)} %collective-permute-done.2.refs_2_), channel_id=1, source_target_pairs={{8,12},{9,13},{10,14},{11,15},{12,8},{13,9},{14,10},{15,11}} | collective-permute-start | bytes 1572872 | tf_op jit(solution)/shard_map/ppermute | solution.py:252
  51.9 10.3 %collective-permute-start.5 = (f32[1024,128]{1,0:T(8,128)}, f32[1024,128]{1,0:T(8,128)S(1)}, u32[]{:S(2)}, u32[]{:S(2)}) collective-permute-start(f32[1024,128]{1,0:T(8,128)} %collective-permute-done.4.refs_4_), channel_id=1, source_target_pairs={{8,12},{9,13},{10,14},{11,15},{12,8},{13,9},{14,10},{15,11}} | collective-permute-start | bytes 1572872 | tf_op jit(solution)/shard_map/ppermute | solution.py:252
  52.6 9.6 %collective-permute-start.16 = (f32[1024,128]{1,0:T(8,128)}, f32[1024,128]{1,0:T(8,128)}, u32[]{:S(2)}, u32[]{:S(2)}) collective-permute-start(f32[1024,128]{1,0:T(8,128)} %block_solve.2), channel_id=1, source_target_pairs={{0,12},{1,13},{2,14},{3,15},{4,8},{5,9},{6,10},{7,11}} | collective-permute-start | bytes 1572872 | tf_op jit(solution)/shard_map/ppermute | solution.py:252
  56.2 19.1 %all-to-all-start.1 = ((f32[16,128,128]{2,1,0:T(8,128)}), f32[16,128,128]{2,1,0:T(8,128)}, u32[]{:S(2)}, u32[]{:S(2)}) async-start(f32[16,128,128]{2,1,0:T(8,128)} %copy-done.13), calls=%async_computation.1 | async-start | bytes 2097152 | tf_op jit(solution)/shard_map/all_to_all | solution.py:352
  66.5 8.9 %collective-permute-start.17 = (f32[1024,128]{1,0:T(8,128)}, f32[1024,128]{1,0:T(8,128)S(1)}, u32[]{:S(2)}, u32[]{:S(2)}) collective-permute-start(f32[1024,128]{1,0:T(8,128)} %block_residual.1), channel_id=1, source_target_pairs={{8,24},{9,25},{10,26},{11,27},{12,28},{13,29},{14,30},{15,31}} | collective-permute-start | bytes 1572872 | tf_op jit(solution)/shard_map/ppermute | solution.py:252
  82.7 65.3 %all-to-all-start.2 = ((f32[16,128,128]{2,1,0:T(8,128)}), f32[16,128,128]{2,1,0:T(8,128)S(1)}, u32[]{:S(2)}, u32[]{:S(2)}) async-start(f32[16,128,128]{2,1,0:T(8,128)} %get-tuple-element.34), calls=%async_computation.2 | async-start | bytes 2097152 | tf_op jit(solution)/shard_map/all_to_all | solution.py:265
  88.7 59.2 %collective-permute-start.22 = (f32[2,256,128]{2,1,0:T(8,128)S(1)}, f32[2,256,128]{2,1,0:T(8,128)S(1)}, u32[]{:S(2)}, u32[]{:S(2)}) collective-permute-start(f32[2,256,128]{2,1,0:T(8,128)S(1)} %collective-permute-done.20), channel_id=1, source_target_pairs={{32,64},{33,65},{34,66},{35,67},{36,68},{37,69},{38,70},{39,71},{4... | collective-permute-start | bytes 786440 | tf_op jit(solution)/shard_map/ppermute | solution.py:252
  150.6 6.5 %collective-permute-start.26 = (f32[2,256,128]{2,1,0:T(8,128)S(1)}, f32[2,256,128]{2,1,0:T(8,128)S(1)}, u32[]{:S(2)}, u32[]{:S(2)}) collective-permute-start(f32[2,256,128]{2,1,0:T(8,128)S(1)} %add_select_fusion), channel_id=1, source_target_pairs={{0,1},{1,2},{2,3},{3,0},{4,5},{5,6},{6,7},{7,4},{8,9},{9,10},{10,1... | collective-permute-start | bytes 786440 | tf_op jit(solution)/shard_map/ppermute | solution.py:252
  162.7 23.8 %collective-permute-start.29 = (f32[4,2,256,128]{3,2,1,0:T(8,128)S(1)}, f32[4,2,256,128]{3,2,1,0:T(8,128)S(1)}, u32[]{:S(2)}, u32[]{:S(2)}) collective-permute-start(f32[4,2,256,128]{3,2,1,0:T(8,128)S(1)} %pad_maximum_fusion.refs_0_), channel_id=1, source_target_pairs={{0,4},{1,5},{2,6},{3,7},{4,8},{5,9},{6,10},{7,11},{8,12},{9,13},{1... | collective-permute-start | bytes 3145736 | tf_op jit(solution)/shard_map/ppermute | solution.py:252
  163.6 22.8 %collective-permute-start.30 = (f32[4,2,256,128]{3,2,1,0:T(8,128)S(1)}, f32[4,2,256,128]{3,2,1,0:T(8,128)S(1)}, u32[]{:S(2)}, u32[]{:S(2)}) collective-permute-start(f32[4,2,256,128]{3,2,1,0:T(8,128)S(1)} %pad_maximum_fusion.refs_0_), channel_id=1, source_target_pairs={{0,12},{1,13},{2,14},{3,15},{4,0},{5,1},{6,2},{7,3},{8,4},{9,5},{1... | collective-permute-start | bytes 3145736 | tf_op jit(solution)/shard_map/ppermute | solution.py:252
  167.7 11.3 %collective-permute-start.23 = (f32[8,128,128]{2,1,0:T(8,128)}, f32[8,128,128]{2,1,0:T(8,128)}, u32[]{:S(2)}, u32[]{:S(2)}) collective-permute-start(f32[8,128,128]{2,1,0:T(8,128)} %bitcast.18), channel_id=1, source_target_pairs={{0,16},{1,17},{2,18},{3,19},{4,20},{5,21},{6,22},{7,23},{8,24},{9,... | collective-permute-start | bytes 1572872 | tf_op jit(solution)/shard_map/ppermute | solution.py:252
  186.5 9.6 %collective-permute-start.31 = (f32[2,2,256,128]{3,2,1,0:T(8,128)S(1)}, f32[2,2,256,128]{3,2,1,0:T(8,128)S(1)}, u32[]{:S(2)}, u32[]{:S(2)}) collective-permute-start(f32[2,2,256,128]{3,2,1,0:T(8,128)S(1)} %slice.90), channel_id=1, source_target_pairs={{0,4},{1,5},{2,6},{3,7},{4,8},{5,9},{6,10},{7,11},{8,12},{9,13},{1... | collective-permute-start | bytes 1572872 | tf_op jit(solution)/shard_map/ppermute | solution.py:252
  186.7 9.5 %collective-permute-start.32 = (f32[2,2,256,128]{3,2,1,0:T(8,128)S(1)}, f32[2,2,256,128]{3,2,1,0:T(8,128)S(1)}, u32[]{:S(2)}, u32[]{:S(2)}) collective-permute-start(f32[2,2,256,128]{3,2,1,0:T(8,128)S(1)} %slice.91), channel_id=1, source_target_pairs={{0,12},{1,13},{2,14},{3,15},{4,0},{5,1},{6,2},{7,3},{8,4},{9,5},{1... | collective-permute-start | bytes 1572872 | tf_op jit(solution)/shard_map/ppermute | solution.py:252
  (29 other events, 145.4 us)

commit v9 on v7

--- a/solution.py
+++ b/solution.py
@@ -1,6 +1,5 @@
 import jax
 import jax.numpy as jnp
-import numpy as np
 from jax import lax
 from jax.experimental import pallas as pl
 from jax.experimental.pallas import tpu as pltpu
@@ -78,6 +77,7 @@
         rhs_ref, out_ref, tri_ref = refs[-3:]
         for ref, parts in zip(refs, places):
             for half, steps, start, to, rows in parts:
+                half = {"own": info[0], "pair": 1 - info[0]}.get(half, half)
                 k = 4 * half + lax.rem(info[1] + steps, 4)
                 tri_ref[k, pl.ds(to, rows), :] = pack_left(ref[pl.ds(start, rows), :])
         out_ref[...] = rhs_ref[...]
@@ -105,11 +105,12 @@
     def body(info, *refs):
         rhs_ref, x_ref, out_ref = refs[-3:]
         out_ref[...] = rhs_ref[...]
-        for ref, (other, steps, row) in zip(refs, places):
-            half = 1 - info[0] if other else info[0]
+        for ref, parts in zip(refs, places):
+            ((half, steps, _, row, rows),) = parts
+            half = {"own": info[0], "pair": 1 - info[0]}[half]
             k = 4 * half + lax.rem(info[1] + steps, 4)
             right = pack_right(x_ref[pl.ds(pl.multiple_of(k * TILE, TILE), TILE), :])
-            for start in range(0, ref.shape[0], TILE):
+            for start in range(0, rows, TILE):
                 there = pl.ds(row + start, TILE)
                 out_ref[there, :] = out_ref[there, :] - packed_product(pack_left(ref[pl.ds(start, TILE), :]), right)
 
@@ -187,19 +188,17 @@
                 cols = pl.ds(pl.multiple_of((4 * bit + pz) * TILE, TILE), TILE)
                 total = None
                 for h in range(2):
-                    x_high, x_low = split(ref[n, h])
-                    wide = mm(high_ref[2 * h + upper], jnp.concatenate([x_high, x_low], 1))
-                    term = wide[:, :TILE] + (wide[:, TILE:] + mm(low_ref[2 * h + upper], x_high))
+                    x_high, x_low = split(ref[n, pl.ds(256 * h, 256), :])
+                    wide = mm(high_ref[2 * upper + h], jnp.concatenate([x_high, x_low], 1))
+                    term = wide[:, :TILE] + (wide[:, TILE:] + mm(low_ref[2 * upper + h], x_high))
                     total = term if total is None else total + term
                 out_ref[:, cols] = out_ref[:, cols] + total
 
-                @pl.when((x == 0) & (col // 4 == 2 * core + upper))
+                @pl.when((x == 0) & (col // 8 == upper))
                 def _():
-                    there = pl.ds(pl.multiple_of(lax.rem(col, 4) * 64, 64), 64)
-                    for side in range(2):
-                        here = pl.ds(256 * side, 64)
-                        block = core if side == 0 else 1 - core
-                        out_ref[here, cols] = out_ref[here, cols] - ref[n, block, there, :]
+                    there = pl.ds(pl.multiple_of(lax.rem(col, 8) * 64, 64), 64)
+                    here = pl.ds(0, 64)
+                    out_ref[here, cols] = out_ref[here, cols] - ref[n, there, :]
 
     start = [] if first else [sums]
     return pl.pallas_call(
@@ -230,19 +229,16 @@
 
 
 def deal(first, second, core, yh, xi):
+    solved = jnp.where(core == 0, first, second)
     lower = yh == 0
-    here = jnp.where(lower, first[:512], second[512:])
-    there = jnp.where(lower, first[512:], second[:512])
-    got = move(there, lambda a, b, c, d: (0, 1 - b, c, d) if a == 0 and b == c // 2 else None)
-    half = jnp.where(core == yh, here, got)
-    here = jnp.where(lower, half[:256], half[256:])
-    there = jnp.where(lower, half[256:], half[:256])
-    got = move(there, lambda a, b, c, d: (0, b, 3 - c, d) if a == 0 else None)
-    both = jnp.stack([jnp.where(lower, here, got), jnp.where(lower, got, here)])
-    one = move(both, lambda a, b, c, d: (1 if b == 0 else 3, b, c, d) if a == 0 else None)
-    two = move(both, lambda a, b, c, d: (3 if b == 0 else 1, b, c, d) if a == 0 else None)
+    here = jnp.where(lower, solved[:512], solved[512:])
+    there = jnp.where(core == 0, solved[512:], solved[:512])
+    got = move(there, lambda a, b, c, d: (0, b, 3 - c, d) if a == 0 and b == c // 2 else None)
+    mine = jnp.where(core == yh, here, got)
+    one = move(mine, lambda a, b, c, d: (1 if b == 0 else 3, b, c, d) if a == 0 else None)
+    two = move(mine, lambda a, b, c, d: (3 if b == 0 else 1, b, c, d) if a == 0 else None)
     far = move(one, lambda a, b, c, d: (2, b, c, d) if a == (1 if b == 0 else 3) else None)
-    return jnp.where(xi == 0, both, one + two + far)
+    return jnp.where(xi == 0, mine, one + two + far)
 
 
 def ring(value, first):
@@ -261,11 +257,11 @@
     return after, far_low, far_high, before
 
 
-def gather_triangles(lead, yl):
+def gather_first(lead, yl):
     def holds(a, b, c):
-        return a == 0 and b == c // 2
-
-    swapped = move(lead, lambda a, b, c, d: (a, b, c + 1 - 2 * (c % 2), d) if holds(a, b, c) else None)
+        return a == 0 and b == 0 and c < 2
+
+    swapped = move(lead, lambda a, b, c, d: (a, b, 1 - c, d) if holds(a, b, c) else None)
     full = jnp.where(yl == 0, lead, swapped)
     lower = jnp.where(yl == 0, swapped[512:], lead[512:])
     pair = jnp.concatenate([full, lower], 0)
@@ -284,23 +280,19 @@
     return pieces, places
 
 
-def gather_square(lead):
-    def holds(a, b, c):
-        return a == 0 and b == 0 and c >= 2
-
+def gather_second(lead):
     def along(step):
-        return lambda a, b, c, d: (a, b, c, d + step) if holds(a, b, c) else None
+        return lambda a, b, c, d: (0, 1, c, d + step) if a == 0 and b == 1 else None
 
     def pair(value):
-        return move(value, lambda a, b, c, d: (a, b, 5 - c, d) if holds(a, b, c) else None)
-
-    own = move(lead, lambda a, b, c, d: (0, 0, 3 - c, d) if (a, b) == (0, 1) and c < 2 else None)
-    before, after = move(own, along(1)), move(own, along(-1))
+        return move(value, lambda a, b, c, d: (0, 1, c + 1 - 2 * (c % 2), d) if a == 0 and b == 1 else None)
+
+    before, after = move(lead, along(1)), move(lead, along(-1))
     far_low, far_high = move(before[:512], along(1)), move(after[512:], along(-1))
     pieces, places = [], []
-    for piece, steps, row in ((own, 0, 0), (after, 1, 0), (before, 3, 0), (far_low, 2, 0), (far_high, 2, 512)):
+    for piece, steps, row in ((lead, 0, 0), (after, 1, 0), (before, 3, 0), (far_low, 2, 0), (far_high, 2, 512)):
         pieces += [piece, pair(piece)]
-        places += [(False, steps, row), (True, steps, row)]
+        places += [[(half, steps, 0, row, piece.shape[0])] for half in ("own", "pair")]
     return pieces, places
 
 
@@ -317,30 +309,29 @@
     lead = invert_diagonal(info, local[0])
 
     own_rhs = rhs[0].reshape(64, 2, 4, TILE).transpose(1, 2, 0, 3)
-    own_rhs = jnp.stack([own_rhs, own_rhs[::-1]]).reshape(16, 64, TILE)
-    columns = lax.all_to_all(own_rhs, COL, 0, 0, tiled=True).reshape(1024, TILE)
-
-    place = jnp.stack([1 - yl, z]).astype(jnp.int32)
-    triangle = gather_triangles(lead, yl)
-    square = gather_square(lead)
-    first = solve(place, *triangle, columns)
-    sent = move(first, lambda a, b, c, d: (0, 0, 3 - c, d) if (a, b) == (0, 0) and c < 2 else None)
-    columns = move(columns, lambda a, b, c, d: (0, 0, c, d) if (a, b) == (0, 1) and c >= 2 else None)
-    rest = residual(place, *square, columns, sent)
-    second_rhs = move(rest, lambda a, b, c, d: (0, 1, c, d) if (a, b) == (0, 0) and c >= 2 else None)
-
-    by_rows, sent = lax.optimization_barrier((arrange(local), sent))
+    own_rhs = jnp.where(yh == 0, own_rhs, own_rhs[::-1]).reshape(8, 64, TILE)
+    half = lax.all_to_all(own_rhs, ("yl", "z"), 0, 0, tiled=True).reshape(512, TILE)
+    other_half = move(half, lambda a, b, c, d: (0, b, 3 - c, d) if a == 0 and c >= 2 else None)
+    columns = jnp.concatenate([half, other_half], 0)
+
+    place = jnp.stack([yl, z]).astype(jnp.int32)
+    upper_left = gather_first(lead, yl)
+    lower_row = gather_second(lead)
+    first = solve(place, *upper_left, columns)
+    sent = move(first, lambda a, b, c, d: (0, 1, c, d) if (a, b) == (0, 0) and c < 2 else None)
+    rest = residual(place, *lower_row, columns, sent)
+    second_rhs = move(rest, lambda a, b, c, d: (0, 1, 3 - c, d) if (a, b) == (0, 1) and c < 2 else None)
+    by_rows, second_rhs = lax.optimization_barrier((arrange(local), second_rhs))
     left = lax.all_to_all(by_rows, COL, 0, 0, tiled=True)
-    second = solve(place, *triangle, second_rhs)
+    second = solve(place, *lower_row, second_rhs)
     mine = deal(first, second, core, yh, xi)
-    mine, left = lax.optimization_barrier((mine, left))
 
     def swap(value):
         return move(value, lambda a, b, c, d: (a, 1 - b, c, d))
 
-    left = left.reshape(2, 2, 4, 256, TILE)
-    kept = jnp.where(core == 0, left[:, 0], left[:, 1]).reshape(8, 256, TILE)
-    given = jnp.where(core == 0, left[:, 1], left[:, 0]).reshape(8, 256, TILE)
+    left = left.reshape(2, 8, 256, TILE)
+    kept = jnp.where(core == 0, left[0], left[1])
+    given = jnp.where(core == 0, left[1], left[0])
     info2 = jnp.stack([xi, core, 2 * yh + yl, z, col_id]).astype(jnp.int32)
 
     after, far_low, far_high, before = ring(mine, True)

time: 198 us -> 176 us (0.89)
  starting transfers between devices: 54.8 us -> 38.8 us
  waiting for transfers between devices: 101 us -> 87.5 us
  blocking collectives: 0 us -> 11.9 us
  local copies, waits for them, and re-layouts: 8.77 us -> 6.57 us
    all_to_all x0 -> x1, blocking collectives: none -> 11.9 us  [shards(): lax.all_to_all(own_rhs, ('yl', 'z'), 0, 0, tiled=True).reshape(512, TILE)]
    ppermute x33 -> x31, starting transfers between devices: 43.4 us -> 34 us  [move(): return lax.ppermute(value, AXES, pairs)]
    all_to_all x1 -> x0, starting transfers between devices: 7.77 us -> none  [shards(): columns = lax.all_to_all(own_rhs, COL, 0, 0, tiled=True).reshape(1024, TILE)]
    all_to_all x1 -> x0, waiting for transfers between devices: 7.33 us -> none  [shards(): columns = lax.all_to_all(own_rhs, COL, 0, 0, tiled=True).reshape(1024, TILE)]
    ppermute x33 -> x31, waiting for transfers between devices: 93.7 us -> 87.5 us  [move(): return lax.ppermute(value, AXES, pairs)]
    slice x4, local copies, waits for them, and re-layouts: 3.49 us -> 1.09 us  [the longest x1 1.02 us: gather_first(): after[768:]]
  transfers between devices with their start and end apart: 35 -> 32, of which waited for: 7 -> 9; matrix products, arithmetic and copies ran while one was open for 6% -> 2% of each run, Pallas kernels for 7% -> 11%
where the time goes in v9:
time: 176 us; the launch traced here: 175 us
  waiting for transfers between devices  87.5 us (50%)
  starting transfers between devices  38.8 us (22%)
  Pallas kernels  25.2 us (14%)
  blocking collectives  11.9 us (7%)
  local copies, waits for them, and re-layouts  6.57 us (4%)
  other arithmetic  4.58 us (3%)
    ppermute x31, waiting for transfers between devices, move(): return lax.ppermute(value, AXES, pairs)  87.5 us
    ppermute x31, starting transfers between devices, move(): return lax.ppermute(value, AXES, pairs)  34 us
    all_to_all x1, blocking collectives, shards(): lax.all_to_all(own_rhs, ('yl', 'z'), 0, 0, tiled=True).reshape(512, TILE)  11.9 us
    pallas_call x3, Pallas kernels, accumulate(): pl.pallas_call(body, out_shape=jax.ShapeDtypeStruct((512, 1024), F32), in...  10.2 us
    pallas_call x2, Pallas kernels, solve(): pl.pallas_call(body, out_shape=jax.ShapeDtypeStruct(rhs.shape, F32), in_s...  8.75 us
    all_to_all x1, starting transfers between devices, shards(): left = lax.all_to_all(by_rows, COL, 0, 0, tiled=True)  4.81 us
  transfers between devices with their start and end apart: 32, of which 9 were waited for; matrix products, arithmetic and copies ran while one was open for 2% of the time, Pallas kernels for 11%

profile of v9, /device:TPU:5, one launch (start us, length us, event | category | flops | bytes accessed | tf_op | source)
XLA Modules:
  0.0 175.3 jit_solution(5954949159389047291)
XLA Ops:
  3.4 1.6 collective-permute-start.11
  5.2 11.9 %all_to_all.10 = f32[8,64,128]{2,1,0:T(8,128)S(1)} all-to-all(f32[8,64,128]{2,1,0:T(8,128)S(1)} %bitcast.30), channel_id=1, replica_groups=mesh['x'=4,'core'=2,'yh'=2,'yl'=2,'z'=4] {'yl','z'}, dimensions={0} | all-to-all | bytes 524288 | tf_op jit(solution)/shard_map/all_to_all | solution.py:313
  25.4 4.0 %block_solve.2 = f32[1024,128]{1,0:T(8,128)S(1)} custom-call(s32[2]{0:T(128)S(1)} %pad_add_fusion.info, f32[1536,128]{1,0:T(8,128)S(1)} %pad_maximum_fusion.1.refs_0_, f32[1536,128]{1,0:T(8,128)} %collective-permute-done.11.refs_1_, f32[1536,128]{1,0:T(8,128)S(1)} %collective-permute-done.12.refs_2_, f32[768,128]{1,0:T(8,128)S(1)} %collective-permute-done.13.refs_3_, ...), custom_call_target="tpu_custom_call" | custom-call | tf_op jit(solution)/shard_map/block_solve/pallas_call | solution.py:93
  31.9 2.7 %block_residual.1 = f32[1024,128]{1,0:T(8,128)} custom-call(s32[2]{0:T(128)S(1)} %pad_add_fusion.info, f32[1024,128]{1,0:T(8,128)S(1)} %invert_diagonal.1.refs_0_, f32[1024,128]{1,0:T(8,128)S(1)} %collective-permute-done.refs_1_, f32[1024,128]{1,0:T(8,128)S(1)} %collective-permute-done.1.refs_2_, f32[1024,128]{1,0:T(8,128)S(1)} %collective-permute-done.2.refs_3_, ...), custom_call_target="tpu_custom_call" | custom-call | tf_op jit(solution)/shard_map/block_residual/pallas_call | solution.py:117
  34.6 1.5 collective-permute-start.16
  36.1 1.5 arrange_rows.1
  37.6 4.8 %all-to-all-start.1 = ((f32[16,256,128]{2,1,0:T(8,128)}), f32[16,256,128]{2,1,0:T(8,128)}, u32[]{:S(2)}, u32[]{:S(2)}) async-start(f32[16,256,128]{2,1,0:T(8,128)} %arrange_rows.1), calls=%async_computation.1 | async-start | bytes 4194304 | tf_op jit(solution)/shard_map/all_to_all | solution.py:325
  45.3 4.8 %block_solve.3 = f32[1024,128]{1,0:T(8,128)S(1)} custom-call(s32[2]{0:T(128)S(1)} %pad_add_fusion.info, f32[1024,128]{1,0:T(8,128)S(1)} %invert_diagonal.1.refs_0_, f32[1024,128]{1,0:T(8,128)S(1)} %copy-done.6, f32[1024,128]{1,0:T(8,128)S(1)} %copy-done.2, f32[1024,128]{1,0:T(8,128)S(1)} %copy-done.8, f32[1024,128]{1,0:T(8,128)S(1)} %collective-permute-done.3.refs_4_, ...), custom_call_target="tpu_custom_call" | custom-call | tf_op jit(solution)/shard_map/block_solve/pallas_call | solution.py:93
  52.3 1.3 collective-permute-start.21
  53.6 69.6 %collective-permute-done.21 = f32[512,128]{1,0:T(8,128)S(1)} collective-permute-done((f32[512,128]{1,0:T(8,128)S(1)}, f32[512,128]{1,0:T(8,128)S(1)}, u32[]{:S(2)}, u32[]{:S(2)}) %collective-permute-start.21) | collective-permute-done | bytes 262176 | tf_op jit(solution)/shard_map/ppermute | solution.py:228
  123.2 2.1 %collective-permute-start.23 = (f32[512,128]{1,0:T(8,128)S(1)}, f32[512,128]{1,0:T(8,128)S(1)}, u32[]{:S(2)}, u32[]{:S(2)}) collective-permute-start(f32[512,128]{1,0:T(8,128)S(1)} %add_select_fusion), channel_id=1, source_target_pairs={{0,1},{1,2},{2,3},{3,0},{4,5},{5,6},{6,7},{7,4},{8,9},{9,10},{10,1... | collective-permute-start | bytes 786440 | tf_op jit(solution)/shard_map/ppermute | solution.py:228
  126.0 3.8 %collective-permute-done.23 = f32[512,128]{1,0:T(8,128)S(1)} collective-permute-done((f32[512,128]{1,0:T(8,128)S(1)}, f32[512,128]{1,0:T(8,128)S(1)}, u32[]{:S(2)}, u32[]{:S(2)}) %collective-permute-start.23) | collective-permute-done | bytes 262176 | tf_op jit(solution)/shard_map/ppermute | solution.py:228
  130.6 2.1 %collective-permute-start.25 = (f32[256,128]{1,0:T(8,128)S(1)}, f32[256,128]{1,0:T(8,128)S(1)}, u32[]{:S(2)}, u32[]{:S(2)}) collective-permute-start(f32[256,128]{1,0:T(8,128)S(1)} %slice.91), channel_id=1, source_target_pairs={{0,3},{1,0},{2,1},{3,2},{4,7},{5,4},{6,5},{7,6},{8,11},{9,8},{10,9... | collective-permute-start | bytes 393224 | tf_op jit(solution)/shard_map/ppermute | solution.py:228
  132.8 2.1 %collective-permute-done.24 = f32[256,128]{1,0:T(8,128)S(1)} collective-permute-done((f32[256,128]{1,0:T(8,128)S(1)}, f32[256,128]{1,0:T(8,128)S(1)}, u32[]{:S(2)}, u32[]{:S(2)}) %collective-permute-start.24) | collective-permute-done | bytes 131104 | tf_op jit(solution)/shard_map/ppermute | solution.py:228
  134.9 2.7 %slice_select_fusion = (f32[8,256,128]{2,1,0:T(8,128)}, f32[8,256,128]{2,1,0:T(8,128)S(1)}) fusion(f32[16,256,128]{2,1,0:T(8,128)} %all-to-all-done.1, pred[]{:T(512)S(6)} %eq.32), kind=kLoop, calls=%fused_computation.4 | loop fusion | flops 524288 | bytes 4194305 | tf_op jit(solution)/shard_map/jit(_where)/select_n | solution.py:334
  137.7 1.6 collective-permute-start.26
  140.6 1.5 prepare_update.1
  142.1 2.5 %update_near.1.refs_0_ = f32[512,1024]{1,0:T(8,128)S(1)} custom-call(s32[5]{0:T(128)S(1)} %stack.57.info, bf16[4,512,256]{2,1,0:T(8,128)(2,1)S(1)} %get-tuple-element.16.high_ref, bf16[4,512,256]{2,1,0:T(8,128)(2,1)S(1)} %get-tuple-element.17.low_ref, f32[4,512,128]{2,1,0:T(8,128)S(1)} %pad_maximum_fusion.refs_0_), custom_call_target="tpu_custom_call" | custom-call | tf_op jit(solution)/shard_map/update_near/pallas_call | solution.py:204
  144.6 8.3 %collective-permute-done.26.refs_2_ = f32[4,512,128]{2,1,0:T(8,128)S(1)} collective-permute-done((f32[4,512,128]{2,1,0:T(8,128)S(1)}, f32[4,512,128]{2,1,0:T(8,128)S(1)}, u32[]{:S(2)}, u32[]{:S(2)}) %collective-permute-start.26) | collective-permute-done | bytes 1048608 | tf_op jit(solution)/shard_map/ppermute | solution.py:228
  155.0 2.2 %collective-permute-start.29 = (f32[2,512,128]{2,1,0:T(8,128)S(1)}, f32[2,512,128]{2,1,0:T(8,128)S(1)}, u32[]{:S(2)}, u32[]{:S(2)}) collective-permute-start(f32[2,512,128]{2,1,0:T(8,128)S(1)} %slice.77), channel_id=1, source_target_pairs={{0,12},{1,13},{2,14},{3,15},{4,0},{5,1},{6,2},{7,3},{8,4},{9,5},{1... | collective-permute-start | bytes 1572872 | tf_op jit(solution)/shard_map/ppermute | solution.py:228
  157.2 5.1 %update_next.1.refs_0_ = f32[512,1024]{1,0:T(8,128)S(1)} custom-call(s32[5]{0:T(128)S(1)} %stack.57.info, bf16[4,512,256]{2,1,0:T(8,128)(2,1)S(1)} %get-tuple-element.16.high_ref, bf16[4,512,256]{2,1,0:T(8,128)(2,1)S(1)} %get-tuple-element.17.low_ref, f32[512,1024]{1,0:T(8,128)S(1)} %update_near.1.refs_0_, ...), custom_call_target="tpu_custom_call", output_to_operand_aliasing={{}: (3, {})} | custom-call | tf_op jit(solution)/shard_map/update_next/pallas_call | solution.py:204
  163.4 2.6 %update_far.1 = f32[512,1024]{1,0:T(8,128)S(1)} custom-call(s32[5]{0:T(128)S(1)} %stack.57.info, bf16[4,512,256]{2,1,0:T(8,128)(2,1)S(1)} %get-tuple-element.16.high_ref, bf16[4,512,256]{2,1,0:T(8,128)(2,1)S(1)} %get-tuple-element.17.low_ref, f32[512,1024]{1,0:T(8,128)S(1)} %update_next.1.refs_0_, ...), custom_call_target="tpu_custom_call", output_to_operand_aliasing={{}: (3, {})} | custom-call | tf_op jit(solution)/shard_map/update_far/pallas_call | solution.py:204
  166.1 5.8 %collective-permute-start.30 = (f32[256,1024]{1,0:T(8,128)S(1)}, f32[256,1024]{1,0:T(8,128)S(1)}, u32[]{:S(2)}, u32[]{:S(2)}) collective-permute-start(f32[256,1024]{1,0:T(8,128)S(1)} %slice.93), channel_id=1, source_target_pairs={{0,16},{1,17},{2,18},{3,19},{4,20},{5,21},{6,22},{7,23},{8,24},{9,... | collective-permute-start | bytes 3145736 | tf_op jit(solution)/shard_map/ppermute | solution.py:228
  171.8 2.3 %collective-permute-done.30 = f32[256,1024]{1,0:T(8,128)S(1)} collective-permute-done((f32[256,1024]{1,0:T(8,128)S(1)}, f32[256,1024]{1,0:T(8,128)S(1)}, u32[]{:S(2)}, u32[]{:S(2)}) %collective-permute-start.30) | collective-permute-done | bytes 1048608 | tf_op jit(solution)/shard_map/ppermute | solution.py:228
  (117 shorter events, 26.5 us)
Async XLA Ops:
  2.6 16.6 %collective-permute-start.12 = (f32[1536,128]{1,0:T(8,128)S(1)}, f32[1536,128]{1,0:T(8,128)S(1)}, u32[]{:S(2)}, u32[]{:S(2)}) collective-permute-start(f32[1536,128]{1,0:T(8,128)S(1)} %pad_maximum_fusion.1.refs_0_), channel_id=1, source_target_pairs={{0,1},{1,2},{2,3},{3,0},{4,5},{5,6},{6,7},{7,4}} | collective-permute-start | bytes 2359304 | tf_op jit(solution)/shard_map/ppermute | solution.py:228
  3.4 16.6 %collective-permute-start.11 = (f32[1536,128]{1,0:T(8,128)S(1)}, f32[1536,128]{1,0:T(8,128)}, u32[]{:S(2)}, u32[]{:S(2)}) collective-permute-start(f32[1536,128]{1,0:T(8,128)S(1)} %pad_maximum_fusion.1.refs_0_), channel_id=1, source_target_pairs={{0,3},{1,0},{2,1},{3,2},{4,7},{5,4},{6,5},{7,6}} | collective-permute-start | bytes 2359304 | tf_op jit(solution)/shard_map/ppermute | solution.py:228
  17.1 4.6 %collective-permute-start.9 = (f32[512,128]{1,0:T(8,128)S(1)}, f32[512,128]{1,0:T(8,128)S(1)}, u32[]{:S(2)}, u32[]{:S(2)}) collective-permute-start(f32[512,128]{1,0:T(8,128)S(1)} %bitcast.31), channel_id=1, source_target_pairs={{8,4},{9,5},{10,6},{11,7},{12,0},{13,1},{14,2},{15,3},{24,20},{25,... | collective-permute-start | bytes 786440 | tf_op jit(solution)/shard_map/ppermute | solution.py:228
  17.8 4.7 %collective-permute-start.3 = (f32[1024,128]{1,0:T(8,128)S(1)}, f32[1024,128]{1,0:T(8,128)S(1)}, u32[]{:S(2)}, u32[]{:S(2)}) collective-permute-start(f32[1024,128]{1,0:T(8,128)S(1)} %invert_diagonal.1.refs_0_), channel_id=1, source_target_pairs={{16,17},{17,18},{18,19},{19,16},{20,21},{21,22},{22,23},{23,20},{2... | collective-permute-start | bytes 1572872 | tf_op jit(solution)/shard_map/ppermute | solution.py:228
  18.5 4.7 %collective-permute-start.1 = (f32[1024,128]{1,0:T(8,128)S(1)}, f32[1024,128]{1,0:T(8,128)S(1)}, u32[]{:S(2)}, u32[]{:S(2)}) collective-permute-start(f32[1024,128]{1,0:T(8,128)S(1)} %invert_diagonal.1.refs_0_), channel_id=1, source_target_pairs={{16,19},{17,16},{18,17},{19,18},{20,23},{21,20},{22,21},{23,22},{2... | collective-permute-start | bytes 1572872 | tf_op jit(solution)/shard_map/ppermute | solution.py:228
  19.2 10.2 %collective-permute-start = (f32[1024,128]{1,0:T(8,128)S(1)}, f32[1024,128]{1,0:T(8,128)S(1)}, u32[]{:S(2)}, u32[]{:S(2)}) collective-permute-start(f32[1024,128]{1,0:T(8,128)S(1)} %invert_diagonal.1.refs_0_), channel_id=1, source_target_pairs={{16,20},{17,21},{18,22},{19,23},{20,16},{21,17},{22,18},{23,19},{2... | collective-permute-start | bytes 1572872 | tf_op jit(solution)/shard_map/ppermute | solution.py:228
  20.0 4.0 %collective-permute-start.13 = (f32[768,128]{1,0:T(8,128)S(1)}, f32[768,128]{1,0:T(8,128)S(1)}, u32[]{:S(2)}, u32[]{:S(2)}) collective-permute-start(f32[768,128]{1,0:T(8,128)S(1)} %slice.84), channel_id=1, source_target_pairs={{0,1},{1,2},{2,3},{3,0},{4,5},{5,6},{6,7},{7,4}} | collective-permute-start | bytes 1179656 | tf_op jit(solution)/shard_map/ppermute | solution.py:228
  21.7 3.0 %collective-permute-start.14 = (f32[768,128]{1,0:T(8,128)S(1)}, f32[768,128]{1,0:T(8,128)S(1)}, u32[]{:S(2)}, u32[]{:S(2)}) collective-permute-start(f32[768,128]{1,0:T(8,128)S(1)} %slice.85), channel_id=1, source_target_pairs={{0,3},{1,0},{2,1},{3,2},{4,7},{5,4},{6,5},{7,6}} | collective-permute-start | bytes 1179656 | tf_op jit(solution)/shard_map/ppermute | solution.py:228
  22.5 7.7 %collective-permute-start.5 = (f32[512,128]{1,0:T(8,128)S(1)}, f32[512,128]{1,0:T(8,128)S(1)}, u32[]{:S(2)}, u32[]{:S(2)}) collective-permute-start(f32[512,128]{1,0:T(8,128)S(1)} %slice.80), channel_id=1, source_target_pairs={{16,17},{17,18},{18,19},{19,16},{20,21},{21,22},{22,23},{23,20},{2... | collective-permute-start | bytes 786440 | tf_op jit(solution)/shard_map/ppermute | solution.py:228
  23.3 7.8 %collective-permute-start.7 = (f32[512,128]{1,0:T(8,128)S(1)}, f32[512,128]{1,0:T(8,128)S(1)}, u32[]{:S(2)}, u32[]{:S(2)}) collective-permute-start(f32[512,128]{1,0:T(8,128)S(1)} %slice.81), channel_id=1, source_target_pairs={{16,19},{17,16},{18,17},{19,18},{20,23},{21,20},{22,21},{23,22},{2... | collective-permute-start | bytes 786440 | tf_op jit(solution)/shard_map/ppermute | solution.py:228
  24.0 7.9 %collective-permute-start.2 = (f32[1024,128]{1,0:T(8,128)S(1)}, f32[1024,128]{1,0:T(8,128)S(1)}, u32[]{:S(2)}, u32[]{:S(2)}) collective-permute-start(f32[1024,128]{1,0:T(8,128)S(1)} %collective-permute-done.1.refs_2_), channel_id=1, source_target_pairs={{16,20},{17,21},{18,22},{19,23},{20,16},{21,17},{22,18},{23,19},{2... | collective-permute-start | bytes 1572872 | tf_op jit(solution)/shard_map/ppermute | solution.py:228
  24.7 7.2 %collective-permute-start.4 = (f32[1024,128]{1,0:T(8,128)S(1)}, f32[1024,128]{1,0:T(8,128)S(1)}, u32[]{:S(2)}, u32[]{:S(2)}) collective-permute-start(f32[1024,128]{1,0:T(8,128)S(1)} %collective-permute-done.3.refs_4_), channel_id=1, source_target_pairs={{16,20},{17,21},{18,22},{19,23},{20,16},{21,17},{22,18},{23,19},{2... | collective-permute-start | bytes 1572872 | tf_op jit(solution)/shard_map/ppermute | solution.py:228
  37.6 97.3 %all-to-all-start.1 = ((f32[16,256,128]{2,1,0:T(8,128)}), f32[16,256,128]{2,1,0:T(8,128)}, u32[]{:S(2)}, u32[]{:S(2)}) async-start(f32[16,256,128]{2,1,0:T(8,128)} %arrange_rows.1), calls=%async_computation.1 | async-start | bytes 4194304 | tf_op jit(solution)/shard_map/all_to_all | solution.py:325
  52.3 70.9 %collective-permute-start.21 = (f32[512,128]{1,0:T(8,128)S(1)}, f32[512,128]{1,0:T(8,128)S(1)}, u32[]{:S(2)}, u32[]{:S(2)}) collective-permute-start(f32[512,128]{1,0:T(8,128)S(1)} %collective-permute-done.19), channel_id=1, source_target_pairs={{32,64},{33,65},{34,66},{35,67},{36,68},{37,69},{38,70},{39,71},{4... | collective-permute-start | bytes 786440 | tf_op jit(solution)/shard_map/ppermute | solution.py:228
  123.2 6.5 %collective-permute-start.23 = (f32[512,128]{1,0:T(8,128)S(1)}, f32[512,128]{1,0:T(8,128)S(1)}, u32[]{:S(2)}, u32[]{:S(2)}) collective-permute-start(f32[512,128]{1,0:T(8,128)S(1)} %add_select_fusion), channel_id=1, source_target_pairs={{0,1},{1,2},{2,3},{3,0},{4,5},{5,6},{6,7},{7,4},{8,9},{9,10},{10,1... | collective-permute-start | bytes 786440 | tf_op jit(solution)/shard_map/ppermute | solution.py:228
  125.3 5.3 %collective-permute-start.22 = (f32[512,128]{1,0:T(8,128)S(1)}, f32[512,128]{1,0:T(8,128)S(1)}, u32[]{:S(2)}, u32[]{:S(2)}) collective-permute-start(f32[512,128]{1,0:T(8,128)S(1)} %add_select_fusion), channel_id=1, source_target_pairs={{0,3},{1,0},{2,1},{3,2},{4,7},{5,4},{6,5},{7,6},{8,11},{9,8},{10,9... | collective-permute-start | bytes 786440 | tf_op jit(solution)/shard_map/ppermute | solution.py:228
  129.7 5.1 %collective-permute-start.24 = (f32[256,128]{1,0:T(8,128)S(1)}, f32[256,128]{1,0:T(8,128)S(1)}, u32[]{:S(2)}, u32[]{:S(2)}) collective-permute-start(f32[256,128]{1,0:T(8,128)S(1)} %slice.90), channel_id=1, source_target_pairs={{0,1},{1,2},{2,3},{3,0},{4,5},{5,6},{6,7},{7,4},{8,9},{9,10},{10,1... | collective-permute-start | bytes 393224 | tf_op jit(solution)/shard_map/ppermute | solution.py:228
  130.6 4.2 %collective-permute-start.25 = (f32[256,128]{1,0:T(8,128)S(1)}, f32[256,128]{1,0:T(8,128)S(1)}, u32[]{:S(2)}, u32[]{:S(2)}) collective-permute-start(f32[256,128]{1,0:T(8,128)S(1)} %slice.91), channel_id=1, source_target_pairs={{0,3},{1,0},{2,1},{3,2},{4,7},{5,4},{6,5},{7,6},{8,11},{9,8},{10,9... | collective-permute-start | bytes 393224 | tf_op jit(solution)/shard_map/ppermute | solution.py:228
  137.6 3.0 %collective-permute-start.17 = (f32[8,256,128]{2,1,0:T(8,128)}, f32[8,256,128]{2,1,0:T(8,128)}, u32[]{:S(2)}, u32[]{:S(2)}) collective-permute-start(f32[8,256,128]{2,1,0:T(8,128)} %get-tuple-element.25), channel_id=1, source_target_pairs={{0,16},{1,17},{2,18},{3,19},{4,20},{5,21},{6,22},{7,23},{8,24},{9,... | collective-permute-start | bytes 3145736 | tf_op jit(solution)/shard_map/ppermute | solution.py:228
  137.7 15.2 %collective-permute-start.26 = (f32[4,512,128]{2,1,0:T(8,128)S(1)}, f32[4,512,128]{2,1,0:T(8,128)S(1)}, u32[]{:S(2)}, u32[]{:S(2)}) collective-permute-start(f32[4,512,128]{2,1,0:T(8,128)S(1)} %pad_maximum_fusion.refs_0_), channel_id=1, source_target_pairs={{0,4},{1,5},{2,6},{3,7},{4,8},{5,9},{6,10},{7,11},{8,12},{9,13},{1... | collective-permute-start | bytes 3145736 | tf_op jit(solution)/shard_map/ppermute | solution.py:228
  139.2 14.0 %collective-permute-start.27 = (f32[4,512,128]{2,1,0:T(8,128)S(1)}, f32[4,512,128]{2,1,0:T(8,128)}, u32[]{:S(2)}, u32[]{:S(2)}) collective-permute-start(f32[4,512,128]{2,1,0:T(8,128)S(1)} %pad_maximum_fusion.refs_0_), channel_id=1, source_target_pairs={{0,12},{1,13},{2,14},{3,15},{4,0},{5,1},{6,2},{7,3},{8,4},{9,5},{1... | collective-permute-start | bytes 3145736 | tf_op jit(solution)/shard_map/ppermute | solution.py:228
  153.3 9.6 %collective-permute-start.28 = (f32[2,512,128]{2,1,0:T(8,128)S(1)}, f32[2,512,128]{2,1,0:T(8,128)S(1)}, u32[]{:S(2)}, u32[]{:S(2)}) collective-permute-start(f32[2,512,128]{2,1,0:T(8,128)S(1)} %slice.76), channel_id=1, source_target_pairs={{0,4},{1,5},{2,6},{3,7},{4,8},{5,9},{6,10},{7,11},{8,12},{9,13},{1... | collective-permute-start | bytes 1572872 | tf_op jit(solution)/shard_map/ppermute | solution.py:228
  155.0 8.4 %collective-permute-start.29 = (f32[2,512,128]{2,1,0:T(8,128)S(1)}, f32[2,512,128]{2,1,0:T(8,128)S(1)}, u32[]{:S(2)}, u32[]{:S(2)}) collective-permute-start(f32[2,512,128]{2,1,0:T(8,128)S(1)} %slice.77), channel_id=1, source_target_pairs={{0,12},{1,13},{2,14},{3,15},{4,0},{5,1},{6,2},{7,3},{8,4},{9,5},{1... | collective-permute-start | bytes 1572872 | tf_op jit(solution)/shard_map/ppermute | solution.py:228
  166.1 8.0 %collective-permute-start.30 = (f32[256,1024]{1,0:T(8,128)S(1)}, f32[256,1024]{1,0:T(8,128)S(1)}, u32[]{:S(2)}, u32[]{:S(2)}) collective-permute-start(f32[256,1024]{1,0:T(8,128)S(1)} %slice.93), channel_id=1, source_target_pairs={{0,16},{1,17},{2,18},{3,19},{4,20},{5,21},{6,22},{7,23},{8,24},{9,... | collective-permute-start | bytes 3145736 | tf_op jit(solution)/shard_map/ppermute | solution.py:228
  (27 other events, 87.5 us)

commit v10 on v9

--- a/solution.py
+++ b/solution.py
@@ -106,13 +106,14 @@
         rhs_ref, x_ref, out_ref = refs[-3:]
         out_ref[...] = rhs_ref[...]
         for ref, parts in zip(refs, places):
-            ((half, steps, _, row, rows),) = parts
-            half = {"own": info[0], "pair": 1 - info[0]}[half]
-            k = 4 * half + lax.rem(info[1] + steps, 4)
-            right = pack_right(x_ref[pl.ds(pl.multiple_of(k * TILE, TILE), TILE), :])
-            for start in range(0, rows, TILE):
-                there = pl.ds(row + start, TILE)
-                out_ref[there, :] = out_ref[there, :] - packed_product(pack_left(ref[pl.ds(start, TILE), :]), right)
+            for half, steps, start, to, rows in parts:
+                half = {"own": info[0], "pair": 1 - info[0]}[half]
+                k = 4 * half + lax.rem(info[1] + steps, 4)
+                right = pack_right(x_ref[pl.ds(pl.multiple_of(k * TILE, TILE), TILE), :])
+                for n in range(0, rows, TILE):
+                    there = pl.ds(to + n, TILE)
+                    left = pack_left(ref[pl.ds(start + n, TILE), :])
+                    out_ref[there, :] = out_ref[there, :] - packed_product(left, right)
 
     return pl.pallas_call(
         body,
@@ -141,11 +142,30 @@
     )(factor)
 
 
-def prepare_body(info, mine_ref, other_ref, high_ref, low_ref):
-    for side, ref in enumerate((mine_ref, other_ref)):
+def arrange_rhs_body(info, rhs_ref, out_ref):
+    for n in range(8):
+        to = jnp.where(info[0] == 0, n, (n + 4) % 8)
+        out_ref[to, :, :] = rhs_ref[0, :, pl.ds(n * TILE, TILE)]
+
+
+def arrange_rhs(yh, rhs):
+    return pl.pallas_call(
+        arrange_rhs_body,
+        grid=(1,),
+        out_shape=jax.ShapeDtypeStruct((8, 64, TILE), F32),
+        in_specs=[SM, pl.BlockSpec((1, 64, 1024), lambda i: (0, 0, 0))],
+        out_specs=pl.BlockSpec((8, 64, TILE), lambda i: (0, 0, 0)),
+        compiler_params=PARAMS,
+        name="arrange_rhs",
+    )(jnp.reshape(yh, (1,)).astype(jnp.int32), rhs)
+
+
+def prepare_body(info, left_ref, other_ref, high_ref, low_ref):
+    for side, ref in enumerate((left_ref, other_ref)):
         rows = pl.ds(256 * side, 256)
+        first = 8 * info[1] if side == 0 else 0
         for n in range(4):
-            high, low = split(jnp.concatenate([ref[2 * n], ref[2 * n + 1]], 1))
+            high, low = split(jnp.concatenate([ref[first + 2 * n], ref[first + 2 * n + 1]], 1))
             high_ref[n, rows, :] = high
             low_ref[n, rows, :] = low
 
@@ -157,7 +177,7 @@
                 low_ref[n, pl.ds(256 * side, 64), :] = jnp.zeros((64, 256), BF16)
 
 
-def prepare(info, mine, other):
+def prepare(info, left, other):
     return pl.pallas_call(
         prepare_body,
         out_shape=[jax.ShapeDtypeStruct((4, 512, 256), BF16)] * 2,
@@ -165,7 +185,7 @@
         out_specs=[VM, VM],
         compiler_params=PARAMS,
         name="prepare_update",
-    )(info, mine, other)
+    )(info, left, other)
 
 
 def accumulate(info, sums, high, low, pieces, places, name):
@@ -257,43 +277,47 @@
     return after, far_low, far_high, before
 
 
-def gather_first(lead, yl):
+def gather(lead, half, core, yl):
     def holds(a, b, c):
-        return a == 0 and b == 0 and c < 2
-
-    swapped = move(lead, lambda a, b, c, d: (a, b, 1 - c, d) if holds(a, b, c) else None)
-    full = jnp.where(yl == 0, lead, swapped)
-    lower = jnp.where(yl == 0, swapped[512:], lead[512:])
-    pair = jnp.concatenate([full, lower], 0)
-
-    def along(step):
-        return lambda a, b, c, d: (a, b, c, d + step) if holds(a, b, c) else None
-
-    before, after = move(pair, along(1)), move(pair, along(-1))
-    far_low, far_high = move(before[:768], along(1)), move(after[768:], along(-1))
-    pieces, places = [], []
-    for piece, steps in ((pair, 0), (after, 1), (before, 3)):
-        pieces.append(piece)
-        places.append([(0, steps, 0, 0, 1024), (1, steps, 1024, 512, 512)])
-    pieces += [far_low, far_high]
-    places += [[(0, 2, 0, 0, 768)], [(0, 2, 0, 768, 256), (1, 2, 256, 512, 512)]]
-    return pieces, places
-
-
-def gather_second(lead):
-    def along(step):
-        return lambda a, b, c, d: (0, 1, c, d + step) if a == 0 and b == 1 else None
-
-    def pair(value):
-        return move(value, lambda a, b, c, d: (0, 1, c + 1 - 2 * (c % 2), d) if a == 0 and b == 1 else None)
-
-    before, after = move(lead, along(1)), move(lead, along(-1))
-    far_low, far_high = move(before[:512], along(1)), move(after[512:], along(-1))
-    pieces, places = [], []
-    for piece, steps, row in ((lead, 0, 0), (after, 1, 0), (before, 3, 0), (far_low, 2, 0), (far_high, 2, 512)):
-        pieces += [piece, pair(piece)]
-        places += [[(half, steps, 0, row, piece.shape[0])] for half in ("own", "pair")]
-    return pieces, places
+        return a == 0 and (b == 1 or c < 2)
+
+    def step(b_on_z, amount):
+        def where(a, b, c, d):
+            if not holds(a, b, c):
+                return None
+            return (a, b, c, d + amount) if b == b_on_z else (a, b, c + 1 - 2 * (c % 2), d)
+
+        return where
+
+    def only(b_only, amount):
+        return lambda a, b, c, d: (a, b, c, d + amount) if holds(a, b, c) and b == b_only else None
+
+    mixed = move(lead, step(1, 1))
+    after = move(lead, only(1, -1))
+    swapped = move(lead, lambda a, b, c, d: (a, b, c + 1 - 2 * (c % 2), d) if holds(a, b, c) and b == 1 else None)
+    mixed, swapped, half = lax.optimization_barrier((mixed, swapped, half))
+    far_low = move(mixed[:512], only(1, 1))
+    far_high = move(after[512:], only(1, -1))
+
+    full = jnp.where(yl == 0, lead, mixed)
+    lower = jnp.where(yl == 0, mixed[512:], lead[512:])
+    zero = core == 0
+    first = jnp.concatenate([jnp.where(zero, full, mixed), jnp.where(zero, lower, far_low)], 0)
+    second = jnp.concatenate([jnp.where(zero, full, after), jnp.where(zero, lower, far_high)], 0)
+    got_first = move(first, step(0, 1))
+    got_second = move(second, step(0, -1))
+    end_low = move(got_first[:768], only(0, 1))
+    end_high = move(got_second[768:], only(0, -1))
+
+    corner_pieces = [first, got_second, got_first, end_low, end_high]
+    corner_places = [[(0, n, 0, 0, 1024), (1, n, 1024, 512, 512)] for n in (0, 1, 3)]
+    corner_places += [[(0, 2, 0, 0, 768)], [(0, 2, 0, 768, 256), (1, 2, 256, 512, 512)]]
+    lower_pieces = [lead, swapped, first, second, got_first, got_second]
+    lower_places = [[("own", 0, 0, 0, 1024)], [("pair", 0, 0, 0, 1024)]]
+    for group in ("own", "pair"):
+        lower_places.append([(group, 3, 0, 0, 1024), (group, 2, 1024, 0, 512)])
+        lower_places.append([(group, 1, 0, 0, 1024), (group, 2, 1024, 512, 512)])
+    return (corner_pieces, corner_places), (lower_pieces, lower_places), half
 
 
 def shards(factor, cross_cov):
@@ -308,30 +332,25 @@
     info = jnp.stack([diagonal.astype(jnp.int32), (4 * yl + z).astype(jnp.int32)])
     lead = invert_diagonal(info, local[0])
 
-    own_rhs = rhs[0].reshape(64, 2, 4, TILE).transpose(1, 2, 0, 3)
-    own_rhs = jnp.where(yh == 0, own_rhs, own_rhs[::-1]).reshape(8, 64, TILE)
-    half = lax.all_to_all(own_rhs, ("yl", "z"), 0, 0, tiled=True).reshape(512, TILE)
+    half = lax.all_to_all(arrange_rhs(yh, rhs), ("yl", "z"), 0, 0, tiled=True).reshape(512, TILE)
+    upper_left, lower_row, half = gather(lead, half, core, yl)
     other_half = move(half, lambda a, b, c, d: (0, b, 3 - c, d) if a == 0 and c >= 2 else None)
     columns = jnp.concatenate([half, other_half], 0)
 
     place = jnp.stack([yl, z]).astype(jnp.int32)
-    upper_left = gather_first(lead, yl)
-    lower_row = gather_second(lead)
     first = solve(place, *upper_left, columns)
     sent = move(first, lambda a, b, c, d: (0, 1, c, d) if (a, b) == (0, 0) and c < 2 else None)
     rest = residual(place, *lower_row, columns, sent)
     second_rhs = move(rest, lambda a, b, c, d: (0, 1, 3 - c, d) if (a, b) == (0, 1) and c < 2 else None)
-    by_rows, second_rhs = lax.optimization_barrier((arrange(local), second_rhs))
+    by_rows, rest = lax.optimization_barrier((arrange(local), rest))
     left = lax.all_to_all(by_rows, COL, 0, 0, tiled=True)
     second = solve(place, *lower_row, second_rhs)
-    mine = deal(first, second, core, yh, xi)
+    mine, left = lax.optimization_barrier((deal(first, second, core, yh, xi), left))
 
     def swap(value):
         return move(value, lambda a, b, c, d: (a, 1 - b, c, d))
 
-    left = left.reshape(2, 8, 256, TILE)
-    kept = jnp.where(core == 0, left[0], left[1])
-    given = jnp.where(core == 0, left[1], left[0])
+    given = swap(lax.dynamic_slice_in_dim(left, 8 * (1 - core), 8, 0))
     info2 = jnp.stack([xi, core, 2 * yh + yl, z, col_id]).astype(jnp.int32)
 
     after, far_low, far_high, before = ring(mine, True)
@@ -341,7 +360,7 @@
         return lambda a, b, c, d: (a, b, c + step, d) if b == 0 else (a, b, c, d + step)
 
     before, after = move(near, along(1)), move(near, along(-1))
-    high, low = prepare(info2[:1], kept, swap(given))
+    high, low = prepare(info2[:2], left, given)
     sums = accumulate(info2, None, high, low, [near], [(0, 0)], "update_near")
     before, after, sums = lax.optimization_barrier((before, after, sums))
     far_low, far_high = move(before[:2], along(1)), move(after[2:], along(-1))

time: 176 us -> 182 us (1.034)
  blocking collectives: 11.9 us -> 0 us
  starting transfers between devices: 38.8 us -> 46.5 us
  waiting for transfers between devices: 87.5 us -> 94.4 us
  local copies, waits for them, and re-layouts: 6.57 us -> 12 us
    all_to_all x1 -> x0, blocking collectives: 11.9 us -> none  [shards(): lax.all_to_all(own_rhs, ('yl', 'z'), 0, 0, tiled=True).reshape(512, TILE)]
    all_to_all x0 -> x1, starting transfers between devices: none -> 6.05 us  [shards(): lax.all_to_all(arrange_rhs(yh, rhs), ('yl', 'z'), 0, 0, tiled=True)]
    all_to_all x0 -> x1, waiting for transfers between devices: none -> 5.39 us  [shards(): lax.all_to_all(arrange_rhs(yh, rhs), ('yl', 'z'), 0, 0, tiled=True)]
    unnamed x36 -> x35, local copies, waits for them, and re-layouts: 2.91 us -> 7.29 us
    select_n x4 -> x2, other arithmetic: 2.85 us -> 0.15 us  [the longest x1 0.09 us: gather(): jnp.where(zero, full, after)]
    ppermute x31 -> x26, starting transfers between devices: 34 us -> 35.9 us  [move(): return lax.ppermute(value, AXES, pairs)]
    ppermute x31 -> x26, waiting for transfers between devices: 87.5 us -> 89 us  [move(): return lax.ppermute(value, AXES, pairs)]
  transfers between devices with their start and end apart: 32 -> 28, of which waited for: 9 -> 10; matrix products, arithmetic and copies ran while one was open for 2% -> 2% of each run, Pallas kernels for 11% -> 9%
where the time goes in v10:
time: 182 us; the launch traced here: 181 us
  waiting for transfers between devices  94.4 us (52%)
  starting transfers between devices  46.5 us (26%)
  Pallas kernels  24.9 us (14%)
  local copies, waits for them, and re-layouts  12 us (7%)
  other arithmetic  2.92 us (2%)
    ppermute x26, waiting for transfers between devices, move(): return lax.ppermute(value, AXES, pairs)  89 us
    ppermute x26, starting transfers between devices, move(): return lax.ppermute(value, AXES, pairs)  35.9 us
    pallas_call x3, Pallas kernels, accumulate(): pl.pallas_call(body, out_shape=jax.ShapeDtypeStruct((512, 1024), F32), in...  11.2 us
    pallas_call x2, Pallas kernels, solve(): pl.pallas_call(body, out_shape=jax.ShapeDtypeStruct(rhs.shape, F32), in_s...  8.16 us
    unnamed x35, local copies, waits for them, and re-layouts  7.29 us
    all_to_all x1, starting transfers between devices, shards(): lax.all_to_all(arrange_rhs(yh, rhs), ('yl', 'z'), 0, 0, tiled=True)  6.05 us
    all_to_all x1, waiting for transfers between devices, shards(): lax.all_to_all(arrange_rhs(yh, rhs), ('yl', 'z'), 0, 0, tiled=True)  5.39 us
    all_to_all x1, starting transfers between devices, shards(): left = lax.all_to_all(by_rows, COL, 0, 0, tiled=True)  4.61 us
  transfers between devices with their start and end apart: 28, of which 10 were waited for; matrix products, arithmetic and copies ran while one was open for 2% of the time, Pallas kernels for 9%

profile of v10, /device:TPU:5, one launch (start us, length us, event | category | flops | bytes accessed | tf_op | source)
XLA Modules:
  0.0 181.4 jit_solution(2162830706408939150)
XLA Ops:
  4.7 6.0 %all-to-all-start = ((f32[8,64,128]{2,1,0:T(8,128)}), f32[8,64,128]{2,1,0:T(8,128)S(1)}, u32[]{:S(2)}, u32[]{:S(2)}) async-start(f32[8,64,128]{2,1,0:T(8,128)} %arrange_rhs.1), calls=%async_computation | async-start | bytes 524288 | tf_op jit(solution)/shard_map/all_to_all | solution.py:335
  11.4 5.4 %all-to-all-done = f32[8,64,128]{2,1,0:T(8,128)S(1)} async-done(((f32[8,64,128]{2,1,0:T(8,128)}), f32[8,64,128]{2,1,0:T(8,128)S(1)}, u32[]{:S(2)}, u32[]{:S(2)}) %all-to-all-start) | async-done | bytes 262176 | tf_op jit(solution)/shard_map/all_to_all | solution.py:335
  22.3 3.4 %block_solve.2 = f32[1024,128]{1,0:T(8,128)S(1)} custom-call(s32[2]{0:T(128)S(1)} %pad_add_fusion.1.info, f32[1536,128]{1,0:T(8,128)S(1)} %pad_maximum_fusion.1.refs_0_.refs_2_, f32[1536,128]{1,0:T(8,128)S(1)} %collective-permute-done.5.refs_1_.refs_5_, f32[1536,128]{1,0:T(8,128)S(1)} %collective-permute-done.6.refs_2_.refs_4_, ...), custom_call_target="tpu_custom_call" | custom-call | tf_op jit(solution)/shard_map/block_solve/pallas_call | solution.py:93
  27.4 2.6 %block_residual.1 = f32[1024,128]{1,0:T(8,128)} custom-call(s32[2]{0:T(128)S(1)} %pad_add_fusion.1.info, f32[1024,128]{1,0:T(8,128)S(1)} %invert_diagonal.1.refs_0_, f32[1024,128]{1,0:T(8,128)S(1)} %copy-done.13, f32[1536,128]{1,0:T(8,128)S(1)} %pad_maximum_fusion.1.refs_0_.refs_2_, f32[1536,128]{1,0:T(8,128)S(1)} %pad_maximum_fusion.2.refs_3_, ...), custom_call_target="tpu_custom_call" | custom-call | tf_op jit(solution)/shard_map/block_residual/pallas_call | solution.py:118
  30.1 1.5 collective-permute-start.11
  31.7 1.3 copy-done.4
  33.0 4.6 %all-to-all-start.1 = ((f32[16,256,128]{2,1,0:T(8,128)}), f32[16,256,128]{2,1,0:T(8,128)S(1)}, u32[]{:S(2)}, u32[]{:S(2)}) async-start(f32[16,256,128]{2,1,0:T(8,128)} %copy-done.4), calls=%async_computation.1 | async-start | bytes 4194304 | tf_op jit(solution)/shard_map/all_to_all | solution.py:346
  42.1 4.8 %block_solve.3 = f32[1024,128]{1,0:T(8,128)S(1)} custom-call(s32[2]{0:T(128)S(1)} %pad_add_fusion.1.info, f32[1024,128]{1,0:T(8,128)S(1)} %invert_diagonal.1.refs_0_, f32[1024,128]{1,0:T(8,128)S(1)} %copy-done.14, f32[1536,128]{1,0:T(8,128)S(1)} %pad_maximum_fusion.1.refs_0_.refs_2_, f32[1536,128]{1,0:T(8,128)S(1)} %copy-done.6, f32[1536,128]{1,0:T(8,128)S(1)} %copy-done.1, ...), custom_call_target="tpu_custom_call" | custom-call | tf_op jit(solution)/shard_map/block_solve/pallas_call | solution.py:93
  50.4 68.3 %collective-permute-done.15 = f32[512,128]{1,0:T(8,128)S(1)} collective-permute-done((f32[512,128]{1,0:T(8,128)S(1)}, f32[512,128]{1,0:T(8,128)S(1)}, u32[]{:S(2)}, u32[]{:S(2)}) %collective-permute-start.15) | collective-permute-done | bytes 262176 | tf_op jit(solution)/shard_map/ppermute | solution.py:248
  118.8 11.2 %collective-permute-start.18 = (f32[512,128]{1,0:T(8,128)S(1)}, f32[512,128]{1,0:T(8,128)S(1)}, u32[]{:S(2)}, u32[]{:S(2)}) collective-permute-start(f32[512,128]{1,0:T(8,128)S(1)} %add_select_fusion), channel_id=1, source_target_pairs={{0,1},{1,2},{2,3},{3,0},{4,5},{5,6},{6,7},{7,4},{8,9},{9,10},{10,1... | collective-permute-start | bytes 786440 | tf_op jit(solution)/shard_map/ppermute | solution.py:248
  130.0 3.3 %collective-permute-done.18 = f32[512,128]{1,0:T(8,128)S(1)} collective-permute-done((f32[512,128]{1,0:T(8,128)S(1)}, f32[512,128]{1,0:T(8,128)S(1)}, u32[]{:S(2)}, u32[]{:S(2)}) %collective-permute-start.18) | collective-permute-done | bytes 262176 | tf_op jit(solution)/shard_map/ppermute | solution.py:248
  133.3 2.1 %collective-permute-start.19 = (f32[256,128]{1,0:T(8,128)S(1)}, f32[256,128]{1,0:T(8,128)S(1)}, u32[]{:S(2)}, u32[]{:S(2)}) collective-permute-start(f32[256,128]{1,0:T(8,128)S(1)} %slice.71), channel_id=1, source_target_pairs={{0,1},{1,2},{2,3},{3,0},{4,5},{5,6},{6,7},{7,4},{8,9},{9,10},{10,1... | collective-permute-start | bytes 393224 | tf_op jit(solution)/shard_map/ppermute | solution.py:248
  140.4 1.6 collective-permute-start.22
  142.2 1.6 prepare_update.1
  143.7 3.2 %update_near.1.refs_0_ = f32[512,1024]{1,0:T(8,128)S(1)} custom-call(s32[5]{0:T(128)S(1)} %stack.59.info, bf16[4,512,256]{2,1,0:T(8,128)(2,1)S(1)} %get-tuple-element.24.high_ref, bf16[4,512,256]{2,1,0:T(8,128)(2,1)S(1)} %get-tuple-element.25.low_ref, f32[4,512,128]{2,1,0:T(8,128)} %pad_maximum_fusion.refs_0_), custom_call_target="tpu_custom_call" | custom-call | tf_op jit(solution)/shard_map/update_near/pallas_call | solution.py:224
  146.9 7.8 %collective-permute-done.22.refs_1_ = f32[4,512,128]{2,1,0:T(8,128)} collective-permute-done((f32[4,512,128]{2,1,0:T(8,128)}, f32[4,512,128]{2,1,0:T(8,128)}, u32[]{:S(2)}, u32[]{:S(2)}) %collective-permute-start.22) | collective-permute-done | bytes 1048608 | tf_op jit(solution)/shard_map/ppermute | solution.py:248
  154.7 2.8 %collective-permute-done.21.refs_2_ = f32[4,512,128]{2,1,0:T(8,128)} collective-permute-done((f32[4,512,128]{2,1,0:T(8,128)}, f32[4,512,128]{2,1,0:T(8,128)}, u32[]{:S(2)}, u32[]{:S(2)}) %collective-permute-start.21) | collective-permute-done | bytes 1048608 | tf_op jit(solution)/shard_map/ppermute | solution.py:248
  159.7 1.5 collective-permute-start.23
  161.2 5.4 %update_next.1.refs_0_ = f32[512,1024]{1,0:T(8,128)S(1)} custom-call(s32[5]{0:T(128)S(1)} %stack.59.info, bf16[4,512,256]{2,1,0:T(8,128)(2,1)S(1)} %get-tuple-element.24.high_ref, bf16[4,512,256]{2,1,0:T(8,128)(2,1)S(1)} %get-tuple-element.25.low_ref, f32[512,1024]{1,0:T(8,128)S(1)} %update_near.1.refs_0_, ...), custom_call_target="tpu_custom_call", output_to_operand_aliasing={{}: (3, {})} | custom-call | tf_op jit(solution)/shard_map/update_next/pallas_call | solution.py:224
  166.6 1.4 collective-permute-done.24.refs_2_
  168.0 1.3 collective-permute-done.23.refs_1_
  169.3 2.6 %update_far.1 = f32[512,1024]{1,0:T(8,128)S(1)} custom-call(s32[5]{0:T(128)S(1)} %stack.59.info, bf16[4,512,256]{2,1,0:T(8,128)(2,1)S(1)} %get-tuple-element.24.high_ref, bf16[4,512,256]{2,1,0:T(8,128)(2,1)S(1)} %get-tuple-element.25.low_ref, f32[512,1024]{1,0:T(8,128)S(1)} %update_next.1.refs_0_, ...), custom_call_target="tpu_custom_call", output_to_operand_aliasing={{}: (3, {})} | custom-call | tf_op jit(solution)/shard_map/update_far/pallas_call | solution.py:224
  172.1 5.9 %collective-permute-start.25 = (f32[256,1024]{1,0:T(8,128)S(1)}, f32[256,1024]{1,0:T(8,128)S(1)}, u32[]{:S(2)}, u32[]{:S(2)}) collective-permute-start(f32[256,1024]{1,0:T(8,128)S(1)} %slice.74), channel_id=1, source_target_pairs={{0,16},{1,17},{2,18},{3,19},{4,20},{5,21},{6,22},{7,23},{8,24},{9,... | collective-permute-start | bytes 3145736 | tf_op jit(solution)/shard_map/ppermute | solution.py:248
  177.9 2.3 %collective-permute-done.25 = f32[256,1024]{1,0:T(8,128)S(1)} collective-permute-done((f32[256,1024]{1,0:T(8,128)S(1)}, f32[256,1024]{1,0:T(8,128)S(1)}, u32[]{:S(2)}, u32[]{:S(2)}) %collective-permute-start.25) | collective-permute-done | bytes 1048608 | tf_op jit(solution)/shard_map/ppermute | solution.py:248
  (105 shorter events, 29.0 us)
Async XLA Ops:
  1.8 8.9 %collective-permute-start.3 = (f32[1024,128]{1,0:T(8,128)S(1)}, f32[1024,128]{1,0:T(8,128)S(1)}, u32[]{:S(2)}, u32[]{:S(2)}) collective-permute-start(f32[1024,128]{1,0:T(8,128)S(1)} %invert_diagonal.1.refs_0_), channel_id=1, source_target_pairs={{16,19},{17,16},{18,17},{19,18},{20,23},{21,20},{22,21},{23,22},{2... | collective-permute-start | bytes 1572872 | tf_op jit(solution)/shard_map/ppermute | solution.py:248
  2.5 14.3 %collective-permute-start.1 = (f32[1024,128]{1,0:T(8,128)S(1)}, f32[1024,128]{1,0:T(8,128)S(1)}, u32[]{:S(2)}, u32[]{:S(2)}) collective-permute-start(f32[1024,128]{1,0:T(8,128)S(1)} %invert_diagonal.1.refs_0_), channel_id=1, source_target_pairs={{16,20},{17,21},{18,22},{19,23},{20,16},{21,17},{22,18},{23,19},{2... | collective-permute-start | bytes 1572872 | tf_op jit(solution)/shard_map/ppermute | solution.py:248
  3.2 13.6 %collective-permute-start = (f32[1024,128]{1,0:T(8,128)S(1)}, f32[1024,128]{1,0:T(8,128)S(1)}, u32[]{:S(2)}, u32[]{:S(2)}) collective-permute-start(f32[1024,128]{1,0:T(8,128)S(1)} %invert_diagonal.1.refs_0_), channel_id=1, source_target_pairs={{0,4},{1,5},{2,6},{3,7},{4,0},{5,1},{6,2},{7,3},{16,17},{17,18},{1... | collective-permute-start | bytes 1572872 | tf_op jit(solution)/shard_map/ppermute | solution.py:248
  4.7 12.2 %all-to-all-start = ((f32[8,64,128]{2,1,0:T(8,128)}), f32[8,64,128]{2,1,0:T(8,128)S(1)}, u32[]{:S(2)}, u32[]{:S(2)}) async-start(f32[8,64,128]{2,1,0:T(8,128)} %arrange_rhs.1), calls=%async_computation | async-start | bytes 524288 | tf_op jit(solution)/shard_map/all_to_all | solution.py:335
  10.8 7.5 %collective-permute-start.4 = (f32[512,128]{1,0:T(8,128)S(1)}, f32[512,128]{1,0:T(8,128)S(1)}, u32[]{:S(2)}, u32[]{:S(2)}) collective-permute-start(f32[512,128]{1,0:T(8,128)S(1)} %slice.66), channel_id=1, source_target_pairs={{16,19},{17,16},{18,17},{19,18},{20,23},{21,20},{22,21},{23,22},{2... | collective-permute-start | bytes 786440 | tf_op jit(solution)/shard_map/ppermute | solution.py:248
  18.5 1.5 collective-permute-start.6
  19.3 1.5 collective-permute-start.5
  20.0 2.3 %collective-permute-start.7 = (f32[768,128]{1,0:T(8,128)S(1)}, f32[768,128]{1,0:T(8,128)S(1)}, u32[]{:S(2)}, u32[]{:S(2)}) collective-permute-start(f32[768,128]{1,0:T(8,128)S(1)} %slice.67), channel_id=1, source_target_pairs={{0,1},{1,2},{2,3},{3,0},{4,5},{5,6},{6,7},{7,4}} | collective-permute-start | bytes 1179656 | tf_op jit(solution)/shard_map/ppermute | solution.py:248
  20.8 1.6 collective-permute-start.8
  30.1 7.6 %collective-permute-start.11 = (f32[1024,128]{1,0:T(8,128)}, f32[1024,128]{1,0:T(8,128)}, u32[]{:S(2)}, u32[]{:S(2)}) collective-permute-start(f32[1024,128]{1,0:T(8,128)} %block_residual.1), channel_id=1, source_target_pairs={{16,28},{17,29},{18,30},{19,31},{20,24},{21,25},{22,26},{23,27}} | collective-permute-start | bytes 1572872 | tf_op jit(solution)/shard_map/ppermute | solution.py:248
  33.0 85.8 %all-to-all-start.1 = ((f32[16,256,128]{2,1,0:T(8,128)}), f32[16,256,128]{2,1,0:T(8,128)S(1)}, u32[]{:S(2)}, u32[]{:S(2)}) async-start(f32[16,256,128]{2,1,0:T(8,128)} %copy-done.4), calls=%async_computation.1 | async-start | bytes 4194304 | tf_op jit(solution)/shard_map/all_to_all | solution.py:346
  47.7 1.4 collective-permute-start.13
  48.4 2.0 %collective-permute-start.14 = (f32[512,128]{1,0:T(8,128)S(1)}, f32[512,128]{1,0:T(8,128)S(1)}, u32[]{:S(2)}, u32[]{:S(2)}) collective-permute-start(f32[512,128]{1,0:T(8,128)S(1)} %select_select_fusion.2), channel_id=1, source_target_pairs={{0,96},{1,97},{2,98},{3,99},{4,100},{5,101},{6,102},{7,103},{8,104... | collective-permute-start | bytes 786440 | tf_op jit(solution)/shard_map/ppermute | solution.py:248
  49.1 69.6 %collective-permute-start.15 = (f32[512,128]{1,0:T(8,128)S(1)}, f32[512,128]{1,0:T(8,128)S(1)}, u32[]{:S(2)}, u32[]{:S(2)}) collective-permute-start(f32[512,128]{1,0:T(8,128)S(1)} %collective-permute-done.13), channel_id=1, source_target_pairs={{32,64},{33,65},{34,66},{35,67},{36,68},{37,69},{38,70},{39,71},{4... | collective-permute-start | bytes 786440 | tf_op jit(solution)/shard_map/ppermute | solution.py:248
  118.8 14.5 %collective-permute-start.18 = (f32[512,128]{1,0:T(8,128)S(1)}, f32[512,128]{1,0:T(8,128)S(1)}, u32[]{:S(2)}, u32[]{:S(2)}) collective-permute-start(f32[512,128]{1,0:T(8,128)S(1)} %add_select_fusion), channel_id=1, source_target_pairs={{0,1},{1,2},{2,3},{3,0},{4,5},{5,6},{6,7},{7,4},{8,9},{9,10},{10,1... | collective-permute-start | bytes 786440 | tf_op jit(solution)/shard_map/ppermute | solution.py:248
  129.9 5.5 %collective-permute-start.17 = (f32[512,128]{1,0:T(8,128)S(1)}, f32[512,128]{1,0:T(8,128)S(1)}, u32[]{:S(2)}, u32[]{:S(2)}) collective-permute-start(f32[512,128]{1,0:T(8,128)S(1)} %add_select_fusion), channel_id=1, source_target_pairs={{0,3},{1,0},{2,1},{3,2},{4,7},{5,4},{6,5},{7,6},{8,11},{9,8},{10,9... | collective-permute-start | bytes 786440 | tf_op jit(solution)/shard_map/ppermute | solution.py:248
  133.3 5.1 %collective-permute-start.19 = (f32[256,128]{1,0:T(8,128)S(1)}, f32[256,128]{1,0:T(8,128)S(1)}, u32[]{:S(2)}, u32[]{:S(2)}) collective-permute-start(f32[256,128]{1,0:T(8,128)S(1)} %slice.71), channel_id=1, source_target_pairs={{0,1},{1,2},{2,3},{3,0},{4,5},{5,6},{6,7},{7,4},{8,9},{9,10},{10,1... | collective-permute-start | bytes 393224 | tf_op jit(solution)/shard_map/ppermute | solution.py:248
  135.4 3.9 %collective-permute-start.20 = (f32[256,128]{1,0:T(8,128)S(1)}, f32[256,128]{1,0:T(8,128)S(1)}, u32[]{:S(2)}, u32[]{:S(2)}) collective-permute-start(f32[256,128]{1,0:T(8,128)S(1)} %slice.72), channel_id=1, source_target_pairs={{0,3},{1,0},{2,1},{3,2},{4,7},{5,4},{6,5},{7,6},{8,11},{9,8},{10,9... | collective-permute-start | bytes 393224 | tf_op jit(solution)/shard_map/ppermute | solution.py:248
  137.5 4.7 %collective-permute-start.16 = (f32[8,256,128]{2,1,0:T(8,128)}, f32[8,256,128]{2,1,0:T(8,128)}, u32[]{:S(2)}, u32[]{:S(2)}) collective-permute-start(f32[8,256,128]{2,1,0:T(8,128)} %constant_dynamic-slice_fusion), channel_id=1, source_target_pairs={{0,16},{1,17},{2,18},{3,19},{4,20},{5,21},{6,22},{7,23},{8,24},{9,... | collective-permute-start | bytes 3145736 | tf_op jit(solution)/shard_map/ppermute | solution.py:248
  140.4 14.3 %collective-permute-start.22 = (f32[4,512,128]{2,1,0:T(8,128)}, f32[4,512,128]{2,1,0:T(8,128)}, u32[]{:S(2)}, u32[]{:S(2)}) collective-permute-start(f32[4,512,128]{2,1,0:T(8,128)} %pad_maximum_fusion.refs_0_), channel_id=1, source_target_pairs={{0,12},{1,13},{2,14},{3,15},{4,0},{5,1},{6,2},{7,3},{8,4},{9,5},{1... | collective-permute-start | bytes 3145736 | tf_op jit(solution)/shard_map/ppermute | solution.py:248
  142.0 15.5 %collective-permute-start.21 = (f32[4,512,128]{2,1,0:T(8,128)}, f32[4,512,128]{2,1,0:T(8,128)}, u32[]{:S(2)}, u32[]{:S(2)}) collective-permute-start(f32[4,512,128]{2,1,0:T(8,128)} %pad_maximum_fusion.refs_0_), channel_id=1, source_target_pairs={{0,4},{1,5},{2,6},{3,7},{4,8},{5,9},{6,10},{7,11},{8,12},{9,13},{1... | collective-permute-start | bytes 3145736 | tf_op jit(solution)/shard_map/ppermute | solution.py:248
  159.6 8.4 %collective-permute-start.24 = (f32[2,512,128]{2,1,0:T(8,128)S(1)}, f32[2,512,128]{2,1,0:T(8,128)S(1)}, u32[]{:S(2)}, u32[]{:S(2)}) collective-permute-start(f32[2,512,128]{2,1,0:T(8,128)S(1)} %slice.62), channel_id=1, source_target_pairs={{0,12},{1,13},{2,14},{3,15},{4,0},{5,1},{6,2},{7,3},{8,4},{9,5},{1... | collective-permute-start | bytes 1572872 | tf_op jit(solution)/shard_map/ppermute | solution.py:248
  159.7 9.6 %collective-permute-start.23 = (f32[2,512,128]{2,1,0:T(8,128)S(1)}, f32[2,512,128]{2,1,0:T(8,128)S(1)}, u32[]{:S(2)}, u32[]{:S(2)}) collective-permute-start(f32[2,512,128]{2,1,0:T(8,128)S(1)} %slice.61), channel_id=1, source_target_pairs={{0,4},{1,5},{2,6},{3,7},{4,8},{5,9},{6,10},{7,11},{8,12},{9,13},{1... | collective-permute-start | bytes 1572872 | tf_op jit(solution)/shard_map/ppermute | solution.py:248
  172.1 8.2 %collective-permute-start.25 = (f32[256,1024]{1,0:T(8,128)S(1)}, f32[256,1024]{1,0:T(8,128)S(1)}, u32[]{:S(2)}, u32[]{:S(2)}) collective-permute-start(f32[256,1024]{1,0:T(8,128)S(1)} %slice.74), channel_id=1, source_target_pairs={{0,16},{1,17},{2,18},{3,19},{4,20},{5,21},{6,22},{7,23},{8,24},{9,... | collective-permute-start | bytes 3145736 | tf_op jit(solution)/shard_map/ppermute | solution.py:248
  (21 other events, 64.3 us)

commit v11 on v10

--- a/solution.py
+++ b/solution.py
@@ -13,6 +13,7 @@
 PARAMS = pltpu.CompilerParams(vmem_limit_bytes=20 * 2**20)
 VM = pl.BlockSpec(memory_space=pltpu.VMEM)
 SM = pl.BlockSpec(memory_space=pltpu.SMEM)
+FAR = pl.BlockSpec(memory_space=pltpu.HBM)
 
 
 def split(value):
@@ -72,54 +73,84 @@
     )(info, lead)
 
 
-def solve(info, pieces, places, rhs):
+def solve(info, pieces, places, rhs, streamed, name):
+    count = len(pieces)
+
     def body(info, *refs):
-        rhs_ref, out_ref, tri_ref = refs[-3:]
-        for ref, parts in zip(refs, places):
-            for half, steps, start, to, rows in parts:
-                half = {"own": info[0], "pair": 1 - info[0]}.get(half, half)
-                k = 4 * half + lax.rem(info[1] + steps, 4)
-                tri_ref[k, pl.ds(to, rows), :] = pack_left(ref[pl.ds(start, rows), :])
-        out_ref[...] = rhs_ref[...]
-        for k in range(8):
-            here = pl.ds(k * TILE, TILE)
-            solved = packed_product(tri_ref[k, here, :], pack_right(out_ref[here, :]))
-            out_ref[here, :] = solved
-            right = pack_right(solved)
-            for i in range(k + 1, 8):
-                there = pl.ds(i * TILE, TILE)
-                out_ref[there, :] = out_ref[there, :] - packed_product(tri_ref[k, there, :], right)
-
+        sources, (rhs_ref, out_ref, tri_ref) = refs[:count], refs[count : count + 3]
+
+        @pl.when(info[2] == 1)
+        def _():
+            copies = []
+            if streamed:
+                buffers, semaphores = refs[count + 3 : 2 * count + 3], refs[-1]
+                for n in range(count):
+                    copies.append(pltpu.make_async_copy(sources[n], buffers[n], semaphores.at[n]))
+                    copies[-1].start()
+            else:
+                buffers = sources
+            for n in range(count):
+                if streamed:
+                    copies[n].wait()
+                for half, steps, start, to, rows in places[n]:
+                    half = {"own": info[0], "pair": 1 - info[0]}.get(half, half)
+                    k = 4 * half + lax.rem(info[1] + steps, 4)
+                    tri_ref[k, pl.ds(to, rows), :] = pack_left(buffers[n][pl.ds(start, rows), :])
+            out_ref[...] = rhs_ref[...]
+            for k in range(8):
+                here = pl.ds(k * TILE, TILE)
+                solved = packed_product(tri_ref[k, here, :], pack_right(out_ref[here, :]))
+                out_ref[here, :] = solved
+                right = pack_right(solved)
+                for i in range(k + 1, 8):
+                    there = pl.ds(i * TILE, TILE)
+                    out_ref[there, :] = out_ref[there, :] - packed_product(tri_ref[k, there, :], right)
+
+    scratch = [pltpu.VMEM((8, 1024, 256), BF16)]
+    if streamed:
+        scratch += [pltpu.VMEM(piece.shape, F32) for piece in pieces] + [pltpu.SemaphoreType.DMA((count,))]
     return pl.pallas_call(
         body,
         out_shape=jax.ShapeDtypeStruct(rhs.shape, F32),
-        in_specs=[SM] + [VM] * (len(pieces) + 1),
+        in_specs=[SM] + [FAR if streamed else VM] * count + [VM],
         out_specs=VM,
-        scratch_shapes=[pltpu.VMEM((8, 1024, 256), BF16)],
-        compiler_params=PARAMS,
-        name="block_solve",
+        scratch_shapes=scratch,
+        compiler_params=PARAMS,
+        name=name,
     )(info, *pieces, rhs)
 
 
 def residual(info, pieces, places, rhs, x):
+    count = len(pieces)
+
     def body(info, *refs):
-        rhs_ref, x_ref, out_ref = refs[-3:]
-        out_ref[...] = rhs_ref[...]
-        for ref, parts in zip(refs, places):
-            for half, steps, start, to, rows in parts:
-                half = {"own": info[0], "pair": 1 - info[0]}[half]
-                k = 4 * half + lax.rem(info[1] + steps, 4)
-                right = pack_right(x_ref[pl.ds(pl.multiple_of(k * TILE, TILE), TILE), :])
-                for n in range(0, rows, TILE):
-                    there = pl.ds(to + n, TILE)
-                    left = pack_left(ref[pl.ds(start + n, TILE), :])
-                    out_ref[there, :] = out_ref[there, :] - packed_product(left, right)
+        sources, (rhs_ref, x_ref, out_ref) = refs[:count], refs[count : count + 3]
+        buffers, semaphores = refs[count + 3 : 2 * count + 3], refs[-1]
+
+        @pl.when(info[2] == 1)
+        def _():
+            copies = []
+            for n in range(count):
+                copies.append(pltpu.make_async_copy(sources[n], buffers[n], semaphores.at[n]))
+                copies[-1].start()
+            out_ref[...] = rhs_ref[...]
+            for copy, ref, parts in zip(copies, buffers, places):
+                copy.wait()
+                for half, steps, start, to, rows in parts:
+                    half = {"own": info[0], "pair": 1 - info[0]}[half]
+                    k = 4 * half + lax.rem(info[1] + steps, 4)
+                    right = pack_right(x_ref[pl.ds(pl.multiple_of(k * TILE, TILE), TILE), :])
+                    for n in range(0, rows, TILE):
+                        there = pl.ds(to + n, TILE)
+                        left = pack_left(ref[pl.ds(start + n, TILE), :])
+                        out_ref[there, :] = out_ref[there, :] - packed_product(left, right)
 
     return pl.pallas_call(
         body,
         out_shape=jax.ShapeDtypeStruct(rhs.shape, F32),
-        in_specs=[SM] + [VM] * (len(pieces) + 2),
+        in_specs=[SM] + [FAR] * count + [VM, VM],
         out_specs=VM,
+        scratch_shapes=[pltpu.VMEM(piece.shape, F32) for piece in pieces] + [pltpu.SemaphoreType.DMA((count,))],
         compiler_params=PARAMS,
         name="block_residual",
     )(info, *pieces, rhs, x)
@@ -142,22 +173,21 @@
     )(factor)
 
 
-def arrange_rhs_body(info, rhs_ref, out_ref):
-    for n in range(8):
-        to = jnp.where(info[0] == 0, n, (n + 4) % 8)
-        out_ref[to, :, :] = rhs_ref[0, :, pl.ds(n * TILE, TILE)]
-
-
-def arrange_rhs(yh, rhs):
+def arrange_rhs_body(rhs_ref, out_ref):
+    for n in range(16):
+        out_ref[n, :, :] = rhs_ref[0, :, pl.ds(n % 8 * TILE, TILE)]
+
+
+def arrange_rhs(rhs):
     return pl.pallas_call(
         arrange_rhs_body,
         grid=(1,),
-        out_shape=jax.ShapeDtypeStruct((8, 64, TILE), F32),
-        in_specs=[SM, pl.BlockSpec((1, 64, 1024), lambda i: (0, 0, 0))],
-        out_specs=pl.BlockSpec((8, 64, TILE), lambda i: (0, 0, 0)),
+        out_shape=jax.ShapeDtypeStruct((16, 64, TILE), F32),
+        in_specs=[pl.BlockSpec((1, 64, 1024), lambda i: (0, 0, 0))],
+        out_specs=pl.BlockSpec((16, 64, TILE), lambda i: (0, 0, 0)),
         compiler_params=PARAMS,
         name="arrange_rhs",
-    )(jnp.reshape(yh, (1,)).astype(jnp.int32), rhs)
+    )(rhs)
 
 
 def prepare_body(info, left_ref, other_ref, high_ref, low_ref):
@@ -277,7 +307,7 @@
     return after, far_low, far_high, before
 
 
-def gather(lead, half, core, yl):
+def gather(lead, columns, core, yl):
     def holds(a, b, c):
         return a == 0 and (b == 1 or c < 2)
 
@@ -295,7 +325,7 @@
     mixed = move(lead, step(1, 1))
     after = move(lead, only(1, -1))
     swapped = move(lead, lambda a, b, c, d: (a, b, c + 1 - 2 * (c % 2), d) if holds(a, b, c) and b == 1 else None)
-    mixed, swapped, half = lax.optimization_barrier((mixed, swapped, half))
+    mixed, swapped, columns = lax.optimization_barrier((mixed, swapped, columns))
     far_low = move(mixed[:512], only(1, 1))
     far_high = move(after[512:], only(1, -1))
 
@@ -317,7 +347,7 @@
     for group in ("own", "pair"):
         lower_places.append([(group, 3, 0, 0, 1024), (group, 2, 1024, 0, 512)])
         lower_places.append([(group, 1, 0, 0, 1024), (group, 2, 1024, 512, 512)])
-    return (corner_pieces, corner_places), (lower_pieces, lower_places), half
+    return (corner_pieces, corner_places), (lower_pieces, lower_places), columns
 
 
 def shards(factor, cross_cov):
@@ -332,19 +362,19 @@
     info = jnp.stack([diagonal.astype(jnp.int32), (4 * yl + z).astype(jnp.int32)])
     lead = invert_diagonal(info, local[0])
 
-    half = lax.all_to_all(arrange_rhs(yh, rhs), ("yl", "z"), 0, 0, tiled=True).reshape(512, TILE)
-    upper_left, lower_row, half = gather(lead, half, core, yl)
-    other_half = move(half, lambda a, b, c, d: (0, b, 3 - c, d) if a == 0 and c >= 2 else None)
-    columns = jnp.concatenate([half, other_half], 0)
-
-    place = jnp.stack([yl, z]).astype(jnp.int32)
-    first = solve(place, *upper_left, columns)
+    columns = lax.all_to_all(arrange_rhs(rhs), COL, 0, 0, tiled=True).reshape(1024, TILE)
+    upper_left, lower_row, columns = gather(lead, columns, core, yl)
+
+    def place(active):
+        return jnp.stack([yl, z, (active & (xi == 0)).astype(jnp.int32)]).astype(jnp.int32)
+
+    first = solve(place((core == 0) & (yh == 0)), *upper_left, columns, False, "solve_first")
     sent = move(first, lambda a, b, c, d: (0, 1, c, d) if (a, b) == (0, 0) and c < 2 else None)
-    rest = residual(place, *lower_row, columns, sent)
+    rest = residual(place((core == 1) & (yh == 0)), *lower_row, columns, sent)
     second_rhs = move(rest, lambda a, b, c, d: (0, 1, 3 - c, d) if (a, b) == (0, 1) and c < 2 else None)
     by_rows, rest = lax.optimization_barrier((arrange(local), rest))
     left = lax.all_to_all(by_rows, COL, 0, 0, tiled=True)
-    second = solve(place, *lower_row, second_rhs)
+    second = solve(place((core == 1) & (yh == 1)), *lower_row, second_rhs, True, "solve_second")
     mine, left = lax.optimization_barrier((deal(first, second, core, yh, xi), left))
 
     def swap(value):

time: 182 us -> 182 us (level)
  waiting for transfers between devices: 94.4 us -> 104 us
  starting transfers between devices: 46.5 us -> 39.6 us
  Pallas kernels: 24.9 us -> 19.4 us
  local copies, waits for them, and re-layouts: 12 us -> 14.2 us
    ppermute x26 -> x25, starting transfers between devices: 35.9 us -> 28.1 us  [move(): return lax.ppermute(value, AXES, pairs)]
    ppermute x26 -> x25, waiting for transfers between devices: 89 us -> 94.7 us  [move(): return lax.ppermute(value, AXES, pairs)]
    pallas_call x2, Pallas kernels: 8.16 us -> 3.05 us  [solve(): pl.pallas_call(body, out_shape=jax.ShapeDtypeStruct(rhs.shape, F32), in_s...]
    all_to_all x1, waiting for transfers between devices: 5.39 us -> 8.87 us  [shards(): lax.all_to_all(arrange_rhs(rhs), COL, 0, 0, tiled=True).reshape(1024, TILE)]
    unnamed x35 -> x32, local copies, waits for them, and re-layouts: 7.29 us -> 7.99 us
  transfers between devices with their start and end apart: 28 -> 27, of which waited for: 10 -> 9; matrix products, arithmetic and copies ran while one was open for 2% -> 3% of each run, Pallas kernels for 9% -> 7%
where the time goes in v11:
time: 182 us; the launch traced here: 181 us
  waiting for transfers between devices  104 us (57%)
  starting transfers between devices  39.6 us (22%)
  Pallas kernels  19.4 us (11%)
  local copies, waits for them, and re-layouts  14.2 us (8%)
  other arithmetic  4.07 us (2%)
    ppermute x25, waiting for transfers between devices, move(): return lax.ppermute(value, AXES, pairs)  94.7 us
    ppermute x25, starting transfers between devices, move(): return lax.ppermute(value, AXES, pairs)  28.1 us
    pallas_call x3, Pallas kernels, accumulate(): pl.pallas_call(body, out_shape=jax.ShapeDtypeStruct((512, 1024), F32), in...  11.2 us
    all_to_all x1, waiting for transfers between devices, shards(): lax.all_to_all(arrange_rhs(rhs), COL, 0, 0, tiled=True).reshape(1024, TILE)  8.87 us
    unnamed x32, local copies, waits for them, and re-layouts  7.99 us
    all_to_all x1, starting transfers between devices, shards(): lax.all_to_all(arrange_rhs(rhs), COL, 0, 0, tiled=True).reshape(1024, TILE)  7.77 us
    all_to_all x1, starting transfers between devices, shards(): left = lax.all_to_all(by_rows, COL, 0, 0, tiled=True)  3.72 us
  transfers between devices with their start and end apart: 27, of which 9 were waited for; matrix products, arithmetic and copies ran while one was open for 3% of the time, Pallas kernels for 7%

profile of v11, /device:TPU:5, one launch (start us, length us, event | category | flops | bytes accessed | tf_op | source)
XLA Modules:
  0.0 181.3 jit_solution(5395408425327385852)
XLA Ops:
  4.8 7.8 %all-to-all-start = ((f32[16,64,128]{2,1,0:T(8,128)}), f32[16,64,128]{2,1,0:T(8,128)S(1)}, u32[]{:S(2)}, u32[]{:S(2)}) async-start(f32[16,64,128]{2,1,0:T(8,128)} %arrange_rhs.1), calls=%async_computation | async-start | bytes 1048576 | tf_op jit(solution)/shard_map/all_to_all | solution.py:365
  14.0 8.9 %all-to-all-done = f32[16,64,128]{2,1,0:T(8,128)S(1)} async-done(((f32[16,64,128]{2,1,0:T(8,128)}), f32[16,64,128]{2,1,0:T(8,128)S(1)}, u32[]{:S(2)}, u32[]{:S(2)}) %all-to-all-start) | async-done | bytes 524320 | tf_op jit(solution)/shard_map/all_to_all | solution.py:365
  27.3 1.4 collective-permute-start.7
  29.5 1.4 collective-permute-start.8
  31.0 1.9 %solve_first.1 = f32[1024,128]{1,0:T(8,128)} custom-call(s32[3]{0:T(128)S(1)} %pad_add_fusion.1.info, f32[1536,128]{1,0:T(8,128)S(1)} %pad_maximum_fusion.1.refs_0_.refs_2_, f32[1536,128]{1,0:T(8,128)S(1)} %collective-permute-done.5.refs_1_.refs_5_, f32[1536,128]{1,0:T(8,128)S(1)} %collective-permute-done.6.refs_2_.refs_4_, ...), custom_call_target="tpu_custom_call" | custom-call | tf_op jit(solution)/shard_map/solve_first/pallas_call | solution.py:112
  33.0 1.5 collective-permute-start.9
  36.7 2.1 %block_residual.1 = f32[1024,128]{1,0:T(8,128)} custom-call(s32[3]{0:T(128)S(1)} %pad_add_fusion.5.info, f32[1024,128]{1,0:T(8,128)S(1)} %invert_diagonal.1.refs_0_, f32[1024,128]{1,0:T(8,128)S(1)} %copy-done.14, f32[1536,128]{1,0:T(8,128)S(1)} %pad_maximum_fusion.1.refs_0_.refs_2_, f32[1536,128]{1,0:T(8,128)S(1)} %copy-done.6, ...), custom_call_target="tpu_custom_call" | custom-call | tf_op jit(solution)/shard_map/block_residual/pallas_call | solution.py:148
  38.8 1.5 collective-permute-start.10
  41.8 3.7 %all-to-all-start.1 = ((f32[16,256,128]{2,1,0:T(8,128)}), f32[16,256,128]{2,1,0:T(8,128)S(1)}, u32[]{:S(2)}, u32[]{:S(2)}) async-start(f32[16,256,128]{2,1,0:T(8,128)} %copy-done.4), calls=%async_computation.1 | async-start | bytes 4194304 | tf_op jit(solution)/shard_map/all_to_all | solution.py:376
  54.7 74.1 %collective-permute-done.14 = f32[512,128]{1,0:T(8,128)S(1)} collective-permute-done((f32[512,128]{1,0:T(8,128)S(1)}, f32[512,128]{1,0:T(8,128)S(1)}, u32[]{:S(2)}, u32[]{:S(2)}) %collective-permute-start.14) | collective-permute-done | bytes 262176 | tf_op jit(solution)/shard_map/ppermute | solution.py:278
  129.0 2.7 %collective-permute-start.16 = (f32[512,128]{1,0:T(8,128)S(1)}, f32[512,128]{1,0:T(8,128)S(1)}, u32[]{:S(2)}, u32[]{:S(2)}) collective-permute-start(f32[512,128]{1,0:T(8,128)S(1)} %add_select_fusion), channel_id=1, source_target_pairs={{0,3},{1,0},{2,1},{3,2},{4,7},{5,4},{6,5},{7,6},{8,11},{9,8},{10,9... | collective-permute-start | bytes 786440 | tf_op jit(solution)/shard_map/ppermute | solution.py:278
  131.6 3.8 %collective-permute-done.17 = f32[512,128]{1,0:T(8,128)S(1)} collective-permute-done((f32[512,128]{1,0:T(8,128)S(1)}, f32[512,128]{1,0:T(8,128)S(1)}, u32[]{:S(2)}, u32[]{:S(2)}) %collective-permute-start.17) | collective-permute-done | bytes 262176 | tf_op jit(solution)/shard_map/ppermute | solution.py:278
  135.5 2.7 %collective-permute-start.19 = (f32[256,128]{1,0:T(8,128)S(1)}, f32[256,128]{1,0:T(8,128)S(1)}, u32[]{:S(2)}, u32[]{:S(2)}) collective-permute-start(f32[256,128]{1,0:T(8,128)S(1)} %slice.72), channel_id=1, source_target_pairs={{0,3},{1,0},{2,1},{3,2},{4,7},{5,4},{6,5},{7,6},{8,11},{9,8},{10,9... | collective-permute-start | bytes 393224 | tf_op jit(solution)/shard_map/ppermute | solution.py:278
  141.6 1.6 collective-permute-start.21
  143.3 1.6 prepare_update.1
  144.9 3.2 %update_near.1.refs_0_ = f32[512,1024]{1,0:T(8,128)S(1)} custom-call(s32[5]{0:T(128)S(1)} %stack.87.info, bf16[4,512,256]{2,1,0:T(8,128)(2,1)S(1)} %get-tuple-element.24.high_ref, bf16[4,512,256]{2,1,0:T(8,128)(2,1)S(1)} %get-tuple-element.25.low_ref, f32[4,512,128]{2,1,0:T(8,128)} %pad_maximum_fusion.refs_0_), custom_call_target="tpu_custom_call" | custom-call | tf_op jit(solution)/shard_map/update_near/pallas_call | solution.py:254
  148.1 7.8 %collective-permute-done.21.refs_1_ = f32[4,512,128]{2,1,0:T(8,128)} collective-permute-done((f32[4,512,128]{2,1,0:T(8,128)}, f32[4,512,128]{2,1,0:T(8,128)}, u32[]{:S(2)}, u32[]{:S(2)}) %collective-permute-start.21) | collective-permute-done | bytes 1048608 | tf_op jit(solution)/shard_map/ppermute | solution.py:278
  155.8 2.8 %collective-permute-done.20.refs_2_ = f32[4,512,128]{2,1,0:T(8,128)} collective-permute-done((f32[4,512,128]{2,1,0:T(8,128)}, f32[4,512,128]{2,1,0:T(8,128)}, u32[]{:S(2)}, u32[]{:S(2)}) %collective-permute-start.20) | collective-permute-done | bytes 1048608 | tf_op jit(solution)/shard_map/ppermute | solution.py:278
  160.9 1.5 collective-permute-start.22
  162.3 5.4 %update_next.1.refs_0_ = f32[512,1024]{1,0:T(8,128)S(1)} custom-call(s32[5]{0:T(128)S(1)} %stack.87.info, bf16[4,512,256]{2,1,0:T(8,128)(2,1)S(1)} %get-tuple-element.24.high_ref, bf16[4,512,256]{2,1,0:T(8,128)(2,1)S(1)} %get-tuple-element.25.low_ref, f32[512,1024]{1,0:T(8,128)S(1)} %update_near.1.refs_0_, ...), custom_call_target="tpu_custom_call", output_to_operand_aliasing={{}: (3, {})} | custom-call | tf_op jit(solution)/shard_map/update_next/pallas_call | solution.py:254
  167.7 1.4 collective-permute-done.23.refs_2_
  170.5 2.6 %update_far.1 = f32[512,1024]{1,0:T(8,128)S(1)} custom-call(s32[5]{0:T(128)S(1)} %stack.87.info, bf16[4,512,256]{2,1,0:T(8,128)(2,1)S(1)} %get-tuple-element.24.high_ref, bf16[4,512,256]{2,1,0:T(8,128)(2,1)S(1)} %get-tuple-element.25.low_ref, f32[512,1024]{1,0:T(8,128)S(1)} %update_next.1.refs_0_, ...), custom_call_target="tpu_custom_call", output_to_operand_aliasing={{}: (3, {})} | custom-call | tf_op jit(solution)/shard_map/update_far/pallas_call | solution.py:254
  173.2 4.6 %collective-permute-start.24 = (f32[256,1024]{1,0:T(8,128)S(1)}, f32[256,1024]{1,0:T(8,128)S(1)}, u32[]{:S(2)}, u32[]{:S(2)}) collective-permute-start(f32[256,1024]{1,0:T(8,128)S(1)} %slice.74), channel_id=1, source_target_pairs={{0,16},{1,17},{2,18},{3,19},{4,20},{5,21},{6,22},{7,23},{8,24},{9,... | collective-permute-start | bytes 3145736 | tf_op jit(solution)/shard_map/ppermute | solution.py:278
  177.8 2.3 %collective-permute-done.24 = f32[256,1024]{1,0:T(8,128)S(1)} collective-permute-done((f32[256,1024]{1,0:T(8,128)S(1)}, f32[256,1024]{1,0:T(8,128)S(1)}, u32[]{:S(2)}, u32[]{:S(2)}) %collective-permute-start.24) | collective-permute-done | bytes 1048608 | tf_op jit(solution)/shard_map/ppermute | solution.py:278
  (101 shorter events, 32.8 us)
Async XLA Ops:
  1.8 10.7 %collective-permute-start.3 = (f32[1024,128]{1,0:T(8,128)S(1)}, f32[1024,128]{1,0:T(8,128)S(1)}, u32[]{:S(2)}, u32[]{:S(2)}) collective-permute-start(f32[1024,128]{1,0:T(8,128)S(1)} %invert_diagonal.1.refs_0_), channel_id=1, source_target_pairs={{16,19},{17,16},{18,17},{19,18},{20,23},{21,20},{22,21},{23,22},{2... | collective-permute-start | bytes 1572872 | tf_op jit(solution)/shard_map/ppermute | solution.py:278
  2.5 20.3 %collective-permute-start.1 = (f32[1024,128]{1,0:T(8,128)S(1)}, f32[1024,128]{1,0:T(8,128)S(1)}, u32[]{:S(2)}, u32[]{:S(2)}) collective-permute-start(f32[1024,128]{1,0:T(8,128)S(1)} %invert_diagonal.1.refs_0_), channel_id=1, source_target_pairs={{16,20},{17,21},{18,22},{19,23},{20,16},{21,17},{22,18},{23,19},{2... | collective-permute-start | bytes 1572872 | tf_op jit(solution)/shard_map/ppermute | solution.py:278
  3.2 19.6 %collective-permute-start = (f32[1024,128]{1,0:T(8,128)S(1)}, f32[1024,128]{1,0:T(8,128)S(1)}, u32[]{:S(2)}, u32[]{:S(2)}) collective-permute-start(f32[1024,128]{1,0:T(8,128)S(1)} %invert_diagonal.1.refs_0_), channel_id=1, source_target_pairs={{0,4},{1,5},{2,6},{3,7},{4,0},{5,1},{6,2},{7,3},{16,17},{17,18},{1... | collective-permute-start | bytes 1572872 | tf_op jit(solution)/shard_map/ppermute | solution.py:278
  4.8 18.1 %all-to-all-start = ((f32[16,64,128]{2,1,0:T(8,128)}), f32[16,64,128]{2,1,0:T(8,128)S(1)}, u32[]{:S(2)}, u32[]{:S(2)}) async-start(f32[16,64,128]{2,1,0:T(8,128)} %arrange_rhs.1), calls=%async_computation | async-start | bytes 1048576 | tf_op jit(solution)/shard_map/all_to_all | solution.py:365
  12.6 11.1 %collective-permute-start.4 = (f32[512,128]{1,0:T(8,128)S(1)}, f32[512,128]{1,0:T(8,128)}, u32[]{:S(2)}, u32[]{:S(2)}) collective-permute-start(f32[512,128]{1,0:T(8,128)S(1)} %slice.66), channel_id=1, source_target_pairs={{16,19},{17,16},{18,17},{19,18},{20,23},{21,20},{22,21},{23,22},{2... | collective-permute-start | bytes 786440 | tf_op jit(solution)/shard_map/ppermute | solution.py:278
  24.8 1.6 collective-permute-start.6
  25.7 3.0 %collective-permute-start.5 = (f32[1536,128]{1,0:T(8,128)S(1)}, f32[1536,128]{1,0:T(8,128)S(1)}, u32[]{:S(2)}, u32[]{:S(2)}) collective-permute-start(f32[1536,128]{1,0:T(8,128)S(1)} %pad_maximum_fusion.2.refs_3_), channel_id=1, source_target_pairs={{0,3},{1,0},{2,1},{3,2},{4,7},{5,4},{6,5},{7,6},{16,20},{17,21},{1... | collective-permute-start | bytes 2359304 | tf_op jit(solution)/shard_map/ppermute | solution.py:278
  27.3 3.7 %collective-permute-start.7 = (f32[768,128]{1,0:T(8,128)}, f32[768,128]{1,0:T(8,128)}, u32[]{:S(2)}, u32[]{:S(2)}) collective-permute-start(f32[768,128]{1,0:T(8,128)} %slice.67), channel_id=1, source_target_pairs={{0,1},{1,2},{2,3},{3,0},{4,5},{5,6},{6,7},{7,4}} | collective-permute-start | bytes 1179656 | tf_op jit(solution)/shard_map/ppermute | solution.py:278
  29.5 1.5 collective-permute-start.8
  33.0 1.6 collective-permute-start.9
  38.8 6.8 %collective-permute-start.10 = (f32[1024,128]{1,0:T(8,128)}, f32[1024,128]{1,0:T(8,128)}, u32[]{:S(2)}, u32[]{:S(2)}) collective-permute-start(f32[1024,128]{1,0:T(8,128)} %block_residual.1), channel_id=1, source_target_pairs={{16,28},{17,29},{18,30},{19,31},{20,24},{21,25},{22,26},{23,27}} | collective-permute-start | bytes 1572872 | tf_op jit(solution)/shard_map/ppermute | solution.py:278
  41.8 87.1 %all-to-all-start.1 = ((f32[16,256,128]{2,1,0:T(8,128)}), f32[16,256,128]{2,1,0:T(8,128)S(1)}, u32[]{:S(2)}, u32[]{:S(2)}) async-start(f32[16,256,128]{2,1,0:T(8,128)} %copy-done.4), calls=%async_computation.1 | async-start | bytes 4194304 | tf_op jit(solution)/shard_map/all_to_all | solution.py:376
  52.7 2.0 %collective-permute-start.13 = (f32[512,128]{1,0:T(8,128)S(1)}, f32[512,128]{1,0:T(8,128)S(1)}, u32[]{:S(2)}, u32[]{:S(2)}) collective-permute-start(f32[512,128]{1,0:T(8,128)S(1)} %select_select_fusion.2), channel_id=1, source_target_pairs={{0,96},{1,97},{2,98},{3,99},{4,100},{5,101},{6,102},{7,103},{8,104... | collective-permute-start | bytes 786440 | tf_op jit(solution)/shard_map/ppermute | solution.py:278
  53.4 75.4 %collective-permute-start.14 = (f32[512,128]{1,0:T(8,128)S(1)}, f32[512,128]{1,0:T(8,128)S(1)}, u32[]{:S(2)}, u32[]{:S(2)}) collective-permute-start(f32[512,128]{1,0:T(8,128)S(1)} %collective-permute-done.12), channel_id=1, source_target_pairs={{32,64},{33,65},{34,66},{35,67},{36,68},{37,69},{38,70},{39,71},{4... | collective-permute-start | bytes 786440 | tf_op jit(solution)/shard_map/ppermute | solution.py:278
  128.9 6.5 %collective-permute-start.17 = (f32[512,128]{1,0:T(8,128)S(1)}, f32[512,128]{1,0:T(8,128)S(1)}, u32[]{:S(2)}, u32[]{:S(2)}) collective-permute-start(f32[512,128]{1,0:T(8,128)S(1)} %add_select_fusion), channel_id=1, source_target_pairs={{0,1},{1,2},{2,3},{3,0},{4,5},{5,6},{6,7},{7,4},{8,9},{9,10},{10,1... | collective-permute-start | bytes 786440 | tf_op jit(solution)/shard_map/ppermute | solution.py:278
  129.0 6.5 %collective-permute-start.16 = (f32[512,128]{1,0:T(8,128)S(1)}, f32[512,128]{1,0:T(8,128)S(1)}, u32[]{:S(2)}, u32[]{:S(2)}) collective-permute-start(f32[512,128]{1,0:T(8,128)S(1)} %add_select_fusion), channel_id=1, source_target_pairs={{0,3},{1,0},{2,1},{3,2},{4,7},{5,4},{6,5},{7,6},{8,11},{9,8},{10,9... | collective-permute-start | bytes 786440 | tf_op jit(solution)/shard_map/ppermute | solution.py:278
  135.4 5.1 %collective-permute-start.18 = (f32[256,128]{1,0:T(8,128)S(1)}, f32[256,128]{1,0:T(8,128)S(1)}, u32[]{:S(2)}, u32[]{:S(2)}) collective-permute-start(f32[256,128]{1,0:T(8,128)S(1)} %slice.71), channel_id=1, source_target_pairs={{0,1},{1,2},{2,3},{3,0},{4,5},{5,6},{6,7},{7,4},{8,9},{9,10},{10,1... | collective-permute-start | bytes 393224 | tf_op jit(solution)/shard_map/ppermute | solution.py:278
  135.5 5.0 %collective-permute-start.19 = (f32[256,128]{1,0:T(8,128)S(1)}, f32[256,128]{1,0:T(8,128)S(1)}, u32[]{:S(2)}, u32[]{:S(2)}) collective-permute-start(f32[256,128]{1,0:T(8,128)S(1)} %slice.72), channel_id=1, source_target_pairs={{0,3},{1,0},{2,1},{3,2},{4,7},{5,4},{6,5},{7,6},{8,11},{9,8},{10,9... | collective-permute-start | bytes 393224 | tf_op jit(solution)/shard_map/ppermute | solution.py:278
  139.3 4.0 %collective-permute-start.15 = (f32[8,256,128]{2,1,0:T(8,128)}, f32[8,256,128]{2,1,0:T(8,128)}, u32[]{:S(2)}, u32[]{:S(2)}) collective-permute-start(f32[8,256,128]{2,1,0:T(8,128)} %constant_dynamic-slice_fusion), channel_id=1, source_target_pairs={{0,16},{1,17},{2,18},{3,19},{4,20},{5,21},{6,22},{7,23},{8,24},{9,... | collective-permute-start | bytes 3145736 | tf_op jit(solution)/shard_map/ppermute | solution.py:278
  141.6 14.3 %collective-permute-start.21 = (f32[4,512,128]{2,1,0:T(8,128)}, f32[4,512,128]{2,1,0:T(8,128)}, u32[]{:S(2)}, u32[]{:S(2)}) collective-permute-start(f32[4,512,128]{2,1,0:T(8,128)} %pad_maximum_fusion.refs_0_), channel_id=1, source_target_pairs={{0,12},{1,13},{2,14},{3,15},{4,0},{5,1},{6,2},{7,3},{8,4},{9,5},{1... | collective-permute-start | bytes 3145736 | tf_op jit(solution)/shard_map/ppermute | solution.py:278
  143.2 15.5 %collective-permute-start.20 = (f32[4,512,128]{2,1,0:T(8,128)}, f32[4,512,128]{2,1,0:T(8,128)}, u32[]{:S(2)}, u32[]{:S(2)}) collective-permute-start(f32[4,512,128]{2,1,0:T(8,128)} %pad_maximum_fusion.refs_0_), channel_id=1, source_target_pairs={{0,4},{1,5},{2,6},{3,7},{4,8},{5,9},{6,10},{7,11},{8,12},{9,13},{1... | collective-permute-start | bytes 3145736 | tf_op jit(solution)/shard_map/ppermute | solution.py:278
  160.8 8.4 %collective-permute-start.23 = (f32[2,512,128]{2,1,0:T(8,128)S(1)}, f32[2,512,128]{2,1,0:T(8,128)S(1)}, u32[]{:S(2)}, u32[]{:S(2)}) collective-permute-start(f32[2,512,128]{2,1,0:T(8,128)S(1)} %slice.62), channel_id=1, source_target_pairs={{0,12},{1,13},{2,14},{3,15},{4,0},{5,1},{6,2},{7,3},{8,4},{9,5},{1... | collective-permute-start | bytes 1572872 | tf_op jit(solution)/shard_map/ppermute | solution.py:278
  160.9 9.6 %collective-permute-start.22 = (f32[2,512,128]{2,1,0:T(8,128)S(1)}, f32[2,512,128]{2,1,0:T(8,128)S(1)}, u32[]{:S(2)}, u32[]{:S(2)}) collective-permute-start(f32[2,512,128]{2,1,0:T(8,128)S(1)} %slice.61), channel_id=1, source_target_pairs={{0,4},{1,5},{2,6},{3,7},{4,8},{5,9},{6,10},{7,11},{8,12},{9,13},{1... | collective-permute-start | bytes 1572872 | tf_op jit(solution)/shard_map/ppermute | solution.py:278
  173.2 6.9 %collective-permute-start.24 = (f32[256,1024]{1,0:T(8,128)S(1)}, f32[256,1024]{1,0:T(8,128)S(1)}, u32[]{:S(2)}, u32[]{:S(2)}) collective-permute-start(f32[256,1024]{1,0:T(8,128)S(1)} %slice.74), channel_id=1, source_target_pairs={{0,16},{1,17},{2,18},{3,19},{4,20},{5,21},{6,22},{7,23},{8,24},{9,... | collective-permute-start | bytes 3145736 | tf_op jit(solution)/shard_map/ppermute | solution.py:278
  (19 other events, 52.3 us)

commit v12 on v10

--- a/solution.py
+++ b/solution.py
@@ -72,57 +72,49 @@
     )(info, lead)
 
 
-def solve(info, pieces, places, rhs):
-    def body(info, *refs):
-        rhs_ref, out_ref, tri_ref = refs[-3:]
-        for ref, parts in zip(refs, places):
-            for half, steps, start, to, rows in parts:
-                half = {"own": info[0], "pair": 1 - info[0]}.get(half, half)
-                k = 4 * half + lax.rem(info[1] + steps, 4)
-                tri_ref[k, pl.ds(to, rows), :] = pack_left(ref[pl.ds(start, rows), :])
-        out_ref[...] = rhs_ref[...]
-        for k in range(8):
-            here = pl.ds(k * TILE, TILE)
-            solved = packed_product(tri_ref[k, here, :], pack_right(out_ref[here, :]))
-            out_ref[here, :] = solved
-            right = pack_right(solved)
-            for i in range(k + 1, 8):
-                there = pl.ds(i * TILE, TILE)
-                out_ref[there, :] = out_ref[there, :] - packed_product(tri_ref[k, there, :], right)
+def solve(active, tri, rhs):
+    def body(active, tri_ref, rhs_ref, out_ref):
+        @pl.when(active[0] == 1)
+        def _():
+            out_ref[...] = rhs_ref[...]
+            for k in range(8):
+                here = pl.ds(k * TILE, TILE)
+                solved = packed_product(pack_left(tri_ref[k, here, :]), pack_right(out_ref[here, :]))
+                out_ref[here, :] = solved
+                right = pack_right(solved)
+                for i in range(k + 1, 8):
+                    there = pl.ds(i * TILE, TILE)
+                    out_ref[there, :] = out_ref[there, :] - packed_product(pack_left(tri_ref[k, there, :]), right)
 
     return pl.pallas_call(
         body,
         out_shape=jax.ShapeDtypeStruct(rhs.shape, F32),
-        in_specs=[SM] + [VM] * (len(pieces) + 1),
-        out_specs=VM,
-        scratch_shapes=[pltpu.VMEM((8, 1024, 256), BF16)],
+        in_specs=[SM, VM, VM],
+        out_specs=VM,
         compiler_params=PARAMS,
         name="block_solve",
-    )(info, *pieces, rhs)
-
-
-def residual(info, pieces, places, rhs, x):
-    def body(info, *refs):
-        rhs_ref, x_ref, out_ref = refs[-3:]
-        out_ref[...] = rhs_ref[...]
-        for ref, parts in zip(refs, places):
-            for half, steps, start, to, rows in parts:
-                half = {"own": info[0], "pair": 1 - info[0]}[half]
-                k = 4 * half + lax.rem(info[1] + steps, 4)
-                right = pack_right(x_ref[pl.ds(pl.multiple_of(k * TILE, TILE), TILE), :])
-                for n in range(0, rows, TILE):
-                    there = pl.ds(to + n, TILE)
-                    left = pack_left(ref[pl.ds(start + n, TILE), :])
-                    out_ref[there, :] = out_ref[there, :] - packed_product(left, right)
+    )(active, tri, rhs)
+
+
+def residual(active, tri, rhs, x):
+    def body(active, tri_ref, rhs_ref, x_ref, out_ref):
+        @pl.when(active[0] == 1)
+        def _():
+            for k in range(8):
+                right = pack_right(x_ref[pl.ds(k * TILE, TILE), :])
+                for i in range(8):
+                    there = pl.ds(i * TILE, TILE)
+                    base = rhs_ref[there, :] if k == 0 else out_ref[there, :]
+                    out_ref[there, :] = base - packed_product(pack_left(tri_ref[k, there, :]), right)
 
     return pl.pallas_call(
         body,
         out_shape=jax.ShapeDtypeStruct(rhs.shape, F32),
-        in_specs=[SM] + [VM] * (len(pieces) + 2),
+        in_specs=[SM, VM, VM, VM],
         out_specs=VM,
         compiler_params=PARAMS,
         name="block_residual",
-    )(info, *pieces, rhs, x)
+    )(active, tri, rhs, x)
 
 
 def arrange_body(factor_ref, out_ref):
@@ -142,22 +134,21 @@
     )(factor)
 
 
-def arrange_rhs_body(info, rhs_ref, out_ref):
-    for n in range(8):
-        to = jnp.where(info[0] == 0, n, (n + 4) % 8)
-        out_ref[to, :, :] = rhs_ref[0, :, pl.ds(n * TILE, TILE)]
-
-
-def arrange_rhs(yh, rhs):
+def arrange_rhs_body(rhs_ref, out_ref):
+    for n in range(16):
+        out_ref[n, :, :] = rhs_ref[0, :, pl.ds(n % 8 * TILE, TILE)]
+
+
+def arrange_rhs(rhs):
     return pl.pallas_call(
         arrange_rhs_body,
         grid=(1,),
-        out_shape=jax.ShapeDtypeStruct((8, 64, TILE), F32),
-        in_specs=[SM, pl.BlockSpec((1, 64, 1024), lambda i: (0, 0, 0))],
-        out_specs=pl.BlockSpec((8, 64, TILE), lambda i: (0, 0, 0)),
+        out_shape=jax.ShapeDtypeStruct((16, 64, TILE), F32),
+        in_specs=[pl.BlockSpec((1, 64, 1024), lambda i: (0, 0, 0))],
+        out_specs=pl.BlockSpec((16, 64, TILE), lambda i: (0, 0, 0)),
         compiler_params=PARAMS,
         name="arrange_rhs",
-    )(jnp.reshape(yh, (1,)).astype(jnp.int32), rhs)
+    )(rhs)
 
 
 def prepare_body(info, left_ref, other_ref, high_ref, low_ref):
@@ -277,49 +268,6 @@
     return after, far_low, far_high, before
 
 
-def gather(lead, half, core, yl):
-    def holds(a, b, c):
-        return a == 0 and (b == 1 or c < 2)
-
-    def step(b_on_z, amount):
-        def where(a, b, c, d):
-            if not holds(a, b, c):
-                return None
-            return (a, b, c, d + amount) if b == b_on_z else (a, b, c + 1 - 2 * (c % 2), d)
-
-        return where
-
-    def only(b_only, amount):
-        return lambda a, b, c, d: (a, b, c, d + amount) if holds(a, b, c) and b == b_only else None
-
-    mixed = move(lead, step(1, 1))
-    after = move(lead, only(1, -1))
-    swapped = move(lead, lambda a, b, c, d: (a, b, c + 1 - 2 * (c % 2), d) if holds(a, b, c) and b == 1 else None)
-    mixed, swapped, half = lax.optimization_barrier((mixed, swapped, half))
-    far_low = move(mixed[:512], only(1, 1))
-    far_high = move(after[512:], only(1, -1))
-
-    full = jnp.where(yl == 0, lead, mixed)
-    lower = jnp.where(yl == 0, mixed[512:], lead[512:])
-    zero = core == 0
-    first = jnp.concatenate([jnp.where(zero, full, mixed), jnp.where(zero, lower, far_low)], 0)
-    second = jnp.concatenate([jnp.where(zero, full, after), jnp.where(zero, lower, far_high)], 0)
-    got_first = move(first, step(0, 1))
-    got_second = move(second, step(0, -1))
-    end_low = move(got_first[:768], only(0, 1))
-    end_high = move(got_second[768:], only(0, -1))
-
-    corner_pieces = [first, got_second, got_first, end_low, end_high]
-    corner_places = [[(0, n, 0, 0, 1024), (1, n, 1024, 512, 512)] for n in (0, 1, 3)]
-    corner_places += [[(0, 2, 0, 0, 768)], [(0, 2, 0, 768, 256), (1, 2, 256, 512, 512)]]
-    lower_pieces = [lead, swapped, first, second, got_first, got_second]
-    lower_places = [[("own", 0, 0, 0, 1024)], [("pair", 0, 0, 0, 1024)]]
-    for group in ("own", "pair"):
-        lower_places.append([(group, 3, 0, 0, 1024), (group, 2, 1024, 0, 512)])
-        lower_places.append([(group, 1, 0, 0, 1024), (group, 2, 1024, 512, 512)])
-    return (corner_pieces, corner_places), (lower_pieces, lower_places), half
-
-
 def shards(factor, cross_cov):
     xi, core = lax.axis_index("x"), lax.axis_index("core")
     yh, yl, z = lax.axis_index("yh"), lax.axis_index("yl"), lax.axis_index("z")
@@ -332,19 +280,20 @@
     info = jnp.stack([diagonal.astype(jnp.int32), (4 * yl + z).astype(jnp.int32)])
     lead = invert_diagonal(info, local[0])
 
-    half = lax.all_to_all(arrange_rhs(yh, rhs), ("yl", "z"), 0, 0, tiled=True).reshape(512, TILE)
-    upper_left, lower_row, half = gather(lead, half, core, yl)
-    other_half = move(half, lambda a, b, c, d: (0, b, 3 - c, d) if a == 0 and c >= 2 else None)
-    columns = jnp.concatenate([half, other_half], 0)
-
-    place = jnp.stack([yl, z]).astype(jnp.int32)
-    first = solve(place, *upper_left, columns)
+    tri = lax.all_gather(lead, ("yl", "z"), axis=0, tiled=False)
+
+    columns = lax.all_to_all(arrange_rhs(rhs), COL, 0, 0, tiled=True).reshape(1024, TILE)
+
+    def only(condition):
+        return jnp.reshape(condition & (xi == 0), (1,)).astype(jnp.int32)
+
+    first = solve(only((core == 0) & (yh == 0)), tri, columns)
     sent = move(first, lambda a, b, c, d: (0, 1, c, d) if (a, b) == (0, 0) and c < 2 else None)
-    rest = residual(place, *lower_row, columns, sent)
+    rest = residual(only((core == 1) & (yh == 0)), tri, columns, sent)
     second_rhs = move(rest, lambda a, b, c, d: (0, 1, 3 - c, d) if (a, b) == (0, 1) and c < 2 else None)
     by_rows, rest = lax.optimization_barrier((arrange(local), rest))
     left = lax.all_to_all(by_rows, COL, 0, 0, tiled=True)
-    second = solve(place, *lower_row, second_rhs)
+    second = solve(only((core == 1) & (yh == 1)), tri, second_rhs)
     mine, left = lax.optimization_barrier((deal(first, second, core, yh, xi), left))
 
     def swap(value):

time: 182 us -> 196 us (1.077)
  waiting for transfers between devices: 94.4 us -> 114 us
  starting transfers between devices: 46.5 us -> 30.7 us
  between operations: 0.61 us -> 13.7 us
  Pallas kernels: 24.9 us -> 17 us
  local copies, waits for them, and re-layouts: 12 us -> 15.2 us
  other arithmetic: 2.92 us -> 5.32 us
    all_gather x0 -> x1, waiting for transfers between devices: none -> 39.6 us  [shards(): tri = lax.all_gather(lead, ('yl', 'z'), axis=0, tiled=False)]
    ppermute x26 -> x16, waiting for transfers between devices: 89 us -> 62.8 us  [move(): return lax.ppermute(value, AXES, pairs)]
    ppermute x26 -> x16, starting transfers between devices: 35.9 us -> 18.9 us  [move(): return lax.ppermute(value, AXES, pairs)]
    pallas_call x2, Pallas kernels: 8.16 us -> 1.1 us  [solve(): pl.pallas_call(body, out_shape=jax.ShapeDtypeStruct(rhs.shape, F32), in_s...]
    all_to_all x1, waiting for transfers between devices: 5.39 us -> 11.1 us  [shards(): lax.all_to_all(arrange_rhs(rhs), COL, 0, 0, tiled=True).reshape(1024, TILE)]
    unnamed x35 -> x18, local copies, waits for them, and re-layouts: 7.29 us -> 8.81 us
  transfers between devices with their start and end apart: 28 -> 19, of which waited for: 10 -> 11; matrix products, arithmetic and copies ran while one was open for 2% -> 4% of each run, Pallas kernels for 9% -> 6%
where the time goes in v12:
time: 196 us; the launch traced here: 195 us
  waiting for transfers between devices  114 us (58%)
  starting transfers between devices  30.7 us (16%)
  Pallas kernels  17 us (9%)
  local copies, waits for them, and re-layouts  15.2 us (8%)
  between operations  13.7 us (7%)
  other arithmetic  5.32 us (3%)
    ppermute x16, waiting for transfers between devices, move(): return lax.ppermute(value, AXES, pairs)  62.8 us
    all_gather x1, waiting for transfers between devices, shards(): tri = lax.all_gather(lead, ('yl', 'z'), axis=0, tiled=False)  39.6 us
    ppermute x16, starting transfers between devices, move(): return lax.ppermute(value, AXES, pairs)  18.9 us
    pallas_call x3, Pallas kernels, accumulate(): pl.pallas_call(body, out_shape=jax.ShapeDtypeStruct((512, 1024), F32), in...  11.2 us
    all_to_all x1, waiting for transfers between devices, shards(): lax.all_to_all(arrange_rhs(rhs), COL, 0, 0, tiled=True).reshape(1024, TILE)  11.1 us
    unnamed x18, local copies, waits for them, and re-layouts  8.81 us
    all_to_all x1, starting transfers between devices, shards(): lax.all_to_all(arrange_rhs(rhs), COL, 0, 0, tiled=True).reshape(1024, TILE)  7.77 us
    all_to_all x1, starting transfers between devices, shards(): left = lax.all_to_all(by_rows, COL, 0, 0, tiled=True)  3.96 us
  transfers between devices with their start and end apart: 19, of which 11 were waited for; matrix products, arithmetic and copies ran while one was open for 4% of the time, Pallas kernels for 6%

profile of v12, /device:TPU:5, one launch (start us, length us, event | category | flops | bytes accessed | tf_op | source)
XLA Modules:
  0.0 195.4 jit_solution(2829496541652786743)
XLA Ops:
  7.8 1.4 invert_diagonal.1
  10.0 7.8 %all-to-all-start = ((f32[16,64,128]{2,1,0:T(8,128)}), f32[16,64,128]{2,1,0:T(8,128)S(1)}, u32[]{:S(2)}, u32[]{:S(2)}) async-start(f32[16,64,128]{2,1,0:T(8,128)} %arrange_rhs.1), calls=%async_computation | async-start | bytes 1048576 | tf_op jit(solution)/shard_map/all_to_all | solution.py:285
  17.8 11.1 %all-to-all-done = f32[16,64,128]{2,1,0:T(8,128)S(1)} async-done(((f32[16,64,128]{2,1,0:T(8,128)}), f32[16,64,128]{2,1,0:T(8,128)S(1)}, u32[]{:S(2)}, u32[]{:S(2)}) %all-to-all-start) | async-done | bytes 524320 | tf_op jit(solution)/shard_map/all_to_all | solution.py:285
  29.0 39.6 %all-gather.3.cloned.1.call-done = f32[8192,128]{1,0:T(8,128)} async-done(((f32[1024,128]{1,0:T(8,128)}), f32[8192,128]{1,0:T(8,128)}) %all-gather.3.cloned.1.call-update) | async-done | bytes 4194320 | tf_op jit(solution)/shard_map/all_gather | solution.py:283
  68.6 2.2 %copy-done = f32[8192,128]{1,0:T(8,128)S(1)} copy-done((f32[8192,128]{1,0:T(8,128)S(1)}, f32[8192,128]{1,0:T(8,128)}, u32[]{:S(2)}) %copy-start) | copy-done | bytes 4194328
  71.5 2.2 %copy-done.1 = f32[8192,128]{1,0:T(8,128)S(1)} copy-done((f32[8192,128]{1,0:T(8,128)S(1)}, f32[8192,128]{1,0:T(8,128)}, u32[]{:S(2)}) %copy-start.1) | copy-done | bytes 4194328
  74.5 1.4 collective-permute-start.1
  77.5 4.0 %all-to-all-start.1 = ((f32[16,256,128]{2,1,0:T(8,128)}), f32[16,256,128]{2,1,0:T(8,128)S(1)}, u32[]{:S(2)}, u32[]{:S(2)}) async-start(f32[16,256,128]{2,1,0:T(8,128)} %copy-done.3), calls=%async_computation.1 | async-start | bytes 4194304 | tf_op jit(solution)/shard_map/all_to_all | solution.py:295
  81.5 2.2 %copy-done.2 = f32[8192,128]{1,0:T(8,128)S(1)} copy-done((f32[8192,128]{1,0:T(8,128)S(1)}, f32[8192,128]{1,0:T(8,128)}, u32[]{:S(2)}) %copy-start.2) | copy-done | bytes 4194328
  90.9 42.5 %collective-permute-done.5 = f32[512,128]{1,0:T(8,128)S(1)} collective-permute-done((f32[512,128]{1,0:T(8,128)S(1)}, f32[512,128]{1,0:T(8,128)S(1)}, u32[]{:S(2)}, u32[]{:S(2)}) %collective-permute-start.5) | collective-permute-done | bytes 262176 | tf_op jit(solution)/shard_map/ppermute | solution.py:239
  133.5 2.7 %collective-permute-start.7 = (f32[512,128]{1,0:T(8,128)S(1)}, f32[512,128]{1,0:T(8,128)}, u32[]{:S(2)}, u32[]{:S(2)}) collective-permute-start(f32[512,128]{1,0:T(8,128)S(1)} %add_select_fusion), channel_id=1, source_target_pairs={{0,3},{1,0},{2,1},{3,2},{4,7},{5,4},{6,5},{7,6},{8,11},{9,8},{10,9... | collective-permute-start | bytes 786440 | tf_op jit(solution)/shard_map/ppermute | solution.py:239
  136.2 3.9 %collective-permute-done.8 = f32[512,128]{1,0:T(8,128)} collective-permute-done((f32[512,128]{1,0:T(8,128)S(1)}, f32[512,128]{1,0:T(8,128)}, u32[]{:S(2)}, u32[]{:S(2)}) %collective-permute-start.8) | collective-permute-done | bytes 262176 | tf_op jit(solution)/shard_map/ppermute | solution.py:239
  142.0 2.7 %collective-permute-start.10 = (f32[256,128]{1,0:T(8,128)S(1)}, f32[256,128]{1,0:T(8,128)S(1)}, u32[]{:S(2)}, u32[]{:S(2)}) collective-permute-start(f32[256,128]{1,0:T(8,128)S(1)} %slice.44), channel_id=1, source_target_pairs={{0,3},{1,0},{2,1},{3,2},{4,7},{5,4},{6,5},{7,6},{8,11},{9,8},{10,9... | collective-permute-start | bytes 393224 | tf_op jit(solution)/shard_map/ppermute | solution.py:239
  146.7 2.1 %pad_maximum_fusion.refs_0_ = f32[4,512,128]{2,1,0:T(8,128)} fusion(f32[1,512,128]{2,1,0:T(8,128)} %bitcast.19, f32[1,512,128]{2,1,0:T(8,128)S(1)} %maximum_bitcast_fusion, f32[1,512,128]{2,1,0:T(8,128)} %bitcast.17, f32[1,512,128]{2,1,0:T(8,128)S(1)} %bitcast.35), kind=kLoop, calls=%fused_computation.2 | loop fusion | flops 786432 | bytes 2097152 | tf_op jit(solution)/shard_map/stack | solution.py:306
  150.4 1.6 prepare_update.1
  152.0 3.2 %update_near.1.refs_0_ = f32[512,1024]{1,0:T(8,128)S(1)} custom-call(s32[5]{0:T(128)S(1)} %stack.52.info, bf16[4,512,256]{2,1,0:T(8,128)(2,1)S(1)} %get-tuple-element.18.high_ref, bf16[4,512,256]{2,1,0:T(8,128)(2,1)S(1)} %get-tuple-element.19.low_ref, f32[4,512,128]{2,1,0:T(8,128)} %pad_maximum_fusion.refs_0_), custom_call_target="tpu_custom_call" | custom-call | tf_op jit(solution)/shard_map/update_near/pallas_call | solution.py:215
  155.1 7.9 %collective-permute-done.12.refs_1_ = f32[4,512,128]{2,1,0:T(8,128)} collective-permute-done((f32[4,512,128]{2,1,0:T(8,128)}, f32[4,512,128]{2,1,0:T(8,128)}, u32[]{:S(2)}, u32[]{:S(2)}) %collective-permute-start.12) | collective-permute-done | bytes 1048608 | tf_op jit(solution)/shard_map/ppermute | solution.py:239
  163.0 2.6 %collective-permute-done.11.refs_2_ = f32[4,512,128]{2,1,0:T(8,128)} collective-permute-done((f32[4,512,128]{2,1,0:T(8,128)}, f32[4,512,128]{2,1,0:T(8,128)}, u32[]{:S(2)}, u32[]{:S(2)}) %collective-permute-start.11) | collective-permute-done | bytes 1048608 | tf_op jit(solution)/shard_map/ppermute | solution.py:239
  168.0 1.5 collective-permute-start.13
  169.5 5.4 %update_next.1.refs_0_ = f32[512,1024]{1,0:T(8,128)S(1)} custom-call(s32[5]{0:T(128)S(1)} %stack.52.info, bf16[4,512,256]{2,1,0:T(8,128)(2,1)S(1)} %get-tuple-element.18.high_ref, bf16[4,512,256]{2,1,0:T(8,128)(2,1)S(1)} %get-tuple-element.19.low_ref, f32[512,1024]{1,0:T(8,128)S(1)} %update_near.1.refs_0_, ...), custom_call_target="tpu_custom_call", output_to_operand_aliasing={{}: (3, {})} | custom-call | tf_op jit(solution)/shard_map/update_next/pallas_call | solution.py:215
  174.9 1.4 collective-permute-done.14.refs_2_
  177.6 2.6 %update_far.1 = f32[512,1024]{1,0:T(8,128)S(1)} custom-call(s32[5]{0:T(128)S(1)} %stack.52.info, bf16[4,512,256]{2,1,0:T(8,128)(2,1)S(1)} %get-tuple-element.18.high_ref, bf16[4,512,256]{2,1,0:T(8,128)(2,1)S(1)} %get-tuple-element.19.low_ref, f32[512,1024]{1,0:T(8,128)S(1)} %update_next.1.refs_0_, ...), custom_call_target="tpu_custom_call", output_to_operand_aliasing={{}: (3, {})} | custom-call | tf_op jit(solution)/shard_map/update_far/pallas_call | solution.py:215
  180.3 4.8 %collective-permute-start.15 = (f32[256,1024]{1,0:T(8,128)S(1)}, f32[256,1024]{1,0:T(8,128)S(1)}, u32[]{:S(2)}, u32[]{:S(2)}) collective-permute-start(f32[256,1024]{1,0:T(8,128)S(1)} %slice.46), channel_id=1, source_target_pairs={{0,16},{1,17},{2,18},{3,19},{4,20},{5,21},{6,22},{7,23},{8,24},{9,... | collective-permute-start | bytes 3145736 | tf_op jit(solution)/shard_map/ppermute | solution.py:239
  185.1 2.3 %collective-permute-done.15 = f32[256,1024]{1,0:T(8,128)S(1)} collective-permute-done((f32[256,1024]{1,0:T(8,128)S(1)}, f32[256,1024]{1,0:T(8,128)S(1)}, u32[]{:S(2)}, u32[]{:S(2)}) %collective-permute-start.15) | collective-permute-done | bytes 1048608 | tf_op jit(solution)/shard_map/ppermute | solution.py:239
  (61 shorter events, 22.9 us)
Async XLA Ops:
  6.5 2.7 %copy-start.4 = (f32[4,1,64,1024]{3,2,1,0:T(8,128)S(1)}, f32[4,1,64,1024]{3,2,1,0:T(8,128)}, u32[]{:S(2)}) copy-start(f32[4,1,64,1024]{3,2,1,0:T(8,128)} %param.3) | copy-start | bytes 3145732
  6.5 62.0 %all-gather.3.cloned.1.call-start = ((), (), s32[]{:S(2)}) async-start(), calls=%async_computation.2 | async-start | bytes 4718592 | tf_op jit(solution)/shard_map/all_gather | solution.py:283
  10.0 18.9 %all-to-all-start = ((f32[16,64,128]{2,1,0:T(8,128)}), f32[16,64,128]{2,1,0:T(8,128)S(1)}, u32[]{:S(2)}, u32[]{:S(2)}) async-start(f32[16,64,128]{2,1,0:T(8,128)} %arrange_rhs.1), calls=%async_computation | async-start | bytes 1048576 | tf_op jit(solution)/shard_map/all_to_all | solution.py:285
  70.8 3.7 %copy-start.6 = (f32[1024,128]{1,0:T(8,128)}, f32[1024,128]{1,0:T(8,128)S(1)}, u32[]{:S(2)}) copy-start(f32[1024,128]{1,0:T(8,128)S(1)} %block_solve.2) | copy-start | bytes 1572868
  70.8 0.7 collective-permute-start
  71.5 2.2 %copy-start.1 = (f32[8192,128]{1,0:T(8,128)S(1)}, f32[8192,128]{1,0:T(8,128)}, u32[]{:S(2)}) copy-start(f32[8192,128]{1,0:T(8,128)} %all-gather.3.cloned.1.call-done) | copy-start | bytes 12582916
  73.7 2.3 %copy-start.5 = (f32[4,1,1024,128]{3,2,1,0:T(8,128)S(1)}, f32[4,1,1024,128]{3,2,1,0:T(8,128)}, u32[]{:S(2)}) copy-start(f32[4,1,1024,128]{3,2,1,0:T(8,128)} %param.2) | copy-start | bytes 6291460
  74.5 6.9 %collective-permute-start.1 = (f32[1024,128]{1,0:T(8,128)}, f32[1024,128]{1,0:T(8,128)}, u32[]{:S(2)}, u32[]{:S(2)}) collective-permute-start(f32[1024,128]{1,0:T(8,128)} %block_residual.1), channel_id=1, source_target_pairs={{16,28},{17,29},{18,30},{19,31},{20,24},{21,25},{22,26},{23,27}} | collective-permute-start | bytes 1572872 | tf_op jit(solution)/shard_map/ppermute | solution.py:239
  77.5 56.0 %all-to-all-start.1 = ((f32[16,256,128]{2,1,0:T(8,128)}), f32[16,256,128]{2,1,0:T(8,128)S(1)}, u32[]{:S(2)}, u32[]{:S(2)}) async-start(f32[16,256,128]{2,1,0:T(8,128)} %copy-done.3), calls=%async_computation.1 | async-start | bytes 4194304 | tf_op jit(solution)/shard_map/all_to_all | solution.py:295
  81.4 2.2 %copy-start.2 = (f32[8192,128]{1,0:T(8,128)S(1)}, f32[8192,128]{1,0:T(8,128)}, u32[]{:S(2)}) copy-start(f32[8192,128]{1,0:T(8,128)} %all-gather.3.cloned.1.call-done) | copy-start | bytes 12582916
  86.4 0.7 collective-permute-start.2
  88.2 1.4 collective-permute-start.3
  88.9 2.0 %collective-permute-start.4 = (f32[512,128]{1,0:T(8,128)S(1)}, f32[512,128]{1,0:T(8,128)S(1)}, u32[]{:S(2)}, u32[]{:S(2)}) collective-permute-start(f32[512,128]{1,0:T(8,128)S(1)} %select_select_fusion), channel_id=1, source_target_pairs={{0,96},{1,97},{2,98},{3,99},{4,100},{5,101},{6,102},{7,103},{8,104... | collective-permute-start | bytes 786440 | tf_op jit(solution)/shard_map/ppermute | solution.py:239
  89.6 43.8 %collective-permute-start.5 = (f32[512,128]{1,0:T(8,128)S(1)}, f32[512,128]{1,0:T(8,128)S(1)}, u32[]{:S(2)}, u32[]{:S(2)}) collective-permute-start(f32[512,128]{1,0:T(8,128)S(1)} %collective-permute-done.3), channel_id=1, source_target_pairs={{32,64},{33,65},{34,66},{35,67},{36,68},{37,69},{38,70},{39,71},{4... | collective-permute-start | bytes 786440 | tf_op jit(solution)/shard_map/ppermute | solution.py:239
  133.5 6.6 %collective-permute-start.8 = (f32[512,128]{1,0:T(8,128)S(1)}, f32[512,128]{1,0:T(8,128)}, u32[]{:S(2)}, u32[]{:S(2)}) collective-permute-start(f32[512,128]{1,0:T(8,128)S(1)} %add_select_fusion), channel_id=1, source_target_pairs={{0,1},{1,2},{2,3},{3,0},{4,5},{5,6},{6,7},{7,4},{8,9},{9,10},{10,1... | collective-permute-start | bytes 786440 | tf_op jit(solution)/shard_map/ppermute | solution.py:239
  133.5 7.5 %collective-permute-start.7 = (f32[512,128]{1,0:T(8,128)S(1)}, f32[512,128]{1,0:T(8,128)}, u32[]{:S(2)}, u32[]{:S(2)}) collective-permute-start(f32[512,128]{1,0:T(8,128)S(1)} %add_select_fusion), channel_id=1, source_target_pairs={{0,3},{1,0},{2,1},{3,2},{4,7},{5,4},{6,5},{7,6},{8,11},{9,8},{10,9... | collective-permute-start | bytes 786440 | tf_op jit(solution)/shard_map/ppermute | solution.py:239
  141.0 5.1 %collective-permute-start.9 = (f32[256,128]{1,0:T(8,128)S(1)}, f32[256,128]{1,0:T(8,128)S(1)}, u32[]{:S(2)}, u32[]{:S(2)}) collective-permute-start(f32[256,128]{1,0:T(8,128)S(1)} %slice.43), channel_id=1, source_target_pairs={{0,1},{1,2},{2,3},{3,0},{4,5},{5,6},{6,7},{7,4},{8,9},{9,10},{10,1... | collective-permute-start | bytes 393224 | tf_op jit(solution)/shard_map/ppermute | solution.py:239
  142.0 4.7 %collective-permute-start.10 = (f32[256,128]{1,0:T(8,128)S(1)}, f32[256,128]{1,0:T(8,128)S(1)}, u32[]{:S(2)}, u32[]{:S(2)}) collective-permute-start(f32[256,128]{1,0:T(8,128)S(1)} %slice.44), channel_id=1, source_target_pairs={{0,3},{1,0},{2,1},{3,2},{4,7},{5,4},{6,5},{7,6},{8,11},{9,8},{10,9... | collective-permute-start | bytes 393224 | tf_op jit(solution)/shard_map/ppermute | solution.py:239
  145.8 4.6 %collective-permute-start.6 = (f32[8,256,128]{2,1,0:T(8,128)}, f32[8,256,128]{2,1,0:T(8,128)}, u32[]{:S(2)}, u32[]{:S(2)}) collective-permute-start(f32[8,256,128]{2,1,0:T(8,128)} %constant_dynamic-slice_fusion), channel_id=1, source_target_pairs={{0,16},{1,17},{2,18},{3,19},{4,20},{5,21},{6,22},{7,23},{8,24},{9,... | collective-permute-start | bytes 3145736 | tf_op jit(solution)/shard_map/ppermute | solution.py:239
  148.8 14.3 %collective-permute-start.12 = (f32[4,512,128]{2,1,0:T(8,128)}, f32[4,512,128]{2,1,0:T(8,128)}, u32[]{:S(2)}, u32[]{:S(2)}) collective-permute-start(f32[4,512,128]{2,1,0:T(8,128)} %pad_maximum_fusion.refs_0_), channel_id=1, source_target_pairs={{0,12},{1,13},{2,14},{3,15},{4,0},{5,1},{6,2},{7,3},{8,4},{9,5},{1... | collective-permute-start | bytes 3145736 | tf_op jit(solution)/shard_map/ppermute | solution.py:239
  150.1 15.5 %collective-permute-start.11 = (f32[4,512,128]{2,1,0:T(8,128)}, f32[4,512,128]{2,1,0:T(8,128)}, u32[]{:S(2)}, u32[]{:S(2)}) collective-permute-start(f32[4,512,128]{2,1,0:T(8,128)} %pad_maximum_fusion.refs_0_), channel_id=1, source_target_pairs={{0,4},{1,5},{2,6},{3,7},{4,8},{5,9},{6,10},{7,11},{8,12},{9,13},{1... | collective-permute-start | bytes 3145736 | tf_op jit(solution)/shard_map/ppermute | solution.py:239
  167.8 8.6 %collective-permute-start.14 = (f32[2,512,128]{2,1,0:T(8,128)S(1)}, f32[2,512,128]{2,1,0:T(8,128)S(1)}, u32[]{:S(2)}, u32[]{:S(2)}) collective-permute-start(f32[2,512,128]{2,1,0:T(8,128)S(1)} %slice.38), channel_id=1, source_target_pairs={{0,12},{1,13},{2,14},{3,15},{4,0},{5,1},{6,2},{7,3},{8,4},{9,5},{1... | collective-permute-start | bytes 1572872 | tf_op jit(solution)/shard_map/ppermute | solution.py:239
  168.0 9.6 %collective-permute-start.13 = (f32[2,512,128]{2,1,0:T(8,128)S(1)}, f32[2,512,128]{2,1,0:T(8,128)S(1)}, u32[]{:S(2)}, u32[]{:S(2)}) collective-permute-start(f32[2,512,128]{2,1,0:T(8,128)S(1)} %slice.37), channel_id=1, source_target_pairs={{0,4},{1,5},{2,6},{3,7},{4,8},{5,9},{6,10},{7,11},{8,12},{9,13},{1... | collective-permute-start | bytes 1572872 | tf_op jit(solution)/shard_map/ppermute | solution.py:239
  180.3 7.1 %collective-permute-start.15 = (f32[256,1024]{1,0:T(8,128)S(1)}, f32[256,1024]{1,0:T(8,128)S(1)}, u32[]{:S(2)}, u32[]{:S(2)}) collective-permute-start(f32[256,1024]{1,0:T(8,128)S(1)} %slice.46), channel_id=1, source_target_pairs={{0,16},{1,17},{2,18},{3,19},{4,20},{5,21},{6,22},{7,23},{8,24},{9,... | collective-permute-start | bytes 3145736 | tf_op jit(solution)/shard_map/ppermute | solution.py:239
  (4 other events, 5.6 us)
Sparse Core Ops, SparseCore 0:
  9.3 59.2 all-gather.2

commit v13 on v10

--- a/solution.py
+++ b/solution.py
@@ -13,6 +13,7 @@
 PARAMS = pltpu.CompilerParams(vmem_limit_bytes=20 * 2**20)
 VM = pl.BlockSpec(memory_space=pltpu.VMEM)
 SM = pl.BlockSpec(memory_space=pltpu.SMEM)
+FAR = pl.BlockSpec(memory_space=pltpu.HBM)
 
 
 def split(value):
@@ -72,23 +73,35 @@
     )(info, lead)
 
 
-def solve(info, pieces, places, rhs):
+def substitute(tri_ref, rhs_ref, out_ref, ready):
+    out_ref[...] = rhs_ref[...]
+    for k in range(8):
+        ready(k)
+        here = pl.ds(k * TILE, TILE)
+        solved = packed_product(tri_ref[k, here, :], pack_right(out_ref[here, :]))
+        out_ref[here, :] = solved
+        right = pack_right(solved)
+        for i in range(k + 1, 8):
+            there = pl.ds(i * TILE, TILE)
+            out_ref[there, :] = out_ref[there, :] - packed_product(tri_ref[k, there, :], right)
+
+
+def pack_pieces(info, refs, places, tri_ref):
+    for ref, parts in zip(refs, places):
+        for half, steps, start, to, rows in parts:
+            half = {"own": info[0], "pair": 1 - info[0]}.get(half, half)
+            k = 4 * half + lax.rem(info[1] + steps, 4)
+            tri_ref[k, pl.ds(to, rows), :] = pack_left(ref[pl.ds(start, rows), :])
+
+
+def solve_first(info, pieces, places, rhs):
     def body(info, *refs):
         rhs_ref, out_ref, tri_ref = refs[-3:]
-        for ref, parts in zip(refs, places):
-            for half, steps, start, to, rows in parts:
-                half = {"own": info[0], "pair": 1 - info[0]}.get(half, half)
-                k = 4 * half + lax.rem(info[1] + steps, 4)
-                tri_ref[k, pl.ds(to, rows), :] = pack_left(ref[pl.ds(start, rows), :])
-        out_ref[...] = rhs_ref[...]
-        for k in range(8):
-            here = pl.ds(k * TILE, TILE)
-            solved = packed_product(tri_ref[k, here, :], pack_right(out_ref[here, :]))
-            out_ref[here, :] = solved
-            right = pack_right(solved)
-            for i in range(k + 1, 8):
-                there = pl.ds(i * TILE, TILE)
-                out_ref[there, :] = out_ref[there, :] - packed_product(tri_ref[k, there, :], right)
+
+        @pl.when(info[2] == 1)
+        def _():
+            pack_pieces(info, refs, places, tri_ref)
+            substitute(tri_ref, rhs_ref, out_ref, lambda k: None)
 
     return pl.pallas_call(
         body,
@@ -97,32 +110,65 @@
         out_specs=VM,
         scratch_shapes=[pltpu.VMEM((8, 1024, 256), BF16)],
         compiler_params=PARAMS,
-        name="block_solve",
+        name="solve_first",
     )(info, *pieces, rhs)
 
 
-def residual(info, pieces, places, rhs, x):
+def residual_or_pack(info, pieces, places, rhs, x):
+    count = len(pieces)
+
     def body(info, *refs):
-        rhs_ref, x_ref, out_ref = refs[-3:]
-        out_ref[...] = rhs_ref[...]
-        for ref, parts in zip(refs, places):
-            for half, steps, start, to, rows in parts:
-                half = {"own": info[0], "pair": 1 - info[0]}[half]
-                k = 4 * half + lax.rem(info[1] + steps, 4)
-                right = pack_right(x_ref[pl.ds(pl.multiple_of(k * TILE, TILE), TILE), :])
-                for n in range(0, rows, TILE):
-                    there = pl.ds(to + n, TILE)
-                    left = pack_left(ref[pl.ds(start + n, TILE), :])
-                    out_ref[there, :] = out_ref[there, :] - packed_product(left, right)
+        rhs_ref, x_ref, out_ref, tri_out, tri_ref, semaphore = refs[count:]
+
+        @pl.when(info[2] == 1)
+        def _():
+            out_ref[...] = rhs_ref[...]
+            for ref, parts in zip(refs, places):
+                for half, steps, start, to, rows in parts:
+                    half = {"own": info[0], "pair": 1 - info[0]}[half]
+                    k = 4 * half + lax.rem(info[1] + steps, 4)
+                    right = pack_right(x_ref[pl.ds(pl.multiple_of(k * TILE, TILE), TILE), :])
+                    for n in range(0, rows, TILE):
+                        there = pl.ds(to + n, TILE)
+                        left = pack_left(ref[pl.ds(start + n, TILE), :])
+                        out_ref[there, :] = out_ref[there, :] - packed_product(left, right)
+
+        @pl.when(info[2] == 2)
+        def _():
+            pack_pieces(info, refs, places, tri_ref)
+            copy = pltpu.make_async_copy(tri_ref, tri_out, semaphore)
+            copy.start()
+            copy.wait()
+
+    return pl.pallas_call(
+        body,
+        out_shape=[jax.ShapeDtypeStruct(rhs.shape, F32), jax.ShapeDtypeStruct((8, 1024, 256), BF16)],
+        in_specs=[SM] + [VM] * (count + 2),
+        out_specs=[VM, FAR],
+        scratch_shapes=[pltpu.VMEM((8, 1024, 256), BF16), pltpu.SemaphoreType.DMA],
+        compiler_params=PARAMS,
+        name="residual_or_pack",
+    )(info, *pieces, rhs, x)
+
+
+def solve_second(info, tri, rhs):
+    def body(info, tri_in, rhs_ref, out_ref, tri_ref, semaphores):
+        @pl.when(info[2] == 1)
+        def _():
+            copies = [pltpu.make_async_copy(tri_in.at[k], tri_ref.at[k], semaphores.at[k]) for k in range(8)]
+            for copy in copies:
+                copy.start()
+            substitute(tri_ref, rhs_ref, out_ref, lambda k: copies[k].wait())
 
     return pl.pallas_call(
         body,
         out_shape=jax.ShapeDtypeStruct(rhs.shape, F32),
-        in_specs=[SM] + [VM] * (len(pieces) + 2),
+        in_specs=[SM, FAR, VM],
         out_specs=VM,
-        compiler_params=PARAMS,
-        name="block_residual",
-    )(info, *pieces, rhs, x)
+        scratch_shapes=[pltpu.VMEM((8, 1024, 256), BF16), pltpu.SemaphoreType.DMA((8,))],
+        compiler_params=PARAMS,
+        name="solve_second",
+    )(info, tri, rhs)
 
 
 def arrange_body(factor_ref, out_ref):
@@ -296,6 +342,7 @@
     after = move(lead, only(1, -1))
     swapped = move(lead, lambda a, b, c, d: (a, b, c + 1 - 2 * (c % 2), d) if holds(a, b, c) and b == 1 else None)
     mixed, swapped, half = lax.optimization_barrier((mixed, swapped, half))
+    other_half = move(half, lambda a, b, c, d: (0, b, 3 - c, d) if a == 0 and c >= 2 else None)
     far_low = move(mixed[:512], only(1, 1))
     far_high = move(after[512:], only(1, -1))
 
@@ -306,6 +353,7 @@
     second = jnp.concatenate([jnp.where(zero, full, after), jnp.where(zero, lower, far_high)], 0)
     got_first = move(first, step(0, 1))
     got_second = move(second, step(0, -1))
+    got_first, other_half = lax.optimization_barrier((got_first, other_half))
     end_low = move(got_first[:768], only(0, 1))
     end_high = move(got_second[768:], only(0, -1))
 
@@ -317,7 +365,7 @@
     for group in ("own", "pair"):
         lower_places.append([(group, 3, 0, 0, 1024), (group, 2, 1024, 0, 512)])
         lower_places.append([(group, 1, 0, 0, 1024), (group, 2, 1024, 512, 512)])
-    return (corner_pieces, corner_places), (lower_pieces, lower_places), half
+    return (corner_pieces, corner_places), (lower_pieces, lower_places), jnp.concatenate([half, other_half], 0)
 
 
 def shards(factor, cross_cov):
@@ -333,18 +381,18 @@
     lead = invert_diagonal(info, local[0])
 
     half = lax.all_to_all(arrange_rhs(yh, rhs), ("yl", "z"), 0, 0, tiled=True).reshape(512, TILE)
-    upper_left, lower_row, half = gather(lead, half, core, yl)
-    other_half = move(half, lambda a, b, c, d: (0, b, 3 - c, d) if a == 0 and c >= 2 else None)
-    columns = jnp.concatenate([half, other_half], 0)
-
-    place = jnp.stack([yl, z]).astype(jnp.int32)
-    first = solve(place, *upper_left, columns)
+    upper_left, lower_row, columns = gather(lead, half, core, yl)
+
+    def place(what):
+        return jnp.stack([yl, z, jnp.where(xi == 0, what, 0)]).astype(jnp.int32)
+
+    first = solve_first(place((core == 0) & (yh == 0)), *upper_left, columns)
     sent = move(first, lambda a, b, c, d: (0, 1, c, d) if (a, b) == (0, 0) and c < 2 else None)
-    rest = residual(place, *lower_row, columns, sent)
+    rest, tri = residual_or_pack(place(core * (1 + yh)), *lower_row, columns, sent)
     second_rhs = move(rest, lambda a, b, c, d: (0, 1, 3 - c, d) if (a, b) == (0, 1) and c < 2 else None)
     by_rows, rest = lax.optimization_barrier((arrange(local), rest))
     left = lax.all_to_all(by_rows, COL, 0, 0, tiled=True)
-    second = solve(place, *lower_row, second_rhs)
+    second = solve_second(place((core == 1) & (yh == 1)), tri, second_rhs)
     mine, left = lax.optimization_barrier((deal(first, second, core, yh, xi), left))
 
     def swap(value):

time: 182 us -> 180 us (0.989)
  Pallas kernels: 24.9 us -> 17.9 us
  starting transfers between devices: 46.5 us -> 39.5 us
  waiting for transfers between devices: 94.4 us -> 101 us
  local copies, waits for them, and re-layouts: 12 us -> 16 us
    ppermute x26, starting transfers between devices: 35.9 us -> 28.9 us  [move(): return lax.ppermute(value, AXES, pairs)]
    ppermute x26, waiting for transfers between devices: 89 us -> 96 us  [move(): return lax.ppermute(value, AXES, pairs)]
    pallas_call x3, Pallas kernels: 10.8 us -> 4.42 us  [the longest x1 1.93 us: solve_first(): pl.pallas_call(body, out_shape=jax.ShapeDtypeStruct(rhs.shape, F32), in_s...]
    unnamed x35 -> x29, local copies, waits for them, and re-layouts: 7.29 us -> 8.84 us
  transfers between devices with their start and end apart: 28 -> 28, of which waited for: 10 -> 9; matrix products, arithmetic and copies ran while one was open for 2% -> 4% of each run, Pallas kernels for 9% -> 6%
where the time goes in v13:
time: 180 us; the launch traced here: 178 us
  waiting for transfers between devices  101 us (56%)
  starting transfers between devices  39.5 us (22%)
  Pallas kernels  17.9 us (10%)
  local copies, waits for them, and re-layouts  16 us (9%)
  other arithmetic  3.16 us (2%)
    ppermute x26, waiting for transfers between devices, move(): return lax.ppermute(value, AXES, pairs)  96 us
    ppermute x26, starting transfers between devices, move(): return lax.ppermute(value, AXES, pairs)  28.9 us
    pallas_call x3, Pallas kernels, accumulate(): pl.pallas_call(body, out_shape=jax.ShapeDtypeStruct((512, 1024), F32), in...  10.5 us
    unnamed x29, local copies, waits for them, and re-layouts  8.84 us
    all_to_all x1, starting transfers between devices, shards(): lax.all_to_all(arrange_rhs(yh, rhs), ('yl', 'z'), 0, 0, tiled=True)  6.05 us
    all_to_all x1, waiting for transfers between devices, shards(): lax.all_to_all(arrange_rhs(yh, rhs), ('yl', 'z'), 0, 0, tiled=True)  5.39 us
    all_to_all x1, starting transfers between devices, shards(): left = lax.all_to_all(by_rows, COL, 0, 0, tiled=True)  4.62 us
  transfers between devices with their start and end apart: 28, of which 9 were waited for; matrix products, arithmetic and copies ran while one was open for 4% of the time, Pallas kernels for 6%

profile of v13, /device:TPU:5, one launch (start us, length us, event | category | flops | bytes accessed | tf_op | source)
XLA Modules:
  0.0 178.4 jit_solution(5134639126047647117)
XLA Ops:
  4.7 6.0 %all-to-all-start = ((f32[8,64,128]{2,1,0:T(8,128)}), f32[8,64,128]{2,1,0:T(8,128)S(1)}, u32[]{:S(2)}, u32[]{:S(2)}) async-start(f32[8,64,128]{2,1,0:T(8,128)} %arrange_rhs.1), calls=%async_computation | async-start | bytes 524288 | tf_op jit(solution)/shard_map/all_to_all | solution.py:383
  11.4 5.4 %all-to-all-done = f32[8,64,128]{2,1,0:T(8,128)S(1)} async-done(((f32[8,64,128]{2,1,0:T(8,128)}), f32[8,64,128]{2,1,0:T(8,128)S(1)}, u32[]{:S(2)}, u32[]{:S(2)}) %all-to-all-start) | async-done | bytes 262176 | tf_op jit(solution)/shard_map/all_to_all | solution.py:383
  20.9 1.4 collective-permute-start.8
  23.1 1.4 collective-permute-start.9
  26.5 1.9 %solve_first.1 = f32[1024,128]{1,0:T(8,128)} custom-call(s32[3]{0:T(128)S(1)} %pad_add_fusion.1.info, f32[1536,128]{1,0:T(8,128)S(1)} %pad_maximum_fusion.1.refs_0_.refs_2_, f32[1536,128]{1,0:T(8,128)S(1)} %collective-permute-done.5.refs_1_.refs_5_, f32[1536,128]{1,0:T(8,128)S(1)} %collective-permute-done.6.refs_2_.refs_4_, ...), custom_call_target="tpu_custom_call" | custom-call | tf_op jit(solution)/shard_map/solve_first/pallas_call | solution.py:106
  28.5 1.5 collective-permute-start.10
  32.3 1.9 %residual_or_pack.1 = (f32[1024,128]{1,0:T(8,128)}, bf16[8,1024,256]{2,1,0:T(8,128)(2,1)S(1)}) custom-call(s32[3]{0:T(128)S(1)} %pad_add_fusion.5.info, f32[1024,128]{1,0:T(8,128)S(1)} %invert_diagonal.1.refs_0_, f32[1024,128]{1,0:T(8,128)S(1)} %copy-done.9, f32[1536,128]{1,0:T(8,128)S(1)} %pad_maximum_fusion.1.refs_0_.refs_2_, f32[1536,128]{1,0:T(8,128)S(1)} %copy-done.7, ...), custom_call_target="tpu_custom_call" | custom-call | tf_op jit(solution)/shard_map/residual_or_pack/pallas_call | solution.py:143
  34.2 2.0 %copy-done.3 = bf16[8,1024,256]{2,1,0:T(8,128)(2,1)} copy-done((bf16[8,1024,256]{2,1,0:T(8,128)(2,1)}, bf16[8,1024,256]{2,1,0:T(8,128)(2,1)S(1)}, u32[]{:S(2)}) %copy-start.3) | copy-done | bytes 4194328
  37.0 1.4 copy-done
  38.4 4.6 %all-to-all-start.1 = ((f32[16,256,128]{2,1,0:T(8,128)}), f32[16,256,128]{2,1,0:T(8,128)S(1)}, u32[]{:S(2)}, u32[]{:S(2)}) async-start(f32[16,256,128]{2,1,0:T(8,128)} %copy-done), calls=%async_computation.1 | async-start | bytes 4194304 | tf_op jit(solution)/shard_map/all_to_all | solution.py:394
  43.1 2.2 %copy-done.4 = bf16[8,1024,256]{2,1,0:T(8,128)(2,1)S(1)} copy-done((bf16[8,1024,256]{2,1,0:T(8,128)(2,1)S(1)}, bf16[8,1024,256]{2,1,0:T(8,128)(2,1)}, u32[]{:S(2)}) %copy-start.4) | copy-done | bytes 4194328
  49.5 76.9 %collective-permute-done.15 = f32[512,128]{1,0:T(8,128)S(1)} collective-permute-done((f32[512,128]{1,0:T(8,128)S(1)}, f32[512,128]{1,0:T(8,128)S(1)}, u32[]{:S(2)}, u32[]{:S(2)}) %collective-permute-start.15) | collective-permute-done | bytes 262176 | tf_op jit(solution)/shard_map/ppermute | solution.py:294
  126.6 1.5 collective-permute-start.18
  128.0 4.0 %collective-permute-done.17 = f32[512,128]{1,0:T(8,128)S(1)} collective-permute-done((f32[512,128]{1,0:T(8,128)S(1)}, f32[512,128]{1,0:T(8,128)S(1)}, u32[]{:S(2)}, u32[]{:S(2)}) %collective-permute-start.17) | collective-permute-done | bytes 262176 | tf_op jit(solution)/shard_map/ppermute | solution.py:294
  135.9 2.4 %collective-permute-done.19 = f32[256,128]{1,0:T(8,128)S(1)} collective-permute-done((f32[256,128]{1,0:T(8,128)S(1)}, f32[256,128]{1,0:T(8,128)S(1)}, u32[]{:S(2)}, u32[]{:S(2)}) %collective-permute-start.19) | collective-permute-done | bytes 131104 | tf_op jit(solution)/shard_map/ppermute | solution.py:294
  140.1 2.2 %collective-permute-start.22 = (f32[4,512,128]{2,1,0:T(8,128)S(1)}, f32[4,512,128]{2,1,0:T(8,128)}, u32[]{:S(2)}, u32[]{:S(2)}) collective-permute-start(f32[4,512,128]{2,1,0:T(8,128)S(1)} %pad_maximum_fusion.refs_0_), channel_id=1, source_target_pairs={{0,12},{1,13},{2,14},{3,15},{4,0},{5,1},{6,2},{7,3},{8,4},{9,5},{1... | collective-permute-start | bytes 3145736 | tf_op jit(solution)/shard_map/ppermute | solution.py:294
  142.4 1.6 prepare_update.1
  144.0 2.5 %update_near.1.refs_0_ = f32[512,1024]{1,0:T(8,128)S(1)} custom-call(s32[5]{0:T(128)S(1)} %stack.78.info, bf16[4,512,256]{2,1,0:T(8,128)(2,1)S(1)} %get-tuple-element.32.high_ref, bf16[4,512,256]{2,1,0:T(8,128)(2,1)S(1)} %get-tuple-element.33.low_ref, f32[4,512,128]{2,1,0:T(8,128)S(1)} %pad_maximum_fusion.refs_0_), custom_call_target="tpu_custom_call" | custom-call | tf_op jit(solution)/shard_map/update_near/pallas_call | solution.py:270
  146.5 8.4 %collective-permute-done.21.refs_2_ = f32[4,512,128]{2,1,0:T(8,128)} collective-permute-done((f32[4,512,128]{2,1,0:T(8,128)S(1)}, f32[4,512,128]{2,1,0:T(8,128)}, u32[]{:S(2)}, u32[]{:S(2)}) %collective-permute-start.21) | collective-permute-done | bytes 1048608 | tf_op jit(solution)/shard_map/ppermute | solution.py:294
  157.2 2.6 %collective-permute-start.24 = (f32[2,512,128]{2,1,0:T(8,128)S(1)}, f32[2,512,128]{2,1,0:T(8,128)S(1)}, u32[]{:S(2)}, u32[]{:S(2)}) collective-permute-start(f32[2,512,128]{2,1,0:T(8,128)S(1)} %slice.62), channel_id=1, source_target_pairs={{0,12},{1,13},{2,14},{3,15},{4,0},{5,1},{6,2},{7,3},{8,4},{9,5},{1... | collective-permute-start | bytes 1572872 | tf_op jit(solution)/shard_map/ppermute | solution.py:294
  159.8 5.4 %update_next.1.refs_0_ = f32[512,1024]{1,0:T(8,128)S(1)} custom-call(s32[5]{0:T(128)S(1)} %stack.78.info, bf16[4,512,256]{2,1,0:T(8,128)(2,1)S(1)} %get-tuple-element.32.high_ref, bf16[4,512,256]{2,1,0:T(8,128)(2,1)S(1)} %get-tuple-element.33.low_ref, f32[512,1024]{1,0:T(8,128)S(1)} %update_near.1.refs_0_, ...), custom_call_target="tpu_custom_call", output_to_operand_aliasing={{}: (3, {})} | custom-call | tf_op jit(solution)/shard_map/update_next/pallas_call | solution.py:270
  166.0 2.6 %update_far.1 = f32[512,1024]{1,0:T(8,128)S(1)} custom-call(s32[5]{0:T(128)S(1)} %stack.78.info, bf16[4,512,256]{2,1,0:T(8,128)(2,1)S(1)} %get-tuple-element.32.high_ref, bf16[4,512,256]{2,1,0:T(8,128)(2,1)S(1)} %get-tuple-element.33.low_ref, f32[512,1024]{1,0:T(8,128)S(1)} %update_next.1.refs_0_, ...), custom_call_target="tpu_custom_call", output_to_operand_aliasing={{}: (3, {})} | custom-call | tf_op jit(solution)/shard_map/update_far/pallas_call | solution.py:270
  168.7 6.3 %collective-permute-start.25 = (f32[256,1024]{1,0:T(8,128)S(1)}, f32[256,1024]{1,0:T(8,128)S(1)}, u32[]{:S(2)}, u32[]{:S(2)}) collective-permute-start(f32[256,1024]{1,0:T(8,128)S(1)} %slice.73), channel_id=1, source_target_pairs={{0,16},{1,17},{2,18},{3,19},{4,20},{5,21},{6,22},{7,23},{8,24},{9,... | collective-permute-start | bytes 3145736 | tf_op jit(solution)/shard_map/ppermute | solution.py:294
  175.0 2.3 %collective-permute-done.25 = f32[256,1024]{1,0:T(8,128)S(1)} collective-permute-done((f32[256,1024]{1,0:T(8,128)S(1)}, f32[256,1024]{1,0:T(8,128)S(1)}, u32[]{:S(2)}, u32[]{:S(2)}) %collective-permute-start.25) | collective-permute-done | bytes 1048608 | tf_op jit(solution)/shard_map/ppermute | solution.py:294
  (101 shorter events, 29.7 us)
Async XLA Ops:
  1.8 8.9 %collective-permute-start.3 = (f32[1024,128]{1,0:T(8,128)S(1)}, f32[1024,128]{1,0:T(8,128)S(1)}, u32[]{:S(2)}, u32[]{:S(2)}) collective-permute-start(f32[1024,128]{1,0:T(8,128)S(1)} %invert_diagonal.1.refs_0_), channel_id=1, source_target_pairs={{16,19},{17,16},{18,17},{19,18},{20,23},{21,20},{22,21},{23,22},{2... | collective-permute-start | bytes 1572872 | tf_op jit(solution)/shard_map/ppermute | solution.py:294
  2.5 14.3 %collective-permute-start = (f32[1024,128]{1,0:T(8,128)S(1)}, f32[1024,128]{1,0:T(8,128)S(1)}, u32[]{:S(2)}, u32[]{:S(2)}) collective-permute-start(f32[1024,128]{1,0:T(8,128)S(1)} %invert_diagonal.1.refs_0_), channel_id=1, source_target_pairs={{0,4},{1,5},{2,6},{3,7},{4,0},{5,1},{6,2},{7,3},{16,17},{17,18},{1... | collective-permute-start | bytes 1572872 | tf_op jit(solution)/shard_map/ppermute | solution.py:294
  3.2 13.6 %collective-permute-start.1 = (f32[1024,128]{1,0:T(8,128)S(1)}, f32[1024,128]{1,0:T(8,128)S(1)}, u32[]{:S(2)}, u32[]{:S(2)}) collective-permute-start(f32[1024,128]{1,0:T(8,128)S(1)} %invert_diagonal.1.refs_0_), channel_id=1, source_target_pairs={{16,20},{17,21},{18,22},{19,23},{20,16},{21,17},{22,18},{23,19},{2... | collective-permute-start | bytes 1572872 | tf_op jit(solution)/shard_map/ppermute | solution.py:294
  4.7 12.2 %all-to-all-start = ((f32[8,64,128]{2,1,0:T(8,128)}), f32[8,64,128]{2,1,0:T(8,128)S(1)}, u32[]{:S(2)}, u32[]{:S(2)}) async-start(f32[8,64,128]{2,1,0:T(8,128)} %arrange_rhs.1), calls=%async_computation | async-start | bytes 524288 | tf_op jit(solution)/shard_map/all_to_all | solution.py:383
  10.8 6.9 %collective-permute-start.4 = (f32[512,128]{1,0:T(8,128)S(1)}, f32[512,128]{1,0:T(8,128)S(1)}, u32[]{:S(2)}, u32[]{:S(2)}) collective-permute-start(f32[512,128]{1,0:T(8,128)S(1)} %slice.66), channel_id=1, source_target_pairs={{16,19},{17,16},{18,17},{19,18},{20,23},{21,20},{22,21},{23,22},{2... | collective-permute-start | bytes 786440 | tf_op jit(solution)/shard_map/ppermute | solution.py:294
  17.8 2.2 %collective-permute-start.6 = (f32[1536,128]{1,0:T(8,128)S(1)}, f32[1536,128]{1,0:T(8,128)S(1)}, u32[]{:S(2)}, u32[]{:S(2)}) collective-permute-start(f32[1536,128]{1,0:T(8,128)S(1)} %pad_maximum_fusion.1.refs_0_.refs_2_), channel_id=1, source_target_pairs={{0,1},{1,2},{2,3},{3,0},{4,5},{5,6},{6,7},{7,4},{16,20},{17,21},{1... | collective-permute-start | bytes 2359304 | tf_op jit(solution)/shard_map/ppermute | solution.py:294
  18.6 3.7 %collective-permute-start.5 = (f32[1536,128]{1,0:T(8,128)S(1)}, f32[1536,128]{1,0:T(8,128)S(1)}, u32[]{:S(2)}, u32[]{:S(2)}) collective-permute-start(f32[1536,128]{1,0:T(8,128)S(1)} %pad_maximum_fusion.2.refs_3_), channel_id=1, source_target_pairs={{0,3},{1,0},{2,1},{3,2},{4,7},{5,4},{6,5},{7,6},{16,20},{17,21},{1... | collective-permute-start | bytes 2359304 | tf_op jit(solution)/shard_map/ppermute | solution.py:294
  20.9 5.6 %collective-permute-start.8 = (f32[768,128]{1,0:T(8,128)}, f32[768,128]{1,0:T(8,128)}, u32[]{:S(2)}, u32[]{:S(2)}) collective-permute-start(f32[768,128]{1,0:T(8,128)} %slice.55), channel_id=1, source_target_pairs={{0,1},{1,2},{2,3},{3,0},{4,5},{5,6},{6,7},{7,4}} | collective-permute-start | bytes 1179656 | tf_op jit(solution)/shard_map/ppermute | solution.py:294
  23.1 3.5 %collective-permute-start.9 = (f32[768,128]{1,0:T(8,128)}, f32[768,128]{1,0:T(8,128)}, u32[]{:S(2)}, u32[]{:S(2)}) collective-permute-start(f32[768,128]{1,0:T(8,128)} %slice.67), channel_id=1, source_target_pairs={{0,3},{1,0},{2,1},{3,2},{4,7},{5,4},{6,5},{7,6}} | collective-permute-start | bytes 1179656 | tf_op jit(solution)/shard_map/ppermute | solution.py:294
  28.5 1.6 collective-permute-start.10
  36.2 6.9 %collective-permute-start.11 = (f32[1024,128]{1,0:T(8,128)}, f32[1024,128]{1,0:T(8,128)S(1)}, u32[]{:S(2)}, u32[]{:S(2)}) collective-permute-start(f32[1024,128]{1,0:T(8,128)} %get-tuple-element.29), channel_id=1, source_target_pairs={{16,28},{17,29},{18,30},{19,31},{20,24},{21,25},{22,26},{23,27}} | collective-permute-start | bytes 1572872 | tf_op jit(solution)/shard_map/ppermute | solution.py:294
  38.4 88.1 %all-to-all-start.1 = ((f32[16,256,128]{2,1,0:T(8,128)}), f32[16,256,128]{2,1,0:T(8,128)S(1)}, u32[]{:S(2)}, u32[]{:S(2)}) async-start(f32[16,256,128]{2,1,0:T(8,128)} %copy-done), calls=%async_computation.1 | async-start | bytes 4194304 | tf_op jit(solution)/shard_map/all_to_all | solution.py:394
  47.5 2.0 %collective-permute-start.14 = (f32[512,128]{1,0:T(8,128)S(1)}, f32[512,128]{1,0:T(8,128)S(1)}, u32[]{:S(2)}, u32[]{:S(2)}) collective-permute-start(f32[512,128]{1,0:T(8,128)S(1)} %select_select_fusion.2), channel_id=1, source_target_pairs={{0,96},{1,97},{2,98},{3,99},{4,100},{5,101},{6,102},{7,103},{8,104... | collective-permute-start | bytes 786440 | tf_op jit(solution)/shard_map/ppermute | solution.py:294
  48.2 78.2 %collective-permute-start.15 = (f32[512,128]{1,0:T(8,128)S(1)}, f32[512,128]{1,0:T(8,128)S(1)}, u32[]{:S(2)}, u32[]{:S(2)}) collective-permute-start(f32[512,128]{1,0:T(8,128)S(1)} %collective-permute-done.13), channel_id=1, source_target_pairs={{32,64},{33,65},{34,66},{35,67},{36,68},{37,69},{38,70},{39,71},{4... | collective-permute-start | bytes 786440 | tf_op jit(solution)/shard_map/ppermute | solution.py:294
  126.5 5.5 %collective-permute-start.17 = (f32[512,128]{1,0:T(8,128)S(1)}, f32[512,128]{1,0:T(8,128)S(1)}, u32[]{:S(2)}, u32[]{:S(2)}) collective-permute-start(f32[512,128]{1,0:T(8,128)S(1)} %add_select_fusion), channel_id=1, source_target_pairs={{0,3},{1,0},{2,1},{3,2},{4,7},{5,4},{6,5},{7,6},{8,11},{9,8},{10,9... | collective-permute-start | bytes 786440 | tf_op jit(solution)/shard_map/ppermute | solution.py:294
  126.6 6.5 %collective-permute-start.18 = (f32[512,128]{1,0:T(8,128)S(1)}, f32[512,128]{1,0:T(8,128)S(1)}, u32[]{:S(2)}, u32[]{:S(2)}) collective-permute-start(f32[512,128]{1,0:T(8,128)S(1)} %add_select_fusion), channel_id=1, source_target_pairs={{0,1},{1,2},{2,3},{3,0},{4,5},{5,6},{6,7},{7,4},{8,9},{9,10},{10,1... | collective-permute-start | bytes 786440 | tf_op jit(solution)/shard_map/ppermute | solution.py:294
  132.0 3.9 %collective-permute-start.20 = (f32[256,128]{1,0:T(8,128)S(1)}, f32[256,128]{1,0:T(8,128)S(1)}, u32[]{:S(2)}, u32[]{:S(2)}) collective-permute-start(f32[256,128]{1,0:T(8,128)S(1)} %slice.71), channel_id=1, source_target_pairs={{0,3},{1,0},{2,1},{3,2},{4,7},{5,4},{6,5},{7,6},{8,11},{9,8},{10,9... | collective-permute-start | bytes 393224 | tf_op jit(solution)/shard_map/ppermute | solution.py:294
  133.1 5.2 %collective-permute-start.19 = (f32[256,128]{1,0:T(8,128)S(1)}, f32[256,128]{1,0:T(8,128)S(1)}, u32[]{:S(2)}, u32[]{:S(2)}) collective-permute-start(f32[256,128]{1,0:T(8,128)S(1)} %slice.70), channel_id=1, source_target_pairs={{0,1},{1,2},{2,3},{3,0},{4,5},{5,6},{6,7},{7,4},{8,9},{9,10},{10,1... | collective-permute-start | bytes 393224 | tf_op jit(solution)/shard_map/ppermute | solution.py:294
  134.7 7.7 %collective-permute-start.16 = (f32[8,256,128]{2,1,0:T(8,128)}, f32[8,256,128]{2,1,0:T(8,128)}, u32[]{:S(2)}, u32[]{:S(2)}) collective-permute-start(f32[8,256,128]{2,1,0:T(8,128)} %constant_dynamic-slice_fusion), channel_id=1, source_target_pairs={{0,16},{1,17},{2,18},{3,19},{4,20},{5,21},{6,22},{7,23},{8,24},{9,... | collective-permute-start | bytes 3145736 | tf_op jit(solution)/shard_map/ppermute | solution.py:294
  139.5 15.3 %collective-permute-start.21 = (f32[4,512,128]{2,1,0:T(8,128)S(1)}, f32[4,512,128]{2,1,0:T(8,128)}, u32[]{:S(2)}, u32[]{:S(2)}) collective-permute-start(f32[4,512,128]{2,1,0:T(8,128)S(1)} %pad_maximum_fusion.refs_0_), channel_id=1, source_target_pairs={{0,4},{1,5},{2,6},{3,7},{4,8},{5,9},{6,10},{7,11},{8,12},{9,13},{1... | collective-permute-start | bytes 3145736 | tf_op jit(solution)/shard_map/ppermute | solution.py:294
  140.1 14.8 %collective-permute-start.22 = (f32[4,512,128]{2,1,0:T(8,128)S(1)}, f32[4,512,128]{2,1,0:T(8,128)}, u32[]{:S(2)}, u32[]{:S(2)}) collective-permute-start(f32[4,512,128]{2,1,0:T(8,128)S(1)} %pad_maximum_fusion.refs_0_), channel_id=1, source_target_pairs={{0,12},{1,13},{2,14},{3,15},{4,0},{5,1},{6,2},{7,3},{8,4},{9,5},{1... | collective-permute-start | bytes 3145736 | tf_op jit(solution)/shard_map/ppermute | solution.py:294
  155.9 9.6 %collective-permute-start.23 = (f32[2,512,128]{2,1,0:T(8,128)S(1)}, f32[2,512,128]{2,1,0:T(8,128)S(1)}, u32[]{:S(2)}, u32[]{:S(2)}) collective-permute-start(f32[2,512,128]{2,1,0:T(8,128)S(1)} %slice.61), channel_id=1, source_target_pairs={{0,4},{1,5},{2,6},{3,7},{4,8},{5,9},{6,10},{7,11},{8,12},{9,13},{1... | collective-permute-start | bytes 1572872 | tf_op jit(solution)/shard_map/ppermute | solution.py:294
  157.2 8.8 %collective-permute-start.24 = (f32[2,512,128]{2,1,0:T(8,128)S(1)}, f32[2,512,128]{2,1,0:T(8,128)S(1)}, u32[]{:S(2)}, u32[]{:S(2)}) collective-permute-start(f32[2,512,128]{2,1,0:T(8,128)S(1)} %slice.62), channel_id=1, source_target_pairs={{0,12},{1,13},{2,14},{3,15},{4,0},{5,1},{6,2},{7,3},{8,4},{9,5},{1... | collective-permute-start | bytes 1572872 | tf_op jit(solution)/shard_map/ppermute | solution.py:294
  168.7 8.6 %collective-permute-start.25 = (f32[256,1024]{1,0:T(8,128)S(1)}, f32[256,1024]{1,0:T(8,128)S(1)}, u32[]{:S(2)}, u32[]{:S(2)}) collective-permute-start(f32[256,1024]{1,0:T(8,128)S(1)} %slice.73), channel_id=1, source_target_pairs={{0,16},{1,17},{2,18},{3,19},{4,20},{5,21},{6,22},{7,23},{8,24},{9,... | collective-permute-start | bytes 3145736 | tf_op jit(solution)/shard_map/ppermute | solution.py:294
  (18 other events, 54.2 us)

commit v14 on v13

--- a/solution.py
+++ b/solution.py
@@ -10,6 +10,7 @@
 F32 = jnp.float32
 BF16 = jnp.bfloat16
 TILE = 128
+STORE = 112
 PARAMS = pltpu.CompilerParams(vmem_limit_bytes=20 * 2**20)
 VM = pl.BlockSpec(memory_space=pltpu.VMEM)
 SM = pl.BlockSpec(memory_space=pltpu.SMEM)
@@ -136,13 +137,13 @@
         @pl.when(info[2] == 2)
         def _():
             pack_pieces(info, refs, places, tri_ref)
-            copy = pltpu.make_async_copy(tri_ref, tri_out, semaphore)
+            copy = pltpu.make_async_copy(tri_ref, tri_out.at[pl.ds(0, 8)], semaphore)
             copy.start()
             copy.wait()
 
     return pl.pallas_call(
         body,
-        out_shape=[jax.ShapeDtypeStruct(rhs.shape, F32), jax.ShapeDtypeStruct((8, 1024, 256), BF16)],
+        out_shape=[jax.ShapeDtypeStruct(rhs.shape, F32), jax.ShapeDtypeStruct((STORE, 1024, 256), BF16)],
         in_specs=[SM] + [VM] * (count + 2),
         out_specs=[VM, FAR],
         scratch_shapes=[pltpu.VMEM((8, 1024, 256), BF16), pltpu.SemaphoreType.DMA],
@@ -294,17 +295,19 @@
     return lax.ppermute(value, AXES, pairs)
 
 
-def deal(first, second, core, yh, xi):
+def deal(first, second, core, yh, xi, by_rows):
     solved = jnp.where(core == 0, first, second)
     lower = yh == 0
     here = jnp.where(lower, solved[:512], solved[512:])
     there = jnp.where(core == 0, solved[512:], solved[:512])
     got = move(there, lambda a, b, c, d: (0, b, 3 - c, d) if a == 0 and b == c // 2 else None)
+    got, by_rows = lax.optimization_barrier((got, by_rows))
+    left = lax.all_to_all(by_rows, COL, 0, 0, tiled=True)
     mine = jnp.where(core == yh, here, got)
     one = move(mine, lambda a, b, c, d: (1 if b == 0 else 3, b, c, d) if a == 0 else None)
     two = move(mine, lambda a, b, c, d: (3 if b == 0 else 1, b, c, d) if a == 0 else None)
     far = move(one, lambda a, b, c, d: (2, b, c, d) if a == (1 if b == 0 else 3) else None)
-    return jnp.where(xi == 0, mine, one + two + far)
+    return jnp.where(xi == 0, mine, one + two + far), left
 
 
 def ring(value, first):
@@ -390,31 +393,39 @@
     sent = move(first, lambda a, b, c, d: (0, 1, c, d) if (a, b) == (0, 0) and c < 2 else None)
     rest, tri = residual_or_pack(place(core * (1 + yh)), *lower_row, columns, sent)
     second_rhs = move(rest, lambda a, b, c, d: (0, 1, 3 - c, d) if (a, b) == (0, 1) and c < 2 else None)
-    by_rows, rest = lax.optimization_barrier((arrange(local), rest))
-    left = lax.all_to_all(by_rows, COL, 0, 0, tiled=True)
     second = solve_second(place((core == 1) & (yh == 1)), tri, second_rhs)
-    mine, left = lax.optimization_barrier((deal(first, second, core, yh, xi), left))
+    mine, left = deal(first, second, core, yh, xi, arrange(local))
 
     def swap(value):
         return move(value, lambda a, b, c, d: (a, 1 - b, c, d))
 
+    info2 = jnp.stack([xi, core, 2 * yh + yl, z, col_id]).astype(jnp.int32)
+
+    after, far_low, far_high, before = ring(mine, True)
+    low = jnp.stack([mine, after])
+    high = jnp.stack([jnp.concatenate([far_low, far_high], 0), before])
+
+    left, _ = lax.optimization_barrier((left, high))
     given = swap(lax.dynamic_slice_in_dim(left, 8 * (1 - core), 8, 0))
-    info2 = jnp.stack([xi, core, 2 * yh + yl, z, col_id]).astype(jnp.int32)
-
-    after, far_low, far_high, before = ring(mine, True)
-    near = jnp.stack([mine, after, jnp.concatenate([far_low, far_high], 0), before])
 
     def along(step):
         return lambda a, b, c, d: (a, b, c + step, d) if b == 0 else (a, b, c, d + step)
 
-    before, after = move(near, along(1)), move(near, along(-1))
-    high, low = prepare(info2[:2], left, given)
-    sums = accumulate(info2, None, high, low, [near], [(0, 0)], "update_near")
-    before, after, sums = lax.optimization_barrier((before, after, sums))
-    far_low, far_high = move(before[:2], along(1)), move(after[2:], along(-1))
-    sums = accumulate(info2, sums, high, low, [after, before], [(1, 0), (3, 0)], "update_next")
+    low_before, low_after = move(low, along(1)), move(low, along(-1))
+    high_after, high_before = move(high, along(-1)), move(high, along(1))
+    parts = prepare(info2[:2], left, given)
+
+    def add(sums, pieces, places, name):
+        return accumulate(info2, sums, *parts, pieces, places, name)
+
+    sums = add(None, [low, high], [(0, 0), (0, 2)], "update_near")
+    low_before, high_after, sums = lax.optimization_barrier((low_before, high_after, sums))
+    far_low, far_high = move(low_before, along(1)), move(high_after, along(-1))
+    sums = add(
+        sums, [low_after, high_after, low_before, high_before], [(1, 0), (1, 2), (3, 0), (3, 2)], "update_next"
+    )
     far_low, far_high, sums = lax.optimization_barrier((far_low, far_high, sums))
-    sums = accumulate(info2, sums, high, low, [far_low, far_high], [(2, 0), (2, 2)], "update_far")
+    sums = add(sums, [far_low, far_high], [(2, 0), (2, 2)], "update_far")
 
     replaced = (xi == 0) & (lax.broadcasted_iota(jnp.int32, (256, 1024), 0) < 64)
     base = jnp.where(replaced, 0.0, rhs.reshape(256, 1024))

time: 180 us -> 171 us (0.950)
  local copies, waits for them, and re-layouts: 16 us -> 10.2 us
  waiting for transfers between devices: 101 us -> 98 us
    unnamed x29 -> x25, local copies, waits for them, and re-layouts: 8.84 us -> 5.17 us
    ppermute x26 -> x28, waiting for transfers between devices: 96 us -> 92.6 us  [move(): return lax.ppermute(value, AXES, pairs)]
    slice x2 -> x0, local copies, waits for them, and re-layouts: 2.15 us -> none  [shards(): far_low, far_high = (move(before[:2], along(1)), move(after[2:], along(-1)))]
    ppermute x26 -> x28, starting transfers between devices: 28.9 us -> 28.4 us  [move(): return lax.ppermute(value, AXES, pairs)]
  transfers between devices with their start and end apart: 28 -> 30, of which waited for: 9 -> 9; matrix products, arithmetic and copies ran while one was open for 4% -> 4% of each run, Pallas kernels for 6% -> 6%
where the time goes in v14:
time: 171 us; the launch traced here: 170 us
  waiting for transfers between devices  98 us (57%)
  starting transfers between devices  39 us (23%)
  Pallas kernels  17.5 us (10%)
  local copies, waits for them, and re-layouts  10.2 us (6%)
  other arithmetic  4.92 us (3%)
    ppermute x28, waiting for transfers between devices, move(): return lax.ppermute(value, AXES, pairs)  92.6 us
    ppermute x28, starting transfers between devices, move(): return lax.ppermute(value, AXES, pairs)  28.4 us
    pallas_call x3, Pallas kernels, accumulate(): pl.pallas_call(body, out_shape=jax.ShapeDtypeStruct((512, 1024), F32), in...  10.1 us
    all_to_all x1, starting transfers between devices, shards(): lax.all_to_all(arrange_rhs(yh, rhs), ('yl', 'z'), 0, 0, tiled=True)  6.05 us
    all_to_all x1, waiting for transfers between devices, shards(): lax.all_to_all(arrange_rhs(yh, rhs), ('yl', 'z'), 0, 0, tiled=True)  5.39 us
    unnamed x25, local copies, waits for them, and re-layouts  5.17 us
    all_to_all x1, starting transfers between devices, deal(): left = lax.all_to_all(by_rows, COL, 0, 0, tiled=True)  4.62 us
  transfers between devices with their start and end apart: 30, of which 9 were waited for; matrix products, arithmetic and copies ran while one was open for 4% of the time, Pallas kernels for 6%

profile of v14, /device:TPU:5, one launch (start us, length us, event | category | flops | bytes accessed | tf_op | source)
XLA Modules:
  0.0 170.2 jit_solution(9175899306384554965)
XLA Ops:
  4.7 6.0 %all-to-all-start = ((f32[8,64,128]{2,1,0:T(8,128)}), f32[8,64,128]{2,1,0:T(8,128)S(1)}, u32[]{:S(2)}, u32[]{:S(2)}) async-start(f32[8,64,128]{2,1,0:T(8,128)} %arrange_rhs.1), calls=%async_computation | async-start | bytes 524288 | tf_op jit(solution)/shard_map/all_to_all | solution.py:386
  11.4 5.4 %all-to-all-done = f32[8,64,128]{2,1,0:T(8,128)S(1)} async-done(((f32[8,64,128]{2,1,0:T(8,128)}), f32[8,64,128]{2,1,0:T(8,128)S(1)}, u32[]{:S(2)}, u32[]{:S(2)}) %all-to-all-start) | async-done | bytes 262176 | tf_op jit(solution)/shard_map/all_to_all | solution.py:386
  20.9 1.4 collective-permute-start.8
  23.1 1.4 collective-permute-start.9
  26.5 1.9 %solve_first.1 = f32[1024,128]{1,0:T(8,128)} custom-call(s32[3]{0:T(128)S(1)} %pad_add_fusion.1.info, f32[1536,128]{1,0:T(8,128)S(1)} %pad_maximum_fusion.refs_0_.refs_2_, f32[1536,128]{1,0:T(8,128)S(1)} %collective-permute-done.5.refs_1_.refs_5_, f32[1536,128]{1,0:T(8,128)S(1)} %collective-permute-done.6.refs_2_.refs_4_, ...), custom_call_target="tpu_custom_call" | custom-call | tf_op jit(solution)/shard_map/solve_first/pallas_call | solution.py:107
  28.5 1.5 collective-permute-start.10
  32.2 1.9 %residual_or_pack.1 = (f32[1024,128]{1,0:T(8,128)}, bf16[112,1024,256]{2,1,0:T(8,128)(2,1)}) custom-call(s32[3]{0:T(128)S(1)} %pad_add_fusion.5.info, f32[1024,128]{1,0:T(8,128)S(1)} %invert_diagonal.1.refs_0_, f32[1024,128]{1,0:T(8,128)S(1)} %copy-done.7, f32[1536,128]{1,0:T(8,128)S(1)} %pad_maximum_fusion.refs_0_.refs_2_, f32[1536,128]{1,0:T(8,128)S(1)} %copy-done.5, ...), custom_call_target="tpu_custom_call" | custom-call | tf_op jit(solution)/shard_map/residual_or_pack/pallas_call | solution.py:144
  38.6 4.6 %all-to-all-start.1 = ((f32[16,256,128]{2,1,0:T(8,128)}), f32[16,256,128]{2,1,0:T(8,128)S(1)}, u32[]{:S(2)}, u32[]{:S(2)}) async-start(f32[16,256,128]{2,1,0:T(8,128)} %copy-done), calls=%async_computation.1 | async-start | bytes 4194304 | tf_op jit(solution)/shard_map/all_to_all | solution.py:305
  45.9 77.4 %collective-permute-done.15 = f32[512,128]{1,0:T(8,128)S(1)} collective-permute-done((f32[512,128]{1,0:T(8,128)S(1)}, f32[512,128]{1,0:T(8,128)S(1)}, u32[]{:S(2)}, u32[]{:S(2)}) %collective-permute-start.15) | collective-permute-done | bytes 262176 | tf_op jit(solution)/shard_map/ppermute | solution.py:295
  123.4 2.6 %collective-permute-start.18 = (f32[512,128]{1,0:T(8,128)S(1)}, f32[512,128]{1,0:T(8,128)S(1)}, u32[]{:S(2)}, u32[]{:S(2)}) collective-permute-start(f32[512,128]{1,0:T(8,128)S(1)} %add_select_fusion), channel_id=1, source_target_pairs={{0,3},{1,0},{2,1},{3,2},{4,7},{5,4},{6,5},{7,6},{8,11},{9,8},{10,9... | collective-permute-start | bytes 786440 | tf_op jit(solution)/shard_map/ppermute | solution.py:295
  126.0 3.3 %collective-permute-done.18 = f32[512,128]{1,0:T(8,128)S(1)} collective-permute-done((f32[512,128]{1,0:T(8,128)S(1)}, f32[512,128]{1,0:T(8,128)S(1)}, u32[]{:S(2)}, u32[]{:S(2)}) %collective-permute-start.18) | collective-permute-done | bytes 262176 | tf_op jit(solution)/shard_map/ppermute | solution.py:295
  129.3 3.2 %collective-permute-start.19 = (f32[256,128]{1,0:T(8,128)S(1)}, f32[256,128]{1,0:T(8,128)S(1)}, u32[]{:S(2)}, u32[]{:S(2)}) collective-permute-start(f32[256,128]{1,0:T(8,128)S(1)} %slice.63), channel_id=1, source_target_pairs={{0,3},{1,0},{2,1},{3,2},{4,7},{5,4},{6,5},{7,6},{8,11},{9,8},{10,9... | collective-permute-start | bytes 393224 | tf_op jit(solution)/shard_map/ppermute | solution.py:295
  132.6 1.8 %collective-permute-done.19 = f32[256,128]{1,0:T(8,128)S(1)} collective-permute-done((f32[256,128]{1,0:T(8,128)S(1)}, f32[256,128]{1,0:T(8,128)S(1)}, u32[]{:S(2)}, u32[]{:S(2)}) %collective-permute-start.19) | collective-permute-done | bytes 131104 | tf_op jit(solution)/shard_map/ppermute | solution.py:295
  134.5 3.3 %collective-permute-done.17 = f32[256,128]{1,0:T(8,128)} collective-permute-done((f32[256,128]{1,0:T(8,128)S(1)}, f32[256,128]{1,0:T(8,128)}, u32[]{:S(2)}, u32[]{:S(2)}) %collective-permute-start.17) | collective-permute-done | bytes 131104 | tf_op jit(solution)/shard_map/ppermute | solution.py:295
  143.0 1.5 collective-permute-start.22
  144.6 1.4 collective-permute-start.25
  146.3 1.6 prepare_update.1
  147.8 2.5 %update_near.1.refs_0_ = f32[512,1024]{1,0:T(8,128)S(1)} custom-call(s32[5]{0:T(128)S(1)} %stack.81.info, bf16[4,512,256]{2,1,0:T(8,128)(2,1)S(1)} %get-tuple-element.33.high_ref, bf16[4,512,256]{2,1,0:T(8,128)(2,1)S(1)} %get-tuple-element.34.low_ref, f32[2,512,128]{2,1,0:T(8,128)S(1)} %pad_maximum_fusion.3.refs_0_, f32[2,512,128]{2,1,0:T(8,128)S(1)} %pad_maximum_fusion.2.refs_1_), custom_call_target="tpu_custom_call" | custom-call | tf_op jit(solution)/shard_map/update_near/pallas_call | solution.py:271
  152.6 1.5 collective-permute-start.24
  154.1 2.8 %collective-permute-done.25.refs_1_ = f32[2,512,128]{2,1,0:T(8,128)S(1)} collective-permute-done((f32[2,512,128]{2,1,0:T(8,128)S(1)}, f32[2,512,128]{2,1,0:T(8,128)S(1)}, u32[]{:S(2)}, u32[]{:S(2)}) %collective-permute-start.25) | collective-permute-done | bytes 524320 | tf_op jit(solution)/shard_map/ppermute | solution.py:295
  156.9 5.1 %update_next.1.refs_0_ = f32[512,1024]{1,0:T(8,128)S(1)} custom-call(s32[5]{0:T(128)S(1)} %stack.81.info, bf16[4,512,256]{2,1,0:T(8,128)(2,1)S(1)} %get-tuple-element.33.high_ref, bf16[4,512,256]{2,1,0:T(8,128)(2,1)S(1)} %get-tuple-element.34.low_ref, f32[512,1024]{1,0:T(8,128)S(1)} %update_near.1.refs_0_, ...), custom_call_target="tpu_custom_call", output_to_operand_aliasing={{}: (3, {})} | custom-call | tf_op jit(solution)/shard_map/update_next/pallas_call | solution.py:271
  162.6 2.6 %update_far.1 = f32[512,1024]{1,0:T(8,128)S(1)} custom-call(s32[5]{0:T(128)S(1)} %stack.81.info, bf16[4,512,256]{2,1,0:T(8,128)(2,1)S(1)} %get-tuple-element.33.high_ref, bf16[4,512,256]{2,1,0:T(8,128)(2,1)S(1)} %get-tuple-element.34.low_ref, f32[512,1024]{1,0:T(8,128)S(1)} %update_next.1.refs_0_, ...), custom_call_target="tpu_custom_call", output_to_operand_aliasing={{}: (3, {})} | custom-call | tf_op jit(solution)/shard_map/update_far/pallas_call | solution.py:271
  165.3 1.4 collective-permute-start.27
  166.7 2.3 %collective-permute-done.27 = f32[256,1024]{1,0:T(8,128)S(1)} collective-permute-done((f32[256,1024]{1,0:T(8,128)S(1)}, f32[256,1024]{1,0:T(8,128)S(1)}, u32[]{:S(2)}, u32[]{:S(2)}) %collective-permute-start.27) | collective-permute-done | bytes 1048608 | tf_op jit(solution)/shard_map/ppermute | solution.py:295
  (100 shorter events, 31.4 us)
Async XLA Ops:
  1.8 8.9 %collective-permute-start.3 = (f32[1024,128]{1,0:T(8,128)S(1)}, f32[1024,128]{1,0:T(8,128)S(1)}, u32[]{:S(2)}, u32[]{:S(2)}) collective-permute-start(f32[1024,128]{1,0:T(8,128)S(1)} %invert_diagonal.1.refs_0_), channel_id=1, source_target_pairs={{16,19},{17,16},{18,17},{19,18},{20,23},{21,20},{22,21},{23,22},{2... | collective-permute-start | bytes 1572872 | tf_op jit(solution)/shard_map/ppermute | solution.py:295
  2.5 14.3 %collective-permute-start = (f32[1024,128]{1,0:T(8,128)S(1)}, f32[1024,128]{1,0:T(8,128)S(1)}, u32[]{:S(2)}, u32[]{:S(2)}) collective-permute-start(f32[1024,128]{1,0:T(8,128)S(1)} %invert_diagonal.1.refs_0_), channel_id=1, source_target_pairs={{0,4},{1,5},{2,6},{3,7},{4,0},{5,1},{6,2},{7,3},{16,17},{17,18},{1... | collective-permute-start | bytes 1572872 | tf_op jit(solution)/shard_map/ppermute | solution.py:295
  3.2 13.6 %collective-permute-start.1 = (f32[1024,128]{1,0:T(8,128)S(1)}, f32[1024,128]{1,0:T(8,128)S(1)}, u32[]{:S(2)}, u32[]{:S(2)}) collective-permute-start(f32[1024,128]{1,0:T(8,128)S(1)} %invert_diagonal.1.refs_0_), channel_id=1, source_target_pairs={{16,20},{17,21},{18,22},{19,23},{20,16},{21,17},{22,18},{23,19},{2... | collective-permute-start | bytes 1572872 | tf_op jit(solution)/shard_map/ppermute | solution.py:295
  4.7 12.2 %all-to-all-start = ((f32[8,64,128]{2,1,0:T(8,128)}), f32[8,64,128]{2,1,0:T(8,128)S(1)}, u32[]{:S(2)}, u32[]{:S(2)}) async-start(f32[8,64,128]{2,1,0:T(8,128)} %arrange_rhs.1), calls=%async_computation | async-start | bytes 524288 | tf_op jit(solution)/shard_map/all_to_all | solution.py:386
  10.8 6.9 %collective-permute-start.4 = (f32[512,128]{1,0:T(8,128)S(1)}, f32[512,128]{1,0:T(8,128)S(1)}, u32[]{:S(2)}, u32[]{:S(2)}) collective-permute-start(f32[512,128]{1,0:T(8,128)S(1)} %slice.58), channel_id=1, source_target_pairs={{16,19},{17,16},{18,17},{19,18},{20,23},{21,20},{22,21},{23,22},{2... | collective-permute-start | bytes 786440 | tf_op jit(solution)/shard_map/ppermute | solution.py:295
  17.8 2.2 %collective-permute-start.6 = (f32[1536,128]{1,0:T(8,128)S(1)}, f32[1536,128]{1,0:T(8,128)S(1)}, u32[]{:S(2)}, u32[]{:S(2)}) collective-permute-start(f32[1536,128]{1,0:T(8,128)S(1)} %pad_maximum_fusion.refs_0_.refs_2_), channel_id=1, source_target_pairs={{0,1},{1,2},{2,3},{3,0},{4,5},{5,6},{6,7},{7,4},{16,20},{17,21},{1... | collective-permute-start | bytes 2359304 | tf_op jit(solution)/shard_map/ppermute | solution.py:295
  18.6 3.7 %collective-permute-start.5 = (f32[1536,128]{1,0:T(8,128)S(1)}, f32[1536,128]{1,0:T(8,128)S(1)}, u32[]{:S(2)}, u32[]{:S(2)}) collective-permute-start(f32[1536,128]{1,0:T(8,128)S(1)} %pad_maximum_fusion.1.refs_3_), channel_id=1, source_target_pairs={{0,3},{1,0},{2,1},{3,2},{4,7},{5,4},{6,5},{7,6},{16,20},{17,21},{1... | collective-permute-start | bytes 2359304 | tf_op jit(solution)/shard_map/ppermute | solution.py:295
  20.9 5.6 %collective-permute-start.8 = (f32[768,128]{1,0:T(8,128)}, f32[768,128]{1,0:T(8,128)}, u32[]{:S(2)}, u32[]{:S(2)}) collective-permute-start(f32[768,128]{1,0:T(8,128)} %slice.49), channel_id=1, source_target_pairs={{0,1},{1,2},{2,3},{3,0},{4,5},{5,6},{6,7},{7,4}} | collective-permute-start | bytes 1179656 | tf_op jit(solution)/shard_map/ppermute | solution.py:295
  23.1 3.5 %collective-permute-start.9 = (f32[768,128]{1,0:T(8,128)}, f32[768,128]{1,0:T(8,128)}, u32[]{:S(2)}, u32[]{:S(2)}) collective-permute-start(f32[768,128]{1,0:T(8,128)} %slice.59), channel_id=1, source_target_pairs={{0,3},{1,0},{2,1},{3,2},{4,7},{5,4},{6,5},{7,6}} | collective-permute-start | bytes 1179656 | tf_op jit(solution)/shard_map/ppermute | solution.py:295
  35.6 3.0 %collective-permute-start.12 = (f32[512,128]{1,0:T(8,128)S(1)}, f32[512,128]{1,0:T(8,128)S(1)}, u32[]{:S(2)}, u32[]{:S(2)}) collective-permute-start(f32[512,128]{1,0:T(8,128)S(1)} %slice_select_fusion.1), channel_id=1, source_target_pairs={{0,12},{1,13},{2,14},{3,15},{4,8},{5,9},{6,10},{7,11},{24,20},{25,... | collective-permute-start | bytes 786440 | tf_op jit(solution)/shard_map/ppermute | solution.py:295
  38.6 101.1 %all-to-all-start.1 = ((f32[16,256,128]{2,1,0:T(8,128)}), f32[16,256,128]{2,1,0:T(8,128)S(1)}, u32[]{:S(2)}, u32[]{:S(2)}) async-start(f32[16,256,128]{2,1,0:T(8,128)} %copy-done), calls=%async_computation.1 | async-start | bytes 4194304 | tf_op jit(solution)/shard_map/all_to_all | solution.py:305
  44.6 78.7 %collective-permute-start.15 = (f32[512,128]{1,0:T(8,128)S(1)}, f32[512,128]{1,0:T(8,128)S(1)}, u32[]{:S(2)}, u32[]{:S(2)}) collective-permute-start(f32[512,128]{1,0:T(8,128)S(1)} %collective-permute-done.13), channel_id=1, source_target_pairs={{32,64},{33,65},{34,66},{35,67},{36,68},{37,69},{38,70},{39,71},{4... | collective-permute-start | bytes 786440 | tf_op jit(solution)/shard_map/ppermute | solution.py:295
  123.4 5.9 %collective-permute-start.18 = (f32[512,128]{1,0:T(8,128)S(1)}, f32[512,128]{1,0:T(8,128)S(1)}, u32[]{:S(2)}, u32[]{:S(2)}) collective-permute-start(f32[512,128]{1,0:T(8,128)S(1)} %add_select_fusion), channel_id=1, source_target_pairs={{0,3},{1,0},{2,1},{3,2},{4,7},{5,4},{6,5},{7,6},{8,11},{9,8},{10,9... | collective-permute-start | bytes 786440 | tf_op jit(solution)/shard_map/ppermute | solution.py:295
  126.0 6.5 %collective-permute-start.16 = (f32[512,128]{1,0:T(8,128)S(1)}, f32[512,128]{1,0:T(8,128)S(1)}, u32[]{:S(2)}, u32[]{:S(2)}) collective-permute-start(f32[512,128]{1,0:T(8,128)S(1)} %add_select_fusion), channel_id=1, source_target_pairs={{0,1},{1,2},{2,3},{3,0},{4,5},{5,6},{6,7},{7,4},{8,9},{9,10},{10,1... | collective-permute-start | bytes 786440 | tf_op jit(solution)/shard_map/ppermute | solution.py:295
  129.3 5.1 %collective-permute-start.19 = (f32[256,128]{1,0:T(8,128)S(1)}, f32[256,128]{1,0:T(8,128)S(1)}, u32[]{:S(2)}, u32[]{:S(2)}) collective-permute-start(f32[256,128]{1,0:T(8,128)S(1)} %slice.63), channel_id=1, source_target_pairs={{0,3},{1,0},{2,1},{3,2},{4,7},{5,4},{6,5},{7,6},{8,11},{9,8},{10,9... | collective-permute-start | bytes 393224 | tf_op jit(solution)/shard_map/ppermute | solution.py:295
  132.5 5.2 %collective-permute-start.17 = (f32[256,128]{1,0:T(8,128)S(1)}, f32[256,128]{1,0:T(8,128)}, u32[]{:S(2)}, u32[]{:S(2)}) collective-permute-start(f32[256,128]{1,0:T(8,128)S(1)} %slice.62), channel_id=1, source_target_pairs={{0,1},{1,2},{2,3},{3,0},{4,5},{5,6},{6,7},{7,4},{8,9},{9,10},{10,1... | collective-permute-start | bytes 393224 | tf_op jit(solution)/shard_map/ppermute | solution.py:295
  140.7 5.5 %collective-permute-start.20 = (f32[8,256,128]{2,1,0:T(8,128)}, f32[8,256,128]{2,1,0:T(8,128)}, u32[]{:S(2)}, u32[]{:S(2)}) collective-permute-start(f32[8,256,128]{2,1,0:T(8,128)} %constant_dynamic-slice_fusion), channel_id=1, source_target_pairs={{0,16},{1,17},{2,18},{3,19},{4,20},{5,21},{6,22},{7,23},{8,24},{9,... | collective-permute-start | bytes 3145736 | tf_op jit(solution)/shard_map/ppermute | solution.py:295
  141.7 9.7 %collective-permute-start.21 = (f32[2,512,128]{2,1,0:T(8,128)S(1)}, f32[2,512,128]{2,1,0:T(8,128)}, u32[]{:S(2)}, u32[]{:S(2)}) collective-permute-start(f32[2,512,128]{2,1,0:T(8,128)S(1)} %pad_maximum_fusion.3.refs_0_), channel_id=1, source_target_pairs={{0,4},{1,5},{2,6},{3,7},{4,8},{5,9},{6,10},{7,11},{8,12},{9,13},{1... | collective-permute-start | bytes 1572872 | tf_op jit(solution)/shard_map/ppermute | solution.py:295
  143.0 8.5 %collective-permute-start.22 = (f32[2,512,128]{2,1,0:T(8,128)S(1)}, f32[2,512,128]{2,1,0:T(8,128)}, u32[]{:S(2)}, u32[]{:S(2)}) collective-permute-start(f32[2,512,128]{2,1,0:T(8,128)S(1)} %pad_maximum_fusion.2.refs_1_), channel_id=1, source_target_pairs={{0,12},{1,13},{2,14},{3,15},{4,0},{5,1},{6,2},{7,3},{8,4},{9,5},{1... | collective-permute-start | bytes 1572872 | tf_op jit(solution)/shard_map/ppermute | solution.py:295
  144.6 12.3 %collective-permute-start.25 = (f32[2,512,128]{2,1,0:T(8,128)S(1)}, f32[2,512,128]{2,1,0:T(8,128)S(1)}, u32[]{:S(2)}, u32[]{:S(2)}) collective-permute-start(f32[2,512,128]{2,1,0:T(8,128)S(1)} %pad_maximum_fusion.3.refs_0_), channel_id=1, source_target_pairs={{0,12},{1,13},{2,14},{3,15},{4,0},{5,1},{6,2},{7,3},{8,4},{9,5},{1... | collective-permute-start | bytes 1572872 | tf_op jit(solution)/shard_map/ppermute | solution.py:295
  146.0 10.9 %collective-permute-start.26 = (f32[2,512,128]{2,1,0:T(8,128)S(1)}, f32[2,512,128]{2,1,0:T(8,128)S(1)}, u32[]{:S(2)}, u32[]{:S(2)}) collective-permute-start(f32[2,512,128]{2,1,0:T(8,128)S(1)} %pad_maximum_fusion.2.refs_1_), channel_id=1, source_target_pairs={{0,4},{1,5},{2,6},{3,7},{4,8},{5,9},{6,10},{7,11},{8,12},{9,13},{1... | collective-permute-start | bytes 1572872 | tf_op jit(solution)/shard_map/ppermute | solution.py:295
  151.4 11.1 %collective-permute-start.23 = (f32[2,512,128]{2,1,0:T(8,128)}, f32[2,512,128]{2,1,0:T(8,128)S(1)}, u32[]{:S(2)}, u32[]{:S(2)}) collective-permute-start(f32[2,512,128]{2,1,0:T(8,128)} %collective-permute-done.21.refs_3_), channel_id=1, source_target_pairs={{0,4},{1,5},{2,6},{3,7},{4,8},{5,9},{6,10},{7,11},{8,12},{9,13},{1... | collective-permute-start | bytes 1572872 | tf_op jit(solution)/shard_map/ppermute | solution.py:295
  152.6 10.0 %collective-permute-start.24 = (f32[2,512,128]{2,1,0:T(8,128)}, f32[2,512,128]{2,1,0:T(8,128)S(1)}, u32[]{:S(2)}, u32[]{:S(2)}) collective-permute-start(f32[2,512,128]{2,1,0:T(8,128)} %collective-permute-done.22.refs_2_), channel_id=1, source_target_pairs={{0,12},{1,13},{2,14},{3,15},{4,0},{5,1},{6,2},{7,3},{8,4},{9,5},{1... | collective-permute-start | bytes 1572872 | tf_op jit(solution)/shard_map/ppermute | solution.py:295
  165.3 3.7 %collective-permute-start.27 = (f32[256,1024]{1,0:T(8,128)S(1)}, f32[256,1024]{1,0:T(8,128)S(1)}, u32[]{:S(2)}, u32[]{:S(2)}) collective-permute-start(f32[256,1024]{1,0:T(8,128)S(1)} %slice.65), channel_id=1, source_target_pairs={{0,16},{1,17},{2,18},{3,19},{4,20},{5,21},{6,22},{7,23},{8,24},{9,... | collective-permute-start | bytes 3145736 | tf_op jit(solution)/shard_map/ppermute | solution.py:295
  (18 other events, 49.2 us)

commit v15 on v14

--- a/solution.py
+++ b/solution.py
@@ -295,19 +295,17 @@
     return lax.ppermute(value, AXES, pairs)
 
 
-def deal(first, second, core, yh, xi, by_rows):
+def deal(first, second, core, yh, xi):
     solved = jnp.where(core == 0, first, second)
     lower = yh == 0
     here = jnp.where(lower, solved[:512], solved[512:])
     there = jnp.where(core == 0, solved[512:], solved[:512])
     got = move(there, lambda a, b, c, d: (0, b, 3 - c, d) if a == 0 and b == c // 2 else None)
-    got, by_rows = lax.optimization_barrier((got, by_rows))
-    left = lax.all_to_all(by_rows, COL, 0, 0, tiled=True)
     mine = jnp.where(core == yh, here, got)
     one = move(mine, lambda a, b, c, d: (1 if b == 0 else 3, b, c, d) if a == 0 else None)
     two = move(mine, lambda a, b, c, d: (3 if b == 0 else 1, b, c, d) if a == 0 else None)
     far = move(one, lambda a, b, c, d: (2, b, c, d) if a == (1 if b == 0 else 3) else None)
-    return jnp.where(xi == 0, mine, one + two + far), left
+    return jnp.where(xi == 0, mine, one + two + far)
 
 
 def ring(value, first):
@@ -394,7 +392,9 @@
     rest, tri = residual_or_pack(place(core * (1 + yh)), *lower_row, columns, sent)
     second_rhs = move(rest, lambda a, b, c, d: (0, 1, 3 - c, d) if (a, b) == (0, 1) and c < 2 else None)
     second = solve_second(place((core == 1) & (yh == 1)), tri, second_rhs)
-    mine, left = deal(first, second, core, yh, xi, arrange(local))
+    mine = deal(first, second, core, yh, xi)
+    by_rows, _ = lax.optimization_barrier((arrange(local), mine))
+    left = lax.all_to_all(by_rows, COL, 0, 0, tiled=True)
 
     def swap(value):
         return move(value, lambda a, b, c, d: (a, 1 - b, c, d))

time: 171 us -> 173 us (1.012)
  waiting for transfers between devices: 98 us -> 100 us
where the time goes in v15:
time: 173 us; the launch traced here: 172 us
  waiting for transfers between devices  100 us (58%)
  starting transfers between devices  38.9 us (22%)
  Pallas kernels  17.6 us (10%)
  local copies, waits for them, and re-layouts  9.54 us (6%)
  other arithmetic  4.91 us (3%)
    ppermute x28, waiting for transfers between devices, move(): return lax.ppermute(value, AXES, pairs)  94.2 us
    ppermute x28, starting transfers between devices, move(): return lax.ppermute(value, AXES, pairs)  28 us
    pallas_call x3, Pallas kernels, accumulate(): pl.pallas_call(body, out_shape=jax.ShapeDtypeStruct((512, 1024), F32), in...  10.1 us
    all_to_all x1, waiting for transfers between devices, shards(): lax.all_to_all(arrange_rhs(yh, rhs), ('yl', 'z'), 0, 0, tiled=True)  6.11 us
    all_to_all x1, starting transfers between devices, shards(): lax.all_to_all(arrange_rhs(yh, rhs), ('yl', 'z'), 0, 0, tiled=True)  6.05 us
    all_to_all x1, starting transfers between devices, shards(): left = lax.all_to_all(by_rows, COL, 0, 0, tiled=True)  4.8 us
    unnamed x25, local copies, waits for them, and re-layouts  4.52 us
  transfers between devices with their start and end apart: 30, of which 9 were waited for; matrix products, arithmetic and copies ran while one was open for 4% of the time, Pallas kernels for 6%

profile of v15, /device:TPU:5, one launch (start us, length us, event | category | flops | bytes accessed | tf_op | source)
XLA Modules:
  0.0 171.7 jit_solution(4606414036607239549)
XLA Ops:
  4.7 6.0 %all-to-all-start = ((f32[8,64,128]{2,1,0:T(8,128)}), f32[8,64,128]{2,1,0:T(8,128)S(1)}, u32[]{:S(2)}, u32[]{:S(2)}) async-start(f32[8,64,128]{2,1,0:T(8,128)} %arrange_rhs.1), calls=%async_computation | async-start | bytes 524288 | tf_op jit(solution)/shard_map/all_to_all | solution.py:384
  10.7 6.1 %all-to-all-done = f32[8,64,128]{2,1,0:T(8,128)S(1)} async-done(((f32[8,64,128]{2,1,0:T(8,128)}), f32[8,64,128]{2,1,0:T(8,128)S(1)}, u32[]{:S(2)}, u32[]{:S(2)}) %all-to-all-start) | async-done | bytes 262176 | tf_op jit(solution)/shard_map/all_to_all | solution.py:384
  21.6 1.4 collective-permute-start.8
  23.8 1.4 collective-permute-start.9
  27.2 1.9 %solve_first.1 = f32[1024,128]{1,0:T(8,128)} custom-call(s32[3]{0:T(128)S(1)} %pad_add_fusion.1.info, f32[1536,128]{1,0:T(8,128)S(1)} %pad_maximum_fusion.refs_0_.refs_2_, f32[1536,128]{1,0:T(8,128)S(1)} %collective-permute-done.5.refs_1_.refs_5_, f32[1536,128]{1,0:T(8,128)S(1)} %collective-permute-done.6.refs_2_.refs_4_, ...), custom_call_target="tpu_custom_call" | custom-call | tf_op jit(solution)/shard_map/solve_first/pallas_call | solution.py:107
  29.2 1.5 collective-permute-start.10
  32.9 1.9 %residual_or_pack.1 = (f32[1024,128]{1,0:T(8,128)}, bf16[112,1024,256]{2,1,0:T(8,128)(2,1)}) custom-call(s32[3]{0:T(128)S(1)} %pad_add_fusion.5.info, f32[1024,128]{1,0:T(8,128)S(1)} %invert_diagonal.1.refs_0_, f32[1024,128]{1,0:T(8,128)S(1)} %copy-done.7, f32[1536,128]{1,0:T(8,128)S(1)} %pad_maximum_fusion.refs_0_.refs_2_, f32[1536,128]{1,0:T(8,128)S(1)} %copy-done.5, ...), custom_call_target="tpu_custom_call" | custom-call | tf_op jit(solution)/shard_map/residual_or_pack/pallas_call | solution.py:144
  40.1 1.3 copy-done
  41.4 66.8 %collective-permute-done.15 = f32[512,128]{1,0:T(8,128)S(1)} collective-permute-done((f32[512,128]{1,0:T(8,128)S(1)}, f32[512,128]{1,0:T(8,128)S(1)}, u32[]{:S(2)}, u32[]{:S(2)}) %collective-permute-start.15) | collective-permute-done | bytes 262176 | tf_op jit(solution)/shard_map/ppermute | solution.py:295
  108.3 4.8 %all-to-all-start.1 = ((f32[16,256,128]{2,1,0:T(8,128)}), f32[16,256,128]{2,1,0:T(8,128)S(1)}, u32[]{:S(2)}, u32[]{:S(2)}) async-start(f32[16,256,128]{2,1,0:T(8,128)} %copy-done), calls=%async_computation.1 | async-start | bytes 4194304 | tf_op jit(solution)/shard_map/all_to_all | solution.py:397
  113.1 1.4 collective-permute-start.16
  114.4 1.4 collective-permute-start.18
  115.8 18.3 %collective-permute-done.16 = f32[512,128]{1,0:T(8,128)S(1)} collective-permute-done((f32[512,128]{1,0:T(8,128)S(1)}, f32[512,128]{1,0:T(8,128)S(1)}, u32[]{:S(2)}, u32[]{:S(2)}) %collective-permute-start.16) | collective-permute-done | bytes 262176 | tf_op jit(solution)/shard_map/ppermute | solution.py:295
  134.3 2.7 %collective-permute-start.19 = (f32[256,128]{1,0:T(8,128)S(1)}, f32[256,128]{1,0:T(8,128)}, u32[]{:S(2)}, u32[]{:S(2)}) collective-permute-start(f32[256,128]{1,0:T(8,128)S(1)} %slice.63), channel_id=1, source_target_pairs={{0,3},{1,0},{2,1},{3,2},{4,7},{5,4},{6,5},{7,6},{8,11},{9,8},{10,9... | collective-permute-start | bytes 393224 | tf_op jit(solution)/shard_map/ppermute | solution.py:295
  137.0 2.3 %collective-permute-done.17 = f32[256,128]{1,0:T(8,128)S(1)} collective-permute-done((f32[256,128]{1,0:T(8,128)S(1)}, f32[256,128]{1,0:T(8,128)S(1)}, u32[]{:S(2)}, u32[]{:S(2)}) %collective-permute-start.17) | collective-permute-done | bytes 131104 | tf_op jit(solution)/shard_map/ppermute | solution.py:295
  143.7 2.3 %collective-permute-start.22 = (f32[2,512,128]{2,1,0:T(8,128)S(1)}, f32[2,512,128]{2,1,0:T(8,128)}, u32[]{:S(2)}, u32[]{:S(2)}) collective-permute-start(f32[2,512,128]{2,1,0:T(8,128)S(1)} %pad_maximum_fusion.2.refs_1_), channel_id=1, source_target_pairs={{0,12},{1,13},{2,14},{3,15},{4,0},{5,1},{6,2},{7,3},{8,4},{9,5},{1... | collective-permute-start | bytes 1572872 | tf_op jit(solution)/shard_map/ppermute | solution.py:295
  147.8 1.6 prepare_update.1
  149.4 2.5 %update_near.1.refs_0_ = f32[512,1024]{1,0:T(8,128)S(1)} custom-call(s32[5]{0:T(128)S(1)} %stack.81.info, bf16[4,512,256]{2,1,0:T(8,128)(2,1)S(1)} %get-tuple-element.31.high_ref, bf16[4,512,256]{2,1,0:T(8,128)(2,1)S(1)} %get-tuple-element.32.low_ref, f32[2,512,128]{2,1,0:T(8,128)S(1)} %pad_maximum_fusion.3.refs_0_, f32[2,512,128]{2,1,0:T(8,128)S(1)} %pad_maximum_fusion.2.refs_1_), custom_call_target="tpu_custom_call" | custom-call | tf_op jit(solution)/shard_map/update_near/pallas_call | solution.py:271
  152.9 2.7 %collective-permute-start.24 = (f32[2,512,128]{2,1,0:T(8,128)}, f32[2,512,128]{2,1,0:T(8,128)S(1)}, u32[]{:S(2)}, u32[]{:S(2)}) collective-permute-start(f32[2,512,128]{2,1,0:T(8,128)} %collective-permute-done.22.refs_2_), channel_id=1, source_target_pairs={{0,12},{1,13},{2,14},{3,15},{4,0},{5,1},{6,2},{7,3},{8,4},{9,5},{1... | collective-permute-start | bytes 1572872 | tf_op jit(solution)/shard_map/ppermute | solution.py:295
  155.6 2.1 %collective-permute-done.25.refs_1_ = f32[2,512,128]{2,1,0:T(8,128)S(1)} collective-permute-done((f32[2,512,128]{2,1,0:T(8,128)S(1)}, f32[2,512,128]{2,1,0:T(8,128)S(1)}, u32[]{:S(2)}, u32[]{:S(2)}) %collective-permute-start.25) | collective-permute-done | bytes 524320 | tf_op jit(solution)/shard_map/ppermute | solution.py:295
  158.5 5.1 %update_next.1.refs_0_ = f32[512,1024]{1,0:T(8,128)S(1)} custom-call(s32[5]{0:T(128)S(1)} %stack.81.info, bf16[4,512,256]{2,1,0:T(8,128)(2,1)S(1)} %get-tuple-element.31.high_ref, bf16[4,512,256]{2,1,0:T(8,128)(2,1)S(1)} %get-tuple-element.32.low_ref, f32[512,1024]{1,0:T(8,128)S(1)} %update_near.1.refs_0_, ...), custom_call_target="tpu_custom_call", output_to_operand_aliasing={{}: (3, {})} | custom-call | tf_op jit(solution)/shard_map/update_next/pallas_call | solution.py:271
  164.1 2.6 %update_far.1 = f32[512,1024]{1,0:T(8,128)S(1)} custom-call(s32[5]{0:T(128)S(1)} %stack.81.info, bf16[4,512,256]{2,1,0:T(8,128)(2,1)S(1)} %get-tuple-element.31.high_ref, bf16[4,512,256]{2,1,0:T(8,128)(2,1)S(1)} %get-tuple-element.32.low_ref, f32[512,1024]{1,0:T(8,128)S(1)} %update_next.1.refs_0_, ...), custom_call_target="tpu_custom_call", output_to_operand_aliasing={{}: (3, {})} | custom-call | tf_op jit(solution)/shard_map/update_far/pallas_call | solution.py:271
  166.8 1.4 collective-permute-start.27
  168.2 2.3 %collective-permute-done.27 = f32[256,1024]{1,0:T(8,128)S(1)} collective-permute-done((f32[256,1024]{1,0:T(8,128)S(1)}, f32[256,1024]{1,0:T(8,128)S(1)}, u32[]{:S(2)}, u32[]{:S(2)}) %collective-permute-start.27) | collective-permute-done | bytes 1048608 | tf_op jit(solution)/shard_map/ppermute | solution.py:295
  (100 shorter events, 29.5 us)
Async XLA Ops:
  1.8 15.0 %collective-permute-start = (f32[1024,128]{1,0:T(8,128)S(1)}, f32[1024,128]{1,0:T(8,128)S(1)}, u32[]{:S(2)}, u32[]{:S(2)}) collective-permute-start(f32[1024,128]{1,0:T(8,128)S(1)} %invert_diagonal.1.refs_0_), channel_id=1, source_target_pairs={{0,4},{1,5},{2,6},{3,7},{4,0},{5,1},{6,2},{7,3},{16,17},{17,18},{1... | collective-permute-start | bytes 1572872 | tf_op jit(solution)/shard_map/ppermute | solution.py:295
  2.5 14.3 %collective-permute-start.1 = (f32[1024,128]{1,0:T(8,128)S(1)}, f32[1024,128]{1,0:T(8,128)S(1)}, u32[]{:S(2)}, u32[]{:S(2)}) collective-permute-start(f32[1024,128]{1,0:T(8,128)S(1)} %invert_diagonal.1.refs_0_), channel_id=1, source_target_pairs={{16,20},{17,21},{18,22},{19,23},{20,16},{21,17},{22,18},{23,19},{2... | collective-permute-start | bytes 1572872 | tf_op jit(solution)/shard_map/ppermute | solution.py:295
  3.2 14.3 %collective-permute-start.3 = (f32[1024,128]{1,0:T(8,128)S(1)}, f32[1024,128]{1,0:T(8,128)S(1)}, u32[]{:S(2)}, u32[]{:S(2)}) collective-permute-start(f32[1024,128]{1,0:T(8,128)S(1)} %invert_diagonal.1.refs_0_), channel_id=1, source_target_pairs={{16,19},{17,16},{18,17},{19,18},{20,23},{21,20},{22,21},{23,22},{2... | collective-permute-start | bytes 1572872 | tf_op jit(solution)/shard_map/ppermute | solution.py:295
  4.7 12.2 %all-to-all-start = ((f32[8,64,128]{2,1,0:T(8,128)}), f32[8,64,128]{2,1,0:T(8,128)S(1)}, u32[]{:S(2)}, u32[]{:S(2)}) async-start(f32[8,64,128]{2,1,0:T(8,128)} %arrange_rhs.1), calls=%async_computation | async-start | bytes 524288 | tf_op jit(solution)/shard_map/all_to_all | solution.py:384
  18.5 2.2 %collective-permute-start.6 = (f32[1536,128]{1,0:T(8,128)S(1)}, f32[1536,128]{1,0:T(8,128)S(1)}, u32[]{:S(2)}, u32[]{:S(2)}) collective-permute-start(f32[1536,128]{1,0:T(8,128)S(1)} %pad_maximum_fusion.refs_0_.refs_2_), channel_id=1, source_target_pairs={{0,1},{1,2},{2,3},{3,0},{4,5},{5,6},{6,7},{7,4},{16,20},{17,21},{1... | collective-permute-start | bytes 2359304 | tf_op jit(solution)/shard_map/ppermute | solution.py:295
  19.3 3.7 %collective-permute-start.5 = (f32[1536,128]{1,0:T(8,128)S(1)}, f32[1536,128]{1,0:T(8,128)S(1)}, u32[]{:S(2)}, u32[]{:S(2)}) collective-permute-start(f32[1536,128]{1,0:T(8,128)S(1)} %pad_maximum_fusion.1.refs_3_), channel_id=1, source_target_pairs={{0,3},{1,0},{2,1},{3,2},{4,7},{5,4},{6,5},{7,6},{16,20},{17,21},{1... | collective-permute-start | bytes 2359304 | tf_op jit(solution)/shard_map/ppermute | solution.py:295
  21.6 5.6 %collective-permute-start.8 = (f32[768,128]{1,0:T(8,128)}, f32[768,128]{1,0:T(8,128)}, u32[]{:S(2)}, u32[]{:S(2)}) collective-permute-start(f32[768,128]{1,0:T(8,128)} %slice.49), channel_id=1, source_target_pairs={{0,1},{1,2},{2,3},{3,0},{4,5},{5,6},{6,7},{7,4}} | collective-permute-start | bytes 1179656 | tf_op jit(solution)/shard_map/ppermute | solution.py:295
  23.8 3.5 %collective-permute-start.9 = (f32[768,128]{1,0:T(8,128)}, f32[768,128]{1,0:T(8,128)}, u32[]{:S(2)}, u32[]{:S(2)}) collective-permute-start(f32[768,128]{1,0:T(8,128)} %slice.59), channel_id=1, source_target_pairs={{0,3},{1,0},{2,1},{3,2},{4,7},{5,4},{6,5},{7,6}} | collective-permute-start | bytes 1179656 | tf_op jit(solution)/shard_map/ppermute | solution.py:295
  29.2 1.6 collective-permute-start.10
  37.9 3.5 %collective-permute-start.14 = (f32[512,128]{1,0:T(8,128)S(1)}, f32[512,128]{1,0:T(8,128)S(1)}, u32[]{:S(2)}, u32[]{:S(2)}) collective-permute-start(f32[512,128]{1,0:T(8,128)S(1)} %select_select_fusion.2), channel_id=1, source_target_pairs={{0,96},{1,97},{2,98},{3,99},{4,100},{5,101},{6,102},{7,103},{8,104... | collective-permute-start | bytes 786440 | tf_op jit(solution)/shard_map/ppermute | solution.py:295
  38.6 69.6 %collective-permute-start.15 = (f32[512,128]{1,0:T(8,128)S(1)}, f32[512,128]{1,0:T(8,128)S(1)}, u32[]{:S(2)}, u32[]{:S(2)}) collective-permute-start(f32[512,128]{1,0:T(8,128)S(1)} %collective-permute-done.13), channel_id=1, source_target_pairs={{32,64},{33,65},{34,66},{35,67},{36,68},{37,69},{38,70},{39,71},{4... | collective-permute-start | bytes 786440 | tf_op jit(solution)/shard_map/ppermute | solution.py:295
  108.3 32.9 %all-to-all-start.1 = ((f32[16,256,128]{2,1,0:T(8,128)}), f32[16,256,128]{2,1,0:T(8,128)S(1)}, u32[]{:S(2)}, u32[]{:S(2)}) async-start(f32[16,256,128]{2,1,0:T(8,128)} %copy-done), calls=%async_computation.1 | async-start | bytes 4194304 | tf_op jit(solution)/shard_map/all_to_all | solution.py:397
  113.1 21.1 %collective-permute-start.16 = (f32[512,128]{1,0:T(8,128)S(1)}, f32[512,128]{1,0:T(8,128)S(1)}, u32[]{:S(2)}, u32[]{:S(2)}) collective-permute-start(f32[512,128]{1,0:T(8,128)S(1)} %add_select_fusion), channel_id=1, source_target_pairs={{0,1},{1,2},{2,3},{3,0},{4,5},{5,6},{6,7},{7,4},{8,9},{9,10},{10,1... | collective-permute-start | bytes 786440 | tf_op jit(solution)/shard_map/ppermute | solution.py:295
  114.4 19.8 %collective-permute-start.18 = (f32[512,128]{1,0:T(8,128)S(1)}, f32[512,128]{1,0:T(8,128)S(1)}, u32[]{:S(2)}, u32[]{:S(2)}) collective-permute-start(f32[512,128]{1,0:T(8,128)S(1)} %add_select_fusion), channel_id=1, source_target_pairs={{0,3},{1,0},{2,1},{3,2},{4,7},{5,4},{6,5},{7,6},{8,11},{9,8},{10,9... | collective-permute-start | bytes 786440 | tf_op jit(solution)/shard_map/ppermute | solution.py:295
  134.1 5.1 %collective-permute-start.17 = (f32[256,128]{1,0:T(8,128)S(1)}, f32[256,128]{1,0:T(8,128)S(1)}, u32[]{:S(2)}, u32[]{:S(2)}) collective-permute-start(f32[256,128]{1,0:T(8,128)S(1)} %slice.62), channel_id=1, source_target_pairs={{0,1},{1,2},{2,3},{3,0},{4,5},{5,6},{6,7},{7,4},{8,9},{9,10},{10,1... | collective-permute-start | bytes 393224 | tf_op jit(solution)/shard_map/ppermute | solution.py:295
  134.3 5.0 %collective-permute-start.19 = (f32[256,128]{1,0:T(8,128)S(1)}, f32[256,128]{1,0:T(8,128)}, u32[]{:S(2)}, u32[]{:S(2)}) collective-permute-start(f32[256,128]{1,0:T(8,128)S(1)} %slice.63), channel_id=1, source_target_pairs={{0,3},{1,0},{2,1},{3,2},{4,7},{5,4},{6,5},{7,6},{8,11},{9,8},{10,9... | collective-permute-start | bytes 393224 | tf_op jit(solution)/shard_map/ppermute | solution.py:295
  142.2 5.5 %collective-permute-start.20 = (f32[8,256,128]{2,1,0:T(8,128)}, f32[8,256,128]{2,1,0:T(8,128)}, u32[]{:S(2)}, u32[]{:S(2)}) collective-permute-start(f32[8,256,128]{2,1,0:T(8,128)} %constant_dynamic-slice_fusion), channel_id=1, source_target_pairs={{0,16},{1,17},{2,18},{3,19},{4,20},{5,21},{6,22},{7,23},{8,24},{9,... | collective-permute-start | bytes 3145736 | tf_op jit(solution)/shard_map/ppermute | solution.py:295
  143.2 9.7 %collective-permute-start.21 = (f32[2,512,128]{2,1,0:T(8,128)S(1)}, f32[2,512,128]{2,1,0:T(8,128)}, u32[]{:S(2)}, u32[]{:S(2)}) collective-permute-start(f32[2,512,128]{2,1,0:T(8,128)S(1)} %pad_maximum_fusion.3.refs_0_), channel_id=1, source_target_pairs={{0,4},{1,5},{2,6},{3,7},{4,8},{5,9},{6,10},{7,11},{8,12},{9,13},{1... | collective-permute-start | bytes 1572872 | tf_op jit(solution)/shard_map/ppermute | solution.py:295
  143.7 9.2 %collective-permute-start.22 = (f32[2,512,128]{2,1,0:T(8,128)S(1)}, f32[2,512,128]{2,1,0:T(8,128)}, u32[]{:S(2)}, u32[]{:S(2)}) collective-permute-start(f32[2,512,128]{2,1,0:T(8,128)S(1)} %pad_maximum_fusion.2.refs_1_), channel_id=1, source_target_pairs={{0,12},{1,13},{2,14},{3,15},{4,0},{5,1},{6,2},{7,3},{8,4},{9,5},{1... | collective-permute-start | bytes 1572872 | tf_op jit(solution)/shard_map/ppermute | solution.py:295
  146.1 11.6 %collective-permute-start.25 = (f32[2,512,128]{2,1,0:T(8,128)S(1)}, f32[2,512,128]{2,1,0:T(8,128)S(1)}, u32[]{:S(2)}, u32[]{:S(2)}) collective-permute-start(f32[2,512,128]{2,1,0:T(8,128)S(1)} %pad_maximum_fusion.3.refs_0_), channel_id=1, source_target_pairs={{0,12},{1,13},{2,14},{3,15},{4,0},{5,1},{6,2},{7,3},{8,4},{9,5},{1... | collective-permute-start | bytes 1572872 | tf_op jit(solution)/shard_map/ppermute | solution.py:295
  146.6 11.8 %collective-permute-start.26 = (f32[2,512,128]{2,1,0:T(8,128)S(1)}, f32[2,512,128]{2,1,0:T(8,128)S(1)}, u32[]{:S(2)}, u32[]{:S(2)}) collective-permute-start(f32[2,512,128]{2,1,0:T(8,128)S(1)} %pad_maximum_fusion.2.refs_1_), channel_id=1, source_target_pairs={{0,4},{1,5},{2,6},{3,7},{4,8},{5,9},{6,10},{7,11},{8,12},{9,13},{1... | collective-permute-start | bytes 1572872 | tf_op jit(solution)/shard_map/ppermute | solution.py:295
  152.9 11.1 %collective-permute-start.23 = (f32[2,512,128]{2,1,0:T(8,128)}, f32[2,512,128]{2,1,0:T(8,128)S(1)}, u32[]{:S(2)}, u32[]{:S(2)}) collective-permute-start(f32[2,512,128]{2,1,0:T(8,128)} %collective-permute-done.21.refs_3_), channel_id=1, source_target_pairs={{0,4},{1,5},{2,6},{3,7},{4,8},{5,9},{6,10},{7,11},{8,12},{9,13},{1... | collective-permute-start | bytes 1572872 | tf_op jit(solution)/shard_map/ppermute | solution.py:295
  152.9 11.1 %collective-permute-start.24 = (f32[2,512,128]{2,1,0:T(8,128)}, f32[2,512,128]{2,1,0:T(8,128)S(1)}, u32[]{:S(2)}, u32[]{:S(2)}) collective-permute-start(f32[2,512,128]{2,1,0:T(8,128)} %collective-permute-done.22.refs_2_), channel_id=1, source_target_pairs={{0,12},{1,13},{2,14},{3,15},{4,0},{5,1},{6,2},{7,3},{8,4},{9,5},{1... | collective-permute-start | bytes 1572872 | tf_op jit(solution)/shard_map/ppermute | solution.py:295
  166.8 3.7 %collective-permute-start.27 = (f32[256,1024]{1,0:T(8,128)S(1)}, f32[256,1024]{1,0:T(8,128)S(1)}, u32[]{:S(2)}, u32[]{:S(2)}) collective-permute-start(f32[256,1024]{1,0:T(8,128)S(1)} %slice.65), channel_id=1, source_target_pairs={{0,16},{1,17},{2,18},{3,19},{4,20},{5,21},{6,22},{7,23},{8,24},{9,... | collective-permute-start | bytes 3145736 | tf_op jit(solution)/shard_map/ppermute | solution.py:295
  (18 other events, 48.0 us)

commit v16 on v15

--- a/solution.py
+++ b/solution.py
@@ -324,7 +324,7 @@
     return after, far_low, far_high, before
 
 
-def gather(lead, half, core, yl):
+def gather(lead, half, by_rows, core, yl):
     def holds(a, b, c):
         return a == 0 and (b == 1 or c < 2)
 
@@ -354,7 +354,7 @@
     second = jnp.concatenate([jnp.where(zero, full, after), jnp.where(zero, lower, far_high)], 0)
     got_first = move(first, step(0, 1))
     got_second = move(second, step(0, -1))
-    got_first, other_half = lax.optimization_barrier((got_first, other_half))
+    got_first, other_half, by_rows = lax.optimization_barrier((got_first, other_half, by_rows))
     end_low = move(got_first[:768], only(0, 1))
     end_high = move(got_second[768:], only(0, -1))
 
@@ -366,7 +366,7 @@
     for group in ("own", "pair"):
         lower_places.append([(group, 3, 0, 0, 1024), (group, 2, 1024, 0, 512)])
         lower_places.append([(group, 1, 0, 0, 1024), (group, 2, 1024, 512, 512)])
-    return (corner_pieces, corner_places), (lower_pieces, lower_places), jnp.concatenate([half, other_half], 0)
+    return (corner_pieces, corner_places), (lower_pieces, lower_places), jnp.concatenate([half, other_half], 0), by_rows
 
 
 def shards(factor, cross_cov):
@@ -382,19 +382,20 @@
     lead = invert_diagonal(info, local[0])
 
     half = lax.all_to_all(arrange_rhs(yh, rhs), ("yl", "z"), 0, 0, tiled=True).reshape(512, TILE)
-    upper_left, lower_row, columns = gather(lead, half, core, yl)
+    upper_left, lower_row, columns, by_rows = gather(lead, half, arrange(local), core, yl)
 
     def place(what):
         return jnp.stack([yl, z, jnp.where(xi == 0, what, 0)]).astype(jnp.int32)
 
     first = solve_first(place((core == 0) & (yh == 0)), *upper_left, columns)
     sent = move(first, lambda a, b, c, d: (0, 1, c, d) if (a, b) == (0, 0) and c < 2 else None)
+    by_rows, _ = lax.optimization_barrier((by_rows, first))
+    left = lax.all_to_all(by_rows, COL, 0, 0, tiled=True)
     rest, tri = residual_or_pack(place(core * (1 + yh)), *lower_row, columns, sent)
     second_rhs = move(rest, lambda a, b, c, d: (0, 1, 3 - c, d) if (a, b) == (0, 1) and c < 2 else None)
     second = solve_second(place((core == 1) & (yh == 1)), tri, second_rhs)
+    second, left = lax.optimization_barrier((second, left))
     mine = deal(first, second, core, yh, xi)
-    by_rows, _ = lax.optimization_barrier((arrange(local), mine))
-    left = lax.all_to_all(by_rows, COL, 0, 0, tiled=True)
 
     def swap(value):
         return move(value, lambda a, b, c, d: (a, 1 - b, c, d))

time: 173 us -> 178 us (1.029)
  local copies, waits for them, and re-layouts: 9.54 us -> 17.5 us
  waiting for transfers between devices: 100 us -> 96.2 us
  other arithmetic: 4.91 us -> 6.99 us
    ppermute x28, waiting for transfers between devices: 94.2 us -> 75.2 us  [move(): return lax.ppermute(value, AXES, pairs)]
    all_to_all x1, waiting for transfers between devices: 0.01 us -> 14.9 us  [shards(): left = lax.all_to_all(by_rows, COL, 0, 0, tiled=True)]
    unnamed x25 -> x49, local copies, waits for them, and re-layouts: 4.52 us -> 11.3 us
  transfers between devices with their start and end apart: 30 -> 30, of which waited for: 9 -> 12; matrix products, arithmetic and copies ran while one was open for 4% -> 4% of each run, Pallas kernels for 6% -> 7%
where the time goes in v16:
time: 178 us; the launch traced here: 177 us
  waiting for transfers between devices  96.2 us (54%)
  starting transfers between devices  38.5 us (22%)
  local copies, waits for them, and re-layouts  17.5 us (10%)
  Pallas kernels  16.9 us (9%)
  other arithmetic  6.99 us (4%)
    ppermute x28, waiting for transfers between devices, move(): return lax.ppermute(value, AXES, pairs)  75.2 us
    ppermute x28, starting transfers between devices, move(): return lax.ppermute(value, AXES, pairs)  27.8 us
    all_to_all x1, waiting for transfers between devices, shards(): left = lax.all_to_all(by_rows, COL, 0, 0, tiled=True)  14.9 us
    unnamed x49, local copies, waits for them, and re-layouts  11.3 us
    pallas_call x3, Pallas kernels, accumulate(): pl.pallas_call(body, out_shape=jax.ShapeDtypeStruct((512, 1024), F32), in...  10.1 us
    all_to_all x1, waiting for transfers between devices, shards(): lax.all_to_all(arrange_rhs(yh, rhs), ('yl', 'z'), 0, 0, tiled=True)  6.11 us
    all_to_all x1, starting transfers between devices, shards(): lax.all_to_all(arrange_rhs(yh, rhs), ('yl', 'z'), 0, 0, tiled=True)  6.05 us
    all_to_all x1, starting transfers between devices, shards(): left = lax.all_to_all(by_rows, COL, 0, 0, tiled=True)  4.62 us
  transfers between devices with their start and end apart: 30, of which 12 were waited for; matrix products, arithmetic and copies ran while one was open for 4% of the time, Pallas kernels for 7%

profile of v16, /device:TPU:5, one launch (start us, length us, event | category | flops | bytes accessed | tf_op | source)
XLA Modules:
  0.0 176.7 jit_solution(11640752352719329956)
XLA Ops:
  3.2 1.5 collective-permute-start.3
  5.4 6.0 %all-to-all-start = ((f32[8,64,128]{2,1,0:T(8,128)}), f32[8,64,128]{2,1,0:T(8,128)S(1)}, u32[]{:S(2)}, u32[]{:S(2)}) async-start(f32[8,64,128]{2,1,0:T(8,128)} %arrange_rhs.1), calls=%async_computation | async-start | bytes 524288 | tf_op jit(solution)/shard_map/all_to_all | solution.py:384
  11.5 6.1 %all-to-all-done = f32[8,64,128]{2,1,0:T(8,128)S(1)} async-done(((f32[8,64,128]{2,1,0:T(8,128)}), f32[8,64,128]{2,1,0:T(8,128)S(1)}, u32[]{:S(2)}, u32[]{:S(2)}) %all-to-all-start) | async-done | bytes 262176 | tf_op jit(solution)/shard_map/all_to_all | solution.py:384
  28.5 1.4 collective-permute-start.9
  34.1 4.6 %all-to-all-start.1 = ((f32[16,256,128]{2,1,0:T(8,128)}), f32[16,256,128]{2,1,0:T(8,128)S(1)}, u32[]{:S(2)}, u32[]{:S(2)}) async-start(f32[16,256,128]{2,1,0:T(8,128)} %copy-done), calls=%async_computation.1 | async-start | bytes 4194304 | tf_op jit(solution)/shard_map/all_to_all | solution.py:393
  38.7 1.5 collective-permute-start.10
  45.8 1.9 %residual_or_pack.1 = (f32[1024,128]{1,0:T(8,128)}, bf16[112,1024,256]{2,1,0:T(8,128)(2,1)}) custom-call(s32[3]{0:T(128)S(1)} %pad_add_fusion.3.info, f32[1024,128]{1,0:T(8,128)S(1)} %invert_diagonal.1.refs_0_, f32[1024,128]{1,0:T(8,128)S(1)} %copy-done.17, f32[1536,128]{1,0:T(8,128)S(1)} %pad_maximum_fusion.refs_0_.refs_2_, f32[1536,128]{1,0:T(8,128)S(1)} %copy-done.11, ...), custom_call_target="tpu_custom_call" | custom-call | tf_op jit(solution)/shard_map/residual_or_pack/pallas_call | solution.py:144
  50.9 14.9 %all-to-all-done.1.left_ref = f32[16,256,128]{2,1,0:T(8,128)S(1)} async-done(((f32[16,256,128]{2,1,0:T(8,128)}), f32[16,256,128]{2,1,0:T(8,128)S(1)}, u32[]{:S(2)}, u32[]{:S(2)}) %all-to-all-start.1) | async-done | bytes 2097184 | tf_op jit(solution)/shard_map/all_to_all | solution.py:393
  71.2 59.1 %collective-permute-done.15 = f32[512,128]{1,0:T(8,128)S(1)} collective-permute-done((f32[512,128]{1,0:T(8,128)S(1)}, f32[512,128]{1,0:T(8,128)S(1)}, u32[]{:S(2)}, u32[]{:S(2)}) %collective-permute-start.15) | collective-permute-done | bytes 262176 | tf_op jit(solution)/shard_map/ppermute | solution.py:295
  130.3 1.9 %collective-permute-start.18 = (f32[512,128]{1,0:T(8,128)S(1)}, f32[512,128]{1,0:T(8,128)S(1)}, u32[]{:S(2)}, u32[]{:S(2)}) collective-permute-start(f32[512,128]{1,0:T(8,128)S(1)} %add_select_fusion), channel_id=1, source_target_pairs={{0,3},{1,0},{2,1},{3,2},{4,7},{5,4},{6,5},{7,6},{8,11},{9,8},{10,9... | collective-permute-start | bytes 786440 | tf_op jit(solution)/shard_map/ppermute | solution.py:295
  132.2 3.7 %collective-permute-done.18 = f32[512,128]{1,0:T(8,128)S(1)} collective-permute-done((f32[512,128]{1,0:T(8,128)S(1)}, f32[512,128]{1,0:T(8,128)S(1)}, u32[]{:S(2)}, u32[]{:S(2)}) %collective-permute-start.18) | collective-permute-done | bytes 262176 | tf_op jit(solution)/shard_map/ppermute | solution.py:295
  135.9 2.8 %collective-permute-start.19 = (f32[256,128]{1,0:T(8,128)S(1)}, f32[256,128]{1,0:T(8,128)S(1)}, u32[]{:S(2)}, u32[]{:S(2)}) collective-permute-start(f32[256,128]{1,0:T(8,128)S(1)} %slice.63), channel_id=1, source_target_pairs={{0,3},{1,0},{2,1},{3,2},{4,7},{5,4},{6,5},{7,6},{8,11},{9,8},{10,9... | collective-permute-start | bytes 393224 | tf_op jit(solution)/shard_map/ppermute | solution.py:295
  139.1 1.5 collective-permute-done.19
  140.6 3.6 %collective-permute-done.17 = f32[256,128]{1,0:T(8,128)} collective-permute-done((f32[256,128]{1,0:T(8,128)S(1)}, f32[256,128]{1,0:T(8,128)}, u32[]{:S(2)}, u32[]{:S(2)}) %collective-permute-start.17) | collective-permute-done | bytes 131104 | tf_op jit(solution)/shard_map/ppermute | solution.py:295
  148.3 2.7 %collective-permute-start.22 = (f32[2,512,128]{2,1,0:T(8,128)S(1)}, f32[2,512,128]{2,1,0:T(8,128)}, u32[]{:S(2)}, u32[]{:S(2)}) collective-permute-start(f32[2,512,128]{2,1,0:T(8,128)S(1)} %pad_maximum_fusion.2.refs_1_), channel_id=1, source_target_pairs={{0,12},{1,13},{2,14},{3,15},{4,0},{5,1},{6,2},{7,3},{8,4},{9,5},{1... | collective-permute-start | bytes 1572872 | tf_op jit(solution)/shard_map/ppermute | solution.py:295
  151.1 1.5 collective-permute-start.26
  152.6 1.6 prepare_update.1
  154.1 2.5 %update_near.1.refs_0_ = f32[512,1024]{1,0:T(8,128)S(1)} custom-call(s32[5]{0:T(128)S(1)} %stack.81.info, bf16[4,512,256]{2,1,0:T(8,128)(2,1)S(1)} %get-tuple-element.37.high_ref, bf16[4,512,256]{2,1,0:T(8,128)(2,1)S(1)} %get-tuple-element.38.low_ref, f32[2,512,128]{2,1,0:T(8,128)S(1)} %pad_maximum_fusion.3.refs_0_, f32[2,512,128]{2,1,0:T(8,128)S(1)} %pad_maximum_fusion.2.refs_1_), custom_call_target="tpu_custom_call" | custom-call | tf_op jit(solution)/shard_map/update_near/pallas_call | solution.py:271
  157.9 2.7 %collective-permute-start.24 = (f32[2,512,128]{2,1,0:T(8,128)}, f32[2,512,128]{2,1,0:T(8,128)S(1)}, u32[]{:S(2)}, u32[]{:S(2)}) collective-permute-start(f32[2,512,128]{2,1,0:T(8,128)} %collective-permute-done.22.refs_2_), channel_id=1, source_target_pairs={{0,12},{1,13},{2,14},{3,15},{4,0},{5,1},{6,2},{7,3},{8,4},{9,5},{1... | collective-permute-start | bytes 1572872 | tf_op jit(solution)/shard_map/ppermute | solution.py:295
  160.6 2.1 %collective-permute-done.25.refs_1_ = f32[2,512,128]{2,1,0:T(8,128)S(1)} collective-permute-done((f32[2,512,128]{2,1,0:T(8,128)S(1)}, f32[2,512,128]{2,1,0:T(8,128)S(1)}, u32[]{:S(2)}, u32[]{:S(2)}) %collective-permute-start.25) | collective-permute-done | bytes 524320 | tf_op jit(solution)/shard_map/ppermute | solution.py:295
  163.4 5.1 %update_next.1.refs_0_ = f32[512,1024]{1,0:T(8,128)S(1)} custom-call(s32[5]{0:T(128)S(1)} %stack.81.info, bf16[4,512,256]{2,1,0:T(8,128)(2,1)S(1)} %get-tuple-element.37.high_ref, bf16[4,512,256]{2,1,0:T(8,128)(2,1)S(1)} %get-tuple-element.38.low_ref, f32[512,1024]{1,0:T(8,128)S(1)} %update_near.1.refs_0_, ...), custom_call_target="tpu_custom_call", output_to_operand_aliasing={{}: (3, {})} | custom-call | tf_op jit(solution)/shard_map/update_next/pallas_call | solution.py:271
  169.0 2.6 %update_far.1 = f32[512,1024]{1,0:T(8,128)S(1)} custom-call(s32[5]{0:T(128)S(1)} %stack.81.info, bf16[4,512,256]{2,1,0:T(8,128)(2,1)S(1)} %get-tuple-element.37.high_ref, bf16[4,512,256]{2,1,0:T(8,128)(2,1)S(1)} %get-tuple-element.38.low_ref, f32[512,1024]{1,0:T(8,128)S(1)} %update_next.1.refs_0_, ...), custom_call_target="tpu_custom_call", output_to_operand_aliasing={{}: (3, {})} | custom-call | tf_op jit(solution)/shard_map/update_far/pallas_call | solution.py:271
  171.8 1.4 collective-permute-start.27
  173.2 2.3 %collective-permute-done.27 = f32[256,1024]{1,0:T(8,128)S(1)} collective-permute-done((f32[256,1024]{1,0:T(8,128)S(1)}, f32[256,1024]{1,0:T(8,128)S(1)}, u32[]{:S(2)}, u32[]{:S(2)}) %collective-permute-start.27) | collective-permute-done | bytes 1048608 | tf_op jit(solution)/shard_map/ppermute | solution.py:295
  (124 shorter events, 41.4 us)
Async XLA Ops:
  1.8 15.8 %collective-permute-start = (f32[1024,128]{1,0:T(8,128)S(1)}, f32[1024,128]{1,0:T(8,128)S(1)}, u32[]{:S(2)}, u32[]{:S(2)}) collective-permute-start(f32[1024,128]{1,0:T(8,128)S(1)} %invert_diagonal.1.refs_0_), channel_id=1, source_target_pairs={{0,4},{1,5},{2,6},{3,7},{4,0},{5,1},{6,2},{7,3},{16,17},{17,18},{1... | collective-permute-start | bytes 1572872 | tf_op jit(solution)/shard_map/ppermute | solution.py:295
  2.5 15.1 %collective-permute-start.1 = (f32[1024,128]{1,0:T(8,128)S(1)}, f32[1024,128]{1,0:T(8,128)S(1)}, u32[]{:S(2)}, u32[]{:S(2)}) collective-permute-start(f32[1024,128]{1,0:T(8,128)S(1)} %invert_diagonal.1.refs_0_), channel_id=1, source_target_pairs={{16,20},{17,21},{18,22},{19,23},{20,16},{21,17},{22,18},{23,19},{2... | collective-permute-start | bytes 1572872 | tf_op jit(solution)/shard_map/ppermute | solution.py:295
  3.2 14.4 %collective-permute-start.3 = (f32[1024,128]{1,0:T(8,128)S(1)}, f32[1024,128]{1,0:T(8,128)}, u32[]{:S(2)}, u32[]{:S(2)}) collective-permute-start(f32[1024,128]{1,0:T(8,128)S(1)} %invert_diagonal.1.refs_0_), channel_id=1, source_target_pairs={{16,19},{17,16},{18,17},{19,18},{20,23},{21,20},{22,21},{23,22},{2... | collective-permute-start | bytes 1572872 | tf_op jit(solution)/shard_map/ppermute | solution.py:295
  5.4 12.2 %all-to-all-start = ((f32[8,64,128]{2,1,0:T(8,128)}), f32[8,64,128]{2,1,0:T(8,128)S(1)}, u32[]{:S(2)}, u32[]{:S(2)}) async-start(f32[8,64,128]{2,1,0:T(8,128)} %arrange_rhs.1), calls=%async_computation | async-start | bytes 524288 | tf_op jit(solution)/shard_map/all_to_all | solution.py:384
  18.8 2.6 %collective-permute-start.4 = (f32[512,128]{1,0:T(8,128)S(1)}, f32[512,128]{1,0:T(8,128)S(1)}, u32[]{:S(2)}, u32[]{:S(2)}) collective-permute-start(f32[512,128]{1,0:T(8,128)S(1)} %slice.58), channel_id=1, source_target_pairs={{16,19},{17,16},{18,17},{19,18},{20,23},{21,20},{22,21},{23,22},{2... | collective-permute-start | bytes 786440 | tf_op jit(solution)/shard_map/ppermute | solution.py:295
  21.5 3.9 %collective-permute-start.5 = (f32[1536,128]{1,0:T(8,128)S(1)}, f32[1536,128]{1,0:T(8,128)S(1)}, u32[]{:S(2)}, u32[]{:S(2)}) collective-permute-start(f32[1536,128]{1,0:T(8,128)S(1)} %pad_maximum_fusion.refs_0_.refs_2_), channel_id=1, source_target_pairs={{0,1},{1,2},{2,3},{3,0},{4,5},{5,6},{6,7},{7,4},{16,20},{17,21},{1... | collective-permute-start | bytes 2359304 | tf_op jit(solution)/shard_map/ppermute | solution.py:295
  22.5 5.2 %collective-permute-start.7 = (f32[1536,128]{1,0:T(8,128)S(1)}, f32[1536,128]{1,0:T(8,128)S(1)}, u32[]{:S(2)}, u32[]{:S(2)}) collective-permute-start(f32[1536,128]{1,0:T(8,128)S(1)} %pad_maximum_fusion.1.refs_3_), channel_id=1, source_target_pairs={{0,3},{1,0},{2,1},{3,2},{4,7},{5,4},{6,5},{7,6},{16,20},{17,21},{1... | collective-permute-start | bytes 2359304 | tf_op jit(solution)/shard_map/ppermute | solution.py:295
  23.2 2.2 %collective-permute-start.6 = (f32[512,128]{1,0:T(8,128)S(1)}, f32[512,128]{1,0:T(8,128)S(1)}, u32[]{:S(2)}, u32[]{:S(2)}) collective-permute-start(f32[512,128]{1,0:T(8,128)S(1)} %bitcast.32), channel_id=1, source_target_pairs={{8,4},{9,5},{10,6},{11,7},{12,0},{13,1},{14,2},{15,3},{24,20},{25,... | collective-permute-start | bytes 786440 | tf_op jit(solution)/shard_map/ppermute | solution.py:295
  26.2 5.7 %collective-permute-start.8 = (f32[768,128]{1,0:T(8,128)}, f32[768,128]{1,0:T(8,128)}, u32[]{:S(2)}, u32[]{:S(2)}) collective-permute-start(f32[768,128]{1,0:T(8,128)} %slice.49), channel_id=1, source_target_pairs={{0,1},{1,2},{2,3},{3,0},{4,5},{5,6},{6,7},{7,4}} | collective-permute-start | bytes 1179656 | tf_op jit(solution)/shard_map/ppermute | solution.py:295
  28.5 3.5 %collective-permute-start.9 = (f32[768,128]{1,0:T(8,128)}, f32[768,128]{1,0:T(8,128)}, u32[]{:S(2)}, u32[]{:S(2)}) collective-permute-start(f32[768,128]{1,0:T(8,128)} %slice.59), channel_id=1, source_target_pairs={{0,3},{1,0},{2,1},{3,2},{4,7},{5,4},{6,5},{7,6}} | collective-permute-start | bytes 1179656 | tf_op jit(solution)/shard_map/ppermute | solution.py:295
  34.1 31.7 %all-to-all-start.1 = ((f32[16,256,128]{2,1,0:T(8,128)}), f32[16,256,128]{2,1,0:T(8,128)S(1)}, u32[]{:S(2)}, u32[]{:S(2)}) async-start(f32[16,256,128]{2,1,0:T(8,128)} %copy-done), calls=%async_computation.1 | async-start | bytes 4194304 | tf_op jit(solution)/shard_map/all_to_all | solution.py:393
  69.8 60.4 %collective-permute-start.15 = (f32[512,128]{1,0:T(8,128)S(1)}, f32[512,128]{1,0:T(8,128)S(1)}, u32[]{:S(2)}, u32[]{:S(2)}) collective-permute-start(f32[512,128]{1,0:T(8,128)S(1)} %collective-permute-done.13), channel_id=1, source_target_pairs={{32,64},{33,65},{34,66},{35,67},{36,68},{37,69},{38,70},{39,71},{4... | collective-permute-start | bytes 786440 | tf_op jit(solution)/shard_map/ppermute | solution.py:295
  130.3 5.6 %collective-permute-start.18 = (f32[512,128]{1,0:T(8,128)S(1)}, f32[512,128]{1,0:T(8,128)S(1)}, u32[]{:S(2)}, u32[]{:S(2)}) collective-permute-start(f32[512,128]{1,0:T(8,128)S(1)} %add_select_fusion), channel_id=1, source_target_pairs={{0,3},{1,0},{2,1},{3,2},{4,7},{5,4},{6,5},{7,6},{8,11},{9,8},{10,9... | collective-permute-start | bytes 786440 | tf_op jit(solution)/shard_map/ppermute | solution.py:295
  132.2 6.8 %collective-permute-start.16 = (f32[512,128]{1,0:T(8,128)S(1)}, f32[512,128]{1,0:T(8,128)S(1)}, u32[]{:S(2)}, u32[]{:S(2)}) collective-permute-start(f32[512,128]{1,0:T(8,128)S(1)} %add_select_fusion), channel_id=1, source_target_pairs={{0,1},{1,2},{2,3},{3,0},{4,5},{5,6},{6,7},{7,4},{8,9},{9,10},{10,1... | collective-permute-start | bytes 786440 | tf_op jit(solution)/shard_map/ppermute | solution.py:295
  135.9 4.7 %collective-permute-start.19 = (f32[256,128]{1,0:T(8,128)S(1)}, f32[256,128]{1,0:T(8,128)S(1)}, u32[]{:S(2)}, u32[]{:S(2)}) collective-permute-start(f32[256,128]{1,0:T(8,128)S(1)} %slice.63), channel_id=1, source_target_pairs={{0,3},{1,0},{2,1},{3,2},{4,7},{5,4},{6,5},{7,6},{8,11},{9,8},{10,9... | collective-permute-start | bytes 393224 | tf_op jit(solution)/shard_map/ppermute | solution.py:295
  139.0 5.2 %collective-permute-start.17 = (f32[256,128]{1,0:T(8,128)S(1)}, f32[256,128]{1,0:T(8,128)}, u32[]{:S(2)}, u32[]{:S(2)}) collective-permute-start(f32[256,128]{1,0:T(8,128)S(1)} %slice.62), channel_id=1, source_target_pairs={{0,1},{1,2},{2,3},{3,0},{4,5},{5,6},{6,7},{7,4},{8,9},{9,10},{10,1... | collective-permute-start | bytes 393224 | tf_op jit(solution)/shard_map/ppermute | solution.py:295
  147.2 5.4 %collective-permute-start.20 = (f32[8,256,128]{2,1,0:T(8,128)}, f32[8,256,128]{2,1,0:T(8,128)}, u32[]{:S(2)}, u32[]{:S(2)}) collective-permute-start(f32[8,256,128]{2,1,0:T(8,128)} %constant_dynamic-slice_fusion), channel_id=1, source_target_pairs={{0,16},{1,17},{2,18},{3,19},{4,20},{5,21},{6,22},{7,23},{8,24},{9,... | collective-permute-start | bytes 3145736 | tf_op jit(solution)/shard_map/ppermute | solution.py:295
  148.2 9.7 %collective-permute-start.21 = (f32[2,512,128]{2,1,0:T(8,128)S(1)}, f32[2,512,128]{2,1,0:T(8,128)}, u32[]{:S(2)}, u32[]{:S(2)}) collective-permute-start(f32[2,512,128]{2,1,0:T(8,128)S(1)} %pad_maximum_fusion.3.refs_0_), channel_id=1, source_target_pairs={{0,4},{1,5},{2,6},{3,7},{4,8},{5,9},{6,10},{7,11},{8,12},{9,13},{1... | collective-permute-start | bytes 1572872 | tf_op jit(solution)/shard_map/ppermute | solution.py:295
  148.3 9.6 %collective-permute-start.22 = (f32[2,512,128]{2,1,0:T(8,128)S(1)}, f32[2,512,128]{2,1,0:T(8,128)}, u32[]{:S(2)}, u32[]{:S(2)}) collective-permute-start(f32[2,512,128]{2,1,0:T(8,128)S(1)} %pad_maximum_fusion.2.refs_1_), channel_id=1, source_target_pairs={{0,12},{1,13},{2,14},{3,15},{4,0},{5,1},{6,2},{7,3},{8,4},{9,5},{1... | collective-permute-start | bytes 1572872 | tf_op jit(solution)/shard_map/ppermute | solution.py:295
  151.1 11.6 %collective-permute-start.25 = (f32[2,512,128]{2,1,0:T(8,128)S(1)}, f32[2,512,128]{2,1,0:T(8,128)S(1)}, u32[]{:S(2)}, u32[]{:S(2)}) collective-permute-start(f32[2,512,128]{2,1,0:T(8,128)S(1)} %pad_maximum_fusion.3.refs_0_), channel_id=1, source_target_pairs={{0,12},{1,13},{2,14},{3,15},{4,0},{5,1},{6,2},{7,3},{8,4},{9,5},{1... | collective-permute-start | bytes 1572872 | tf_op jit(solution)/shard_map/ppermute | solution.py:295
  151.1 12.3 %collective-permute-start.26 = (f32[2,512,128]{2,1,0:T(8,128)S(1)}, f32[2,512,128]{2,1,0:T(8,128)S(1)}, u32[]{:S(2)}, u32[]{:S(2)}) collective-permute-start(f32[2,512,128]{2,1,0:T(8,128)S(1)} %pad_maximum_fusion.2.refs_1_), channel_id=1, source_target_pairs={{0,4},{1,5},{2,6},{3,7},{4,8},{5,9},{6,10},{7,11},{8,12},{9,13},{1... | collective-permute-start | bytes 1572872 | tf_op jit(solution)/shard_map/ppermute | solution.py:295
  157.9 11.1 %collective-permute-start.23 = (f32[2,512,128]{2,1,0:T(8,128)}, f32[2,512,128]{2,1,0:T(8,128)S(1)}, u32[]{:S(2)}, u32[]{:S(2)}) collective-permute-start(f32[2,512,128]{2,1,0:T(8,128)} %collective-permute-done.21.refs_3_), channel_id=1, source_target_pairs={{0,4},{1,5},{2,6},{3,7},{4,8},{5,9},{6,10},{7,11},{8,12},{9,13},{1... | collective-permute-start | bytes 1572872 | tf_op jit(solution)/shard_map/ppermute | solution.py:295
  157.9 11.1 %collective-permute-start.24 = (f32[2,512,128]{2,1,0:T(8,128)}, f32[2,512,128]{2,1,0:T(8,128)S(1)}, u32[]{:S(2)}, u32[]{:S(2)}) collective-permute-start(f32[2,512,128]{2,1,0:T(8,128)} %collective-permute-done.22.refs_2_), channel_id=1, source_target_pairs={{0,12},{1,13},{2,14},{3,15},{4,0},{5,1},{6,2},{7,3},{8,4},{9,5},{1... | collective-permute-start | bytes 1572872 | tf_op jit(solution)/shard_map/ppermute | solution.py:295
  171.8 3.7 %collective-permute-start.27 = (f32[256,1024]{1,0:T(8,128)S(1)}, f32[256,1024]{1,0:T(8,128)S(1)}, u32[]{:S(2)}, u32[]{:S(2)}) collective-permute-start(f32[256,1024]{1,0:T(8,128)S(1)} %slice.65), channel_id=1, source_target_pairs={{0,16},{1,17},{2,18},{3,19},{4,20},{5,21},{6,22},{7,23},{8,24},{9,... | collective-permute-start | bytes 3145736 | tf_op jit(solution)/shard_map/ppermute | solution.py:295
  (30 other events, 93.0 us)

commit v17 on v16

--- a/solution.py
+++ b/solution.py
@@ -394,8 +394,8 @@
     rest, tri = residual_or_pack(place(core * (1 + yh)), *lower_row, columns, sent)
     second_rhs = move(rest, lambda a, b, c, d: (0, 1, 3 - c, d) if (a, b) == (0, 1) and c < 2 else None)
     second = solve_second(place((core == 1) & (yh == 1)), tri, second_rhs)
-    second, left = lax.optimization_barrier((second, left))
     mine = deal(first, second, core, yh, xi)
+    mine, left = lax.optimization_barrier((mine, left))
 
     def swap(value):
         return move(value, lambda a, b, c, d: (a, 1 - b, c, d))

time: 178 us -> 173 us (0.972)
  local copies, waits for them, and re-layouts: 17.5 us -> 9.57 us
  starting transfers between devices: 38.5 us -> 41 us
  waiting for transfers between devices: 96.2 us -> 98.5 us
  other arithmetic: 6.99 us -> 4.93 us
    ppermute x28, waiting for transfers between devices: 75.2 us -> 93.1 us  [move(): return lax.ppermute(value, AXES, pairs)]
    all_to_all x1, waiting for transfers between devices: 14.9 us -> 0.01 us  [shards(): left = lax.all_to_all(by_rows, COL, 0, 0, tiled=True)]
    unnamed x49 -> x25, local copies, waits for them, and re-layouts: 11.3 us -> 4.55 us
    ppermute x28, starting transfers between devices: 27.8 us -> 30.4 us  [move(): return lax.ppermute(value, AXES, pairs)]
  transfers between devices with their start and end apart: 30 -> 30, of which waited for: 12 -> 11; matrix products, arithmetic and copies ran while one was open for 4% -> 3% of each run, Pallas kernels for 7% -> 6%
where the time goes in v17:
time: 173 us; the launch traced here: 172 us
  waiting for transfers between devices  98.5 us (57%)
  starting transfers between devices  41 us (24%)
  Pallas kernels  17.6 us (10%)
  local copies, waits for them, and re-layouts  9.57 us (6%)
  other arithmetic  4.93 us (3%)
    ppermute x28, waiting for transfers between devices, move(): return lax.ppermute(value, AXES, pairs)  93.1 us
    ppermute x28, starting transfers between devices, move(): return lax.ppermute(value, AXES, pairs)  30.4 us
    pallas_call x3, Pallas kernels, accumulate(): pl.pallas_call(body, out_shape=jax.ShapeDtypeStruct((512, 1024), F32), in...  10.1 us
    all_to_all x1, starting transfers between devices, shards(): lax.all_to_all(arrange_rhs(yh, rhs), ('yl', 'z'), 0, 0, tiled=True)  6.05 us
    all_to_all x1, waiting for transfers between devices, shards(): lax.all_to_all(arrange_rhs(yh, rhs), ('yl', 'z'), 0, 0, tiled=True)  5.39 us
    all_to_all x1, starting transfers between devices, shards(): left = lax.all_to_all(by_rows, COL, 0, 0, tiled=True)  4.63 us
    unnamed x25, local copies, waits for them, and re-layouts  4.55 us
  transfers between devices with their start and end apart: 30, of which 11 were waited for; matrix products, arithmetic and copies ran while one was open for 3% of the time, Pallas kernels for 6%

profile of v17, /device:TPU:5, one launch (start us, length us, event | category | flops | bytes accessed | tf_op | source)
XLA Modules:
  0.0 172.1 jit_solution(17150453939864360671)
XLA Ops:
  4.7 6.0 %all-to-all-start = ((f32[8,64,128]{2,1,0:T(8,128)}), f32[8,64,128]{2,1,0:T(8,128)S(1)}, u32[]{:S(2)}, u32[]{:S(2)}) async-start(f32[8,64,128]{2,1,0:T(8,128)} %arrange_rhs.1), calls=%async_computation | async-start | bytes 524288 | tf_op jit(solution)/shard_map/all_to_all | solution.py:384
  11.4 5.4 %all-to-all-done = f32[8,64,128]{2,1,0:T(8,128)S(1)} async-done(((f32[8,64,128]{2,1,0:T(8,128)}), f32[8,64,128]{2,1,0:T(8,128)S(1)}, u32[]{:S(2)}, u32[]{:S(2)}) %all-to-all-start) | async-done | bytes 262176 | tf_op jit(solution)/shard_map/all_to_all | solution.py:384
  22.5 1.4 collective-permute-start.8
  24.7 1.4 collective-permute-start.9
  28.2 1.9 %solve_first.1 = f32[1024,128]{1,0:T(8,128)} custom-call(s32[3]{0:T(128)S(1)} %pad_add_fusion.1.info, f32[1536,128]{1,0:T(8,128)S(1)} %pad_maximum_fusion.refs_0_.refs_2_, f32[1536,128]{1,0:T(8,128)S(1)} %collective-permute-done.5.refs_1_.refs_5_, f32[1536,128]{1,0:T(8,128)S(1)} %collective-permute-done.6.refs_2_.refs_4_, ...), custom_call_target="tpu_custom_call" | custom-call | tf_op jit(solution)/shard_map/solve_first/pallas_call | solution.py:107
  30.1 1.5 collective-permute-start.10
  33.9 1.9 %residual_or_pack.1 = (f32[1024,128]{1,0:T(8,128)}, bf16[112,1024,256]{2,1,0:T(8,128)(2,1)}) custom-call(s32[3]{0:T(128)S(1)} %pad_add_fusion.5.info, f32[1024,128]{1,0:T(8,128)S(1)} %invert_diagonal.1.refs_0_, f32[1024,128]{1,0:T(8,128)S(1)} %copy-done.7, f32[1536,128]{1,0:T(8,128)S(1)} %pad_maximum_fusion.refs_0_.refs_2_, f32[1536,128]{1,0:T(8,128)S(1)} %copy-done.5, ...), custom_call_target="tpu_custom_call" | custom-call | tf_op jit(solution)/shard_map/residual_or_pack/pallas_call | solution.py:144
  36.4 4.6 %all-to-all-start.1 = ((f32[16,256,128]{2,1,0:T(8,128)}), f32[16,256,128]{2,1,0:T(8,128)S(1)}, u32[]{:S(2)}, u32[]{:S(2)}) async-start(f32[16,256,128]{2,1,0:T(8,128)} %copy-done), calls=%async_computation.1 | async-start | bytes 4194304 | tf_op jit(solution)/shard_map/all_to_all | solution.py:393
  45.3 76.8 %collective-permute-done.15 = f32[512,128]{1,0:T(8,128)S(1)} collective-permute-done((f32[512,128]{1,0:T(8,128)S(1)}, f32[512,128]{1,0:T(8,128)S(1)}, u32[]{:S(2)}, u32[]{:S(2)}) %collective-permute-start.15) | collective-permute-done | bytes 262176 | tf_op jit(solution)/shard_map/ppermute | solution.py:295
  122.3 1.5 collective-permute-start.16
  123.8 4.1 %collective-permute-done.18 = f32[512,128]{1,0:T(8,128)S(1)} collective-permute-done((f32[512,128]{1,0:T(8,128)S(1)}, f32[512,128]{1,0:T(8,128)S(1)}, u32[]{:S(2)}, u32[]{:S(2)}) %collective-permute-start.18) | collective-permute-done | bytes 262176 | tf_op jit(solution)/shard_map/ppermute | solution.py:295
  129.5 2.6 %collective-permute-done.19 = f32[256,128]{1,0:T(8,128)S(1)} collective-permute-done((f32[256,128]{1,0:T(8,128)S(1)}, f32[256,128]{1,0:T(8,128)S(1)}, u32[]{:S(2)}, u32[]{:S(2)}) %collective-permute-start.19) | collective-permute-done | bytes 131104 | tf_op jit(solution)/shard_map/ppermute | solution.py:295
  132.0 2.6 %collective-permute-done.17 = f32[256,128]{1,0:T(8,128)} collective-permute-done((f32[256,128]{1,0:T(8,128)S(1)}, f32[256,128]{1,0:T(8,128)}, u32[]{:S(2)}, u32[]{:S(2)}) %collective-permute-start.17) | collective-permute-done | bytes 131104 | tf_op jit(solution)/shard_map/ppermute | solution.py:295
  137.6 1.7 %collective-permute-start.20 = (f32[8,256,128]{2,1,0:T(8,128)}, f32[8,256,128]{2,1,0:T(8,128)}, u32[]{:S(2)}, u32[]{:S(2)}) collective-permute-start(f32[8,256,128]{2,1,0:T(8,128)} %constant_dynamic-slice_fusion), channel_id=1, source_target_pairs={{0,16},{1,17},{2,18},{3,19},{4,20},{5,21},{6,22},{7,23},{8,24},{9,... | collective-permute-start | bytes 3145736 | tf_op jit(solution)/shard_map/ppermute | solution.py:295
  140.4 2.7 %collective-permute-start.22 = (f32[2,512,128]{2,1,0:T(8,128)S(1)}, f32[2,512,128]{2,1,0:T(8,128)}, u32[]{:S(2)}, u32[]{:S(2)}) collective-permute-start(f32[2,512,128]{2,1,0:T(8,128)S(1)} %pad_maximum_fusion.2.refs_1_), channel_id=1, source_target_pairs={{0,12},{1,13},{2,14},{3,15},{4,0},{5,1},{6,2},{7,3},{8,4},{9,5},{1... | collective-permute-start | bytes 1572872 | tf_op jit(solution)/shard_map/ppermute | solution.py:295
  143.5 1.5 collective-permute-start.26
  144.9 1.6 prepare_update.1
  146.5 2.5 %update_near.1.refs_0_ = f32[512,1024]{1,0:T(8,128)S(1)} custom-call(s32[5]{0:T(128)S(1)} %stack.81.info, bf16[4,512,256]{2,1,0:T(8,128)(2,1)S(1)} %get-tuple-element.37.high_ref, bf16[4,512,256]{2,1,0:T(8,128)(2,1)S(1)} %get-tuple-element.38.low_ref, f32[2,512,128]{2,1,0:T(8,128)S(1)} %pad_maximum_fusion.3.refs_0_, f32[2,512,128]{2,1,0:T(8,128)S(1)} %pad_maximum_fusion.2.refs_1_), custom_call_target="tpu_custom_call" | custom-call | tf_op jit(solution)/shard_map/update_near/pallas_call | solution.py:271
  150.1 2.7 %collective-permute-start.24 = (f32[2,512,128]{2,1,0:T(8,128)}, f32[2,512,128]{2,1,0:T(8,128)S(1)}, u32[]{:S(2)}, u32[]{:S(2)}) collective-permute-start(f32[2,512,128]{2,1,0:T(8,128)} %collective-permute-done.22.refs_2_), channel_id=1, source_target_pairs={{0,12},{1,13},{2,14},{3,15},{4,0},{5,1},{6,2},{7,3},{8,4},{9,5},{1... | collective-permute-start | bytes 1572872 | tf_op jit(solution)/shard_map/ppermute | solution.py:295
  152.8 2.1 %collective-permute-done.25.refs_1_ = f32[2,512,128]{2,1,0:T(8,128)S(1)} collective-permute-done((f32[2,512,128]{2,1,0:T(8,128)S(1)}, f32[2,512,128]{2,1,0:T(8,128)S(1)}, u32[]{:S(2)}, u32[]{:S(2)}) %collective-permute-start.25) | collective-permute-done | bytes 524320 | tf_op jit(solution)/shard_map/ppermute | solution.py:295
  155.6 5.1 %update_next.1.refs_0_ = f32[512,1024]{1,0:T(8,128)S(1)} custom-call(s32[5]{0:T(128)S(1)} %stack.81.info, bf16[4,512,256]{2,1,0:T(8,128)(2,1)S(1)} %get-tuple-element.37.high_ref, bf16[4,512,256]{2,1,0:T(8,128)(2,1)S(1)} %get-tuple-element.38.low_ref, f32[512,1024]{1,0:T(8,128)S(1)} %update_near.1.refs_0_, ...), custom_call_target="tpu_custom_call", output_to_operand_aliasing={{}: (3, {})} | custom-call | tf_op jit(solution)/shard_map/update_next/pallas_call | solution.py:271
  161.2 2.6 %update_far.1 = f32[512,1024]{1,0:T(8,128)S(1)} custom-call(s32[5]{0:T(128)S(1)} %stack.81.info, bf16[4,512,256]{2,1,0:T(8,128)(2,1)S(1)} %get-tuple-element.37.high_ref, bf16[4,512,256]{2,1,0:T(8,128)(2,1)S(1)} %get-tuple-element.38.low_ref, f32[512,1024]{1,0:T(8,128)S(1)} %update_next.1.refs_0_, ...), custom_call_target="tpu_custom_call", output_to_operand_aliasing={{}: (3, {})} | custom-call | tf_op jit(solution)/shard_map/update_far/pallas_call | solution.py:271
  163.9 4.7 %collective-permute-start.27 = (f32[256,1024]{1,0:T(8,128)S(1)}, f32[256,1024]{1,0:T(8,128)S(1)}, u32[]{:S(2)}, u32[]{:S(2)}) collective-permute-start(f32[256,1024]{1,0:T(8,128)S(1)} %slice.65), channel_id=1, source_target_pairs={{0,16},{1,17},{2,18},{3,19},{4,20},{5,21},{6,22},{7,23},{8,24},{9,... | collective-permute-start | bytes 3145736 | tf_op jit(solution)/shard_map/ppermute | solution.py:295
  168.7 2.3 %collective-permute-done.27 = f32[256,1024]{1,0:T(8,128)S(1)} collective-permute-done((f32[256,1024]{1,0:T(8,128)S(1)}, f32[256,1024]{1,0:T(8,128)S(1)}, u32[]{:S(2)}, u32[]{:S(2)}) %collective-permute-start.27) | collective-permute-done | bytes 1048608 | tf_op jit(solution)/shard_map/ppermute | solution.py:295
  (100 shorter events, 30.6 us)
Async XLA Ops:
  1.8 8.9 %collective-permute-start.3 = (f32[1024,128]{1,0:T(8,128)S(1)}, f32[1024,128]{1,0:T(8,128)S(1)}, u32[]{:S(2)}, u32[]{:S(2)}) collective-permute-start(f32[1024,128]{1,0:T(8,128)S(1)} %invert_diagonal.1.refs_0_), channel_id=1, source_target_pairs={{16,19},{17,16},{18,17},{19,18},{20,23},{21,20},{22,21},{23,22},{2... | collective-permute-start | bytes 1572872 | tf_op jit(solution)/shard_map/ppermute | solution.py:295
  2.5 14.3 %collective-permute-start = (f32[1024,128]{1,0:T(8,128)S(1)}, f32[1024,128]{1,0:T(8,128)S(1)}, u32[]{:S(2)}, u32[]{:S(2)}) collective-permute-start(f32[1024,128]{1,0:T(8,128)S(1)} %invert_diagonal.1.refs_0_), channel_id=1, source_target_pairs={{0,4},{1,5},{2,6},{3,7},{4,0},{5,1},{6,2},{7,3},{16,17},{17,18},{1... | collective-permute-start | bytes 1572872 | tf_op jit(solution)/shard_map/ppermute | solution.py:295
  3.2 13.6 %collective-permute-start.1 = (f32[1024,128]{1,0:T(8,128)S(1)}, f32[1024,128]{1,0:T(8,128)S(1)}, u32[]{:S(2)}, u32[]{:S(2)}) collective-permute-start(f32[1024,128]{1,0:T(8,128)S(1)} %invert_diagonal.1.refs_0_), channel_id=1, source_target_pairs={{16,20},{17,21},{18,22},{19,23},{20,16},{21,17},{22,18},{23,19},{2... | collective-permute-start | bytes 1572872 | tf_op jit(solution)/shard_map/ppermute | solution.py:295
  4.7 12.2 %all-to-all-start = ((f32[8,64,128]{2,1,0:T(8,128)}), f32[8,64,128]{2,1,0:T(8,128)S(1)}, u32[]{:S(2)}, u32[]{:S(2)}) async-start(f32[8,64,128]{2,1,0:T(8,128)} %arrange_rhs.1), calls=%async_computation | async-start | bytes 524288 | tf_op jit(solution)/shard_map/all_to_all | solution.py:384
  10.8 6.9 %collective-permute-start.4 = (f32[512,128]{1,0:T(8,128)S(1)}, f32[512,128]{1,0:T(8,128)S(1)}, u32[]{:S(2)}, u32[]{:S(2)}) collective-permute-start(f32[512,128]{1,0:T(8,128)S(1)} %slice.58), channel_id=1, source_target_pairs={{16,19},{17,16},{18,17},{19,18},{20,23},{21,20},{22,21},{23,22},{2... | collective-permute-start | bytes 786440 | tf_op jit(solution)/shard_map/ppermute | solution.py:295
  17.8 3.9 %collective-permute-start.6 = (f32[1536,128]{1,0:T(8,128)S(1)}, f32[1536,128]{1,0:T(8,128)S(1)}, u32[]{:S(2)}, u32[]{:S(2)}) collective-permute-start(f32[1536,128]{1,0:T(8,128)S(1)} %pad_maximum_fusion.refs_0_.refs_2_), channel_id=1, source_target_pairs={{0,1},{1,2},{2,3},{3,0},{4,5},{5,6},{6,7},{7,4},{16,20},{17,21},{1... | collective-permute-start | bytes 2359304 | tf_op jit(solution)/shard_map/ppermute | solution.py:295
  18.8 5.2 %collective-permute-start.5 = (f32[1536,128]{1,0:T(8,128)S(1)}, f32[1536,128]{1,0:T(8,128)S(1)}, u32[]{:S(2)}, u32[]{:S(2)}) collective-permute-start(f32[1536,128]{1,0:T(8,128)S(1)} %pad_maximum_fusion.1.refs_3_), channel_id=1, source_target_pairs={{0,3},{1,0},{2,1},{3,2},{4,7},{5,4},{6,5},{7,6},{16,20},{17,21},{1... | collective-permute-start | bytes 2359304 | tf_op jit(solution)/shard_map/ppermute | solution.py:295
  22.5 5.6 %collective-permute-start.8 = (f32[768,128]{1,0:T(8,128)}, f32[768,128]{1,0:T(8,128)}, u32[]{:S(2)}, u32[]{:S(2)}) collective-permute-start(f32[768,128]{1,0:T(8,128)} %slice.49), channel_id=1, source_target_pairs={{0,1},{1,2},{2,3},{3,0},{4,5},{5,6},{6,7},{7,4}} | collective-permute-start | bytes 1179656 | tf_op jit(solution)/shard_map/ppermute | solution.py:295
  24.7 3.5 %collective-permute-start.9 = (f32[768,128]{1,0:T(8,128)}, f32[768,128]{1,0:T(8,128)}, u32[]{:S(2)}, u32[]{:S(2)}) collective-permute-start(f32[768,128]{1,0:T(8,128)} %slice.59), channel_id=1, source_target_pairs={{0,3},{1,0},{2,1},{3,2},{4,7},{5,4},{6,5},{7,6}} | collective-permute-start | bytes 1179656 | tf_op jit(solution)/shard_map/ppermute | solution.py:295
  35.7 5.4 %collective-permute-start.11 = (f32[1024,128]{1,0:T(8,128)}, f32[1024,128]{1,0:T(8,128)S(1)}, u32[]{:S(2)}, u32[]{:S(2)}) collective-permute-start(f32[1024,128]{1,0:T(8,128)} %get-tuple-element.31), channel_id=1, source_target_pairs={{16,28},{17,29},{18,30},{19,31},{20,24},{21,25},{22,26},{23,27}} | collective-permute-start | bytes 1572872 | tf_op jit(solution)/shard_map/ppermute | solution.py:295
  36.4 85.8 %all-to-all-start.1 = ((f32[16,256,128]{2,1,0:T(8,128)}), f32[16,256,128]{2,1,0:T(8,128)S(1)}, u32[]{:S(2)}, u32[]{:S(2)}) async-start(f32[16,256,128]{2,1,0:T(8,128)} %copy-done), calls=%async_computation.1 | async-start | bytes 4194304 | tf_op jit(solution)/shard_map/all_to_all | solution.py:393
  44.0 78.1 %collective-permute-start.15 = (f32[512,128]{1,0:T(8,128)S(1)}, f32[512,128]{1,0:T(8,128)S(1)}, u32[]{:S(2)}, u32[]{:S(2)}) collective-permute-start(f32[512,128]{1,0:T(8,128)S(1)} %collective-permute-done.13), channel_id=1, source_target_pairs={{32,64},{33,65},{34,66},{35,67},{36,68},{37,69},{38,70},{39,71},{4... | collective-permute-start | bytes 786440 | tf_op jit(solution)/shard_map/ppermute | solution.py:295
  122.3 5.6 %collective-permute-start.18 = (f32[512,128]{1,0:T(8,128)S(1)}, f32[512,128]{1,0:T(8,128)S(1)}, u32[]{:S(2)}, u32[]{:S(2)}) collective-permute-start(f32[512,128]{1,0:T(8,128)S(1)} %add_select_fusion), channel_id=1, source_target_pairs={{0,3},{1,0},{2,1},{3,2},{4,7},{5,4},{6,5},{7,6},{8,11},{9,8},{10,9... | collective-permute-start | bytes 786440 | tf_op jit(solution)/shard_map/ppermute | solution.py:295
  122.3 6.8 %collective-permute-start.16 = (f32[512,128]{1,0:T(8,128)S(1)}, f32[512,128]{1,0:T(8,128)S(1)}, u32[]{:S(2)}, u32[]{:S(2)}) collective-permute-start(f32[512,128]{1,0:T(8,128)S(1)} %add_select_fusion), channel_id=1, source_target_pairs={{0,1},{1,2},{2,3},{3,0},{4,5},{5,6},{6,7},{7,4},{8,9},{9,10},{10,1... | collective-permute-start | bytes 786440 | tf_op jit(solution)/shard_map/ppermute | solution.py:295
  127.9 4.2 %collective-permute-start.19 = (f32[256,128]{1,0:T(8,128)S(1)}, f32[256,128]{1,0:T(8,128)S(1)}, u32[]{:S(2)}, u32[]{:S(2)}) collective-permute-start(f32[256,128]{1,0:T(8,128)S(1)} %slice.63), channel_id=1, source_target_pairs={{0,3},{1,0},{2,1},{3,2},{4,7},{5,4},{6,5},{7,6},{8,11},{9,8},{10,9... | collective-permute-start | bytes 393224 | tf_op jit(solution)/shard_map/ppermute | solution.py:295
  129.2 5.5 %collective-permute-start.17 = (f32[256,128]{1,0:T(8,128)S(1)}, f32[256,128]{1,0:T(8,128)}, u32[]{:S(2)}, u32[]{:S(2)}) collective-permute-start(f32[256,128]{1,0:T(8,128)S(1)} %slice.62), channel_id=1, source_target_pairs={{0,1},{1,2},{2,3},{3,0},{4,5},{5,6},{6,7},{7,4},{8,9},{9,10},{10,1... | collective-permute-start | bytes 393224 | tf_op jit(solution)/shard_map/ppermute | solution.py:295
  137.6 7.3 %collective-permute-start.20 = (f32[8,256,128]{2,1,0:T(8,128)}, f32[8,256,128]{2,1,0:T(8,128)}, u32[]{:S(2)}, u32[]{:S(2)}) collective-permute-start(f32[8,256,128]{2,1,0:T(8,128)} %constant_dynamic-slice_fusion), channel_id=1, source_target_pairs={{0,16},{1,17},{2,18},{3,19},{4,20},{5,21},{6,22},{7,23},{8,24},{9,... | collective-permute-start | bytes 3145736 | tf_op jit(solution)/shard_map/ppermute | solution.py:295
  140.4 9.7 %collective-permute-start.21 = (f32[2,512,128]{2,1,0:T(8,128)S(1)}, f32[2,512,128]{2,1,0:T(8,128)}, u32[]{:S(2)}, u32[]{:S(2)}) collective-permute-start(f32[2,512,128]{2,1,0:T(8,128)S(1)} %pad_maximum_fusion.3.refs_0_), channel_id=1, source_target_pairs={{0,4},{1,5},{2,6},{3,7},{4,8},{5,9},{6,10},{7,11},{8,12},{9,13},{1... | collective-permute-start | bytes 1572872 | tf_op jit(solution)/shard_map/ppermute | solution.py:295
  140.4 9.6 %collective-permute-start.22 = (f32[2,512,128]{2,1,0:T(8,128)S(1)}, f32[2,512,128]{2,1,0:T(8,128)}, u32[]{:S(2)}, u32[]{:S(2)}) collective-permute-start(f32[2,512,128]{2,1,0:T(8,128)S(1)} %pad_maximum_fusion.2.refs_1_), channel_id=1, source_target_pairs={{0,12},{1,13},{2,14},{3,15},{4,0},{5,1},{6,2},{7,3},{8,4},{9,5},{1... | collective-permute-start | bytes 1572872 | tf_op jit(solution)/shard_map/ppermute | solution.py:295
  143.3 11.6 %collective-permute-start.25 = (f32[2,512,128]{2,1,0:T(8,128)S(1)}, f32[2,512,128]{2,1,0:T(8,128)S(1)}, u32[]{:S(2)}, u32[]{:S(2)}) collective-permute-start(f32[2,512,128]{2,1,0:T(8,128)S(1)} %pad_maximum_fusion.3.refs_0_), channel_id=1, source_target_pairs={{0,12},{1,13},{2,14},{3,15},{4,0},{5,1},{6,2},{7,3},{8,4},{9,5},{1... | collective-permute-start | bytes 1572872 | tf_op jit(solution)/shard_map/ppermute | solution.py:295
  143.5 12.1 %collective-permute-start.26 = (f32[2,512,128]{2,1,0:T(8,128)S(1)}, f32[2,512,128]{2,1,0:T(8,128)S(1)}, u32[]{:S(2)}, u32[]{:S(2)}) collective-permute-start(f32[2,512,128]{2,1,0:T(8,128)S(1)} %pad_maximum_fusion.2.refs_1_), channel_id=1, source_target_pairs={{0,4},{1,5},{2,6},{3,7},{4,8},{5,9},{6,10},{7,11},{8,12},{9,13},{1... | collective-permute-start | bytes 1572872 | tf_op jit(solution)/shard_map/ppermute | solution.py:295
  150.1 11.1 %collective-permute-start.23 = (f32[2,512,128]{2,1,0:T(8,128)}, f32[2,512,128]{2,1,0:T(8,128)S(1)}, u32[]{:S(2)}, u32[]{:S(2)}) collective-permute-start(f32[2,512,128]{2,1,0:T(8,128)} %collective-permute-done.21.refs_3_), channel_id=1, source_target_pairs={{0,4},{1,5},{2,6},{3,7},{4,8},{5,9},{6,10},{7,11},{8,12},{9,13},{1... | collective-permute-start | bytes 1572872 | tf_op jit(solution)/shard_map/ppermute | solution.py:295
  150.1 11.1 %collective-permute-start.24 = (f32[2,512,128]{2,1,0:T(8,128)}, f32[2,512,128]{2,1,0:T(8,128)S(1)}, u32[]{:S(2)}, u32[]{:S(2)}) collective-permute-start(f32[2,512,128]{2,1,0:T(8,128)} %collective-permute-done.22.refs_2_), channel_id=1, source_target_pairs={{0,12},{1,13},{2,14},{3,15},{4,0},{5,1},{6,2},{7,3},{8,4},{9,5},{1... | collective-permute-start | bytes 1572872 | tf_op jit(solution)/shard_map/ppermute | solution.py:295
  163.9 7.0 %collective-permute-start.27 = (f32[256,1024]{1,0:T(8,128)S(1)}, f32[256,1024]{1,0:T(8,128)S(1)}, u32[]{:S(2)}, u32[]{:S(2)}) collective-permute-start(f32[256,1024]{1,0:T(8,128)S(1)} %slice.65), channel_id=1, source_target_pairs={{0,16},{1,17},{2,18},{3,19},{4,20},{5,21},{6,22},{7,23},{8,24},{9,... | collective-permute-start | bytes 3145736 | tf_op jit(solution)/shard_map/ppermute | solution.py:295
  (18 other events, 53.3 us)

commit v18 on v17

--- a/solution.py
+++ b/solution.py
@@ -296,32 +296,14 @@
 
 
 def deal(first, second, core, yh, xi):
-    solved = jnp.where(core == 0, first, second)
-    lower = yh == 0
-    here = jnp.where(lower, solved[:512], solved[512:])
-    there = jnp.where(core == 0, solved[512:], solved[:512])
+    here = jnp.where(core == 0, first[:512], second[512:])
+    there = jnp.where(core == 0, first[512:], second[:512])
     got = move(there, lambda a, b, c, d: (0, b, 3 - c, d) if a == 0 and b == c // 2 else None)
     mine = jnp.where(core == yh, here, got)
     one = move(mine, lambda a, b, c, d: (1 if b == 0 else 3, b, c, d) if a == 0 else None)
     two = move(mine, lambda a, b, c, d: (3 if b == 0 else 1, b, c, d) if a == 0 else None)
     far = move(one, lambda a, b, c, d: (2, b, c, d) if a == (1 if b == 0 else 3) else None)
     return jnp.where(xi == 0, mine, one + two + far)
-
-
-def ring(value, first):
-    def along(step):
-        def where(a, b, c, d):
-            on_z = (b == 0) == first
-            return (a, b, c, d + step) if on_z else (a, b, c + step, d)
-
-        return where
-
-    before = move(value, along(1))
-    after = move(value, along(-1))
-    cut = value.shape[0] // 2
-    far_low = move(before[:cut], along(1))
-    far_high = move(after[cut:], along(-1))
-    return after, far_low, far_high, before
 
 
 def gather(lead, half, by_rows, core, yl):
@@ -402,18 +384,20 @@
 
     info2 = jnp.stack([xi, core, 2 * yh + yl, z, col_id]).astype(jnp.int32)
 
-    after, far_low, far_high, before = ring(mine, True)
-    low = jnp.stack([mine, after])
-    high = jnp.stack([jnp.concatenate([far_low, far_high], 0), before])
-
-    left, _ = lax.optimization_barrier((left, high))
+    def first_step(step):
+        return lambda a, b, c, d: (a, b, c, d + step) if b == 0 else (a, b, c + step, d)
+
+    def second_step(step):
+        return lambda a, b, c, d: (a, b, c + step, d) if b == 0 else (a, b, c, d + step)
+
+    before, after = lax.optimization_barrier((move(mine, first_step(1)), move(mine, first_step(-1))))
+    far_low, far_high = move(before[:256], first_step(1)), move(after[256:], first_step(-1))
+    low = jnp.concatenate([mine, after], 0).reshape(2, 512, TILE)
+    low_before, low_after = move(low, second_step(1)), move(low, second_step(-1))
+    left, _ = lax.optimization_barrier((left, low))
     given = swap(lax.dynamic_slice_in_dim(left, 8 * (1 - core), 8, 0))
-
-    def along(step):
-        return lambda a, b, c, d: (a, b, c + step, d) if b == 0 else (a, b, c, d + step)
-
-    low_before, low_after = move(low, along(1)), move(low, along(-1))
-    high_after, high_before = move(high, along(-1)), move(high, along(1))
+    high = jnp.concatenate([far_low, far_high, before], 0).reshape(2, 512, TILE)
+    high_after, high_before = move(high, second_step(-1)), move(high, second_step(1))
     parts = prepare(info2[:2], left, given)
 
     def add(sums, pieces, places, name):
@@ -421,7 +405,7 @@
 
     sums = add(None, [low, high], [(0, 0), (0, 2)], "update_near")
     low_before, high_after, sums = lax.optimization_barrier((low_before, high_after, sums))
-    far_low, far_high = move(low_before, along(1)), move(high_after, along(-1))
+    far_low, far_high = move(low_before, second_step(1)), move(high_after, second_step(-1))
     sums = add(
         sums, [low_after, high_after, low_before, high_before], [(1, 0), (1, 2), (3, 0), (3, 2)], "update_next"
     )

time: 173 us -> 173 us (level)
  starting transfers between devices: 41 us -> 44.3 us
  waiting for transfers between devices: 98.5 us -> 95.8 us
    ppermute x28, waiting for transfers between devices: 93.1 us -> 89.7 us  [move(): return lax.ppermute(value, AXES, pairs)]
    ppermute x28, starting transfers between devices: 30.4 us -> 33.7 us  [move(): return lax.ppermute(value, AXES, pairs)]
    another operation x3 -> x0, other arithmetic: 2.89 us -> none  [the longest x2 1.91 us: shards(): high = jnp.stack([jnp.concatenate([far_low, far_high], 0), before])]
    unnamed x25 -> x21, local copies, waits for them, and re-layouts: 4.55 us -> 4.53 us
  transfers between devices with their start and end apart: 30 -> 30, of which waited for: 11 -> 9; matrix products, arithmetic and copies ran while one was open for 3% -> 4% of each run, Pallas kernels for 6% -> 6%
where the time goes in v18:
time: 173 us; the launch traced here: 172 us
  waiting for transfers between devices  95.8 us (55%)
  starting transfers between devices  44.3 us (26%)
  Pallas kernels  17.6 us (10%)
  local copies, waits for them, and re-layouts  9.57 us (6%)
  other arithmetic  3.94 us (2%)
    ppermute x28, waiting for transfers between devices, move(): return lax.ppermute(value, AXES, pairs)  89.7 us
    ppermute x28, starting transfers between devices, move(): return lax.ppermute(value, AXES, pairs)  33.7 us
    pallas_call x3, Pallas kernels, accumulate(): pl.pallas_call(body, out_shape=jax.ShapeDtypeStruct((512, 1024), F32), in...  10.1 us
    all_to_all x1, waiting for transfers between devices, shards(): lax.all_to_all(arrange_rhs(yh, rhs), ('yl', 'z'), 0, 0, tiled=True)  6.11 us
    all_to_all x1, starting transfers between devices, shards(): lax.all_to_all(arrange_rhs(yh, rhs), ('yl', 'z'), 0, 0, tiled=True)  6.05 us
    all_to_all x1, starting transfers between devices, shards(): left = lax.all_to_all(by_rows, COL, 0, 0, tiled=True)  4.63 us
    unnamed x21, local copies, waits for them, and re-layouts  4.53 us
  transfers between devices with their start and end apart: 30, of which 9 were waited for; matrix products, arithmetic and copies ran while one was open for 4% of the time, Pallas kernels for 6%

profile of v18, /device:TPU:5, one launch (start us, length us, event | category | flops | bytes accessed | tf_op | source)
XLA Modules:
  0.0 171.7 jit_solution(12436076757012334654)
XLA Ops:
  4.7 6.0 %all-to-all-start = ((f32[8,64,128]{2,1,0:T(8,128)}), f32[8,64,128]{2,1,0:T(8,128)S(1)}, u32[]{:S(2)}, u32[]{:S(2)}) async-start(f32[8,64,128]{2,1,0:T(8,128)} %arrange_rhs.1), calls=%async_computation | async-start | bytes 524288 | tf_op jit(solution)/shard_map/all_to_all | solution.py:366
  10.7 6.1 %all-to-all-done = f32[8,64,128]{2,1,0:T(8,128)S(1)} async-done(((f32[8,64,128]{2,1,0:T(8,128)}), f32[8,64,128]{2,1,0:T(8,128)S(1)}, u32[]{:S(2)}, u32[]{:S(2)}) %all-to-all-start) | async-done | bytes 262176 | tf_op jit(solution)/shard_map/all_to_all | solution.py:366
  23.3 1.4 collective-permute-start.8
  25.5 1.4 collective-permute-start.9
  28.9 1.9 %solve_first.1 = f32[1024,128]{1,0:T(8,128)} custom-call(s32[3]{0:T(128)S(1)} %pad_add_fusion.1.info, f32[1536,128]{1,0:T(8,128)S(1)} %pad_maximum_fusion.refs_0_.refs_2_, f32[1536,128]{1,0:T(8,128)S(1)} %collective-permute-done.5.refs_1_.refs_5_, f32[1536,128]{1,0:T(8,128)S(1)} %collective-permute-done.6.refs_2_.refs_4_, ...), custom_call_target="tpu_custom_call" | custom-call | tf_op jit(solution)/shard_map/solve_first/pallas_call | solution.py:107
  30.8 1.5 collective-permute-start.10
  34.6 1.9 %residual_or_pack.1 = (f32[1024,128]{1,0:T(8,128)}, bf16[112,1024,256]{2,1,0:T(8,128)(2,1)}) custom-call(s32[3]{0:T(128)S(1)} %pad_add_fusion.5.info, f32[1024,128]{1,0:T(8,128)S(1)} %invert_diagonal.1.refs_0_, f32[1024,128]{1,0:T(8,128)S(1)} %copy-done.7, f32[1536,128]{1,0:T(8,128)S(1)} %pad_maximum_fusion.refs_0_.refs_2_, f32[1536,128]{1,0:T(8,128)S(1)} %copy-done.5, ...), custom_call_target="tpu_custom_call" | custom-call | tf_op jit(solution)/shard_map/residual_or_pack/pallas_call | solution.py:144
  37.1 4.6 %all-to-all-start.1 = ((f32[16,256,128]{2,1,0:T(8,128)}), f32[16,256,128]{2,1,0:T(8,128)S(1)}, u32[]{:S(2)}, u32[]{:S(2)}) async-start(f32[16,256,128]{2,1,0:T(8,128)} %copy-done), calls=%async_computation.1 | async-start | bytes 4194304 | tf_op jit(solution)/shard_map/all_to_all | solution.py:375
  47.9 75.7 %collective-permute-done.15 = f32[512,128]{1,0:T(8,128)S(1)} collective-permute-done((f32[512,128]{1,0:T(8,128)S(1)}, f32[512,128]{1,0:T(8,128)S(1)}, u32[]{:S(2)}, u32[]{:S(2)}) %collective-permute-start.15) | collective-permute-done | bytes 262176 | tf_op jit(solution)/shard_map/ppermute | solution.py:295
  123.7 2.7 %collective-permute-start.17 = (f32[512,128]{1,0:T(8,128)S(1)}, f32[512,128]{1,0:T(8,128)S(1)}, u32[]{:S(2)}, u32[]{:S(2)}) collective-permute-start(f32[512,128]{1,0:T(8,128)S(1)} %add_select_fusion), channel_id=1, source_target_pairs={{0,3},{1,0},{2,1},{3,2},{4,7},{5,4},{6,5},{7,6},{8,11},{9,8},{10,9... | collective-permute-start | bytes 786440 | tf_op jit(solution)/shard_map/ppermute | solution.py:295
  126.4 4.1 %collective-permute-done.16 = f32[512,128]{1,0:T(8,128)S(1)} collective-permute-done((f32[512,128]{1,0:T(8,128)S(1)}, f32[512,128]{1,0:T(8,128)S(1)}, u32[]{:S(2)}, u32[]{:S(2)}) %collective-permute-start.16) | collective-permute-done | bytes 262176 | tf_op jit(solution)/shard_map/ppermute | solution.py:295
  132.4 2.9 %collective-permute-start.21 = (f32[256,128]{1,0:T(8,128)S(1)}, f32[256,128]{1,0:T(8,128)S(1)}, u32[]{:S(2)}, u32[]{:S(2)}) collective-permute-start(f32[256,128]{1,0:T(8,128)S(1)} %slice.60), channel_id=1, source_target_pairs={{0,3},{1,0},{2,1},{3,2},{4,7},{5,4},{6,5},{7,6},{8,11},{9,8},{10,9... | collective-permute-start | bytes 393224 | tf_op jit(solution)/shard_map/ppermute | solution.py:295
  136.7 2.0 %collective-permute-done.21 = f32[256,128]{1,0:T(8,128)S(1)} collective-permute-done((f32[256,128]{1,0:T(8,128)S(1)}, f32[256,128]{1,0:T(8,128)S(1)}, u32[]{:S(2)}, u32[]{:S(2)}) %collective-permute-start.21) | collective-permute-done | bytes 131104 | tf_op jit(solution)/shard_map/ppermute | solution.py:295
  138.8 2.5 %collective-permute-done.20 = f32[256,128]{1,0:T(8,128)S(1)} collective-permute-done((f32[256,128]{1,0:T(8,128)S(1)}, f32[256,128]{1,0:T(8,128)S(1)}, u32[]{:S(2)}, u32[]{:S(2)}) %collective-permute-start.20) | collective-permute-done | bytes 131104 | tf_op jit(solution)/shard_map/ppermute | solution.py:295
  141.3 3.3 %collective-permute-start.22 = (f32[2,512,128]{2,1,0:T(8,128)S(1)}, f32[2,512,128]{2,1,0:T(8,128)}, u32[]{:S(2)}, u32[]{:S(2)}) collective-permute-start(f32[2,512,128]{2,1,0:T(8,128)S(1)} %bitcast.31), channel_id=1, source_target_pairs={{0,12},{1,13},{2,14},{3,15},{4,0},{5,1},{6,2},{7,3},{8,4},{9,5},{1... | collective-permute-start | bytes 1572872 | tf_op jit(solution)/shard_map/ppermute | solution.py:295
  146.4 1.6 prepare_update.1
  148.0 2.5 %update_near.1.refs_0_ = f32[512,1024]{1,0:T(8,128)S(1)} custom-call(s32[5]{0:T(128)S(1)} %stack.63.info, bf16[4,512,256]{2,1,0:T(8,128)(2,1)S(1)} %get-tuple-element.40.high_ref, bf16[4,512,256]{2,1,0:T(8,128)(2,1)S(1)} %get-tuple-element.41.low_ref, f32[2,512,128]{2,1,0:T(8,128)S(1)} %bitcast.30, f32[2,512,128]{2,1,0:T(8,128)S(1)} %bitcast.33), custom_call_target="tpu_custom_call" | custom-call | tf_op jit(solution)/shard_map/update_near/pallas_call | solution.py:271
  150.7 1.4 collective-permute-start.23
  152.1 2.1 %collective-permute-start.24 = (f32[2,512,128]{2,1,0:T(8,128)}, f32[2,512,128]{2,1,0:T(8,128)S(1)}, u32[]{:S(2)}, u32[]{:S(2)}) collective-permute-start(f32[2,512,128]{2,1,0:T(8,128)} %collective-permute-done.22.refs_2_), channel_id=1, source_target_pairs={{0,12},{1,13},{2,14},{3,15},{4,0},{5,1},{6,2},{7,3},{8,4},{9,5},{1... | collective-permute-start | bytes 1572872 | tf_op jit(solution)/shard_map/ppermute | solution.py:295
  154.2 2.2 %collective-permute-done.25.refs_1_ = f32[2,512,128]{2,1,0:T(8,128)S(1)} collective-permute-done((f32[2,512,128]{2,1,0:T(8,128)S(1)}, f32[2,512,128]{2,1,0:T(8,128)S(1)}, u32[]{:S(2)}, u32[]{:S(2)}) %collective-permute-start.25) | collective-permute-done | bytes 524320 | tf_op jit(solution)/shard_map/ppermute | solution.py:295
  156.4 5.1 %update_next.1.refs_0_ = f32[512,1024]{1,0:T(8,128)S(1)} custom-call(s32[5]{0:T(128)S(1)} %stack.63.info, bf16[4,512,256]{2,1,0:T(8,128)(2,1)S(1)} %get-tuple-element.40.high_ref, bf16[4,512,256]{2,1,0:T(8,128)(2,1)S(1)} %get-tuple-element.41.low_ref, f32[512,1024]{1,0:T(8,128)S(1)} %update_near.1.refs_0_, ...), custom_call_target="tpu_custom_call", output_to_operand_aliasing={{}: (3, {})} | custom-call | tf_op jit(solution)/shard_map/update_next/pallas_call | solution.py:271
  162.1 2.6 %update_far.1 = f32[512,1024]{1,0:T(8,128)S(1)} custom-call(s32[5]{0:T(128)S(1)} %stack.63.info, bf16[4,512,256]{2,1,0:T(8,128)(2,1)S(1)} %get-tuple-element.40.high_ref, bf16[4,512,256]{2,1,0:T(8,128)(2,1)S(1)} %get-tuple-element.41.low_ref, f32[512,1024]{1,0:T(8,128)S(1)} %update_next.1.refs_0_, ...), custom_call_target="tpu_custom_call", output_to_operand_aliasing={{}: (3, {})} | custom-call | tf_op jit(solution)/shard_map/update_far/pallas_call | solution.py:271
  164.8 3.4 %collective-permute-start.27 = (f32[256,1024]{1,0:T(8,128)S(1)}, f32[256,1024]{1,0:T(8,128)S(1)}, u32[]{:S(2)}, u32[]{:S(2)}) collective-permute-start(f32[256,1024]{1,0:T(8,128)S(1)} %slice.71), channel_id=1, source_target_pairs={{0,16},{1,17},{2,18},{3,19},{4,20},{5,21},{6,22},{7,23},{8,24},{9,... | collective-permute-start | bytes 3145736 | tf_op jit(solution)/shard_map/ppermute | solution.py:295
  168.2 2.3 %collective-permute-done.27 = f32[256,1024]{1,0:T(8,128)S(1)} collective-permute-done((f32[256,1024]{1,0:T(8,128)S(1)}, f32[256,1024]{1,0:T(8,128)S(1)}, u32[]{:S(2)}, u32[]{:S(2)}) %collective-permute-start.27) | collective-permute-done | bytes 1048608 | tf_op jit(solution)/shard_map/ppermute | solution.py:295
  (94 shorter events, 30.2 us)
Async XLA Ops:
  1.8 15.0 %collective-permute-start = (f32[1024,128]{1,0:T(8,128)S(1)}, f32[1024,128]{1,0:T(8,128)S(1)}, u32[]{:S(2)}, u32[]{:S(2)}) collective-permute-start(f32[1024,128]{1,0:T(8,128)S(1)} %invert_diagonal.1.refs_0_), channel_id=1, source_target_pairs={{0,4},{1,5},{2,6},{3,7},{4,0},{5,1},{6,2},{7,3},{16,17},{17,18},{1... | collective-permute-start | bytes 1572872 | tf_op jit(solution)/shard_map/ppermute | solution.py:295
  2.5 14.3 %collective-permute-start.1 = (f32[1024,128]{1,0:T(8,128)S(1)}, f32[1024,128]{1,0:T(8,128)S(1)}, u32[]{:S(2)}, u32[]{:S(2)}) collective-permute-start(f32[1024,128]{1,0:T(8,128)S(1)} %invert_diagonal.1.refs_0_), channel_id=1, source_target_pairs={{16,20},{17,21},{18,22},{19,23},{20,16},{21,17},{22,18},{23,19},{2... | collective-permute-start | bytes 1572872 | tf_op jit(solution)/shard_map/ppermute | solution.py:295
  3.2 13.6 %collective-permute-start.3 = (f32[1024,128]{1,0:T(8,128)S(1)}, f32[1024,128]{1,0:T(8,128)S(1)}, u32[]{:S(2)}, u32[]{:S(2)}) collective-permute-start(f32[1024,128]{1,0:T(8,128)S(1)} %invert_diagonal.1.refs_0_), channel_id=1, source_target_pairs={{16,19},{17,16},{18,17},{19,18},{20,23},{21,20},{22,21},{23,22},{2... | collective-permute-start | bytes 1572872 | tf_op jit(solution)/shard_map/ppermute | solution.py:295
  4.7 12.2 %all-to-all-start = ((f32[8,64,128]{2,1,0:T(8,128)}), f32[8,64,128]{2,1,0:T(8,128)S(1)}, u32[]{:S(2)}, u32[]{:S(2)}) async-start(f32[8,64,128]{2,1,0:T(8,128)} %arrange_rhs.1), calls=%async_computation | async-start | bytes 524288 | tf_op jit(solution)/shard_map/all_to_all | solution.py:366
  18.6 3.9 %collective-permute-start.6 = (f32[1536,128]{1,0:T(8,128)S(1)}, f32[1536,128]{1,0:T(8,128)S(1)}, u32[]{:S(2)}, u32[]{:S(2)}) collective-permute-start(f32[1536,128]{1,0:T(8,128)S(1)} %pad_maximum_fusion.refs_0_.refs_2_), channel_id=1, source_target_pairs={{0,1},{1,2},{2,3},{3,0},{4,5},{5,6},{6,7},{7,4},{16,20},{17,21},{1... | collective-permute-start | bytes 2359304 | tf_op jit(solution)/shard_map/ppermute | solution.py:295
  19.5 5.2 %collective-permute-start.5 = (f32[1536,128]{1,0:T(8,128)S(1)}, f32[1536,128]{1,0:T(8,128)S(1)}, u32[]{:S(2)}, u32[]{:S(2)}) collective-permute-start(f32[1536,128]{1,0:T(8,128)S(1)} %pad_maximum_fusion.1.refs_3_), channel_id=1, source_target_pairs={{0,3},{1,0},{2,1},{3,2},{4,7},{5,4},{6,5},{7,6},{16,20},{17,21},{1... | collective-permute-start | bytes 2359304 | tf_op jit(solution)/shard_map/ppermute | solution.py:295
  20.2 2.2 %collective-permute-start.7 = (f32[512,128]{1,0:T(8,128)S(1)}, f32[512,128]{1,0:T(8,128)S(1)}, u32[]{:S(2)}, u32[]{:S(2)}) collective-permute-start(f32[512,128]{1,0:T(8,128)S(1)} %bitcast.34), channel_id=1, source_target_pairs={{8,4},{9,5},{10,6},{11,7},{12,0},{13,1},{14,2},{15,3},{24,20},{25,... | collective-permute-start | bytes 786440 | tf_op jit(solution)/shard_map/ppermute | solution.py:295
  23.3 5.6 %collective-permute-start.8 = (f32[768,128]{1,0:T(8,128)}, f32[768,128]{1,0:T(8,128)}, u32[]{:S(2)}, u32[]{:S(2)}) collective-permute-start(f32[768,128]{1,0:T(8,128)} %slice.53), channel_id=1, source_target_pairs={{0,1},{1,2},{2,3},{3,0},{4,5},{5,6},{6,7},{7,4}} | collective-permute-start | bytes 1179656 | tf_op jit(solution)/shard_map/ppermute | solution.py:295
  25.5 3.4 %collective-permute-start.9 = (f32[768,128]{1,0:T(8,128)}, f32[768,128]{1,0:T(8,128)}, u32[]{:S(2)}, u32[]{:S(2)}) collective-permute-start(f32[768,128]{1,0:T(8,128)} %slice.65), channel_id=1, source_target_pairs={{0,3},{1,0},{2,1},{3,2},{4,7},{5,4},{6,5},{7,6}} | collective-permute-start | bytes 1179656 | tf_op jit(solution)/shard_map/ppermute | solution.py:295
  36.4 5.4 %collective-permute-start.11 = (f32[1024,128]{1,0:T(8,128)}, f32[1024,128]{1,0:T(8,128)S(1)}, u32[]{:S(2)}, u32[]{:S(2)}) collective-permute-start(f32[1024,128]{1,0:T(8,128)} %get-tuple-element.33), channel_id=1, source_target_pairs={{16,28},{17,29},{18,30},{19,31},{20,24},{21,25},{22,26},{23,27}} | collective-permute-start | bytes 1572872 | tf_op jit(solution)/shard_map/ppermute | solution.py:295
  37.1 86.5 %all-to-all-start.1 = ((f32[16,256,128]{2,1,0:T(8,128)}), f32[16,256,128]{2,1,0:T(8,128)S(1)}, u32[]{:S(2)}, u32[]{:S(2)}) async-start(f32[16,256,128]{2,1,0:T(8,128)} %copy-done), calls=%async_computation.1 | async-start | bytes 4194304 | tf_op jit(solution)/shard_map/all_to_all | solution.py:375
  46.6 77.0 %collective-permute-start.15 = (f32[512,128]{1,0:T(8,128)S(1)}, f32[512,128]{1,0:T(8,128)S(1)}, u32[]{:S(2)}, u32[]{:S(2)}) collective-permute-start(f32[512,128]{1,0:T(8,128)S(1)} %collective-permute-done.13), channel_id=1, source_target_pairs={{32,64},{33,65},{34,66},{35,67},{36,68},{37,69},{38,70},{39,71},{4... | collective-permute-start | bytes 786440 | tf_op jit(solution)/shard_map/ppermute | solution.py:295
  123.6 6.8 %collective-permute-start.16 = (f32[512,128]{1,0:T(8,128)S(1)}, f32[512,128]{1,0:T(8,128)S(1)}, u32[]{:S(2)}, u32[]{:S(2)}) collective-permute-start(f32[512,128]{1,0:T(8,128)S(1)} %add_select_fusion), channel_id=1, source_target_pairs={{0,1},{1,2},{2,3},{3,0},{4,5},{5,6},{6,7},{7,4},{8,9},{9,10},{10,1... | collective-permute-start | bytes 786440 | tf_op jit(solution)/shard_map/ppermute | solution.py:295
  123.7 6.7 %collective-permute-start.17 = (f32[512,128]{1,0:T(8,128)S(1)}, f32[512,128]{1,0:T(8,128)S(1)}, u32[]{:S(2)}, u32[]{:S(2)}) collective-permute-start(f32[512,128]{1,0:T(8,128)S(1)} %add_select_fusion), channel_id=1, source_target_pairs={{0,3},{1,0},{2,1},{3,2},{4,7},{5,4},{6,5},{7,6},{8,11},{9,8},{10,9... | collective-permute-start | bytes 786440 | tf_op jit(solution)/shard_map/ppermute | solution.py:295
  131.5 14.9 %collective-permute-start.18 = (f32[8,256,128]{2,1,0:T(8,128)}, f32[8,256,128]{2,1,0:T(8,128)}, u32[]{:S(2)}, u32[]{:S(2)}) collective-permute-start(f32[8,256,128]{2,1,0:T(8,128)} %constant_dynamic-slice_fusion), channel_id=1, source_target_pairs={{0,16},{1,17},{2,18},{3,19},{4,20},{5,21},{6,22},{7,23},{8,24},{9,... | collective-permute-start | bytes 3145736 | tf_op jit(solution)/shard_map/ppermute | solution.py:295
  132.4 6.4 %collective-permute-start.21 = (f32[256,128]{1,0:T(8,128)S(1)}, f32[256,128]{1,0:T(8,128)S(1)}, u32[]{:S(2)}, u32[]{:S(2)}) collective-permute-start(f32[256,128]{1,0:T(8,128)S(1)} %slice.60), channel_id=1, source_target_pairs={{0,3},{1,0},{2,1},{3,2},{4,7},{5,4},{6,5},{7,6},{8,11},{9,8},{10,9... | collective-permute-start | bytes 393224 | tf_op jit(solution)/shard_map/ppermute | solution.py:295
  135.3 6.0 %collective-permute-start.20 = (f32[256,128]{1,0:T(8,128)S(1)}, f32[256,128]{1,0:T(8,128)S(1)}, u32[]{:S(2)}, u32[]{:S(2)}) collective-permute-start(f32[256,128]{1,0:T(8,128)S(1)} %slice.59), channel_id=1, source_target_pairs={{0,1},{1,2},{2,3},{3,0},{4,5},{5,6},{6,7},{7,4},{8,9},{9,10},{10,1... | collective-permute-start | bytes 393224 | tf_op jit(solution)/shard_map/ppermute | solution.py:295
  136.5 14.0 %collective-permute-start.19 = (f32[2,512,128]{2,1,0:T(8,128)S(1)}, f32[2,512,128]{2,1,0:T(8,128)}, u32[]{:S(2)}, u32[]{:S(2)}) collective-permute-start(f32[2,512,128]{2,1,0:T(8,128)S(1)} %bitcast.28), channel_id=1, source_target_pairs={{0,4},{1,5},{2,6},{3,7},{4,8},{5,9},{6,10},{7,11},{8,12},{9,13},{1... | collective-permute-start | bytes 1572872 | tf_op jit(solution)/shard_map/ppermute | solution.py:295
  141.3 9.4 %collective-permute-start.22 = (f32[2,512,128]{2,1,0:T(8,128)S(1)}, f32[2,512,128]{2,1,0:T(8,128)}, u32[]{:S(2)}, u32[]{:S(2)}) collective-permute-start(f32[2,512,128]{2,1,0:T(8,128)S(1)} %bitcast.31), channel_id=1, source_target_pairs={{0,12},{1,13},{2,14},{3,15},{4,0},{5,1},{6,2},{7,3},{8,4},{9,5},{1... | collective-permute-start | bytes 1572872 | tf_op jit(solution)/shard_map/ppermute | solution.py:295
  144.8 11.6 %collective-permute-start.25 = (f32[2,512,128]{2,1,0:T(8,128)S(1)}, f32[2,512,128]{2,1,0:T(8,128)S(1)}, u32[]{:S(2)}, u32[]{:S(2)}) collective-permute-start(f32[2,512,128]{2,1,0:T(8,128)S(1)} %bitcast.29), channel_id=1, source_target_pairs={{0,12},{1,13},{2,14},{3,15},{4,0},{5,1},{6,2},{7,3},{8,4},{9,5},{1... | collective-permute-start | bytes 1572872 | tf_op jit(solution)/shard_map/ppermute | solution.py:295
  146.1 10.3 %collective-permute-start.26 = (f32[2,512,128]{2,1,0:T(8,128)S(1)}, f32[2,512,128]{2,1,0:T(8,128)S(1)}, u32[]{:S(2)}, u32[]{:S(2)}) collective-permute-start(f32[2,512,128]{2,1,0:T(8,128)S(1)} %bitcast.32), channel_id=1, source_target_pairs={{0,4},{1,5},{2,6},{3,7},{4,8},{5,9},{6,10},{7,11},{8,12},{9,13},{1... | collective-permute-start | bytes 1572872 | tf_op jit(solution)/shard_map/ppermute | solution.py:295
  150.7 10.7 %collective-permute-start.23 = (f32[2,512,128]{2,1,0:T(8,128)}, f32[2,512,128]{2,1,0:T(8,128)S(1)}, u32[]{:S(2)}, u32[]{:S(2)}) collective-permute-start(f32[2,512,128]{2,1,0:T(8,128)} %collective-permute-done.19.refs_3_), channel_id=1, source_target_pairs={{0,4},{1,5},{2,6},{3,7},{4,8},{5,9},{6,10},{7,11},{8,12},{9,13},{1... | collective-permute-start | bytes 1572872 | tf_op jit(solution)/shard_map/ppermute | solution.py:295
  152.1 10.0 %collective-permute-start.24 = (f32[2,512,128]{2,1,0:T(8,128)}, f32[2,512,128]{2,1,0:T(8,128)S(1)}, u32[]{:S(2)}, u32[]{:S(2)}) collective-permute-start(f32[2,512,128]{2,1,0:T(8,128)} %collective-permute-done.22.refs_2_), channel_id=1, source_target_pairs={{0,12},{1,13},{2,14},{3,15},{4,0},{5,1},{6,2},{7,3},{8,4},{9,5},{1... | collective-permute-start | bytes 1572872 | tf_op jit(solution)/shard_map/ppermute | solution.py:295
  164.8 5.7 %collective-permute-start.27 = (f32[256,1024]{1,0:T(8,128)S(1)}, f32[256,1024]{1,0:T(8,128)S(1)}, u32[]{:S(2)}, u32[]{:S(2)}) collective-permute-start(f32[256,1024]{1,0:T(8,128)S(1)} %slice.71), channel_id=1, source_target_pairs={{0,16},{1,17},{2,18},{3,19},{4,20},{5,21},{6,22},{7,23},{8,24},{9,... | collective-permute-start | bytes 3145736 | tf_op jit(solution)/shard_map/ppermute | solution.py:295
  (16 other events, 34.8 us)

commit v19 on v18

--- a/solution.py
+++ b/solution.py
@@ -295,15 +295,17 @@
     return lax.ppermute(value, AXES, pairs)
 
 
-def deal(first, second, core, yh, xi):
+def deal(first, second, core, yh, xi, by_rows):
     here = jnp.where(core == 0, first[:512], second[512:])
     there = jnp.where(core == 0, first[512:], second[:512])
     got = move(there, lambda a, b, c, d: (0, b, 3 - c, d) if a == 0 and b == c // 2 else None)
+    got, by_rows = lax.optimization_barrier((got, by_rows))
+    left = lax.all_to_all(by_rows, COL, 0, 0, tiled=True)
     mine = jnp.where(core == yh, here, got)
     one = move(mine, lambda a, b, c, d: (1 if b == 0 else 3, b, c, d) if a == 0 else None)
     two = move(mine, lambda a, b, c, d: (3 if b == 0 else 1, b, c, d) if a == 0 else None)
     far = move(one, lambda a, b, c, d: (2, b, c, d) if a == (1 if b == 0 else 3) else None)
-    return jnp.where(xi == 0, mine, one + two + far)
+    return jnp.where(xi == 0, mine, one + two + far), left
 
 
 def gather(lead, half, by_rows, core, yl):
@@ -371,13 +373,10 @@
 
     first = solve_first(place((core == 0) & (yh == 0)), *upper_left, columns)
     sent = move(first, lambda a, b, c, d: (0, 1, c, d) if (a, b) == (0, 0) and c < 2 else None)
-    by_rows, _ = lax.optimization_barrier((by_rows, first))
-    left = lax.all_to_all(by_rows, COL, 0, 0, tiled=True)
     rest, tri = residual_or_pack(place(core * (1 + yh)), *lower_row, columns, sent)
     second_rhs = move(rest, lambda a, b, c, d: (0, 1, 3 - c, d) if (a, b) == (0, 1) and c < 2 else None)
     second = solve_second(place((core == 1) & (yh == 1)), tri, second_rhs)
-    mine = deal(first, second, core, yh, xi)
-    mine, left = lax.optimization_barrier((mine, left))
+    mine, left = deal(first, second, core, yh, xi, by_rows)
 
     def swap(value):
         return move(value, lambda a, b, c, d: (a, 1 - b, c, d))
@@ -394,9 +393,9 @@
     far_low, far_high = move(before[:256], first_step(1)), move(after[256:], first_step(-1))
     low = jnp.concatenate([mine, after], 0).reshape(2, 512, TILE)
     low_before, low_after = move(low, second_step(1)), move(low, second_step(-1))
-    left, _ = lax.optimization_barrier((left, low))
+    high = jnp.concatenate([far_low, far_high, before], 0).reshape(2, 512, TILE)
+    left, _ = lax.optimization_barrier((left, high))
     given = swap(lax.dynamic_slice_in_dim(left, 8 * (1 - core), 8, 0))
-    high = jnp.concatenate([far_low, far_high, before], 0).reshape(2, 512, TILE)
     high_after, high_before = move(high, second_step(-1)), move(high, second_step(1))
     parts = prepare(info2[:2], left, given)
 

time: 173 us -> 171 us (0.988)
  starting transfers between devices: 44.3 us -> 38.7 us
  waiting for transfers between devices: 95.8 us -> 99.3 us
    ppermute x28, starting transfers between devices: 33.7 us -> 28 us  [move(): return lax.ppermute(value, AXES, pairs)]
    ppermute x28, waiting for transfers between devices: 89.7 us -> 93.2 us  [move(): return lax.ppermute(value, AXES, pairs)]
    unnamed x21 -> x25, local copies, waits for them, and re-layouts: 4.53 us -> 4.55 us
  transfers between devices with their start and end apart: 30 -> 30, of which waited for: 9 -> 9; matrix products, arithmetic and copies ran while one was open for 4% -> 3% of each run, Pallas kernels for 6% -> 6%
where the time goes in v19:
time: 171 us; the launch traced here: 169 us
  waiting for transfers between devices  99.3 us (58%)
  starting transfers between devices  38.7 us (23%)
  Pallas kernels  17.5 us (10%)
  local copies, waits for them, and re-layouts  9.57 us (6%)
  other arithmetic  3.93 us (2%)
    ppermute x28, waiting for transfers between devices, move(): return lax.ppermute(value, AXES, pairs)  93.2 us
    ppermute x28, starting transfers between devices, move(): return lax.ppermute(value, AXES, pairs)  28 us
    pallas_call x3, Pallas kernels, accumulate(): pl.pallas_call(body, out_shape=jax.ShapeDtypeStruct((512, 1024), F32), in...  10.1 us
    all_to_all x1, waiting for transfers between devices, shards(): lax.all_to_all(arrange_rhs(yh, rhs), ('yl', 'z'), 0, 0, tiled=True)  6.11 us
    all_to_all x1, starting transfers between devices, shards(): lax.all_to_all(arrange_rhs(yh, rhs), ('yl', 'z'), 0, 0, tiled=True)  6.05 us
    all_to_all x1, starting transfers between devices, deal(): left = lax.all_to_all(by_rows, COL, 0, 0, tiled=True)  4.63 us
    unnamed x25, local copies, waits for them, and re-layouts  4.55 us
  transfers between devices with their start and end apart: 30, of which 9 were waited for; matrix products, arithmetic and copies ran while one was open for 3% of the time, Pallas kernels for 6%

profile of v19, /device:TPU:5, one launch (start us, length us, event | category | flops | bytes accessed | tf_op | source)
XLA Modules:
  0.0 169.5 jit_solution(14337871807440154653)
XLA Ops:
  4.7 6.0 %all-to-all-start = ((f32[8,64,128]{2,1,0:T(8,128)}), f32[8,64,128]{2,1,0:T(8,128)S(1)}, u32[]{:S(2)}, u32[]{:S(2)}) async-start(f32[8,64,128]{2,1,0:T(8,128)} %arrange_rhs.1), calls=%async_computation | async-start | bytes 524288 | tf_op jit(solution)/shard_map/all_to_all | solution.py:368
  10.7 6.1 %all-to-all-done = f32[8,64,128]{2,1,0:T(8,128)S(1)} async-done(((f32[8,64,128]{2,1,0:T(8,128)}), f32[8,64,128]{2,1,0:T(8,128)S(1)}, u32[]{:S(2)}, u32[]{:S(2)}) %all-to-all-start) | async-done | bytes 262176 | tf_op jit(solution)/shard_map/all_to_all | solution.py:368
  23.3 1.4 collective-permute-start.8
  25.4 1.4 collective-permute-start.9
  28.9 1.9 %solve_first.1 = f32[1024,128]{1,0:T(8,128)} custom-call(s32[3]{0:T(128)S(1)} %pad_add_fusion.1.info, f32[1536,128]{1,0:T(8,128)S(1)} %pad_maximum_fusion.refs_0_.refs_2_, f32[1536,128]{1,0:T(8,128)S(1)} %collective-permute-done.5.refs_1_.refs_5_, f32[1536,128]{1,0:T(8,128)S(1)} %collective-permute-done.6.refs_2_.refs_4_, ...), custom_call_target="tpu_custom_call" | custom-call | tf_op jit(solution)/shard_map/solve_first/pallas_call | solution.py:107
  30.8 1.5 collective-permute-start.10
  34.6 1.9 %residual_or_pack.1 = (f32[1024,128]{1,0:T(8,128)}, bf16[112,1024,256]{2,1,0:T(8,128)(2,1)}) custom-call(s32[3]{0:T(128)S(1)} %pad_add_fusion.5.info, f32[1024,128]{1,0:T(8,128)S(1)} %invert_diagonal.1.refs_0_, f32[1024,128]{1,0:T(8,128)S(1)} %copy-done.7, f32[1536,128]{1,0:T(8,128)S(1)} %pad_maximum_fusion.refs_0_.refs_2_, f32[1536,128]{1,0:T(8,128)S(1)} %copy-done.5, ...), custom_call_target="tpu_custom_call" | custom-call | tf_op jit(solution)/shard_map/residual_or_pack/pallas_call | solution.py:144
  39.6 4.6 %all-to-all-start.1 = ((f32[16,256,128]{2,1,0:T(8,128)}), f32[16,256,128]{2,1,0:T(8,128)S(1)}, u32[]{:S(2)}, u32[]{:S(2)}) async-start(f32[16,256,128]{2,1,0:T(8,128)} %copy-done), calls=%async_computation.1 | async-start | bytes 4194304 | tf_op jit(solution)/shard_map/all_to_all | solution.py:303
  47.9 77.5 %collective-permute-done.15 = f32[512,128]{1,0:T(8,128)S(1)} collective-permute-done((f32[512,128]{1,0:T(8,128)S(1)}, f32[512,128]{1,0:T(8,128)S(1)}, u32[]{:S(2)}, u32[]{:S(2)}) %collective-permute-start.15) | collective-permute-done | bytes 262176 | tf_op jit(solution)/shard_map/ppermute | solution.py:295
  126.8 1.4 collective-permute-start.17
  128.2 3.8 %collective-permute-done.16 = f32[512,128]{1,0:T(8,128)S(1)} collective-permute-done((f32[512,128]{1,0:T(8,128)S(1)}, f32[512,128]{1,0:T(8,128)S(1)}, u32[]{:S(2)}, u32[]{:S(2)}) %collective-permute-start.16) | collective-permute-done | bytes 262176 | tf_op jit(solution)/shard_map/ppermute | solution.py:295
  132.1 2.7 %collective-permute-start.19 = (f32[256,128]{1,0:T(8,128)S(1)}, f32[256,128]{1,0:T(8,128)S(1)}, u32[]{:S(2)}, u32[]{:S(2)}) collective-permute-start(f32[256,128]{1,0:T(8,128)S(1)} %slice.60), channel_id=1, source_target_pairs={{0,3},{1,0},{2,1},{3,2},{4,7},{5,4},{6,5},{7,6},{8,11},{9,8},{10,9... | collective-permute-start | bytes 393224 | tf_op jit(solution)/shard_map/ppermute | solution.py:295
  134.9 1.8 %collective-permute-done.19 = f32[256,128]{1,0:T(8,128)S(1)} collective-permute-done((f32[256,128]{1,0:T(8,128)S(1)}, f32[256,128]{1,0:T(8,128)S(1)}, u32[]{:S(2)}, u32[]{:S(2)}) %collective-permute-start.19) | collective-permute-done | bytes 131104 | tf_op jit(solution)/shard_map/ppermute | solution.py:295
  136.7 3.2 %collective-permute-done.18 = f32[256,128]{1,0:T(8,128)S(1)} collective-permute-done((f32[256,128]{1,0:T(8,128)S(1)}, f32[256,128]{1,0:T(8,128)S(1)}, u32[]{:S(2)}, u32[]{:S(2)}) %collective-permute-start.18) | collective-permute-done | bytes 131104 | tf_op jit(solution)/shard_map/ppermute | solution.py:295
  142.3 1.4 collective-permute-start.22
  143.9 1.4 collective-permute-start.25
  145.6 1.6 prepare_update.1
  147.1 2.5 %update_near.1.refs_0_ = f32[512,1024]{1,0:T(8,128)S(1)} custom-call(s32[5]{0:T(128)S(1)} %stack.63.info, bf16[4,512,256]{2,1,0:T(8,128)(2,1)S(1)} %get-tuple-element.39.high_ref, bf16[4,512,256]{2,1,0:T(8,128)(2,1)S(1)} %get-tuple-element.40.low_ref, f32[2,512,128]{2,1,0:T(8,128)S(1)} %bitcast.33, f32[2,512,128]{2,1,0:T(8,128)S(1)} %bitcast.30), custom_call_target="tpu_custom_call" | custom-call | tf_op jit(solution)/shard_map/update_near/pallas_call | solution.py:271
  152.0 1.5 collective-permute-start.24
  153.4 2.8 %collective-permute-done.25.refs_1_ = f32[2,512,128]{2,1,0:T(8,128)S(1)} collective-permute-done((f32[2,512,128]{2,1,0:T(8,128)S(1)}, f32[2,512,128]{2,1,0:T(8,128)S(1)}, u32[]{:S(2)}, u32[]{:S(2)}) %collective-permute-start.25) | collective-permute-done | bytes 524320 | tf_op jit(solution)/shard_map/ppermute | solution.py:295
  156.3 5.1 %update_next.1.refs_0_ = f32[512,1024]{1,0:T(8,128)S(1)} custom-call(s32[5]{0:T(128)S(1)} %stack.63.info, bf16[4,512,256]{2,1,0:T(8,128)(2,1)S(1)} %get-tuple-element.39.high_ref, bf16[4,512,256]{2,1,0:T(8,128)(2,1)S(1)} %get-tuple-element.40.low_ref, f32[512,1024]{1,0:T(8,128)S(1)} %update_near.1.refs_0_, ...), custom_call_target="tpu_custom_call", output_to_operand_aliasing={{}: (3, {})} | custom-call | tf_op jit(solution)/shard_map/update_next/pallas_call | solution.py:271
  161.9 2.6 %update_far.1 = f32[512,1024]{1,0:T(8,128)S(1)} custom-call(s32[5]{0:T(128)S(1)} %stack.63.info, bf16[4,512,256]{2,1,0:T(8,128)(2,1)S(1)} %get-tuple-element.39.high_ref, bf16[4,512,256]{2,1,0:T(8,128)(2,1)S(1)} %get-tuple-element.40.low_ref, f32[512,1024]{1,0:T(8,128)S(1)} %update_next.1.refs_0_, ...), custom_call_target="tpu_custom_call", output_to_operand_aliasing={{}: (3, {})} | custom-call | tf_op jit(solution)/shard_map/update_far/pallas_call | solution.py:271
  164.6 1.4 collective-permute-start.27
  166.0 2.3 %collective-permute-done.27 = f32[256,1024]{1,0:T(8,128)S(1)} collective-permute-done((f32[256,1024]{1,0:T(8,128)S(1)}, f32[256,1024]{1,0:T(8,128)S(1)}, u32[]{:S(2)}, u32[]{:S(2)}) %collective-permute-start.27) | collective-permute-done | bytes 1048608 | tf_op jit(solution)/shard_map/ppermute | solution.py:295
  (98 shorter events, 31.1 us)
Async XLA Ops:
  1.8 15.0 %collective-permute-start = (f32[1024,128]{1,0:T(8,128)S(1)}, f32[1024,128]{1,0:T(8,128)S(1)}, u32[]{:S(2)}, u32[]{:S(2)}) collective-permute-start(f32[1024,128]{1,0:T(8,128)S(1)} %invert_diagonal.1.refs_0_), channel_id=1, source_target_pairs={{0,4},{1,5},{2,6},{3,7},{4,0},{5,1},{6,2},{7,3},{16,17},{17,18},{1... | collective-permute-start | bytes 1572872 | tf_op jit(solution)/shard_map/ppermute | solution.py:295
  2.5 14.3 %collective-permute-start.1 = (f32[1024,128]{1,0:T(8,128)S(1)}, f32[1024,128]{1,0:T(8,128)S(1)}, u32[]{:S(2)}, u32[]{:S(2)}) collective-permute-start(f32[1024,128]{1,0:T(8,128)S(1)} %invert_diagonal.1.refs_0_), channel_id=1, source_target_pairs={{16,20},{17,21},{18,22},{19,23},{20,16},{21,17},{22,18},{23,19},{2... | collective-permute-start | bytes 1572872 | tf_op jit(solution)/shard_map/ppermute | solution.py:295
  3.2 13.6 %collective-permute-start.3 = (f32[1024,128]{1,0:T(8,128)S(1)}, f32[1024,128]{1,0:T(8,128)S(1)}, u32[]{:S(2)}, u32[]{:S(2)}) collective-permute-start(f32[1024,128]{1,0:T(8,128)S(1)} %invert_diagonal.1.refs_0_), channel_id=1, source_target_pairs={{16,19},{17,16},{18,17},{19,18},{20,23},{21,20},{22,21},{23,22},{2... | collective-permute-start | bytes 1572872 | tf_op jit(solution)/shard_map/ppermute | solution.py:295
  4.7 12.2 %all-to-all-start = ((f32[8,64,128]{2,1,0:T(8,128)}), f32[8,64,128]{2,1,0:T(8,128)S(1)}, u32[]{:S(2)}, u32[]{:S(2)}) async-start(f32[8,64,128]{2,1,0:T(8,128)} %arrange_rhs.1), calls=%async_computation | async-start | bytes 524288 | tf_op jit(solution)/shard_map/all_to_all | solution.py:368
  18.6 3.9 %collective-permute-start.6 = (f32[1536,128]{1,0:T(8,128)S(1)}, f32[1536,128]{1,0:T(8,128)S(1)}, u32[]{:S(2)}, u32[]{:S(2)}) collective-permute-start(f32[1536,128]{1,0:T(8,128)S(1)} %pad_maximum_fusion.refs_0_.refs_2_), channel_id=1, source_target_pairs={{0,1},{1,2},{2,3},{3,0},{4,5},{5,6},{6,7},{7,4},{16,20},{17,21},{1... | collective-permute-start | bytes 2359304 | tf_op jit(solution)/shard_map/ppermute | solution.py:295
  19.5 5.2 %collective-permute-start.5 = (f32[1536,128]{1,0:T(8,128)S(1)}, f32[1536,128]{1,0:T(8,128)S(1)}, u32[]{:S(2)}, u32[]{:S(2)}) collective-permute-start(f32[1536,128]{1,0:T(8,128)S(1)} %pad_maximum_fusion.1.refs_3_), channel_id=1, source_target_pairs={{0,3},{1,0},{2,1},{3,2},{4,7},{5,4},{6,5},{7,6},{16,20},{17,21},{1... | collective-permute-start | bytes 2359304 | tf_op jit(solution)/shard_map/ppermute | solution.py:295
  20.2 2.2 %collective-permute-start.7 = (f32[512,128]{1,0:T(8,128)S(1)}, f32[512,128]{1,0:T(8,128)S(1)}, u32[]{:S(2)}, u32[]{:S(2)}) collective-permute-start(f32[512,128]{1,0:T(8,128)S(1)} %bitcast.34), channel_id=1, source_target_pairs={{8,4},{9,5},{10,6},{11,7},{12,0},{13,1},{14,2},{15,3},{24,20},{25,... | collective-permute-start | bytes 786440 | tf_op jit(solution)/shard_map/ppermute | solution.py:295
  23.3 5.6 %collective-permute-start.8 = (f32[768,128]{1,0:T(8,128)}, f32[768,128]{1,0:T(8,128)}, u32[]{:S(2)}, u32[]{:S(2)}) collective-permute-start(f32[768,128]{1,0:T(8,128)} %slice.53), channel_id=1, source_target_pairs={{0,1},{1,2},{2,3},{3,0},{4,5},{5,6},{6,7},{7,4}} | collective-permute-start | bytes 1179656 | tf_op jit(solution)/shard_map/ppermute | solution.py:295
  25.4 3.5 %collective-permute-start.9 = (f32[768,128]{1,0:T(8,128)}, f32[768,128]{1,0:T(8,128)}, u32[]{:S(2)}, u32[]{:S(2)}) collective-permute-start(f32[768,128]{1,0:T(8,128)} %slice.65), channel_id=1, source_target_pairs={{0,3},{1,0},{2,1},{3,2},{4,7},{5,4},{6,5},{7,6}} | collective-permute-start | bytes 1179656 | tf_op jit(solution)/shard_map/ppermute | solution.py:295
  39.6 100.4 %all-to-all-start.1 = ((f32[16,256,128]{2,1,0:T(8,128)}), f32[16,256,128]{2,1,0:T(8,128)S(1)}, u32[]{:S(2)}, u32[]{:S(2)}) async-start(f32[16,256,128]{2,1,0:T(8,128)} %copy-done), calls=%async_computation.1 | async-start | bytes 4194304 | tf_op jit(solution)/shard_map/all_to_all | solution.py:303
  45.9 2.0 %collective-permute-start.14 = (f32[512,128]{1,0:T(8,128)S(1)}, f32[512,128]{1,0:T(8,128)S(1)}, u32[]{:S(2)}, u32[]{:S(2)}) collective-permute-start(f32[512,128]{1,0:T(8,128)S(1)} %fusion.1), channel_id=1, source_target_pairs={{0,96},{1,97},{2,98},{3,99},{4,100},{5,101},{6,102},{7,103},{8,104... | collective-permute-start | bytes 786440 | tf_op jit(solution)/shard_map/ppermute | solution.py:295
  46.6 78.8 %collective-permute-start.15 = (f32[512,128]{1,0:T(8,128)S(1)}, f32[512,128]{1,0:T(8,128)S(1)}, u32[]{:S(2)}, u32[]{:S(2)}) collective-permute-start(f32[512,128]{1,0:T(8,128)S(1)} %collective-permute-done.13), channel_id=1, source_target_pairs={{32,64},{33,65},{34,66},{35,67},{36,68},{37,69},{38,70},{39,71},{4... | collective-permute-start | bytes 786440 | tf_op jit(solution)/shard_map/ppermute | solution.py:295
  125.5 6.5 %collective-permute-start.16 = (f32[512,128]{1,0:T(8,128)S(1)}, f32[512,128]{1,0:T(8,128)S(1)}, u32[]{:S(2)}, u32[]{:S(2)}) collective-permute-start(f32[512,128]{1,0:T(8,128)S(1)} %add_select_fusion), channel_id=1, source_target_pairs={{0,1},{1,2},{2,3},{3,0},{4,5},{5,6},{6,7},{7,4},{8,9},{9,10},{10,1... | collective-permute-start | bytes 786440 | tf_op jit(solution)/shard_map/ppermute | solution.py:295
  126.8 5.2 %collective-permute-start.17 = (f32[512,128]{1,0:T(8,128)S(1)}, f32[512,128]{1,0:T(8,128)S(1)}, u32[]{:S(2)}, u32[]{:S(2)}) collective-permute-start(f32[512,128]{1,0:T(8,128)S(1)} %add_select_fusion), channel_id=1, source_target_pairs={{0,3},{1,0},{2,1},{3,2},{4,7},{5,4},{6,5},{7,6},{8,11},{9,8},{10,9... | collective-permute-start | bytes 786440 | tf_op jit(solution)/shard_map/ppermute | solution.py:295
  132.1 4.6 %collective-permute-start.19 = (f32[256,128]{1,0:T(8,128)S(1)}, f32[256,128]{1,0:T(8,128)S(1)}, u32[]{:S(2)}, u32[]{:S(2)}) collective-permute-start(f32[256,128]{1,0:T(8,128)S(1)} %slice.60), channel_id=1, source_target_pairs={{0,3},{1,0},{2,1},{3,2},{4,7},{5,4},{6,5},{7,6},{8,11},{9,8},{10,9... | collective-permute-start | bytes 393224 | tf_op jit(solution)/shard_map/ppermute | solution.py:295
  134.8 5.1 %collective-permute-start.18 = (f32[256,128]{1,0:T(8,128)S(1)}, f32[256,128]{1,0:T(8,128)S(1)}, u32[]{:S(2)}, u32[]{:S(2)}) collective-permute-start(f32[256,128]{1,0:T(8,128)S(1)} %slice.59), channel_id=1, source_target_pairs={{0,1},{1,2},{2,3},{3,0},{4,5},{5,6},{6,7},{7,4},{8,9},{9,10},{10,1... | collective-permute-start | bytes 393224 | tf_op jit(solution)/shard_map/ppermute | solution.py:295
  141.0 4.6 %collective-permute-start.20 = (f32[8,256,128]{2,1,0:T(8,128)}, f32[8,256,128]{2,1,0:T(8,128)}, u32[]{:S(2)}, u32[]{:S(2)}) collective-permute-start(f32[8,256,128]{2,1,0:T(8,128)} %constant_dynamic-slice_fusion), channel_id=1, source_target_pairs={{0,16},{1,17},{2,18},{3,19},{4,20},{5,21},{6,22},{7,23},{8,24},{9,... | collective-permute-start | bytes 3145736 | tf_op jit(solution)/shard_map/ppermute | solution.py:295
  141.0 9.7 %collective-permute-start.21 = (f32[2,512,128]{2,1,0:T(8,128)S(1)}, f32[2,512,128]{2,1,0:T(8,128)}, u32[]{:S(2)}, u32[]{:S(2)}) collective-permute-start(f32[2,512,128]{2,1,0:T(8,128)S(1)} %bitcast.31), channel_id=1, source_target_pairs={{0,4},{1,5},{2,6},{3,7},{4,8},{5,9},{6,10},{7,11},{8,12},{9,13},{1... | collective-permute-start | bytes 1572872 | tf_op jit(solution)/shard_map/ppermute | solution.py:295
  142.3 8.4 %collective-permute-start.22 = (f32[2,512,128]{2,1,0:T(8,128)S(1)}, f32[2,512,128]{2,1,0:T(8,128)}, u32[]{:S(2)}, u32[]{:S(2)}) collective-permute-start(f32[2,512,128]{2,1,0:T(8,128)S(1)} %bitcast.28), channel_id=1, source_target_pairs={{0,12},{1,13},{2,14},{3,15},{4,0},{5,1},{6,2},{7,3},{8,4},{9,5},{1... | collective-permute-start | bytes 1572872 | tf_op jit(solution)/shard_map/ppermute | solution.py:295
  143.9 12.3 %collective-permute-start.25 = (f32[2,512,128]{2,1,0:T(8,128)S(1)}, f32[2,512,128]{2,1,0:T(8,128)S(1)}, u32[]{:S(2)}, u32[]{:S(2)}) collective-permute-start(f32[2,512,128]{2,1,0:T(8,128)S(1)} %bitcast.32), channel_id=1, source_target_pairs={{0,12},{1,13},{2,14},{3,15},{4,0},{5,1},{6,2},{7,3},{8,4},{9,5},{1... | collective-permute-start | bytes 1572872 | tf_op jit(solution)/shard_map/ppermute | solution.py:295
  145.4 10.9 %collective-permute-start.26 = (f32[2,512,128]{2,1,0:T(8,128)S(1)}, f32[2,512,128]{2,1,0:T(8,128)S(1)}, u32[]{:S(2)}, u32[]{:S(2)}) collective-permute-start(f32[2,512,128]{2,1,0:T(8,128)S(1)} %bitcast.29), channel_id=1, source_target_pairs={{0,4},{1,5},{2,6},{3,7},{4,8},{5,9},{6,10},{7,11},{8,12},{9,13},{1... | collective-permute-start | bytes 1572872 | tf_op jit(solution)/shard_map/ppermute | solution.py:295
  150.8 11.1 %collective-permute-start.23 = (f32[2,512,128]{2,1,0:T(8,128)}, f32[2,512,128]{2,1,0:T(8,128)S(1)}, u32[]{:S(2)}, u32[]{:S(2)}) collective-permute-start(f32[2,512,128]{2,1,0:T(8,128)} %collective-permute-done.21.refs_3_), channel_id=1, source_target_pairs={{0,4},{1,5},{2,6},{3,7},{4,8},{5,9},{6,10},{7,11},{8,12},{9,13},{1... | collective-permute-start | bytes 1572872 | tf_op jit(solution)/shard_map/ppermute | solution.py:295
  152.0 9.9 %collective-permute-start.24 = (f32[2,512,128]{2,1,0:T(8,128)}, f32[2,512,128]{2,1,0:T(8,128)S(1)}, u32[]{:S(2)}, u32[]{:S(2)}) collective-permute-start(f32[2,512,128]{2,1,0:T(8,128)} %collective-permute-done.22.refs_2_), channel_id=1, source_target_pairs={{0,12},{1,13},{2,14},{3,15},{4,0},{5,1},{6,2},{7,3},{8,4},{9,5},{1... | collective-permute-start | bytes 1572872 | tf_op jit(solution)/shard_map/ppermute | solution.py:295
  164.6 3.7 %collective-permute-start.27 = (f32[256,1024]{1,0:T(8,128)S(1)}, f32[256,1024]{1,0:T(8,128)S(1)}, u32[]{:S(2)}, u32[]{:S(2)}) collective-permute-start(f32[256,1024]{1,0:T(8,128)S(1)} %slice.71), channel_id=1, source_target_pairs={{0,16},{1,17},{2,18},{3,19},{4,20},{5,21},{6,22},{7,23},{8,24},{9,... | collective-permute-start | bytes 3145736 | tf_op jit(solution)/shard_map/ppermute | solution.py:295
  (18 other events, 37.3 us)

commit v20 on v19

--- a/solution.py
+++ b/solution.py
@@ -299,12 +299,12 @@
     here = jnp.where(core == 0, first[:512], second[512:])
     there = jnp.where(core == 0, first[512:], second[:512])
     got = move(there, lambda a, b, c, d: (0, b, 3 - c, d) if a == 0 and b == c // 2 else None)
-    got, by_rows = lax.optimization_barrier((got, by_rows))
-    left = lax.all_to_all(by_rows, COL, 0, 0, tiled=True)
     mine = jnp.where(core == yh, here, got)
     one = move(mine, lambda a, b, c, d: (1 if b == 0 else 3, b, c, d) if a == 0 else None)
     two = move(mine, lambda a, b, c, d: (3 if b == 0 else 1, b, c, d) if a == 0 else None)
     far = move(one, lambda a, b, c, d: (2, b, c, d) if a == (1 if b == 0 else 3) else None)
+    by_rows, _ = lax.optimization_barrier((by_rows, one))
+    left = lax.all_to_all(by_rows, COL, 0, 0, tiled=True)
     return jnp.where(xi == 0, mine, one + two + far), left
 
 

time: 171 us -> 167 us (0.977)
  the two profiles are of different devices: /device:TPU:5 before, /device:TPU:1 now
where the time goes in v20:
time: 167 us; the launch traced here: 166 us
  waiting for transfers between devices  76.5 us (46%)
  starting transfers between devices  56.8 us (34%)
  Pallas kernels  18.9 us (11%)
  local copies, waits for them, and re-layouts  9.57 us (6%)
  other arithmetic  3.9 us (2%)
    ppermute x28, waiting for transfers between devices, move(): return lax.ppermute(value, AXES, pairs)  70.9 us
    ppermute x28, starting transfers between devices, move(): return lax.ppermute(value, AXES, pairs)  49.1 us
    pallas_call x3, Pallas kernels, accumulate(): pl.pallas_call(body, out_shape=jax.ShapeDtypeStruct((512, 1024), F32), in...  10.1 us
    all_to_all x1, waiting for transfers between devices, shards(): lax.all_to_all(arrange_rhs(yh, rhs), ('yl', 'z'), 0, 0, tiled=True)  5.61 us
    unnamed x25, local copies, waits for them, and re-layouts  4.54 us
    all_to_all x1, starting transfers between devices, shards(): lax.all_to_all(arrange_rhs(yh, rhs), ('yl', 'z'), 0, 0, tiled=True)  3.94 us
    all_to_all x1, starting transfers between devices, deal(): left = lax.all_to_all(by_rows, COL, 0, 0, tiled=True)  3.78 us
  transfers between devices with their start and end apart: 30, of which 18 were waited for; matrix products, arithmetic and copies ran while one was open for 3% of the time, Pallas kernels for 6%

profile of v20, /device:TPU:1, one launch (start us, length us, event | category | flops | bytes accessed | tf_op | source)
XLA Modules:
  0.0 166.1 jit_solution(10013857827313422458)
XLA Ops:
  1.8 6.5 %collective-permute-start.5 = (f32[1024,128]{1,0:T(8,128)S(1)}, f32[1024,128]{1,0:T(8,128)S(1)}, u32[]{:S(2)}, u32[]{:S(2)}) collective-permute-start(f32[1024,128]{1,0:T(8,128)S(1)} %invert_diagonal.1.refs_0_), channel_id=1, source_target_pairs={{16,19},{17,16},{18,17},{19,18},{20,23},{21,20},{22,21},{23,22},{2... | collective-permute-start | bytes 1572872 | tf_op jit(solution)/shard_map/ppermute | solution.py:295
  10.3 3.2 %collective-permute-start.1 = (f32[1024,128]{1,0:T(8,128)S(1)}, f32[1024,128]{1,0:T(8,128)S(1)}, u32[]{:S(2)}, u32[]{:S(2)}) collective-permute-start(f32[1024,128]{1,0:T(8,128)S(1)} %invert_diagonal.1.refs_0_), channel_id=1, source_target_pairs={{16,20},{17,21},{18,22},{19,23},{20,16},{21,17},{22,18},{23,19},{2... | collective-permute-start | bytes 1572872 | tf_op jit(solution)/shard_map/ppermute | solution.py:295
  14.2 3.9 %all-to-all-start = ((f32[8,64,128]{2,1,0:T(8,128)}), f32[8,64,128]{2,1,0:T(8,128)S(1)}, u32[]{:S(2)}, u32[]{:S(2)}) async-start(f32[8,64,128]{2,1,0:T(8,128)} %arrange_rhs.1), calls=%async_computation | async-start | bytes 524288 | tf_op jit(solution)/shard_map/all_to_all | solution.py:368
  18.2 4.6 %collective-permute-start.6 = (f32[512,128]{1,0:T(8,128)S(1)}, f32[512,128]{1,0:T(8,128)S(1)}, u32[]{:S(2)}, u32[]{:S(2)}) collective-permute-start(f32[512,128]{1,0:T(8,128)S(1)} %slice.64), channel_id=1, source_target_pairs={{16,19},{17,16},{18,17},{19,18},{20,23},{21,20},{22,21},{23,22},{2... | collective-permute-start | bytes 786440 | tf_op jit(solution)/shard_map/ppermute | solution.py:295
  22.8 5.6 %all-to-all-done = f32[8,64,128]{2,1,0:T(8,128)S(1)} async-done(((f32[8,64,128]{2,1,0:T(8,128)}), f32[8,64,128]{2,1,0:T(8,128)S(1)}, u32[]{:S(2)}, u32[]{:S(2)}) %all-to-all-start) | async-done | bytes 262176 | tf_op jit(solution)/shard_map/all_to_all | solution.py:368
  30.8 9.1 %collective-permute-done.2 = f32[512,128]{1,0:T(8,128)S(1)} collective-permute-done((f32[512,128]{1,0:T(8,128)S(1)}, f32[512,128]{1,0:T(8,128)S(1)}, u32[]{:S(2)}, u32[]{:S(2)}) %collective-permute-start.2) | collective-permute-done | bytes 262176 | tf_op jit(solution)/shard_map/ppermute | solution.py:295
  40.0 3.2 %collective-permute-start.3 = (f32[1536,128]{1,0:T(8,128)S(1)}, f32[1536,128]{1,0:T(8,128)S(1)}, u32[]{:S(2)}, u32[]{:S(2)}) collective-permute-start(f32[1536,128]{1,0:T(8,128)S(1)} %pad_maximum_fusion.refs_0_.refs_2_), channel_id=1, source_target_pairs={{0,1},{1,2},{2,3},{3,0},{4,5},{5,6},{6,7},{7,4},{16,20},{17,21},{1... | collective-permute-start | bytes 2359304 | tf_op jit(solution)/shard_map/ppermute | solution.py:295
  48.2 5.9 %collective-permute-done.4 = f32[512,128]{1,0:T(8,128)S(1)} collective-permute-done((f32[512,128]{1,0:T(8,128)S(1)}, f32[512,128]{1,0:T(8,128)S(1)}, u32[]{:S(2)}, u32[]{:S(2)}) %collective-permute-start.4) | collective-permute-done | bytes 262176 | tf_op jit(solution)/shard_map/ppermute | solution.py:295
  56.3 4.8 %collective-permute-done.7.refs_1_.refs_5_ = f32[1536,128]{1,0:T(8,128)S(1)} collective-permute-done((f32[1536,128]{1,0:T(8,128)S(1)}, f32[1536,128]{1,0:T(8,128)S(1)}, u32[]{:S(2)}, u32[]{:S(2)}) %collective-permute-start.7) | collective-permute-done | bytes 786464 | tf_op jit(solution)/shard_map/ppermute | solution.py:295
  68.7 2.8 %collective-permute-done.10.refs_7_ = f32[1024,128]{1,0:T(8,128)} collective-permute-done((f32[1024,128]{1,0:T(8,128)}, f32[1024,128]{1,0:T(8,128)}, u32[]{:S(2)}, u32[]{:S(2)}) %collective-permute-start.10) | collective-permute-done | bytes 524320 | tf_op jit(solution)/shard_map/ppermute | solution.py:295
  73.6 3.1 %residual_or_pack.1 = (f32[1024,128]{1,0:T(8,128)}, bf16[112,1024,256]{2,1,0:T(8,128)(2,1)}) custom-call(s32[3]{0:T(128)S(1)} %pad_add_fusion.5.info, f32[1024,128]{1,0:T(8,128)S(1)} %invert_diagonal.1.refs_0_, f32[1024,128]{1,0:T(8,128)S(1)} %copy-done.7, f32[1536,128]{1,0:T(8,128)S(1)} %pad_maximum_fusion.refs_0_.refs_2_, f32[1536,128]{1,0:T(8,128)S(1)} %copy-done.5, ...), custom_call_target="tpu_custom_call" | custom-call | tf_op jit(solution)/shard_map/residual_or_pack/pallas_call | solution.py:144
  78.2 9.1 %collective-permute-done.11.rhs_ref = f32[1024,128]{1,0:T(8,128)S(1)} collective-permute-done((f32[1024,128]{1,0:T(8,128)}, f32[1024,128]{1,0:T(8,128)S(1)}, u32[]{:S(2)}, u32[]{:S(2)}) %collective-permute-start.11) | collective-permute-done | bytes 524320 | tf_op jit(solution)/shard_map/ppermute | solution.py:295
  90.2 10.9 %collective-permute-done.12 = f32[512,128]{1,0:T(8,128)S(1)} collective-permute-done((f32[512,128]{1,0:T(8,128)S(1)}, f32[512,128]{1,0:T(8,128)S(1)}, u32[]{:S(2)}, u32[]{:S(2)}) %collective-permute-start.12) | collective-permute-done | bytes 262176 | tf_op jit(solution)/shard_map/ppermute | solution.py:295
  103.4 3.3 %collective-permute-done.13 = f32[512,128]{1,0:T(8,128)S(1)} collective-permute-done((f32[512,128]{1,0:T(8,128)S(1)}, f32[512,128]{1,0:T(8,128)S(1)}, u32[]{:S(2)}, u32[]{:S(2)}) %collective-permute-start.13) | collective-permute-done | bytes 262176 | tf_op jit(solution)/shard_map/ppermute | solution.py:295
  106.7 3.8 %all-to-all-start.1 = ((f32[16,256,128]{2,1,0:T(8,128)}), f32[16,256,128]{2,1,0:T(8,128)S(1)}, u32[]{:S(2)}, u32[]{:S(2)}) async-start(f32[16,256,128]{2,1,0:T(8,128)} %copy-done), calls=%async_computation.1 | async-start | bytes 4194304 | tf_op jit(solution)/shard_map/all_to_all | solution.py:307
  112.5 2.6 %collective-permute-done.14 = f32[512,128]{1,0:T(8,128)S(1)} collective-permute-done((f32[512,128]{1,0:T(8,128)S(1)}, f32[512,128]{1,0:T(8,128)S(1)}, u32[]{:S(2)}, u32[]{:S(2)}) %collective-permute-start.14) | collective-permute-done | bytes 262176 | tf_op jit(solution)/shard_map/ppermute | solution.py:295
  117.9 10.4 %collective-permute-done.16 = f32[512,128]{1,0:T(8,128)S(1)} collective-permute-done((f32[512,128]{1,0:T(8,128)S(1)}, f32[512,128]{1,0:T(8,128)S(1)}, u32[]{:S(2)}, u32[]{:S(2)}) %collective-permute-start.16) | collective-permute-done | bytes 262176 | tf_op jit(solution)/shard_map/ppermute | solution.py:295
  130.0 2.5 %collective-permute-done.19 = f32[256,128]{1,0:T(8,128)S(1)} collective-permute-done((f32[256,128]{1,0:T(8,128)S(1)}, f32[256,128]{1,0:T(8,128)S(1)}, u32[]{:S(2)}, u32[]{:S(2)}) %collective-permute-start.19) | collective-permute-done | bytes 131104 | tf_op jit(solution)/shard_map/ppermute | solution.py:295
  132.5 2.5 %collective-permute-done.18 = f32[256,128]{1,0:T(8,128)S(1)} collective-permute-done((f32[256,128]{1,0:T(8,128)S(1)}, f32[256,128]{1,0:T(8,128)S(1)}, u32[]{:S(2)}, u32[]{:S(2)}) %collective-permute-start.18) | collective-permute-done | bytes 131104 | tf_op jit(solution)/shard_map/ppermute | solution.py:295
  142.3 2.5 %update_near.1.refs_0_ = f32[512,1024]{1,0:T(8,128)S(1)} custom-call(s32[5]{0:T(128)S(1)} %stack.63.info, bf16[4,512,256]{2,1,0:T(8,128)(2,1)S(1)} %get-tuple-element.37.high_ref, bf16[4,512,256]{2,1,0:T(8,128)(2,1)S(1)} %get-tuple-element.38.low_ref, f32[2,512,128]{2,1,0:T(8,128)S(1)} %bitcast.33, f32[2,512,128]{2,1,0:T(8,128)S(1)} %bitcast.30), custom_call_target="tpu_custom_call" | custom-call | tf_op jit(solution)/shard_map/update_near/pallas_call | solution.py:271
  148.9 2.8 %collective-permute-done.25.refs_1_ = f32[2,512,128]{2,1,0:T(8,128)S(1)} collective-permute-done((f32[2,512,128]{2,1,0:T(8,128)S(1)}, f32[2,512,128]{2,1,0:T(8,128)S(1)}, u32[]{:S(2)}, u32[]{:S(2)}) %collective-permute-start.25) | collective-permute-done | bytes 524320 | tf_op jit(solution)/shard_map/ppermute | solution.py:295
  151.7 5.1 %update_next.1.refs_0_ = f32[512,1024]{1,0:T(8,128)S(1)} custom-call(s32[5]{0:T(128)S(1)} %stack.63.info, bf16[4,512,256]{2,1,0:T(8,128)(2,1)S(1)} %get-tuple-element.37.high_ref, bf16[4,512,256]{2,1,0:T(8,128)(2,1)S(1)} %get-tuple-element.38.low_ref, f32[512,1024]{1,0:T(8,128)S(1)} %update_near.1.refs_0_, ...), custom_call_target="tpu_custom_call", output_to_operand_aliasing={{}: (3, {})} | custom-call | tf_op jit(solution)/shard_map/update_next/pallas_call | solution.py:271
  157.3 2.6 %update_far.1 = f32[512,1024]{1,0:T(8,128)S(1)} custom-call(s32[5]{0:T(128)S(1)} %stack.63.info, bf16[4,512,256]{2,1,0:T(8,128)(2,1)S(1)} %get-tuple-element.37.high_ref, bf16[4,512,256]{2,1,0:T(8,128)(2,1)S(1)} %get-tuple-element.38.low_ref, f32[512,1024]{1,0:T(8,128)S(1)} %update_next.1.refs_0_, ...), custom_call_target="tpu_custom_call", output_to_operand_aliasing={{}: (3, {})} | custom-call | tf_op jit(solution)/shard_map/update_far/pallas_call | solution.py:271
  160.1 2.6 %collective-permute-start.27 = (f32[256,1024]{1,0:T(8,128)S(1)}, f32[256,1024]{1,0:T(8,128)S(1)}, u32[]{:S(2)}, u32[]{:S(2)}) collective-permute-start(f32[256,1024]{1,0:T(8,128)S(1)} %slice.71), channel_id=1, source_target_pairs={{0,16},{1,17},{2,18},{3,19},{4,20},{5,21},{6,22},{7,23},{8,24},{9,... | collective-permute-start | bytes 3145736 | tf_op jit(solution)/shard_map/ppermute | solution.py:295
  (98 shorter events, 52.3 us)
Async XLA Ops:
  1.8 16.3 %collective-permute-start.5 = (f32[1024,128]{1,0:T(8,128)S(1)}, f32[1024,128]{1,0:T(8,128)S(1)}, u32[]{:S(2)}, u32[]{:S(2)}) collective-permute-start(f32[1024,128]{1,0:T(8,128)S(1)} %invert_diagonal.1.refs_0_), channel_id=1, source_target_pairs={{16,19},{17,16},{18,17},{19,18},{20,23},{21,20},{22,21},{23,22},{2... | collective-permute-start | bytes 1572872 | tf_op jit(solution)/shard_map/ppermute | solution.py:295
  8.3 20.1 %collective-permute-start = (f32[1024,128]{1,0:T(8,128)S(1)}, f32[1024,128]{1,0:T(8,128)S(1)}, u32[]{:S(2)}, u32[]{:S(2)}) collective-permute-start(f32[1024,128]{1,0:T(8,128)S(1)} %invert_diagonal.1.refs_0_), channel_id=1, source_target_pairs={{0,4},{1,5},{2,6},{3,7},{4,0},{5,1},{6,2},{7,3},{16,17},{17,18},{1... | collective-permute-start | bytes 1572872 | tf_op jit(solution)/shard_map/ppermute | solution.py:295
  10.3 18.1 %collective-permute-start.1 = (f32[1024,128]{1,0:T(8,128)S(1)}, f32[1024,128]{1,0:T(8,128)S(1)}, u32[]{:S(2)}, u32[]{:S(2)}) collective-permute-start(f32[1024,128]{1,0:T(8,128)S(1)} %invert_diagonal.1.refs_0_), channel_id=1, source_target_pairs={{16,20},{17,21},{18,22},{19,23},{20,16},{21,17},{22,18},{23,19},{2... | collective-permute-start | bytes 1572872 | tf_op jit(solution)/shard_map/ppermute | solution.py:295
  14.2 14.2 %all-to-all-start = ((f32[8,64,128]{2,1,0:T(8,128)}), f32[8,64,128]{2,1,0:T(8,128)S(1)}, u32[]{:S(2)}, u32[]{:S(2)}) async-start(f32[8,64,128]{2,1,0:T(8,128)} %arrange_rhs.1), calls=%async_computation | async-start | bytes 524288 | tf_op jit(solution)/shard_map/all_to_all | solution.py:368
  18.2 12.6 %collective-permute-start.6 = (f32[512,128]{1,0:T(8,128)S(1)}, f32[512,128]{1,0:T(8,128)S(1)}, u32[]{:S(2)}, u32[]{:S(2)}) collective-permute-start(f32[512,128]{1,0:T(8,128)S(1)} %slice.64), channel_id=1, source_target_pairs={{16,19},{17,16},{18,17},{19,18},{20,23},{21,20},{22,21},{23,22},{2... | collective-permute-start | bytes 786440 | tf_op jit(solution)/shard_map/ppermute | solution.py:295
  28.4 11.4 %collective-permute-start.2 = (f32[512,128]{1,0:T(8,128)S(1)}, f32[512,128]{1,0:T(8,128)S(1)}, u32[]{:S(2)}, u32[]{:S(2)}) collective-permute-start(f32[512,128]{1,0:T(8,128)S(1)} %slice.51), channel_id=1, source_target_pairs={{16,17},{17,18},{18,19},{19,16},{20,21},{21,22},{22,23},{23,20},{2... | collective-permute-start | bytes 786440 | tf_op jit(solution)/shard_map/ppermute | solution.py:295
  40.0 14.1 %collective-permute-start.3 = (f32[1536,128]{1,0:T(8,128)S(1)}, f32[1536,128]{1,0:T(8,128)S(1)}, u32[]{:S(2)}, u32[]{:S(2)}) collective-permute-start(f32[1536,128]{1,0:T(8,128)S(1)} %pad_maximum_fusion.refs_0_.refs_2_), channel_id=1, source_target_pairs={{0,1},{1,2},{2,3},{3,0},{4,5},{5,6},{6,7},{7,4},{16,20},{17,21},{1... | collective-permute-start | bytes 2359304 | tf_op jit(solution)/shard_map/ppermute | solution.py:295
  43.3 17.9 %collective-permute-start.7 = (f32[1536,128]{1,0:T(8,128)S(1)}, f32[1536,128]{1,0:T(8,128)S(1)}, u32[]{:S(2)}, u32[]{:S(2)}) collective-permute-start(f32[1536,128]{1,0:T(8,128)S(1)} %pad_maximum_fusion.1.refs_3_), channel_id=1, source_target_pairs={{0,3},{1,0},{2,1},{3,2},{4,7},{5,4},{6,5},{7,6},{16,20},{17,21},{1... | collective-permute-start | bytes 2359304 | tf_op jit(solution)/shard_map/ppermute | solution.py:295
  45.4 8.7 %collective-permute-start.4 = (f32[512,128]{1,0:T(8,128)S(1)}, f32[512,128]{1,0:T(8,128)S(1)}, u32[]{:S(2)}, u32[]{:S(2)}) collective-permute-start(f32[512,128]{1,0:T(8,128)S(1)} %bitcast.34), channel_id=1, source_target_pairs={{8,4},{9,5},{10,6},{11,7},{12,0},{13,1},{14,2},{15,3},{24,20},{25,... | collective-permute-start | bytes 786440 | tf_op jit(solution)/shard_map/ppermute | solution.py:295
  54.9 10.4 %collective-permute-start.8 = (f32[768,128]{1,0:T(8,128)}, f32[768,128]{1,0:T(8,128)}, u32[]{:S(2)}, u32[]{:S(2)}) collective-permute-start(f32[768,128]{1,0:T(8,128)} %slice.53), channel_id=1, source_target_pairs={{0,1},{1,2},{2,3},{3,0},{4,5},{5,6},{6,7},{7,4}} | collective-permute-start | bytes 1179656 | tf_op jit(solution)/shard_map/ppermute | solution.py:295
  76.8 10.5 %collective-permute-start.11 = (f32[1024,128]{1,0:T(8,128)}, f32[1024,128]{1,0:T(8,128)S(1)}, u32[]{:S(2)}, u32[]{:S(2)}) collective-permute-start(f32[1024,128]{1,0:T(8,128)} %get-tuple-element.32), channel_id=1, source_target_pairs={{16,28},{17,29},{18,30},{19,31},{20,24},{21,25},{22,26},{23,27}} | collective-permute-start | bytes 1572872 | tf_op jit(solution)/shard_map/ppermute | solution.py:295
  88.9 12.2 %collective-permute-start.12 = (f32[512,128]{1,0:T(8,128)S(1)}, f32[512,128]{1,0:T(8,128)S(1)}, u32[]{:S(2)}, u32[]{:S(2)}) collective-permute-start(f32[512,128]{1,0:T(8,128)S(1)} %slice_select_fusion), channel_id=1, source_target_pairs={{0,12},{1,13},{2,14},{3,15},{4,8},{5,9},{6,10},{7,11},{24,20},{25,... | collective-permute-start | bytes 786440 | tf_op jit(solution)/shard_map/ppermute | solution.py:295
  106.7 28.3 %all-to-all-start.1 = ((f32[16,256,128]{2,1,0:T(8,128)}), f32[16,256,128]{2,1,0:T(8,128)S(1)}, u32[]{:S(2)}, u32[]{:S(2)}) async-start(f32[16,256,128]{2,1,0:T(8,128)} %copy-done), calls=%async_computation.1 | async-start | bytes 4194304 | tf_op jit(solution)/shard_map/all_to_all | solution.py:307
  115.2 13.2 %collective-permute-start.16 = (f32[512,128]{1,0:T(8,128)S(1)}, f32[512,128]{1,0:T(8,128)S(1)}, u32[]{:S(2)}, u32[]{:S(2)}) collective-permute-start(f32[512,128]{1,0:T(8,128)S(1)} %add_select_fusion), channel_id=1, source_target_pairs={{0,1},{1,2},{2,3},{3,0},{4,5},{5,6},{6,7},{7,4},{8,9},{9,10},{10,1... | collective-permute-start | bytes 786440 | tf_op jit(solution)/shard_map/ppermute | solution.py:295
  116.6 11.7 %collective-permute-start.17 = (f32[512,128]{1,0:T(8,128)S(1)}, f32[512,128]{1,0:T(8,128)S(1)}, u32[]{:S(2)}, u32[]{:S(2)}) collective-permute-start(f32[512,128]{1,0:T(8,128)S(1)} %add_select_fusion), channel_id=1, source_target_pairs={{0,3},{1,0},{2,1},{3,2},{4,7},{5,4},{6,5},{7,6},{8,11},{9,8},{10,9... | collective-permute-start | bytes 786440 | tf_op jit(solution)/shard_map/ppermute | solution.py:295
  129.9 5.1 %collective-permute-start.18 = (f32[256,128]{1,0:T(8,128)S(1)}, f32[256,128]{1,0:T(8,128)S(1)}, u32[]{:S(2)}, u32[]{:S(2)}) collective-permute-start(f32[256,128]{1,0:T(8,128)S(1)} %slice.59), channel_id=1, source_target_pairs={{0,1},{1,2},{2,3},{3,0},{4,5},{5,6},{6,7},{7,4},{8,9},{9,10},{10,1... | collective-permute-start | bytes 393224 | tf_op jit(solution)/shard_map/ppermute | solution.py:295
  136.1 4.6 %collective-permute-start.20 = (f32[8,256,128]{2,1,0:T(8,128)}, f32[8,256,128]{2,1,0:T(8,128)}, u32[]{:S(2)}, u32[]{:S(2)}) collective-permute-start(f32[8,256,128]{2,1,0:T(8,128)} %constant_dynamic-slice_fusion), channel_id=1, source_target_pairs={{0,16},{1,17},{2,18},{3,19},{4,20},{5,21},{6,22},{7,23},{8,24},{9,... | collective-permute-start | bytes 3145736 | tf_op jit(solution)/shard_map/ppermute | solution.py:295
  136.1 9.7 %collective-permute-start.21 = (f32[2,512,128]{2,1,0:T(8,128)S(1)}, f32[2,512,128]{2,1,0:T(8,128)}, u32[]{:S(2)}, u32[]{:S(2)}) collective-permute-start(f32[2,512,128]{2,1,0:T(8,128)S(1)} %bitcast.31), channel_id=1, source_target_pairs={{0,4},{1,5},{2,6},{3,7},{4,8},{5,9},{6,10},{7,11},{8,12},{9,13},{1... | collective-permute-start | bytes 1572872 | tf_op jit(solution)/shard_map/ppermute | solution.py:295
  137.8 8.4 %collective-permute-start.22 = (f32[2,512,128]{2,1,0:T(8,128)S(1)}, f32[2,512,128]{2,1,0:T(8,128)}, u32[]{:S(2)}, u32[]{:S(2)}) collective-permute-start(f32[2,512,128]{2,1,0:T(8,128)S(1)} %bitcast.28), channel_id=1, source_target_pairs={{0,12},{1,13},{2,14},{3,15},{4,0},{5,1},{6,2},{7,3},{8,4},{9,5},{1... | collective-permute-start | bytes 1572872 | tf_op jit(solution)/shard_map/ppermute | solution.py:295
  139.0 12.7 %collective-permute-start.25 = (f32[2,512,128]{2,1,0:T(8,128)S(1)}, f32[2,512,128]{2,1,0:T(8,128)S(1)}, u32[]{:S(2)}, u32[]{:S(2)}) collective-permute-start(f32[2,512,128]{2,1,0:T(8,128)S(1)} %bitcast.32), channel_id=1, source_target_pairs={{0,12},{1,13},{2,14},{3,15},{4,0},{5,1},{6,2},{7,3},{8,4},{9,5},{1... | collective-permute-start | bytes 1572872 | tf_op jit(solution)/shard_map/ppermute | solution.py:295
  140.5 11.2 %collective-permute-start.26 = (f32[2,512,128]{2,1,0:T(8,128)S(1)}, f32[2,512,128]{2,1,0:T(8,128)S(1)}, u32[]{:S(2)}, u32[]{:S(2)}) collective-permute-start(f32[2,512,128]{2,1,0:T(8,128)S(1)} %bitcast.29), channel_id=1, source_target_pairs={{0,4},{1,5},{2,6},{3,7},{4,8},{5,9},{6,10},{7,11},{8,12},{9,13},{1... | collective-permute-start | bytes 1572872 | tf_op jit(solution)/shard_map/ppermute | solution.py:295
  146.2 10.8 %collective-permute-start.23 = (f32[2,512,128]{2,1,0:T(8,128)}, f32[2,512,128]{2,1,0:T(8,128)S(1)}, u32[]{:S(2)}, u32[]{:S(2)}) collective-permute-start(f32[2,512,128]{2,1,0:T(8,128)} %collective-permute-done.21.refs_3_), channel_id=1, source_target_pairs={{0,4},{1,5},{2,6},{3,7},{4,8},{5,9},{6,10},{7,11},{8,12},{9,13},{1... | collective-permute-start | bytes 1572872 | tf_op jit(solution)/shard_map/ppermute | solution.py:295
  147.1 10.2 %collective-permute-start.24 = (f32[2,512,128]{2,1,0:T(8,128)}, f32[2,512,128]{2,1,0:T(8,128)S(1)}, u32[]{:S(2)}, u32[]{:S(2)}) collective-permute-start(f32[2,512,128]{2,1,0:T(8,128)} %collective-permute-done.22.refs_2_), channel_id=1, source_target_pairs={{0,12},{1,13},{2,14},{3,15},{4,0},{5,1},{6,2},{7,3},{8,4},{9,5},{1... | collective-permute-start | bytes 1572872 | tf_op jit(solution)/shard_map/ppermute | solution.py:295
  160.1 4.9 %collective-permute-start.27 = (f32[256,1024]{1,0:T(8,128)S(1)}, f32[256,1024]{1,0:T(8,128)S(1)}, u32[]{:S(2)}, u32[]{:S(2)}) collective-permute-start(f32[256,1024]{1,0:T(8,128)S(1)} %slice.71), channel_id=1, source_target_pairs={{0,16},{1,17},{2,18},{3,19},{4,20},{5,21},{6,22},{7,23},{8,24},{9,... | collective-permute-start | bytes 3145736 | tf_op jit(solution)/shard_map/ppermute | solution.py:295
  (18 other events, 108.8 us)

commit v21 on v20

--- a/solution.py
+++ b/solution.py
@@ -303,7 +303,7 @@
     one = move(mine, lambda a, b, c, d: (1 if b == 0 else 3, b, c, d) if a == 0 else None)
     two = move(mine, lambda a, b, c, d: (3 if b == 0 else 1, b, c, d) if a == 0 else None)
     far = move(one, lambda a, b, c, d: (2, b, c, d) if a == (1 if b == 0 else 3) else None)
-    by_rows, _ = lax.optimization_barrier((by_rows, one))
+    by_rows, _, _ = lax.optimization_barrier((by_rows, one, two))
     left = lax.all_to_all(by_rows, COL, 0, 0, tiled=True)
     return jnp.where(xi == 0, mine, one + two + far), left
 

time: 167 us -> 167 us (level)
  the two profiles are of different devices: /device:TPU:1 before, /device:TPU:27 now
where the time goes in v21:
time: 167 us; the launch traced here: 166 us
  waiting for transfers between devices  93.2 us (56%)
  starting transfers between devices  41.4 us (25%)
  Pallas kernels  17.5 us (10%)
  local copies, waits for them, and re-layouts  9.57 us (6%)
  other arithmetic  3.9 us (2%)
    ppermute x28, waiting for transfers between devices, move(): return lax.ppermute(value, AXES, pairs)  88.9 us
    ppermute x28, starting transfers between devices, move(): return lax.ppermute(value, AXES, pairs)  28.5 us
    pallas_call x3, Pallas kernels, accumulate(): pl.pallas_call(body, out_shape=jax.ShapeDtypeStruct((512, 1024), F32), in...  10.1 us
    all_to_all x1, starting transfers between devices, deal(): left = lax.all_to_all(by_rows, COL, 0, 0, tiled=True)  6.7 us
    all_to_all x1, starting transfers between devices, shards(): lax.all_to_all(arrange_rhs(yh, rhs), ('yl', 'z'), 0, 0, tiled=True)  6.21 us
    unnamed x25, local copies, waits for them, and re-layouts  4.55 us
    all_to_all x1, waiting for transfers between devices, shards(): lax.all_to_all(arrange_rhs(yh, rhs), ('yl', 'z'), 0, 0, tiled=True)  4.25 us
  transfers between devices with their start and end apart: 30, of which 11 were waited for; matrix products, arithmetic and copies ran while one was open for 3% of the time, Pallas kernels for 6%

profile of v21, /device:TPU:27, one launch (start us, length us, event | category | flops | bytes accessed | tf_op | source)
XLA Modules:
  0.0 166.1 jit_solution(10247468546982104110)
XLA Ops:
  4.7 6.2 %all-to-all-start = ((f32[8,64,128]{2,1,0:T(8,128)}), f32[8,64,128]{2,1,0:T(8,128)S(1)}, u32[]{:S(2)}, u32[]{:S(2)}) async-start(f32[8,64,128]{2,1,0:T(8,128)} %arrange_rhs.1), calls=%async_computation | async-start | bytes 524288 | tf_op jit(solution)/shard_map/all_to_all | solution.py:368
  11.6 4.2 %all-to-all-done = f32[8,64,128]{2,1,0:T(8,128)S(1)} async-done(((f32[8,64,128]{2,1,0:T(8,128)}), f32[8,64,128]{2,1,0:T(8,128)S(1)}, u32[]{:S(2)}, u32[]{:S(2)}) %all-to-all-start) | async-done | bytes 262176 | tf_op jit(solution)/shard_map/all_to_all | solution.py:368
  21.6 1.4 collective-permute-start.8
  23.7 1.4 collective-permute-start.9
  27.2 1.9 %solve_first.1 = f32[1024,128]{1,0:T(8,128)} custom-call(s32[3]{0:T(128)S(1)} %pad_add_fusion.2.info, f32[1536,128]{1,0:T(8,128)S(1)} %pad_maximum_fusion.refs_0_.refs_2_, f32[1536,128]{1,0:T(8,128)S(1)} %collective-permute-done.7.refs_1_.refs_5_, f32[1536,128]{1,0:T(8,128)S(1)} %collective-permute-done.3.refs_2_.refs_4_, ...), custom_call_target="tpu_custom_call" | custom-call | tf_op jit(solution)/shard_map/solve_first/pallas_call | solution.py:107
  29.1 1.5 collective-permute-start.10
  32.9 1.9 %residual_or_pack.1 = (f32[1024,128]{1,0:T(8,128)}, bf16[112,1024,256]{2,1,0:T(8,128)(2,1)}) custom-call(s32[3]{0:T(128)S(1)} %pad_add_fusion.5.info, f32[1024,128]{1,0:T(8,128)S(1)} %invert_diagonal.1.refs_0_, f32[1024,128]{1,0:T(8,128)S(1)} %copy-done.7, f32[1536,128]{1,0:T(8,128)S(1)} %pad_maximum_fusion.refs_0_.refs_2_, f32[1536,128]{1,0:T(8,128)S(1)} %copy-done.5, ...), custom_call_target="tpu_custom_call" | custom-call | tf_op jit(solution)/shard_map/residual_or_pack/pallas_call | solution.py:144
  40.8 64.2 %collective-permute-done.14 = f32[512,128]{1,0:T(8,128)S(1)} collective-permute-done((f32[512,128]{1,0:T(8,128)S(1)}, f32[512,128]{1,0:T(8,128)S(1)}, u32[]{:S(2)}, u32[]{:S(2)}) %collective-permute-start.14) | collective-permute-done | bytes 262176 | tf_op jit(solution)/shard_map/ppermute | solution.py:295
  105.0 6.7 %all-to-all-start.1 = ((f32[16,256,128]{2,1,0:T(8,128)}), f32[16,256,128]{2,1,0:T(8,128)S(1)}, u32[]{:S(2)}, u32[]{:S(2)}) async-start(f32[16,256,128]{2,1,0:T(8,128)} %copy-done), calls=%async_computation.1 | async-start | bytes 4194304 | tf_op jit(solution)/shard_map/all_to_all | solution.py:307
  114.0 14.1 %collective-permute-done.16 = f32[512,128]{1,0:T(8,128)S(1)} collective-permute-done((f32[512,128]{1,0:T(8,128)S(1)}, f32[512,128]{1,0:T(8,128)S(1)}, u32[]{:S(2)}, u32[]{:S(2)}) %collective-permute-start.16) | collective-permute-done | bytes 262176 | tf_op jit(solution)/shard_map/ppermute | solution.py:295
  128.3 2.3 %collective-permute-start.19 = (f32[256,128]{1,0:T(8,128)S(1)}, f32[256,128]{1,0:T(8,128)S(1)}, u32[]{:S(2)}, u32[]{:S(2)}) collective-permute-start(f32[256,128]{1,0:T(8,128)S(1)} %slice.60), channel_id=1, source_target_pairs={{0,3},{1,0},{2,1},{3,2},{4,7},{5,4},{6,5},{7,6},{8,11},{9,8},{10,9... | collective-permute-start | bytes 393224 | tf_op jit(solution)/shard_map/ppermute | solution.py:295
  131.1 2.3 %collective-permute-done.19 = f32[256,128]{1,0:T(8,128)S(1)} collective-permute-done((f32[256,128]{1,0:T(8,128)S(1)}, f32[256,128]{1,0:T(8,128)S(1)}, u32[]{:S(2)}, u32[]{:S(2)}) %collective-permute-start.19) | collective-permute-done | bytes 131104 | tf_op jit(solution)/shard_map/ppermute | solution.py:295
  133.4 1.4 collective-permute-done.18
  135.9 1.7 %collective-permute-start.20 = (f32[8,256,128]{2,1,0:T(8,128)}, f32[8,256,128]{2,1,0:T(8,128)}, u32[]{:S(2)}, u32[]{:S(2)}) collective-permute-start(f32[8,256,128]{2,1,0:T(8,128)} %constant_dynamic-slice_fusion), channel_id=1, source_target_pairs={{0,16},{1,17},{2,18},{3,19},{4,20},{5,21},{6,22},{7,23},{8,24},{9,... | collective-permute-start | bytes 3145736 | tf_op jit(solution)/shard_map/ppermute | solution.py:295
  137.7 2.7 %collective-permute-start.22 = (f32[2,512,128]{2,1,0:T(8,128)S(1)}, f32[2,512,128]{2,1,0:T(8,128)}, u32[]{:S(2)}, u32[]{:S(2)}) collective-permute-start(f32[2,512,128]{2,1,0:T(8,128)S(1)} %bitcast.28), channel_id=1, source_target_pairs={{0,12},{1,13},{2,14},{3,15},{4,0},{5,1},{6,2},{7,3},{8,4},{9,5},{1... | collective-permute-start | bytes 1572872 | tf_op jit(solution)/shard_map/ppermute | solution.py:295
  140.7 1.5 collective-permute-start.26
  142.2 1.6 prepare_update.1
  143.7 2.5 %update_near.1.refs_0_ = f32[512,1024]{1,0:T(8,128)S(1)} custom-call(s32[5]{0:T(128)S(1)} %stack.63.info, bf16[4,512,256]{2,1,0:T(8,128)(2,1)S(1)} %get-tuple-element.37.high_ref, bf16[4,512,256]{2,1,0:T(8,128)(2,1)S(1)} %get-tuple-element.38.low_ref, f32[2,512,128]{2,1,0:T(8,128)S(1)} %bitcast.33, f32[2,512,128]{2,1,0:T(8,128)S(1)} %bitcast.30), custom_call_target="tpu_custom_call" | custom-call | tf_op jit(solution)/shard_map/update_near/pallas_call | solution.py:271
  147.3 2.7 %collective-permute-start.24 = (f32[2,512,128]{2,1,0:T(8,128)}, f32[2,512,128]{2,1,0:T(8,128)S(1)}, u32[]{:S(2)}, u32[]{:S(2)}) collective-permute-start(f32[2,512,128]{2,1,0:T(8,128)} %collective-permute-done.22.refs_2_), channel_id=1, source_target_pairs={{0,12},{1,13},{2,14},{3,15},{4,0},{5,1},{6,2},{7,3},{8,4},{9,5},{1... | collective-permute-start | bytes 1572872 | tf_op jit(solution)/shard_map/ppermute | solution.py:295
  150.0 2.1 %collective-permute-done.25.refs_1_ = f32[2,512,128]{2,1,0:T(8,128)S(1)} collective-permute-done((f32[2,512,128]{2,1,0:T(8,128)S(1)}, f32[2,512,128]{2,1,0:T(8,128)S(1)}, u32[]{:S(2)}, u32[]{:S(2)}) %collective-permute-start.25) | collective-permute-done | bytes 524320 | tf_op jit(solution)/shard_map/ppermute | solution.py:295
  152.8 5.1 %update_next.1.refs_0_ = f32[512,1024]{1,0:T(8,128)S(1)} custom-call(s32[5]{0:T(128)S(1)} %stack.63.info, bf16[4,512,256]{2,1,0:T(8,128)(2,1)S(1)} %get-tuple-element.37.high_ref, bf16[4,512,256]{2,1,0:T(8,128)(2,1)S(1)} %get-tuple-element.38.low_ref, f32[512,1024]{1,0:T(8,128)S(1)} %update_near.1.refs_0_, ...), custom_call_target="tpu_custom_call", output_to_operand_aliasing={{}: (3, {})} | custom-call | tf_op jit(solution)/shard_map/update_next/pallas_call | solution.py:271
  158.4 2.6 %update_far.1 = f32[512,1024]{1,0:T(8,128)S(1)} custom-call(s32[5]{0:T(128)S(1)} %stack.63.info, bf16[4,512,256]{2,1,0:T(8,128)(2,1)S(1)} %get-tuple-element.37.high_ref, bf16[4,512,256]{2,1,0:T(8,128)(2,1)S(1)} %get-tuple-element.38.low_ref, f32[512,1024]{1,0:T(8,128)S(1)} %update_next.1.refs_0_, ...), custom_call_target="tpu_custom_call", output_to_operand_aliasing={{}: (3, {})} | custom-call | tf_op jit(solution)/shard_map/update_far/pallas_call | solution.py:271
  161.2 1.4 collective-permute-start.27
  162.6 2.3 %collective-permute-done.27 = f32[256,1024]{1,0:T(8,128)S(1)} collective-permute-done((f32[256,1024]{1,0:T(8,128)S(1)}, f32[256,1024]{1,0:T(8,128)S(1)}, u32[]{:S(2)}, u32[]{:S(2)}) %collective-permute-start.27) | collective-permute-done | bytes 1048608 | tf_op jit(solution)/shard_map/ppermute | solution.py:295
  (98 shorter events, 30.2 us)
Async XLA Ops:
  1.8 9.1 %collective-permute-start.5 = (f32[1024,128]{1,0:T(8,128)S(1)}, f32[1024,128]{1,0:T(8,128)S(1)}, u32[]{:S(2)}, u32[]{:S(2)}) collective-permute-start(f32[1024,128]{1,0:T(8,128)S(1)} %invert_diagonal.1.refs_0_), channel_id=1, source_target_pairs={{16,19},{17,16},{18,17},{19,18},{20,23},{21,20},{22,21},{23,22},{2... | collective-permute-start | bytes 1572872 | tf_op jit(solution)/shard_map/ppermute | solution.py:295
  2.5 13.3 %collective-permute-start = (f32[1024,128]{1,0:T(8,128)S(1)}, f32[1024,128]{1,0:T(8,128)S(1)}, u32[]{:S(2)}, u32[]{:S(2)}) collective-permute-start(f32[1024,128]{1,0:T(8,128)S(1)} %invert_diagonal.1.refs_0_), channel_id=1, source_target_pairs={{0,4},{1,5},{2,6},{3,7},{4,0},{5,1},{6,2},{7,3},{16,17},{17,18},{1... | collective-permute-start | bytes 1572872 | tf_op jit(solution)/shard_map/ppermute | solution.py:295
  3.2 12.6 %collective-permute-start.1 = (f32[1024,128]{1,0:T(8,128)S(1)}, f32[1024,128]{1,0:T(8,128)S(1)}, u32[]{:S(2)}, u32[]{:S(2)}) collective-permute-start(f32[1024,128]{1,0:T(8,128)S(1)} %invert_diagonal.1.refs_0_), channel_id=1, source_target_pairs={{16,20},{17,21},{18,22},{19,23},{20,16},{21,17},{22,18},{23,19},{2... | collective-permute-start | bytes 1572872 | tf_op jit(solution)/shard_map/ppermute | solution.py:295
  4.7 11.2 %all-to-all-start = ((f32[8,64,128]{2,1,0:T(8,128)}), f32[8,64,128]{2,1,0:T(8,128)S(1)}, u32[]{:S(2)}, u32[]{:S(2)}) async-start(f32[8,64,128]{2,1,0:T(8,128)} %arrange_rhs.1), calls=%async_computation | async-start | bytes 524288 | tf_op jit(solution)/shard_map/all_to_all | solution.py:368
  10.9 5.8 %collective-permute-start.6 = (f32[512,128]{1,0:T(8,128)S(1)}, f32[512,128]{1,0:T(8,128)S(1)}, u32[]{:S(2)}, u32[]{:S(2)}) collective-permute-start(f32[512,128]{1,0:T(8,128)S(1)} %slice.64), channel_id=1, source_target_pairs={{16,19},{17,16},{18,17},{19,18},{20,23},{21,20},{22,21},{23,22},{2... | collective-permute-start | bytes 786440 | tf_op jit(solution)/shard_map/ppermute | solution.py:295
  16.8 3.9 %collective-permute-start.3 = (f32[1536,128]{1,0:T(8,128)S(1)}, f32[1536,128]{1,0:T(8,128)S(1)}, u32[]{:S(2)}, u32[]{:S(2)}) collective-permute-start(f32[1536,128]{1,0:T(8,128)S(1)} %pad_maximum_fusion.refs_0_.refs_2_), channel_id=1, source_target_pairs={{0,1},{1,2},{2,3},{3,0},{4,5},{5,6},{6,7},{7,4},{16,20},{17,21},{1... | collective-permute-start | bytes 2359304 | tf_op jit(solution)/shard_map/ppermute | solution.py:295
  17.8 5.2 %collective-permute-start.7 = (f32[1536,128]{1,0:T(8,128)S(1)}, f32[1536,128]{1,0:T(8,128)S(1)}, u32[]{:S(2)}, u32[]{:S(2)}) collective-permute-start(f32[1536,128]{1,0:T(8,128)S(1)} %pad_maximum_fusion.1.refs_3_), channel_id=1, source_target_pairs={{0,3},{1,0},{2,1},{3,2},{4,7},{5,4},{6,5},{7,6},{16,20},{17,21},{1... | collective-permute-start | bytes 2359304 | tf_op jit(solution)/shard_map/ppermute | solution.py:295
  18.5 2.2 %collective-permute-start.4 = (f32[512,128]{1,0:T(8,128)S(1)}, f32[512,128]{1,0:T(8,128)S(1)}, u32[]{:S(2)}, u32[]{:S(2)}) collective-permute-start(f32[512,128]{1,0:T(8,128)S(1)} %bitcast.34), channel_id=1, source_target_pairs={{8,4},{9,5},{10,6},{11,7},{12,0},{13,1},{14,2},{15,3},{24,20},{25,... | collective-permute-start | bytes 786440 | tf_op jit(solution)/shard_map/ppermute | solution.py:295
  21.6 5.6 %collective-permute-start.8 = (f32[768,128]{1,0:T(8,128)}, f32[768,128]{1,0:T(8,128)}, u32[]{:S(2)}, u32[]{:S(2)}) collective-permute-start(f32[768,128]{1,0:T(8,128)} %slice.53), channel_id=1, source_target_pairs={{0,1},{1,2},{2,3},{3,0},{4,5},{5,6},{6,7},{7,4}} | collective-permute-start | bytes 1179656 | tf_op jit(solution)/shard_map/ppermute | solution.py:295
  23.7 3.5 %collective-permute-start.9 = (f32[768,128]{1,0:T(8,128)}, f32[768,128]{1,0:T(8,128)}, u32[]{:S(2)}, u32[]{:S(2)}) collective-permute-start(f32[768,128]{1,0:T(8,128)} %slice.65), channel_id=1, source_target_pairs={{0,3},{1,0},{2,1},{3,2},{4,7},{5,4},{6,5},{7,6}} | collective-permute-start | bytes 1179656 | tf_op jit(solution)/shard_map/ppermute | solution.py:295
  39.5 65.5 %collective-permute-start.14 = (f32[512,128]{1,0:T(8,128)S(1)}, f32[512,128]{1,0:T(8,128)S(1)}, u32[]{:S(2)}, u32[]{:S(2)}) collective-permute-start(f32[512,128]{1,0:T(8,128)S(1)} %fusion.1), channel_id=1, source_target_pairs={{0,96},{1,97},{2,98},{3,99},{4,100},{5,101},{6,102},{7,103},{8,104... | collective-permute-start | bytes 786440 | tf_op jit(solution)/shard_map/ppermute | solution.py:295
  105.0 29.8 %all-to-all-start.1 = ((f32[16,256,128]{2,1,0:T(8,128)}), f32[16,256,128]{2,1,0:T(8,128)S(1)}, u32[]{:S(2)}, u32[]{:S(2)}) async-start(f32[16,256,128]{2,1,0:T(8,128)} %copy-done), calls=%async_computation.1 | async-start | bytes 4194304 | tf_op jit(solution)/shard_map/all_to_all | solution.py:307
  112.5 15.6 %collective-permute-start.16 = (f32[512,128]{1,0:T(8,128)S(1)}, f32[512,128]{1,0:T(8,128)S(1)}, u32[]{:S(2)}, u32[]{:S(2)}) collective-permute-start(f32[512,128]{1,0:T(8,128)S(1)} %add_select_fusion), channel_id=1, source_target_pairs={{0,1},{1,2},{2,3},{3,0},{4,5},{5,6},{6,7},{7,4},{8,9},{9,10},{10,1... | collective-permute-start | bytes 786440 | tf_op jit(solution)/shard_map/ppermute | solution.py:295
  112.7 15.6 %collective-permute-start.17 = (f32[512,128]{1,0:T(8,128)S(1)}, f32[512,128]{1,0:T(8,128)S(1)}, u32[]{:S(2)}, u32[]{:S(2)}) collective-permute-start(f32[512,128]{1,0:T(8,128)S(1)} %add_select_fusion), channel_id=1, source_target_pairs={{0,3},{1,0},{2,1},{3,2},{4,7},{5,4},{6,5},{7,6},{8,11},{9,8},{10,9... | collective-permute-start | bytes 786440 | tf_op jit(solution)/shard_map/ppermute | solution.py:295
  128.3 5.1 %collective-permute-start.19 = (f32[256,128]{1,0:T(8,128)S(1)}, f32[256,128]{1,0:T(8,128)S(1)}, u32[]{:S(2)}, u32[]{:S(2)}) collective-permute-start(f32[256,128]{1,0:T(8,128)S(1)} %slice.60), channel_id=1, source_target_pairs={{0,3},{1,0},{2,1},{3,2},{4,7},{5,4},{6,5},{7,6},{8,11},{9,8},{10,9... | collective-permute-start | bytes 393224 | tf_op jit(solution)/shard_map/ppermute | solution.py:295
  130.6 4.2 %collective-permute-start.18 = (f32[256,128]{1,0:T(8,128)S(1)}, f32[256,128]{1,0:T(8,128)S(1)}, u32[]{:S(2)}, u32[]{:S(2)}) collective-permute-start(f32[256,128]{1,0:T(8,128)S(1)} %slice.59), channel_id=1, source_target_pairs={{0,1},{1,2},{2,3},{3,0},{4,5},{5,6},{6,7},{7,4},{8,9},{9,10},{10,1... | collective-permute-start | bytes 393224 | tf_op jit(solution)/shard_map/ppermute | solution.py:295
  135.9 6.3 %collective-permute-start.20 = (f32[8,256,128]{2,1,0:T(8,128)}, f32[8,256,128]{2,1,0:T(8,128)}, u32[]{:S(2)}, u32[]{:S(2)}) collective-permute-start(f32[8,256,128]{2,1,0:T(8,128)} %constant_dynamic-slice_fusion), channel_id=1, source_target_pairs={{0,16},{1,17},{2,18},{3,19},{4,20},{5,21},{6,22},{7,23},{8,24},{9,... | collective-permute-start | bytes 3145736 | tf_op jit(solution)/shard_map/ppermute | solution.py:295
  137.6 9.7 %collective-permute-start.21 = (f32[2,512,128]{2,1,0:T(8,128)S(1)}, f32[2,512,128]{2,1,0:T(8,128)}, u32[]{:S(2)}, u32[]{:S(2)}) collective-permute-start(f32[2,512,128]{2,1,0:T(8,128)S(1)} %bitcast.31), channel_id=1, source_target_pairs={{0,4},{1,5},{2,6},{3,7},{4,8},{5,9},{6,10},{7,11},{8,12},{9,13},{1... | collective-permute-start | bytes 1572872 | tf_op jit(solution)/shard_map/ppermute | solution.py:295
  137.7 9.6 %collective-permute-start.22 = (f32[2,512,128]{2,1,0:T(8,128)S(1)}, f32[2,512,128]{2,1,0:T(8,128)}, u32[]{:S(2)}, u32[]{:S(2)}) collective-permute-start(f32[2,512,128]{2,1,0:T(8,128)S(1)} %bitcast.28), channel_id=1, source_target_pairs={{0,12},{1,13},{2,14},{3,15},{4,0},{5,1},{6,2},{7,3},{8,4},{9,5},{1... | collective-permute-start | bytes 1572872 | tf_op jit(solution)/shard_map/ppermute | solution.py:295
  140.5 11.6 %collective-permute-start.25 = (f32[2,512,128]{2,1,0:T(8,128)S(1)}, f32[2,512,128]{2,1,0:T(8,128)S(1)}, u32[]{:S(2)}, u32[]{:S(2)}) collective-permute-start(f32[2,512,128]{2,1,0:T(8,128)S(1)} %bitcast.32), channel_id=1, source_target_pairs={{0,12},{1,13},{2,14},{3,15},{4,0},{5,1},{6,2},{7,3},{8,4},{9,5},{1... | collective-permute-start | bytes 1572872 | tf_op jit(solution)/shard_map/ppermute | solution.py:295
  140.7 12.1 %collective-permute-start.26 = (f32[2,512,128]{2,1,0:T(8,128)S(1)}, f32[2,512,128]{2,1,0:T(8,128)S(1)}, u32[]{:S(2)}, u32[]{:S(2)}) collective-permute-start(f32[2,512,128]{2,1,0:T(8,128)S(1)} %bitcast.29), channel_id=1, source_target_pairs={{0,4},{1,5},{2,6},{3,7},{4,8},{5,9},{6,10},{7,11},{8,12},{9,13},{1... | collective-permute-start | bytes 1572872 | tf_op jit(solution)/shard_map/ppermute | solution.py:295
  147.3 11.1 %collective-permute-start.23 = (f32[2,512,128]{2,1,0:T(8,128)}, f32[2,512,128]{2,1,0:T(8,128)S(1)}, u32[]{:S(2)}, u32[]{:S(2)}) collective-permute-start(f32[2,512,128]{2,1,0:T(8,128)} %collective-permute-done.21.refs_3_), channel_id=1, source_target_pairs={{0,4},{1,5},{2,6},{3,7},{4,8},{5,9},{6,10},{7,11},{8,12},{9,13},{1... | collective-permute-start | bytes 1572872 | tf_op jit(solution)/shard_map/ppermute | solution.py:295
  147.3 11.1 %collective-permute-start.24 = (f32[2,512,128]{2,1,0:T(8,128)}, f32[2,512,128]{2,1,0:T(8,128)S(1)}, u32[]{:S(2)}, u32[]{:S(2)}) collective-permute-start(f32[2,512,128]{2,1,0:T(8,128)} %collective-permute-done.22.refs_2_), channel_id=1, source_target_pairs={{0,12},{1,13},{2,14},{3,15},{4,0},{5,1},{6,2},{7,3},{8,4},{9,5},{1... | collective-permute-start | bytes 1572872 | tf_op jit(solution)/shard_map/ppermute | solution.py:295
  161.2 3.7 %collective-permute-start.27 = (f32[256,1024]{1,0:T(8,128)S(1)}, f32[256,1024]{1,0:T(8,128)S(1)}, u32[]{:S(2)}, u32[]{:S(2)}) collective-permute-start(f32[256,1024]{1,0:T(8,128)S(1)} %slice.71), channel_id=1, source_target_pairs={{0,16},{1,17},{2,18},{3,19},{4,20},{5,21},{6,22},{7,23},{8,24},{9,... | collective-permute-start | bytes 3145736 | tf_op jit(solution)/shard_map/ppermute | solution.py:295
  (18 other events, 37.8 us)
